TPU v7x, 32 devices: a whole 2x2x4 slice. The times are simulated.
32 devices in a mesh: dp: 32 (over z, y, x, core).
Axes of the slice: x: 2, y: 2, z: 4, core: 2. Of those that a mesh axis runs over, the one named last changes fastest.
Arguments:
- hidden_in: bfloat16 [4096, 1024], P('dp'), may hold values from -6 to 6
- seq_start: int32 [4096], P('dp'), may hold values from 0 to 1, as said below
- mixer_gain: bfloat16 [1, 1024], P(None, 'dp'), may hold values from 0.5 to 1.5
- in_weight: bfloat16 [1, 1024, 3072], P(None, 'dp'), may hold values from -0.1875 to 0.1875
- conv_weight: bfloat16 [1, 1024, 3], P(None, 'dp'), may hold values from -3.5 to 3.5
- out_weight: bfloat16 [1, 1024, 1024], P(None, 'dp'), may hold values from -0.1875 to 0.1875
- ffn_gain: bfloat16 [1, 1024], P(None, 'dp'), may hold values from 0.5 to 1.5
- gate_weight: bfloat16 [1, 1024, 4608], P(None, 'dp'), may hold values from -0.1875 to 0.1875
- up_weight: bfloat16 [1, 1024, 4608], P(None, 'dp'), may hold values from -0.1875 to 0.1875
- down_weight: bfloat16 [1, 4608, 1024], P(None, 'dp'), may hold values from -0.09375 to 0.09375
- cotangent: bfloat16 [4096, 1024], P('dp'), may hold values from -6 to 6
Outputs:
- hidden_out: bfloat16 [4096, 1024], P('dp')
- grad_hidden: float32 [4096, 1024], P('dp')
- grad_mixer_gain: float32 [1, 1024], P(None, 'dp')
- grad_in_weight: float32 [1, 1024, 3072], P(None, 'dp')
- grad_conv_weight: float32 [1, 1024, 3], P(None, 'dp')
- grad_out_weight: float32 [1, 1024, 1024], P(None, 'dp')
- grad_ffn_gain: float32 [1, 1024], P(None, 'dp')
- grad_gate_weight: float32 [1, 1024, 4608], P(None, 'dp')
- grad_up_weight: float32 [1, 1024, 4608], P(None, 'dp')
- grad_down_weight: float32 [1, 4608, 1024], P(None, 'dp')
Inputs may be any that keep to these rules, and one draw needn't show every extreme that they name: `seq_start`: 1 marks the first token of a sequence; token 0 is marked, and 4 tokens are marked in all.
All inputs are finite; a program needn't handle non-finite values.
Results may differ from a plain program's by a relative error of at most 0.0098.
Values may be sent and summed in bfloat16 or wider, within the bound.
No kernel may reach another device: no remote copies, remote signals or barrier semaphores. Data moves between devices by JAX's collectives and lax.ppermute only.
A program may use at most 256 MiB of HBM per device.

v0:
```python
import jax
import jax.numpy as jnp
from jax import lax
from jax.experimental import pallas as pl
from jax.experimental.pallas import tpu as pltpu
from jax.sharding import PartitionSpec as P

epsilon = 1e-05
TEAM = 8
HALO = 16
WIDE = jnp.float32
NARROW = jnp.bfloat16


def dot(left, right, contract):
    return lax.dot_general(left, right, (contract, ((), ())), preferred_element_type=WIDE)


def fetch(pairs, sems):
    copies = [pltpu.make_async_copy(a, b, sems.at[i]) for i, (a, b) in enumerate(pairs)]
    for copy in copies:
        copy.start()
    return copies


def shape(kind, *sizes):
    return jax.ShapeDtypeStruct(sizes, kind)


def call(kernel, name, out_shape, operands, scratch=(), flops=0, in_place=False):
    places = {}
    if in_place:
        places["in_specs"] = [pl.BlockSpec(memory_space=pl.ANY)] * len(operands)
    size = sum(x.size * x.dtype.itemsize for x in operands)
    return pl.pallas_call(
        kernel,
        out_shape=out_shape,
        scratch_shapes=list(scratch),
        compiler_params=pltpu.CompilerParams(vmem_limit_bytes=60 * 2**20),
        cost_estimate=pl.CostEstimate(flops=flops, bytes_accessed=size, transcendentals=0),
        name=name,
        **places,
    )(*operands)


def result_of(results, at):
    return lambda k: results[k][at]


class Job:
    def __init__(self, steps):
        self.steps = steps
        self.result = None
        self.open = True
        self.request = None
        self.held = False
        self.send(None)

    def send(self, value):
        try:
            self.request = self.steps.send(value)
        except StopIteration as stop:
            self.result, self.open, self.request = stop.value, False, None


class Net:
    def __init__(self):
        self.count = lax.axis_size("dp")
        self.teams = self.count // TEAM
        self.index = lax.axis_index("dp")
        self.place = self.index % TEAM
        self.team = self.index // TEAM
        self.core = self.index % 2
        self.peer = (self.index // 2) % 4
        self.jobs = []
        self.waiting = []
        self.gate = []
        self.extra = []

    def pairs(self, move):
        if move[0] == "swap":
            return [(i, i ^ move[1]) for i in range(self.count)]
        if move[0] == "ring":
            return [(i, (i + move[1] * TEAM) % self.count) for i in range(self.count)]
        if move[0] == "mixed":
            return [(i, i ^ (2 if i % 2 == 0 else 4)) for i in range(self.count)]
        return [(i, i - TEAM) for i in range(TEAM, self.count)]

    def do(self, call, *operands):
        def steps():
            (got,) = yield [(operands, ("call", call))]
            return got

        return self.spawn(steps())

    def spawn(self, steps):
        job = Job(steps)
        if job.open:
            self.jobs.append(job)
        return job

    def need(self, *values):
        self.extra.extend(values)

    def while_moving(self, values):
        mark = [got for move, got in self.raw if move == ("swap", 1)][0]
        return lax.optimization_barrier((values, mark))[0]

    def later(self, *values):
        return lax.optimization_barrier((values, self.gate))[0]

    def step(self, times=1):
        for _ in range(times):
            self.one_step()

    def one_step(self):
        ready = [job for job in self.jobs if job.request is not None and not job.held]
        values = [move[0] for job in ready for move in job.request]
        self.raw = []
        if values or self.waiting:
            values, _ = lax.optimization_barrier((values, (self.gate, self.extra)))
            self.extra = []
            at = 0
            for job in ready:
                span = 1
                got = []
                moves = job.request
                for move in moves:
                    if len(move) > 2:
                        span = move[2]
                    if move[1][0] == "call":
                        got.append(move[1][1](*values[at]))
                    else:
                        got.append(lax.ppermute(values[at], "dp", self.pairs(move[1])))
                    at += 1
                job.request = None
                self.raw.extend(zip([move[1] for move in moves], got))
                self.waiting.append([span, job, got])
        for entry in self.waiting:
            entry[0] -= 1
        done = [entry for entry in self.waiting if entry[0] <= 0]
        self.waiting = [entry for entry in self.waiting if entry[0] > 0]
        results = lax.optimization_barrier([entry[2] for entry in done])
        self.gate = results
        for (_, job, _), got in zip(done, results):
            job.send(got)
        self.jobs = [job for job in self.jobs if job.open]

    def until(self, *jobs):
        while any(job.open for job in jobs):
            self.one_step()
        return [job.result for job in jobs] if len(jobs) > 1 else jobs[0].result


    def blocks(self, value):
        across, along, twin = yield [
            (value, ("swap", 2)),
            (value, ("swap", 4)),
            (value, ("swap", 1)),
        ]
        corner, across_twin, along_twin = yield [
            (jnp.where(self.core == 0, along, across), ("mixed",)),
            (across, ("swap", 1)),
            (along, ("swap", 1)),
        ]
        (corner_twin,) = yield [(corner, ("swap", 1))]
        return [value, twin, across, across_twin, along, along_twin, corner, corner_twin]

    def team_sum(self, even, odd):
        arrived, even = yield [(odd, ("swap", 1)), (even[1], ("call", even[0]))]
        ((own, across, along, corner),) = yield [((even, arrived), ("call", fold_twin))]
        (by,) = yield [(corner, ("mixed",))]
        across, along = fold_corner(across, along, by)
        from_across, from_along = yield [(across, ("swap", 2)), (along, ("swap", 4))]
        return own, from_across, from_along

    def exchange(self, blocks):
        groups = [[base + q for q in range(TEAM)] for base in range(0, self.count, TEAM)]
        return lax.all_to_all(blocks, "dp", 0, 0, axis_index_groups=groups, tiled=True)

    def line_exchange(self, blocks):
        groups = [
            [TEAM * z + 2 * u + c for z in range(self.teams) for c in range(2)] for u in range(4)
        ]
        return lax.all_to_all(blocks, "dp", 0, 0, axis_index_groups=groups, tiled=True)

    def peer_groups(self):
        chips = range(0, self.count, TEAM)
        return [[base + c + 2 * u for u in range(4)] for base in chips for c in range(2)]

    def ring_blocks(self, value, found):
        moving = value
        for step in range(self.teams):
            moves = [(moving, ("swap", 1))]
            if step < self.teams - 1:
                moves.append((moving, ("ring", 1)))
            got = yield moves
            found.append((moving, got[0]))
            moving = got[-1]

    def ring_through(self, value, found, results, compute):
        teams = self.teams
        moving, total, twins = value, None, {}
        for step in range(teams + 3):
            moves, tags = [], []
            k, ready = (step - 2) % teams, (step - 1) % teams
            if step < teams:
                moves.append((moving, ("swap", 1)))
                tags.append("twin")
                if step < teams - 1:
                    moves.append((moving, ("ring", 1)))
                    tags.append("next")
            if step > 2:
                moves.append((results[k][3], ("swap", 1)))
                tags.append("back")
            hop = step - 3
            if 1 <= hop <= teams - 1:
                mine = results[hop][2] + twins[hop].astype(WIDE)
                if total is not None:
                    mine = mine + total.astype(WIDE)
                moves.append((mine.astype(NARROW), ("ring", 1)))
                tags.append("total")
            if 2 <= step <= teams + 1:
                call, operands = compute(ready, found[ready])
                moves.append((operands, ("call", call)))
                tags.append("work")
            got = dict(zip(tags, (yield moves)))
            if "twin" in got:
                found.append((moving, got["twin"]))
                moving = got.get("next")
            if "back" in got:
                twins[k] = got["back"]
            if "work" in got:
                results[ready] = got["work"]
            total = got.get("total", total)
        return results[0][2], twins[0], total

    def ring_sum(self, own, odd):
        order = list(range(1, self.teams)) + [0]
        total = None
        (twin,) = yield [(odd(order[0]), ("swap", 1))]
        for step, k in enumerate(order):
            if k == 0:
                return own(k), twin, total
            mine = own(k) + twin.astype(WIDE)
            if total is not None:
                mine = mine + total.astype(WIDE)
            total, twin = yield [
                (mine.astype(NARROW), ("ring", 1)),
                (odd(order[step + 1]), ("swap", 1)),
            ]

    def line_blocks(self, value):
        found = [value]
        for _ in range(1, self.teams):
            (value,) = yield [(value, ("ring", 1))]
            found.append(value)
        return found

    def line_send(self, parts, span=1):
        return (yield [(part, ("ring", k + 1), span) for k, part in enumerate(parts)])

    def line_sum(self, shares):
        total = shares[-1].astype(NARROW)
        for share in reversed(shares[:-1]):
            (got,) = yield [(total, ("ring", 1))]
            total = share + got.astype(WIDE)
            total = total if share is shares[0] else total.astype(NARROW)
        return total

    def line_all(self, value, span=1):
        return [value] + (yield from self.line_send([value] * (self.teams - 1), span))


def scale_of(values):
    return lax.rsqrt(jnp.mean(values * values, axis=1, keepdims=True) + epsilon)


def norm_back(upstream, normed, scaler, gain):
    scaled = upstream * gain
    return scaler * (scaled - normed * jnp.mean(scaled * normed, axis=1, keepdims=True))


def where_am_i():
    index = lax.axis_index("dp")
    return index % TEAM, index // TEAM


def at(start, size, step=16):
    return pl.ds(pl.multiple_of(start, step), size)


def fold_twin(even, arrived):
    rows, width = even.shape[0] // 4, even.shape[1]

    def kernel(even, arrived, own, across, along, corner):
        for k, out in enumerate((own, across, along, corner)):
            span = slice(k * rows, (k + 1) * rows)
            out[...] = (even[span, :] + arrived[span, :].astype(WIDE)).astype(out.dtype)

    outs = (shape(WIDE, rows, width),) * 3 + (shape(NARROW, rows, width),)
    return call(kernel, "fold_twin", outs, (even, arrived))


def fold_corner(across, along, by):
    def kernel(across, along, by, out_across, out_along):
        even_core = lax.axis_index("dp") % 2 == 0
        by = by[...].astype(WIDE)
        none = jnp.zeros_like(by)
        out_across[...] = (across[...] + jnp.where(even_core, none, by)).astype(NARROW)
        out_along[...] = (along[...] + jnp.where(even_core, by, none)).astype(NARROW)

    return call(kernel, "fold_corner", (shape(NARROW, *by.shape),) * 2, (across, along, by))


def pieces(ffpart, even, own):
    runs = []
    for u in range(4):
        for start, stop in ((0, even), (even, own)):
            low, high = max(u * ffpart, start), min((u + 1) * ffpart, stop)
            if low < high:
                at_gate = low if start == 0 else 2 * even + low - even
                at_up = even + low if start == 0 else own + low
                runs.append((u, low, high, at_gate, at_up))
    return runs


def in_prepare(weight, gains, marks, taps, teams):
    part, width = weight.shape
    features = width // 3
    channels = features // TEAM
    slots = max(128, TEAM * part) // part

    def kernel(weight, gain_one, gain_two, marks, taps, out, wide, small):
        index = lax.axis_index("dp")
        whole = weight[...].astype(WIDE)
        small[...] = jnp.zeros_like(small)
        for slot in range(slots):
            mine = lax.rem(index, slots) == slot
            for row, gain in enumerate((gain_one, gain_two)):
                value = gain[...].astype(WIDE)
                value = jnp.where(mine, value, jnp.zeros_like(value))
                small[row : row + 1, slot * part : (slot + 1) * part] = value
        small[0:1, 2 * channels :] = marks[...].astype(WIDE)
        for slot in range(teams):
            value = taps[...].astype(WIDE)
            value = jnp.where(index // TEAM == slot, value, jnp.zeros_like(value))
            for k in range(3):
                to = k * channels + slot * part
                small[2:3, to : to + part] = value[k : k + 1, :]
        for p in range(TEAM):
            for k in range(3):
                for z in range(teams):
                    source = k * features + (z * TEAM + p) * part
                    to = k * channels + z * part
                    wide[:, to : to + part] = whole[:, source : source + part]
            out[p, :part, :] = wide[...].astype(NARROW)
            out[p, part:, :] = small[...].astype(NARROW)

    return call(
        kernel,
        "in_prepare",
        shape(NARROW, TEAM, part + 8, 3 * channels),
        (weight, *gains, marks, taps),
        [pltpu.VMEM((part, 3 * channels), WIDE), pltpu.VMEM((8, 3 * channels), WIDE)],
    )


def in_finish(blocks, weight, gain, teams):
    part, width = weight.shape
    features = width // 3
    channels = features // TEAM

    def kernel(blocks, weight, gain, out, gain_grad):
        for p in range(TEAM):
            block = blocks[p].astype(WIDE)
            for k in range(3):
                for z in range(teams):
                    to = k * features + (z * TEAM + p) * part
                    source = k * channels + z * part
                    out[:, to : to + part] = block[:, source : source + part]
        product = jnp.sum(weight[...].astype(WIDE) * out[...], axis=1, keepdims=True)
        gain_grad[...] = product / gain[...].astype(WIDE)

    outs = (shape(WIDE, part, width), shape(WIDE, part, 1))
    return call(kernel, "in_finish", outs, (blocks, weight, gain))


def pair_prepare(gate, up, teams):
    part, inner = gate.shape
    ffpart = inner // (TEAM * teams)
    own = 4 * ffpart
    even = own // 128 * 128
    runs = pieces(ffpart, even, own)

    def kernel(gate, up, out, wide):
        gates, ups = gate[...].astype(WIDE), up[...].astype(WIDE)
        for z in range(teams):
            for c in range(2):
                for u, low, high, at_gate, at_up in runs:
                    source = ((z * 4 + u) * 2 + c) * ffpart + low - u * ffpart
                    size = high - low
                    wide[:, at_gate : at_gate + size] = gates[:, source : source + size]
                    wide[:, at_up : at_up + size] = ups[:, source : source + size]
                out[2 * z + c] = wide[...].astype(NARROW)

    out = shape(NARROW, 2 * teams, part, 2 * own)
    scratch = [pltpu.VMEM((part, 2 * own), WIDE)]
    return call(kernel, "pair_prepare", out, (gate, up), scratch)


def pair_finish(blocks, gate, up, gain, teams):
    part, inner = gate.shape
    ffpart = inner // (TEAM * teams)
    own = 4 * ffpart
    even = own // 128 * 128
    runs = pieces(ffpart, even, own)

    def kernel(blocks, gate, up, gain, gate_grad, up_grad, gain_grad):
        for z in range(teams):
            for c in range(2):
                block = blocks[2 * z + c].astype(WIDE)
                for u, low, high, at_gate, at_up in runs:
                    to = ((z * 4 + u) * 2 + c) * ffpart + low - u * ffpart
                    size = high - low
                    gate_grad[:, to : to + size] = block[:, at_gate : at_gate + size]
                    up_grad[:, to : to + size] = block[:, at_up : at_up + size]
        product = gate[...].astype(WIDE) * gate_grad[...] + up[...].astype(WIDE) * up_grad[...]
        gain_grad[...] = jnp.sum(product, axis=1, keepdims=True) / gain[...].astype(WIDE)

    outs = (shape(WIDE, part, inner), shape(WIDE, part, inner), shape(WIDE, part, 1))
    return call(kernel, "pair_finish", outs, (blocks, gate, up, gain))


def mixer_forward(blocks, before, weights):
    rows, features = blocks[0].shape
    tokens = TEAM * rows
    teams = len(weights)
    share = features // teams
    channels = weights[0].shape[2] // 3
    part = share // TEAM

    def kernel(*refs):
        blocks, refs = refs[:TEAM], refs[TEAM:]
        before, refs = refs[0], refs[1:]
        weights, refs = refs[:teams], refs[teams:]
        normed, mixed, gated, conv, mixer_in, in_own, gain, gain_two, taps, keeps = refs[:10]
        hs, small, sems = refs[10:]
        place, team = where_am_i()
        copies = []
        for k in range(teams):
            owner = lax.rem(team - k + teams, teams)
            for p in range(TEAM):
                to = in_own.at[at(owner * share + p * part, part, 8), :]
                copies.append((weights[k].at[p, :part, :], to))
            copies.append((weights[k].at[:, part:, :], small.at[k]))
        for m in range(TEAM):
            copies.append((blocks[m], hs.at[at(HALO + (place ^ m) * rows, rows), :]))
        copies.append((before, hs.at[:HALO, :]))
        for copy in fetch(copies, sems):
            copy.wait()
        first = hs[:HALO, :]
        hs[:HALO, :] = jnp.where(team > 0, first, jnp.zeros_like(first))
        total = jnp.zeros((1, 3 * channels), WIDE)
        gain[...] = jnp.zeros_like(gain)
        gain_two[...] = jnp.zeros_like(gain_two)
        span = max(share, 128)
        for k in range(teams):
            owner = lax.rem(team - k + teams, teams)
            both = sum(small[k, p].astype(WIDE) for p in range(TEAM))
            one, two = both[0:1], both[1:2]
            total = total + small[k, place].astype(WIDE)[2:3]
            to = at(owner * share // span * span, span, 128)
            gain[:, to] = gain[:, to] + one[:, :span]
            gain_two[:, to] = gain_two[:, to] + two[:, :span]
        taps[...] = jnp.zeros_like(taps)
        for k in range(3):
            taps[k : k + 1, :] = total[:, k * channels : (k + 1) * channels]
        marks = [1.0 - small[0, p].astype(WIDE)[0:1, 2 * channels :] for p in range(TEAM)]
        keep = jnp.concatenate([mark.reshape(rows, 1) for mark in marks], 0)
        keeps[8:, 0:1] = keep
        last = 1.0 - small[1, TEAM - 1].astype(WIDE)[0:1, 3 * channels - 1 :]
        keeps[7:8, 0:1] = last
        keeps[8:, 1:2] = keep * keeps[7 : 7 + tokens, 0:1]
        scale = gain[...]

        def norm(start, size):
            values = hs[at(start, size), :].astype(WIDE)
            values = values * scale_of(values) * scale
            normed[at(start, size), :] = values.astype(NARROW)

        norm(0, HALO)

        @pl.loop(0, TEAM)
        def _(step):
            norm(HALO + step * rows, rows)

        mixed[...] = dot(normed[...], in_own[...], ((1,), (0,)))
        gated[...] = (mixed[:, :channels] * mixed[:, 2 * channels :]).astype(NARROW).astype(WIDE)
        conv_out = (
            taps[2:3, :] * gated[HALO:, :]
            + taps[1:2, :] * (keeps[8:, 0:1] * gated[HALO - 1 : HALO - 1 + tokens, :])
            + taps[0:1, :] * (keeps[8:, 1:2] * gated[HALO - 2 : HALO - 2 + tokens, :])
        )
        conv[...] = conv_out
        mixer_in[...] = (mixed[HALO:, channels : 2 * channels] * conv_out).astype(NARROW)

    outs = (
        shape(NARROW, HALO + tokens, features),
        shape(WIDE, HALO + tokens, 3 * channels),
        shape(WIDE, HALO + tokens, channels),
        shape(WIDE, tokens, channels),
        shape(NARROW, tokens, channels),
        shape(NARROW, features, 3 * channels),
        shape(WIDE, 1, features),
        shape(WIDE, 1, features),
        shape(WIDE, 8, channels),
        shape(WIDE, 8 + tokens, 2),
    )
    return call(
        kernel,
        "mixer_forward",
        outs,
        (*blocks, before, *weights),
        [
            pltpu.VMEM((HALO + tokens, features), NARROW),
            pltpu.VMEM((teams, TEAM, 8, 3 * channels), NARROW),
            pltpu.SemaphoreType.DMA(((teams + 1) * (TEAM + 1),)),
        ],
        2 * tokens * features * 3 * channels,
        in_place=True,
    )


def out_project(mixer_local, out_blocks, hidden, gain):
    rows, features = hidden.shape

    def kernel(local, *refs):
        out_blocks, (hidden, gain, resid, ffn_in) = refs[:TEAM], refs[TEAM:]
        place, _ = where_am_i()
        total = hidden[...].astype(WIDE)
        for m in range(TEAM):
            total = total + dot(local[place ^ m], out_blocks[m][...], ((1,), (0,)))
        resid[...] = total
        ffn_in[...] = (total * scale_of(total) * gain[...]).astype(NARROW)

    outs = (shape(WIDE, rows, features), shape(NARROW, rows, features))
    return call(
        kernel,
        "out_project",
        outs,
        (mixer_local, *out_blocks, hidden, gain),
        flops=2 * rows * features * features,
    )


def ffn_parts(gate, up, grad):
    sigmoid = 1.0 / (1.0 + jnp.exp(-gate))
    scaled = gate * sigmoid
    gate_grad = grad * up * sigmoid * (1.0 + gate * (1.0 - sigmoid))
    return scaled * up, gate_grad, grad * scaled


def ffn_block(inputs, upstream, pair, down):
    rows, features = inputs[0].shape
    own = down.shape[0]
    even = own // 128 * 128
    width = own - even
    total = 2 * rows
    teams, size = pair.shape[1:3]

    def kernel(*refs):
        x0, x1, g0, g1, pair_in, down_in, act, grads, back0, back1, out0, out1 = refs[:12]
        xs, gs, pair, down, last, sems = refs[12:]
        first = [(x0, xs.at[:rows, :]), (x1, xs.at[rows:, :])]
        for u in range(4):
            for z in range(teams):
                to = (z * 4 + u) * size
                first.append((pair_in.at[u, z], pair.at[to : to + size, :]))
        second = [(g0, gs.at[:rows, :]), (g1, gs.at[rows:, :]), (down_in, down)]
        copies = fetch(first + second, sems)
        for copy in copies[: len(first)]:
            copy.wait()
        x = xs[...]
        gate = dot(x, pair[:, :even], ((1,), (0,)))
        up = dot(x, pair[:, even : 2 * even], ((1,), (0,)))
        for copy in copies[len(first) :]:
            copy.wait()
        g = gs[...]
        grad = dot(g, down[:even, :], ((1,), (1,)))
        value, gate_grad, up_grad = ffn_parts(gate, up, grad)
        act[:, :even] = value.astype(NARROW)
        grads[:, :even] = gate_grad.astype(NARROW)
        grads[:, even : 2 * even] = up_grad.astype(NARROW)
        if width == 64:
            last[:width, :] = down[even:, :]
            last[width:, :] = down[even:, :]
            both = dot(x, pair[:, 2 * even :], ((1,), (0,)))
            turned = pltpu.roll(both, width, 1)
            lower = lax.broadcasted_iota(jnp.int32, both.shape, 1) < width
            grad = dot(g, last[...], ((1,), (1,)))
            value, gate_grad, up_grad = ffn_parts(
                jnp.where(lower, both, turned), jnp.where(lower, turned, both), grad
            )
            act[:, even:] = value[:, :width].astype(NARROW)
            grads[:, 2 * even :] = jnp.where(lower, gate_grad, up_grad).astype(NARROW)
        else:
            gate = dot(x, pair[:, 2 * even : even + own], ((1,), (0,)))
            up = dot(x, pair[:, even + own :], ((1,), (0,)))
            grad = dot(g, down[even:, :], ((1,), (1,)))
            value, gate_grad, up_grad = ffn_parts(gate, up, grad)
            act[:, even:] = value.astype(NARROW)
            grads[:, 2 * even : even + own] = gate_grad.astype(NARROW)
            grads[:, even + own :] = up_grad.astype(NARROW)
        back = dot(grads[...], pair[...], ((1,), (1,)))
        back0[...] = back[:rows]
        back1[...] = back[rows:].astype(NARROW)
        out = dot(act[...], down[...], ((1,), (0,)))
        out0[...] = out[:rows]
        out1[...] = out[rows:].astype(NARROW)

    outs = (
        shape(NARROW, total, own),
        shape(NARROW, total, 2 * own),
        shape(WIDE, rows, features),
        shape(NARROW, rows, features),
        shape(WIDE, rows, features),
        shape(NARROW, rows, features),
    )
    return call(
        kernel,
        "ffn",
        outs,
        (*inputs, *upstream, pair, down),
        [
            pltpu.VMEM((total, features), NARROW),
            pltpu.VMEM((total, features), NARROW),
            pltpu.VMEM((features, 2 * own), NARROW),
            pltpu.VMEM((own, features), NARROW),
            pltpu.VMEM((2 * width, features), NARROW),
            pltpu.SemaphoreType.DMA((5 + 4 * teams,)),
        ],
        12 * total * features * own,
        in_place=True,
    )


def weight_grads(lefts, rights, groups, name):
    deep, wide = lefts[0].shape[1], rights[0].shape[1]
    tokens = sum(left.shape[0] for left in lefts)
    outer, inner, size = groups

    def kernel(*refs):
        ins, (out, left, right, sems) = refs[: len(lefts) + len(rights)], refs[-4:]
        pairs = []
        for blocks, whole in ((ins[: len(lefts)], left), (ins[len(lefts) :], right)):
            row = 0
            for block in blocks:
                pairs.append((block, whole.at[row : row + block.shape[0], :]))
                row += block.shape[0]
        for copy in fetch(pairs, sems):
            copy.wait()
        step = max(256 // (inner * size), 1) * inner * size
        step = step if step % 128 == 0 else deep
        step = 256 if size == deep else step
        for start in range(0, deep, step):
            stop = min(start + step, deep)
            total = dot(left[:, start:stop], right[...], ((0,), (0,))).astype(NARROW)
            if size == deep:
                out[start:stop, :] = total
                continue
            for row in range(start, stop, size):
                a, b = row // size // inner, row // size % inner
                to = (b * outer + a) * size
                out[to : to + size, :] = total[row - start : row - start + size]

    return call(
        kernel,
        name,
        shape(NARROW, deep, wide),
        (*lefts, *rights),
        [
            pltpu.VMEM((tokens, deep), NARROW),
            pltpu.VMEM((tokens, wide), NARROW),
            pltpu.SemaphoreType.DMA((len(lefts) + len(rights),)),
        ],
        2 * tokens * deep * wide,
        in_place=True,
    )


def resid_back(parts, resid, gain, upstream, out_blocks):
    rows, features = resid.shape
    channels = features // TEAM

    def kernel(own, across, along, resid, gain, upstream, *refs):
        out_blocks, (resid_grad, rounded, mixer_grad) = refs[:TEAM], refs[TEAM:]
        place, _ = where_am_i()
        grad = own[...] + across[...].astype(WIDE) + along[...].astype(WIDE)
        values = resid[...]
        scale = scale_of(values)
        grad = upstream[...].astype(WIDE) + norm_back(grad, values * scale, scale, gain[...])
        resid_grad[...] = grad
        rounded[...] = grad.astype(NARROW)
        for m in range(TEAM):
            product = dot(rounded[...], out_blocks[m][...], ((1,), (1,)))
            mixer_grad[place ^ m] = product.astype(NARROW)

    outs = (
        shape(WIDE, rows, features),
        shape(NARROW, rows, features),
        shape(NARROW, TEAM, rows, channels),
    )
    return call(
        kernel,
        "resid_back",
        outs,
        (*parts, resid, gain, upstream, *out_blocks),
        flops=2 * rows * features * features,
    )


def conv_back(mixer_grad, mixed, gated, conv, taps, keeps):
    tokens, channels = conv.shape

    def kernel(mixer_grad, mixed, gated, conv, taps, keeps, part, rim, taps_grad, ones, twos):
        grad = mixer_grad[...].astype(WIDE)
        conv_grad = grad * mixed[HALO:, channels : 2 * channels]
        one, two = keeps[8:, 0:1] * conv_grad, keeps[8:, 1:2] * conv_grad
        zeros = jnp.zeros((8, channels), WIDE)
        taps_grad[...] = zeros
        for k, (left, back) in enumerate(((two, 2), (one, 1), (conv_grad, 0))):
            product = left * gated[HALO - back : HALO - back + tokens, :]
            taps_grad[k : k + 1, :] = jnp.sum(product, axis=0, keepdims=True)
        ones[:tokens, :] = taps[1:2, :] * one
        twos[:tokens, :] = taps[0:1, :] * two
        ones[tokens:, :] = zeros
        twos[tokens:, :] = zeros
        rim[...] = zeros
        rim[6:7, :] = twos[0:1, :]
        rim[7:8, :] = twos[1:2, :] + ones[0:1, :]
        part[...] = taps[2:3, :] * conv_grad + ones[1 : tokens + 1, :] + twos[2 : tokens + 2, :]

    outs = (shape(WIDE, tokens, channels), shape(WIDE, 8, channels), shape(WIDE, 8, channels))
    scratch = [pltpu.VMEM((tokens + 8, channels), WIDE)] * 2
    return call(
        kernel, "conv_back", outs, (mixer_grad, mixed, gated, conv, taps, keeps), scratch
    )


def mixer_back(part, returned, mixer_grad, mixed, conv, normed, in_own, teams):
    tokens, channels = conv.shape
    features = in_own.shape[0]
    rows, share = tokens // TEAM, features // teams

    def kernel(*refs):
        part, returned, mixer_grad, mixed, conv, normed, in_own, grads, odd = refs[:9]
        shares, (side, whole, weight) = refs[9 : 9 + teams], refs[9 + teams :]
        place, team = where_am_i()
        whole[...] = part[...]
        whole[tokens - 8 :, :] = part[tokens - 8 :, :] + returned[...]
        gated_grad = whole[...]
        grads[:, :channels] = (gated_grad * mixed[HALO:, 2 * channels :]).astype(NARROW)
        grads[:, channels : 2 * channels] = (
            mixer_grad[...].astype(WIDE) * conv[...]
        ).astype(NARROW)
        grads[:, 2 * channels :] = (gated_grad * mixed[HALO:, :channels]).astype(NARROW)
        for chip in range(TEAM // 2):
            at_place = place ^ (2 * chip + 1)
            side[chip * rows : (chip + 1) * rows, :] = grads[at(at_place * rows, rows), :]
        step = features // 4
        for start in range(0, features, step):
            span = slice(start, start + step)
            weight[span, :] = dot(normed[HALO:, span], grads[...], ((0,), (0,)))
        for k in range(teams):
            owner = lax.rem(team + k, teams)
            shares[k][...] = weight[at(owner * share, share), :].astype(shares[k].dtype)
        odd[...] = dot(side[...], in_own[...], ((1,), (1,))).astype(NARROW)

    outs = (shape(NARROW, tokens, 3 * channels), shape(NARROW, tokens // 2, features))
    outs += tuple(
        shape(NARROW if k == teams - 1 else WIDE, share, 3 * channels) for k in range(teams)
    )
    grads, odd, *shares = call(
        kernel,
        "mixer_back",
        outs,
        (part, returned, mixer_grad, mixed, conv, normed, in_own),
        [
            pltpu.VMEM((tokens // 2, 3 * channels), NARROW),
            pltpu.VMEM((tokens, channels), WIDE),
            pltpu.VMEM((features, 3 * channels), WIDE),
        ],
        3 * tokens * features * 3 * channels,
    )
    return grads, odd, shares


def out_back(mixer_in, blocks, taps_grad, teams):
    rows, features = blocks[0].shape
    channels = mixer_in.shape[1]
    share = channels // teams
    low = (share + 15) // 16 * 16

    def kernel(*refs):
        mixer_in, blocks, taps_grad = refs[0], refs[1 : 1 + TEAM], refs[1 + TEAM]
        shares, (total,) = refs[2 + TEAM : 2 + TEAM + teams], refs[2 + TEAM + teams :]
        place, team = where_am_i()
        total[...] = sum(
            dot(mixer_in[at((place ^ m) * rows, rows), :], blocks[m][...], ((0,), (0,)))
            for m in range(TEAM)
        )
        for k in range(teams):
            owner = lax.rem(team + k, teams)
            kind = shares[k].dtype
            shares[k][...] = jnp.zeros_like(shares[k])
            shares[k][:share, :] = total[at(owner * share, share, 8), :].astype(kind)
            shares[k][low : low + 8, :channels] = taps_grad[...].astype(kind)

    outs = tuple(shape(NARROW if k else WIDE, low + 16, features) for k in range(teams))
    return call(
        kernel,
        "out_back",
        outs,
        (mixer_in, *blocks, taps_grad),
        [pltpu.VMEM((channels, features), WIDE)],
        2 * TEAM * rows * channels * features,
    ), low


def mixer_back_own(grads, in_own):
    tokens, width = grads.shape
    rows = tokens // TEAM

    def kernel(grads, in_own, even, side):
        place, _ = where_am_i()
        for chip in range(TEAM // 2):
            at_place = place ^ (2 * chip)
            side[chip * rows : (chip + 1) * rows, :] = grads[at(at_place * rows, rows), :]
        even[...] = dot(side[...], in_own[...], ((1,), (1,)))

    return call(
        kernel,
        "mixer_back_own",
        shape(WIDE, tokens // 2, in_own.shape[0]),
        (grads, in_own),
        [pltpu.VMEM((tokens // 2, width), NARROW)],
        tokens * in_own.size,
    )


def body(
    hidden_in,
    seq_start,
    mixer_gain,
    in_weight,
    conv_weight,
    out_weight,
    ffn_gain,
    gate_weight,
    up_weight,
    down_weight,
    cotangent,
):
    net = Net()
    teams = net.teams
    rows, features = hidden_in.shape
    inner = gate_weight.shape[2]
    part = features // net.count
    ffpart = inner // net.count
    channels = features // TEAM
    ffown = 4 * ffpart
    even = ffown // 128 * 128
    peers = net.peer_groups()

    down_own = lax.all_gather(down_weight[0], "dp", axis=0, tiled=True, axis_index_groups=peers)
    upstream, found, results = [], [], {}
    hidden_job = net.spawn(net.blocks(hidden_in))
    upstream_job = net.spawn(net.ring_blocks(cotangent, upstream))
    out_job = net.spawn(net.line_all(out_weight[0]))
    sent = in_prepare(
        in_weight[0],
        (mixer_gain, ffn_gain),
        seq_start.reshape(1, rows),
        conv_weight[0].T,
        teams,
    )
    net.need(sent)
    got_job = net.do(net.exchange, sent)
    pair_job = net.do(lambda *x: pair_prepare(*x, teams), gate_weight[0], up_weight[0])
    net.step()
    upstream_job.held = True
    pair_job = net.do(net.line_exchange, pair_job.result)
    in_job = net.spawn(net.line_blocks(got_job.result))
    net.until(pair_job)
    pair = pair_job.result.reshape(2 * teams * part, 2 * ffown)
    pair_own = lax.all_gather(pair, "dp", axis=0, tiled=True, axis_index_groups=peers)
    pair_own = pair_own.reshape(4, teams, 2 * part, 2 * ffown)
    out_own = jnp.zeros((channels, features), NARROW)
    for k, block in enumerate(out_job.result):
        out_own = lax.dynamic_update_slice(out_own, block, ((net.team - k) % teams * part, 0))
    net.until(hidden_job)

    def last_rows():
        last = hidden_job.result[0][-HALO:]
        for m in range(1, TEAM):
            block = hidden_job.result[m][-HALO:]
            last = jnp.where(net.place == (TEAM - 1) ^ m, block, last)
        (before,) = yield [(last, ("ring", 1))]
        return before

    halo_job = net.spawn(last_rows())
    out_job = net.spawn(net.blocks(out_own))
    before, weights = net.until(halo_job, in_job)

    upstream_job.held = False
    mix_job = net.do(lambda *x: mixer_forward(x[:TEAM], x[TEAM], x[TEAM + 1 :]),
                     *hidden_job.result, before, *weights)
    (normed, mixed, gated, conv, mixer_in, in_own, gain_one, gain_two, taps, keeps) = net.until(
        mix_job
    )
    mixer_local = net.until(net.do(net.exchange, mixer_in.reshape(TEAM, rows, channels)))
    out_blocks = net.until(out_job)
    resid, ffn_in = out_project(mixer_local, out_blocks, hidden_in, gain_two)

    def compute(k, inputs):
        operands = (*inputs, *upstream[k], pair_own, down_own)
        return (lambda *x: ffn_block(x[:2], x[2:4], *x[4:])), operands

    ffn_job = net.spawn(net.ring_through(ffn_in, found, results, compute))
    net.step(teams + 2)
    order = list(range(teams))
    acts, grads = [[results[k][i] for k in order] for i in (0, 1)]
    inputs, cots = [[block for k in order for block in b[k]] for b in (found, upstream)]

    def pair_grads(*blocks):
        count = 2 * teams
        return weight_grads(blocks[:count], blocks[count:], (teams, 4, 2 * part), "pair_grads")

    def down_grads(*blocks):
        return weight_grads(blocks[:teams], blocks[teams:], (1, 1, ffown), "down_grads")

    pair_job = net.do(pair_grads, *inputs, *grads)
    output_job = net.spawn(net.ring_sum(result_of(results, 4), result_of(results, 5)))
    ffn_grad = net.until(ffn_job)
    pair_sum = lax.psum_scatter(
        pair_job.result, "dp", scatter_dimension=0, tiled=True, axis_index_groups=peers
    )

    output_job.held = True
    back_job = net.do(
        lambda *x: resid_back(x[:3], *x[3:6], x[6:]),
        *ffn_grad, resid, gain_two, cotangent, *out_blocks,
    )
    resid_grad, rounded, mixer_grad = net.until(back_job)
    output_job.held = False
    down_job = net.do(down_grads, *acts, *cots)
    mixer_grad = net.until(net.do(net.exchange, mixer_grad)).reshape(TEAM * rows, channels)
    output_job.held = True
    down_sum = lax.psum_scatter(
        down_job.result, "dp", scatter_dimension=0, tiled=True, axis_index_groups=peers
    )
    gated_part, rim, taps_grad = net.until(
        net.do(conv_back, mixer_grad, mixed, gated, conv, taps, keeps)
    )

    def rim_steps():
        (returned,) = yield [(rim, ("back",))]
        return returned

    rounded_job = net.spawn(net.blocks(rounded))
    returned = net.until(net.spawn(rim_steps()))
    output_job.held = False
    mixed_grad, normed_odd, shares = net.until(
        net.do(
            lambda *x: mixer_back(*x, teams),
            gated_part, returned, mixer_grad, mixed, conv, normed, in_own,
        )
    )
    output_job.held = True
    in_job = net.spawn(net.line_sum(shares))
    normed_job = net.spawn(
        net.team_sum((mixer_back_own, (mixed_grad, in_own)), normed_odd)
    )
    net.until(rounded_job)
    low = (part + 15) // 16 * 16
    out_job = net.do(
        lambda *x: out_back(x[0], x[1 : 1 + TEAM], x[1 + TEAM], teams)[0],
        mixer_in, *rounded_job.result, taps_grad,
    )
    in_grad = net.until(in_job).astype(NARROW)
    in_job = net.do(net.exchange, in_grad.reshape(TEAM, part, 3 * channels))
    output_job.held = False
    in_grad = net.until(in_job)
    out_shares = net.until(out_job)
    out_job = net.spawn(net.line_send(out_shares[1:]))
    pair_job = net.do(net.line_exchange, pair_sum.reshape(teams * 2, part, 2 * ffown))
    in_job = net.do(
        lambda *x: in_finish(*x, teams), in_grad, in_weight[0], mixer_gain.reshape(part, 1)
    )
    normed_grad, ffn_out, arrived = net.until(normed_job, output_job, out_job)
    in_grad, grad_mixer_gain = net.until(in_job)
    grad_gate, grad_up, grad_ffn_gain = pair_finish(
        net.until(pair_job), gate_weight[0], up_weight[0], ffn_gain.reshape(part, 1), teams
    )
    out_pack = sum([part.astype(WIDE) for part in arrived], out_shares[0])

    def total(parts):
        return parts[0] + parts[1].astype(WIDE) + parts[2].astype(WIDE)

    own_hidden = hidden_in.astype(WIDE)
    scale_one = scale_of(own_hidden)
    grad_hidden = resid_grad + norm_back(
        total(normed_grad), own_hidden * scale_one, scale_one, gain_one
    )
    hidden_out = (resid + total(ffn_out)).astype(NARROW)
    grad_out = out_pack[:part]
    grad_conv = lax.dynamic_slice(out_pack, (low, net.team * part), (3, part)).T
    return (
        hidden_out,
        grad_hidden,
        grad_mixer_gain.reshape(1, part),
        in_grad[None],
        grad_conv[None],
        grad_out[None],
        grad_ffn_gain.reshape(1, part),
        grad_gate[None],
        grad_up[None],
        down_sum.astype(WIDE)[None],
    )


def solution(mesh):
    tokens, wide, deep = P("dp", None), P(None, "dp"), P(None, "dp", None)
    return jax.shard_map(
        body,
        mesh=mesh,
        in_specs=(tokens, P("dp"), wide, deep, deep, deep, wide, deep, deep, deep, tokens),
        out_specs=(tokens, tokens, wide, deep, deep, deep, wide, deep, deep, deep),
        check_vma=False,
    )
```

profile of v0, /device:TPU:0, one launch (start us, length us, event | category | flops | bytes accessed | tf_op | source)
XLA Modules:
  0.0 306.1 jit_solution(11647212197580548673)
XLA Ops:
  7.9 2.0 in_prepare.1
  9.9 3.0 collective-permute-start.5
  12.9 2.6 collective-permute-start.6
  15.5 1.3 collective-permute-start.7
  16.8 1.5 collective-permute-start
  18.3 1.5 collective-permute-start.1
  20.5 1.5 collective-permute-start.4
  22.0 3.7 %all-to-all-start = ((bf16[8,40,384]{2,1,0:T(8,128)(2,1)}), bf16[8,40,384]{2,1,0:T(8,128)(2,1)S(1)}, u32[]{:S(2)}, u32[]{:S(2)}) async-start(bf16[8,40,384]{2,1,0:T(8,128)(2,1)} %in_prepare.1), calls=%async_computation | async-start | bytes 491520 | tf_op jit(solution)/shard_map/all_to_all | solution.py:179
  25.7 2.2 pair_prepare.1
  28.0 4.5 %all-to-all-done.refs_9_ = bf16[8,40,384]{2,1,0:T(8,128)(2,1)S(1)} async-done(((bf16[8,40,384]{2,1,0:T(8,128)(2,1)}), bf16[8,40,384]{2,1,0:T(8,128)(2,1)S(1)}, u32[]{:S(2)}, u32[]{:S(2)}) %all-to-all-start) | async-done | bytes 245792 | tf_op jit(solution)/shard_map/all_to_all | solution.py:179
  32.6 3.6 %all-to-all-start.1 = ((bf16[8,32,1152]{2,1,0:T(8,128)(2,1)}), bf16[8,32,1152]{2,1,0:T(8,128)(2,1)S(1)}, u32[]{:S(2)}, u32[]{:S(2)}) async-start(bf16[8,32,1152]{2,1,0:T(8,128)(2,1)} %pair_prepare.1), calls=%async_computation.1 | async-start | bytes 1179648 | tf_op jit(solution)/shard_map/all_to_all | solution.py:185
  37.4 1.9 collective-permute-start.11
  39.4 16.8 %collective-permute-done.11.refs_10_ = bf16[8,40,384]{2,1,0:T(8,128)(2,1)S(1)} collective-permute-done((bf16[8,40,384]{2,1,0:T(8,128)(2,1)S(1)}, bf16[8,40,384]{2,1,0:T(8,128)(2,1)S(1)}, u32[]{:S(2)}, u32[]{:S(2)}) %collective-permute-start.11) | collective-permute-done | bytes 245792 | tf_op jit(solution)/shard_map/ppermute | solution.py:134
  56.2 2.1 all-to-all-done.1
  62.0 7.5 %collective-permute-done.13.refs_11_ = bf16[8,40,384]{2,1,0:T(8,128)(2,1)S(1)} collective-permute-done((bf16[8,40,384]{2,1,0:T(8,128)(2,1)S(1)}, bf16[8,40,384]{2,1,0:T(8,128)(2,1)S(1)}, u32[]{:S(2)}, u32[]{:S(2)}) %collective-permute-start.13) | collective-permute-done | bytes 245792 | tf_op jit(solution)/shard_map/ppermute | solution.py:134
  72.0 10.9 %collective-permute-done.15.refs_8_ = bf16[16,1024]{1,0:T(8,128)(2,1)S(1)} collective-permute-done((bf16[16,1024]{1,0:T(8,128)(2,1)S(1)}, bf16[16,1024]{1,0:T(8,128)(2,1)S(1)}, u32[]{:S(2)}, u32[]{:S(2)}) %collective-permute-start.15) | collective-permute-done | bytes 32800 | tf_op jit(solution)/shard_map/ppermute | solution.py:134
  86.3 7.0 %mixer_forward.1 = (bf16[1040,1024]{1,0:T(8,128)(2,1)}, f32[1040,384]{1,0:T(8,128)}, f32[1040,128]{1,0:T(8,128)}, f32[1024,128]{1,0:T(8,128)}, bf16[1024,128]{1,...) custom-call(bf16[128,1024]{1,0:T(8,128)(2,1)} %refs_8_.1, ...), custom_call_target="tpu_custom_call" | custom-call | flops 805306368 | bytes 3112960 | tf_op jit(solution)/shard_map/mixer_forward/pallas_call | solution.py:35
  93.3 1.7 collective-permute-done.20.refs_2_.refs_8_
  95.0 1.8 collective-permute-done.21.refs_6_
  97.4 11.0 %all_to_all.30.local = bf16[8,128,128]{2,1,0:T(8,128)(2,1)} all-to-all(bf16[8,128,128]{2,1,0:T(8,128)(2,1)} %bitcast.40), channel_id=1, replica_groups={{0,1,2,3,4,5,6,7},{8,9,10,11,12,13,14,15},{16,17,18,19,20,21,22,23},{24..., dimensions={0} | all-to-all | bytes 524288 | tf_op jit(solution)/shard_map/all_to_all | solution.py:179
  109.3 3.3 %out_project.1 = (f32[128,1024]{1,0:T(8,128)}, bf16[128,1024]{1,0:T(8,128)(2,1)}) custom-call(bf16[8,128,128]{2,1,0:T(8,128)(2,1)} %all_to_all.30.local, bf16[128,1024]{1,0:T(8,128)(2,1)} %copy-done.1, bf16[128,1024]{1,0:T(8,128)(2,1)} %copy-done.12, bf16[128,1024]{1,0:T(8,128)(2,1)} %copy-done.2, bf16[128,1024]{1,0:T(8,128)(2,1)} %copy-done.14, ...), custom_call_target="tpu_custom_call" | custom-call | flops 268435456 | bytes 2625536 | tf_op jit(solution)/shard_map/out_project/pallas_call | solution.py:35
  114.7 8.8 %collective-permute-done.29.refs_0_.refs_2_ = bf16[128,1024]{1,0:T(8,128)(2,1)S(1)} collective-permute-done((bf16[128,1024]{1,0:T(8,128)(2,1)}, bf16[128,1024]{1,0:T(8,128)(2,1)S(1)}, u32[]{:S(2)}, u32[]{:S(2)}) %collective-permute-start.29) | collective-permute-done | bytes 262176 | tf_op jit(solution)/shard_map/ppermute | solution.py:134
  123.7 1.3 collective-permute-done.30.refs_1_.refs_3_
  125.0 9.0 %collective-permute-done.31.refs_0_.refs_4_ = bf16[128,1024]{1,0:T(8,128)(2,1)S(1)} collective-permute-done((bf16[128,1024]{1,0:T(8,128)(2,1)S(1)}, bf16[128,1024]{1,0:T(8,128)(2,1)S(1)}, u32[]{:S(2)}, u32[]{:S(2)}) %collective-permute-start.31) | collective-permute-done | bytes 262176 | tf_op jit(solution)/shard_map/ppermute | solution.py:134
  134.3 5.7 %ffn.4 = (bf16[256,576]{1,0:T(8,128)(2,1)}, bf16[256,1152]{1,0:T(8,128)(2,1)}, f32[128,1024]{1,0:T(8,128)}, bf16[128,1024]{1,0:T(8,128)(2,1)}, f32[128,1024]{1,0:T(8,128)}, /*index=5*/bf16[128,1024]{1,0:T(8,128)(2,1)}) custom-call(bf16[128,1024]{1,0:T(8,128)(2,1)} %copy-done.70, bf16[128,1024]{1,0:T(8,128)(2,1)} %copy-done.71, bf16[128,1024]{1,0:T(8,128)(2,1)} %copy-done.37, ...), custom_call_target="tpu_custom_call" | custom-call | flops 1811939328 | bytes 4587520 | tf_op jit(solution)/shard_map/ffn/pallas_call | solution.py:35
  140.0 4.5 %collective-permute-done.33.refs_0_.refs_6_ = bf16[128,1024]{1,0:T(8,128)(2,1)S(1)} collective-permute-done((bf16[128,1024]{1,0:T(8,128)(2,1)S(1)}, bf16[128,1024]{1,0:T(8,128)(2,1)S(1)}, u32[]{:S(2)}, u32[]{:S(2)}) %collective-permute-start.33) | collective-permute-done | bytes 262176 | tf_op jit(solution)/shard_map/ppermute | solution.py:134
  145.0 5.7 %ffn.5 = (bf16[256,576]{1,0:T(8,128)(2,1)}, bf16[256,1152]{1,0:T(8,128)(2,1)}, f32[128,1024]{1,0:T(8,128)}, bf16[128,1024]{1,0:T(8,128)(2,1)}, f32[128,1024]{1,0:T(8,128)}, /*index=5*/bf16[128,1024]{1,0:T(8,128)(2,1)}) custom-call(bf16[128,1024]{1,0:T(8,128)(2,1)} %copy-done.72, bf16[128,1024]{1,0:T(8,128)(2,1)} %copy-done.74, bf16[128,1024]{1,0:T(8,128)(2,1)} %copy-done.39, ...), custom_call_target="tpu_custom_call" | custom-call | flops 1811939328 | bytes 4587520 | tf_op jit(solution)/shard_map/ffn/pallas_call | solution.py:35
  151.5 5.7 %ffn.6 = (bf16[256,576]{1,0:T(8,128)(2,1)}, bf16[256,1152]{1,0:T(8,128)(2,1)}, f32[128,1024]{1,0:T(8,128)}, bf16[128,1024]{1,0:T(8,128)(2,1)}, f32[128,1024]{1,0:T(8,128)}, /*index=5*/bf16[128,1024]{1,0:T(8,128)(2,1)}) custom-call(bf16[128,1024]{1,0:T(8,128)(2,1)} %copy-done.75, bf16[128,1024]{1,0:T(8,128)(2,1)} %copy-done.76, bf16[128,1024]{1,0:T(8,128)(2,1)} %copy-done.41, ...), custom_call_target="tpu_custom_call" | custom-call | flops 1811939328 | bytes 4587520 | tf_op jit(solution)/shard_map/ffn/pallas_call | solution.py:35
  157.1 4.3 %collective-permute-done.37 = bf16[128,1024]{1,0:T(8,128)(2,1)S(1)} collective-permute-done((bf16[128,1024]{1,0:T(8,128)(2,1)S(1)}, bf16[128,1024]{1,0:T(8,128)(2,1)S(1)}, u32[]{:S(2)}, u32[]{:S(2)}) %collective-permute-start.37) | collective-permute-done | bytes 262176 | tf_op jit(solution)/shard_map/ppermute | solution.py:134
  161.7 5.7 %ffn.7 = (bf16[256,576]{1,0:T(8,128)(2,1)}, bf16[256,1152]{1,0:T(8,128)(2,1)}, f32[128,1024]{1,0:T(8,128)}, bf16[128,1024]{1,0:T(8,128)(2,1)}, f32[128,1024]{1,0:T(8,128)}, /*index=5*/bf16[128,1024]{1,0:T(8,128)(2,1)}) custom-call(bf16[128,1024]{1,0:T(8,128)(2,1)} %get-tuple-element.578.refs_0_, bf16[128,1024]{1,0:T(8,128)(2,1)} %copy-done.69, ...), custom_call_target="tpu_custom_call" | custom-call | flops 1811939328 | bytes 4587520 | tf_op jit(solution)/shard_map/ffn/pallas_call | solution.py:35
  167.5 4.7 %collective-permute-done.39 = bf16[128,1024]{1,0:T(8,128)(2,1)S(1)} collective-permute-done((bf16[128,1024]{1,0:T(8,128)(2,1)S(1)}, bf16[128,1024]{1,0:T(8,128)(2,1)S(1)}, u32[]{:S(2)}, u32[]{:S(2)}) %collective-permute-start.39) | collective-permute-done | bytes 262176 | tf_op jit(solution)/shard_map/ppermute | solution.py:134
  172.8 6.7 %pair_grads.1 = bf16[1024,1152]{1,0:T(8,128)(2,1)} custom-call(bf16[128,1024]{1,0:T(8,128)(2,1)} %get-tuple-element.578.refs_0_, bf16[128,1024]{1,0:T(8,128)(2,1)} %copy-done.69, bf16[128,1024]{1,0:T(8,128)(2,1)} %copy-done.70, bf16[128,1024]{1,0:T(8,128)(2,1)} %copy-done.71, bf16[128,1024]{1,0:T(8,128)(2,1)} %copy-done.72, bf16[128,1024]{1,0:T(8,128)(2,1)} %copy-done.74, ...), custom_call_target="tpu_custom_call" | custom-call | flops 2415919104 | bytes 4456448 | tf_op jit(solution)/shard_map/pair_grads/pallas_call | solution.py:35
  179.5 3.3 %collective-permute-done.41.along = bf16[128,1024]{1,0:T(8,128)(2,1)S(1)} collective-permute-done((bf16[128,1024]{1,0:T(8,128)(2,1)S(1)}, bf16[128,1024]{1,0:T(8,128)(2,1)S(1)}, u32[]{:S(2)}, u32[]{:S(2)}) %collective-permute-start.41) | collective-permute-done | bytes 262176 | tf_op jit(solution)/shard_map/ppermute | solution.py:134
  183.5 3.8 %resid_back.1 = (f32[128,1024]{1,0:T(8,128)}, bf16[128,1024]{1,0:T(8,128)(2,1)}, bf16[8,128,128]{2,1,0:T(8,128)(2,1)}) custom-call(f32[128,1024]{1,0:T(8,128)} %get-tuple-element.595.own, bf16[128,1024]{1,0:T(8,128)(2,1)} %copy-done.48, bf16[128,1024]{1,0:T(8,128)(2,1)} %copy-done.49, f32[128,1024]{1,0:T(8,128)} %get-tuple-element.598.resid, ...), custom_call_target="tpu_custom_call" | custom-call | flops 268435456 | bytes 3936256 | tf_op jit(solution)/shard_map/resid_back/pallas_call | solution.py:35
  187.5 3.4 %all-to-all-start.3 = ((bf16[8,128,128]{2,1,0:T(8,128)(2,1)}), bf16[8,128,128]{2,1,0:T(8,128)(2,1)S(1)}, u32[]{:S(2)}, u32[]{:S(2)}) async-start(bf16[8,128,128]{2,1,0:T(8,128)(2,1)} %get-tuple-element.626), calls=%async_computation.3 | async-start | bytes 524288 | tf_op jit(solution)/shard_map/all_to_all | solution.py:179
  191.0 4.8 %down_grads.1 = bf16[576,1024]{1,0:T(8,128)(2,1)} custom-call(bf16[256,576]{1,0:T(8,128)(2,1)} %get-tuple-element.614.refs_0_, bf16[256,576]{1,0:T(8,128)(2,1)} %get-tuple-element.615.refs_1_, bf16[256,576]{1,0:T(8,128)(2,1)} %get-tuple-element.616.refs_2_, bf16[256,576]{1,0:T(8,128)(2,1)} %get-tuple-element.617.refs_3_, bf16[128,1024]{1,0:T(8,128)(2,1)} %refs_4_, ...), custom_call_target="tpu_custom_call" | custom-call | flops 1207959552 | bytes 3276800 | tf_op jit(solution)/shard_map/down_grads/pallas_call | solution.py:35
  195.8 5.2 %all-to-all-done.3 = bf16[8,128,128]{2,1,0:T(8,128)(2,1)S(1)} async-done(((bf16[8,128,128]{2,1,0:T(8,128)(2,1)}), bf16[8,128,128]{2,1,0:T(8,128)(2,1)S(1)}, u32[]{:S(2)}, u32[]{:S(2)}) %all-to-all-start.3) | async-done | bytes 262176 | tf_op jit(solution)/shard_map/all_to_all | solution.py:179
  201.7 3.2 %conv_back.1 = (f32[1024,128]{1,0:T(8,128)}, f32[8,128]{1,0:T(8,128)}, f32[8,128]{1,0:T(8,128)}) custom-call(bf16[1024,128]{1,0:T(8,128)(2,1)} %bitcast.34, f32[1040,384]{1,0:T(8,128)} %get-tuple-element.656.mixed.refs_3_, f32[1040,128]{1,0:T(8,128)} %get-tuple-element.633.gated, f32[1024,128]{1,0:T(8,128)} %get-tuple-element.657.conv.refs_4_, ...), custom_call_target="tpu_custom_call" | custom-call | bytes 2928704 | tf_op jit(solution)/shard_map/conv_back/pallas_call | solution.py:35
  207.4 4.3 %collective-permute-done.48.refs_1_ = f32[8,128]{1,0:T(8,128)S(1)} collective-permute-done((f32[8,128]{1,0:T(8,128)}, f32[8,128]{1,0:T(8,128)S(1)}, u32[]{:S(2)}, u32[]{:S(2)}) %collective-permute-start.48) | collective-permute-done | bytes 4128 | tf_op jit(solution)/shard_map/ppermute | solution.py:134
  212.0 1.6 collective-permute-start.51
  214.0 5.9 %mixer_back.1 = (bf16[1024,384]{1,0:T(8,128)(2,1)}, bf16[512,1024]{1,0:T(8,128)(2,1)}, f32[256,384]{1,0:T(8,128)}, f32[256,384]{1,0:T(8,128)}, f32[256,384]{1,0:T(8,128)}, /*index=5*/bf16[256,384]{1,0:T(8,128)(2,1)}) custom-call(f32[1024,128]{1,0:T(8,128)} %get-tuple-element.653.refs_0_, f32[8,128]{1,0:T(8,128)} %copy-done.64, bf16[1024,128]{1,0:T(8,128)(2,1)} %bitcast.35, ...), custom_call_target="tpu_custom_call" | custom-call | flops 1207959552 | bytes 5828608 | tf_op jit(solution)/shard_map/mixer_back/pallas_call | solution.py:35
  220.0 1.5 collective-permute-done.49
  222.2 1.4 collective-permute-start.55
  223.6 3.5 %mixer_back_own.1.even = f32[512,1024]{1,0:T(8,128)} custom-call(bf16[1024,384]{1,0:T(8,128)(2,1)} %get-tuple-element.680.grads, bf16[1024,384]{1,0:T(8,128)(2,1)} %get-tuple-element.681.refs_6_.in_own), custom_call_target="tpu_custom_call" | custom-call | flops 402653184 | bytes 1572864 | tf_op jit(solution)/shard_map/mixer_back_own/pallas_call | solution.py:35
  227.1 3.9 %collective-permute-done.55 = bf16[256,384]{1,0:T(8,128)(2,1)S(1)} collective-permute-done((bf16[256,384]{1,0:T(8,128)(2,1)}, bf16[256,384]{1,0:T(8,128)(2,1)S(1)}, u32[]{:S(2)}, u32[]{:S(2)}) %collective-permute-start.55) | collective-permute-done | bytes 196640 | tf_op jit(solution)/shard_map/ppermute | solution.py:134
  232.1 3.1 %fold_twin.1 = (f32[128,1024]{1,0:T(8,128)}, f32[128,1024]{1,0:T(8,128)}, f32[128,1024]{1,0:T(8,128)}, bf16[128,1024]{1,0:T(8,128)(2,1)}) custom-call(f32[512,1024]{1,0:T(8,128)} %mixer_back_own.1.even, bf16[512,1024]{1,0:T(8,128)(2,1)} %copy-done.11), custom_call_target="tpu_custom_call" | custom-call | bytes 3145728 | tf_op jit(solution)/shard_map/fold_twin/pallas_call | solution.py:35
  235.2 3.3 %out_back.1 = (f32[48,1024]{1,0:T(8,128)}, bf16[48,1024]{1,0:T(8,128)(2,1)}, bf16[48,1024]{1,0:T(8,128)(2,1)}, bf16[48,1024]{1,0:T(8,128)(2,1)}) custom-call(bf16[1024,128]{1,0:T(8,128)(2,1)} %get-tuple-element.693.refs_0_, bf16[128,1024]{1,0:T(8,128)(2,1)} %get-tuple-element.694.refs_1_, bf16[128,1024]{1,0:T(8,128)(2,1)} %copy-done.44, ...), custom_call_target="tpu_custom_call" | custom-call | flops 268435456 | bytes 2363392 | tf_op jit(solution)/shard_map/out_back/pallas_call | solution.py:35
  239.1 1.5 collective-permute-start.59
  240.8 7.3 %collective-permute-done.58 = bf16[256,384]{1,0:T(8,128)(2,1)S(1)} collective-permute-done((bf16[256,384]{1,0:T(8,128)(2,1)S(1)}, bf16[256,384]{1,0:T(8,128)(2,1)S(1)}, u32[]{:S(2)}, u32[]{:S(2)}) %collective-permute-start.58) | collective-permute-done | bytes 196640 | tf_op jit(solution)/shard_map/ppermute | solution.py:134
  248.8 2.1 fold_corner.1
  253.6 3.4 %all-to-all-start.4 = ((bf16[8,32,384]{2,1,0:T(8,128)(2,1)}), bf16[8,32,384]{2,1,0:T(8,128)(2,1)S(1)}, u32[]{:S(2)}, u32[]{:S(2)}) async-start(bf16[8,32,384]{2,1,0:T(8,128)(2,1)} %bitcast.12), calls=%async_computation.4 | async-start | bytes 393216 | tf_op jit(solution)/shard_map/all_to_all | solution.py:179
  257.2 6.1 %all-to-all-done.4.blocks = bf16[8,32,384]{2,1,0:T(8,128)(2,1)S(1)} async-done(((bf16[8,32,384]{2,1,0:T(8,128)(2,1)}), bf16[8,32,384]{2,1,0:T(8,128)(2,1)S(1)}, u32[]{:S(2)}, u32[]{:S(2)}) %all-to-all-start.4) | async-done | bytes 196640 | tf_op jit(solution)/shard_map/all_to_all | solution.py:179
  264.1 5.1 %all-to-all-start.5 = ((bf16[8,32,1152]{2,1,0:T(8,128)(2,1)}), bf16[8,32,1152]{2,1,0:T(8,128)(2,1)S(1)}, u32[]{:S(2)}, u32[]{:S(2)}) async-start(bf16[8,32,1152]{2,1,0:T(8,128)(2,1)} %bitcast.43), calls=%async_computation.6 | async-start | bytes 1179648 | tf_op jit(solution)/shard_map/all_to_all | solution.py:185
  270.2 2.4 fusion.5
  272.6 2.0 collective-permute-start.64
  274.6 2.4 collective-permute-start.65
  277.0 1.5 collective-permute-start.66
  278.4 1.8 bitcast_convert_fusion
  281.0 2.0 in_finish.1
  283.0 3.4 %collective-permute-done.64 = bf16[48,1024]{1,0:T(8,128)(2,1)S(1)} collective-permute-done((bf16[48,1024]{1,0:T(8,128)(2,1)}, bf16[48,1024]{1,0:T(8,128)(2,1)S(1)}, u32[]{:S(2)}, u32[]{:S(2)}) %collective-permute-start.64) | collective-permute-done | bytes 98336 | tf_op jit(solution)/shard_map/ppermute | solution.py:134
  286.4 6.3 %collective-permute-done.65 = bf16[48,1024]{1,0:T(8,128)(2,1)S(1)} collective-permute-done((bf16[48,1024]{1,0:T(8,128)(2,1)}, bf16[48,1024]{1,0:T(8,128)(2,1)S(1)}, u32[]{:S(2)}, u32[]{:S(2)}) %collective-permute-start.65) | collective-permute-done | bytes 98336 | tf_op jit(solution)/shard_map/ppermute | solution.py:134
  294.3 1.3 reduce
  295.6 2.6 pair_finish.1
  298.2 1.3 reduce.1
  (302 shorter events, 32.6 us)
Async XLA Ops:
  7.2 126.8 %all-gather.6.cloned.1.call-start = ((), (), s32[]{:S(2)}) async-start(), calls=%async_computation.11 | async-start | bytes 1474560 | tf_op jit(solution)/shard_map/all_gather | solution.py:876
  9.9 10.0 %collective-permute-start.5 = (bf16[32,1024]{1,0:T(8,128)(2,1)}, bf16[32,1024]{1,0:T(8,128)(2,1)S(1)}, u32[]{:S(2)}, u32[]{:S(2)}) collective-permute-start(bf16[32,1024]{1,0:T(8,128)(2,1)} %bitcast.44), channel_id=1, source_target_pairs={{0,8},{1,9},{2,10},{3,11},{4,12},{5,13},{6,14},{7,15},{8,16},{9,17... | collective-permute-start | bytes 196616 | tf_op jit(solution)/shard_map/ppermute | solution.py:134
  12.9 7.3 %collective-permute-start.6 = (bf16[32,1024]{1,0:T(8,128)(2,1)}, bf16[32,1024]{1,0:T(8,128)(2,1)S(1)}, u32[]{:S(2)}, u32[]{:S(2)}) collective-permute-start(bf16[32,1024]{1,0:T(8,128)(2,1)} %bitcast.45), channel_id=1, source_target_pairs={{0,16},{1,17},{2,18},{3,19},{4,20},{5,21},{6,22},{7,23},{8,24},{9,... | collective-permute-start | bytes 196616 | tf_op jit(solution)/shard_map/ppermute | solution.py:134
  16.8 15.7 %collective-permute-start = (bf16[128,1024]{1,0:T(8,128)(2,1)}, bf16[128,1024]{1,0:T(8,128)(2,1)S(1)}, u32[]{:S(2)}, u32[]{:S(2)}) collective-permute-start(bf16[128,1024]{1,0:T(8,128)(2,1)} %refs_8_.1), channel_id=1, source_target_pairs={{0,2},{1,3},{2,0},{3,1},{4,6},{5,7},{6,4},{7,5},{8,10},{9,11},{10,... | collective-permute-start | bytes 786440 | tf_op jit(solution)/shard_map/ppermute | solution.py:134
  18.3 14.2 %collective-permute-start.1 = (bf16[128,1024]{1,0:T(8,128)(2,1)}, bf16[128,1024]{1,0:T(8,128)(2,1)S(1)}, u32[]{:S(2)}, u32[]{:S(2)}) collective-permute-start(bf16[128,1024]{1,0:T(8,128)(2,1)} %refs_8_.1), channel_id=1, source_target_pairs={{0,4},{1,5},{2,6},{3,7},{4,0},{5,1},{6,2},{7,3},{8,12},{9,13},{10,... | collective-permute-start | bytes 786440 | tf_op jit(solution)/shard_map/ppermute | solution.py:134
  19.8 12.7 %collective-permute-start.2 = (bf16[128,1024]{1,0:T(8,128)(2,1)}, bf16[128,1024]{1,0:T(8,128)(2,1)S(1)}, u32[]{:S(2)}, u32[]{:S(2)}) collective-permute-start(bf16[128,1024]{1,0:T(8,128)(2,1)} %refs_8_.1), channel_id=1, source_target_pairs={{0,1},{1,0},{2,3},{3,2},{4,5},{5,4},{6,7},{7,6},{8,9},{9,8},{10,11... | collective-permute-start | bytes 786440 | tf_op jit(solution)/shard_map/ppermute | solution.py:134
  20.2 12.4 %collective-permute-start.3 = (bf16[128,1024]{1,0:T(8,128)(2,1)}, bf16[128,1024]{1,0:T(8,128)(2,1)S(1)}, u32[]{:S(2)}, u32[]{:S(2)}) collective-permute-start(bf16[128,1024]{1,0:T(8,128)(2,1)} %refs_4_), channel_id=1, source_target_pairs={{0,1},{1,0},{2,3},{3,2},{4,5},{5,4},{6,7},{7,6},{8,9},{9,8},{10,11... | collective-permute-start | bytes 786440 | tf_op jit(solution)/shard_map/ppermute | solution.py:134
  20.5 12.1 %collective-permute-start.4 = (bf16[128,1024]{1,0:T(8,128)(2,1)}, bf16[128,1024]{1,0:T(8,128)(2,1)S(1)}, u32[]{:S(2)}, u32[]{:S(2)}) collective-permute-start(bf16[128,1024]{1,0:T(8,128)(2,1)} %refs_4_), channel_id=1, source_target_pairs={{0,8},{1,9},{2,10},{3,11},{4,12},{5,13},{6,14},{7,15},{8,16},{9,17... | collective-permute-start | bytes 786440 | tf_op jit(solution)/shard_map/ppermute | solution.py:134
  22.0 10.5 %all-to-all-start = ((bf16[8,40,384]{2,1,0:T(8,128)(2,1)}), bf16[8,40,384]{2,1,0:T(8,128)(2,1)S(1)}, u32[]{:S(2)}, u32[]{:S(2)}) async-start(bf16[8,40,384]{2,1,0:T(8,128)(2,1)} %in_prepare.1), calls=%async_computation | async-start | bytes 491520 | tf_op jit(solution)/shard_map/all_to_all | solution.py:179
  32.6 25.7 %all-to-all-start.1 = ((bf16[8,32,1152]{2,1,0:T(8,128)(2,1)}), bf16[8,32,1152]{2,1,0:T(8,128)(2,1)S(1)}, u32[]{:S(2)}, u32[]{:S(2)}) async-start(bf16[8,32,1152]{2,1,0:T(8,128)(2,1)} %pair_prepare.1), calls=%async_computation.1 | async-start | bytes 1179648 | tf_op jit(solution)/shard_map/all_to_all | solution.py:185
  36.3 97.7 %all-gather.4.cloned.1.call-start = ((), (), s32[]{:S(2)}) async-start(), calls=%async_computation.8 | async-start | bytes 2949120 | tf_op jit(solution)/shard_map/all_gather | solution.py:897
  36.3 19.9 %collective-permute-start.8 = (bf16[128,1024]{1,0:T(8,128)(2,1)S(1)}, bf16[128,1024]{1,0:T(8,128)(2,1)S(1)}, u32[]{:S(2)}, u32[]{:S(2)}) collective-permute-start(bf16[128,1024]{1,0:T(8,128)(2,1)S(1)} %broadcast_select_fusion.2), channel_id=1, source_target_pairs={{0,2},{1,5},{2,0},{3,7},{4,6},{5,1},{6,4},{7,3},{8,10},{9,13},{10,... | collective-permute-start | bytes 786440 | tf_op jit(solution)/shard_map/ppermute | solution.py:134
  36.9 19.2 %collective-permute-start.9 = (bf16[128,1024]{1,0:T(8,128)(2,1)S(1)}, bf16[128,1024]{1,0:T(8,128)(2,1)S(1)}, u32[]{:S(2)}, u32[]{:S(2)}) collective-permute-start(bf16[128,1024]{1,0:T(8,128)(2,1)S(1)} %collective-permute-done.refs_2_), channel_id=1, source_target_pairs={{0,1},{1,0},{2,3},{3,2},{4,5},{5,4},{6,7},{7,6},{8,9},{9,8},{10,11... | collective-permute-start | bytes 786440 | tf_op jit(solution)/shard_map/ppermute | solution.py:134
  37.0 19.1 %collective-permute-start.10 = (bf16[128,1024]{1,0:T(8,128)(2,1)S(1)}, bf16[128,1024]{1,0:T(8,128)(2,1)S(1)}, u32[]{:S(2)}, u32[]{:S(2)}) collective-permute-start(bf16[128,1024]{1,0:T(8,128)(2,1)S(1)} %collective-permute-done.1.refs_4_), channel_id=1, source_target_pairs={{0,1},{1,0},{2,3},{3,2},{4,5},{5,4},{6,7},{7,6},{8,9},{9,8},{10,11... | collective-permute-start | bytes 786440 | tf_op jit(solution)/shard_map/ppermute | solution.py:134
  37.4 18.7 %collective-permute-start.11 = (bf16[8,40,384]{2,1,0:T(8,128)(2,1)S(1)}, bf16[8,40,384]{2,1,0:T(8,128)(2,1)S(1)}, u32[]{:S(2)}, u32[]{:S(2)}) collective-permute-start(bf16[8,40,384]{2,1,0:T(8,128)(2,1)S(1)} %all-to-all-done.refs_9_), channel_id=1, source_target_pairs={{0,8},{1,9},{2,10},{3,11},{4,12},{5,13},{6,14},{7,15},{8,16},{9,17... | collective-permute-start | bytes 737288 | tf_op jit(solution)/shard_map/ppermute | solution.py:134
  59.1 204.2 %reduce-scatter.3.cloned.1.call-start = ((), (), s32[]{:S(2)}) async-start(), calls=%async_computation.9 | async-start | bytes 2949120 | tf_op jit(solution)/shard_map/reduce_scatter | solution.py:946
  59.4 10.2 %collective-permute-start.12 = (bf16[128,1024]{1,0:T(8,128)(2,1)S(1)}, bf16[128,1024]{1,0:T(8,128)(2,1)S(1)}, u32[]{:S(2)}, u32[]{:S(2)}) collective-permute-start(bf16[128,1024]{1,0:T(8,128)(2,1)S(1)} %collective-permute-done.8.refs_6_), channel_id=1, source_target_pairs={{0,1},{1,0},{2,3},{3,2},{4,5},{5,4},{6,7},{7,6},{8,9},{9,8},{10,11... | collective-permute-start | bytes 786440 | tf_op jit(solution)/shard_map/ppermute | solution.py:134
  59.4 10.2 %collective-permute-start.13 = (bf16[8,40,384]{2,1,0:T(8,128)(2,1)S(1)}, bf16[8,40,384]{2,1,0:T(8,128)(2,1)S(1)}, u32[]{:S(2)}, u32[]{:S(2)}) collective-permute-start(bf16[8,40,384]{2,1,0:T(8,128)(2,1)S(1)} %collective-permute-done.11.refs_10_), channel_id=1, source_target_pairs={{0,8},{1,9},{2,10},{3,11},{4,12},{5,13},{6,14},{7,15},{8,16},{9,17... | collective-permute-start | bytes 737288 | tf_op jit(solution)/shard_map/ppermute | solution.py:134
  70.4 12.4 %collective-permute-start.16 = (bf16[128,1024]{1,0:T(8,128)(2,1)S(1)}, bf16[128,1024]{1,0:T(8,128)(2,1)S(1)}, u32[]{:S(2)}, u32[]{:S(2)}) collective-permute-start(bf16[128,1024]{1,0:T(8,128)(2,1)S(1)} %constant_dynamic-update-slice_fusion.refs_0_), channel_id=1, source_target_pairs={{0,2},{1,3},{2,0},{3,1},{4,6},{5,7},{6,4},{7,5},{8,10},{9,11},{10,... | collective-permute-start | bytes 786440 | tf_op jit(solution)/shard_map/ppermute | solution.py:134
  71.0 11.8 %collective-permute-start.17 = (bf16[128,1024]{1,0:T(8,128)(2,1)S(1)}, bf16[128,1024]{1,0:T(8,128)(2,1)S(1)}, u32[]{:S(2)}, u32[]{:S(2)}) collective-permute-start(bf16[128,1024]{1,0:T(8,128)(2,1)S(1)} %constant_dynamic-update-slice_fusion.refs_0_), channel_id=1, source_target_pairs={{0,4},{1,5},{2,6},{3,7},{4,0},{5,1},{6,2},{7,3},{8,12},{9,13},{10,... | collective-permute-start | bytes 786440 | tf_op jit(solution)/shard_map/ppermute | solution.py:134
  72.0 11.6 %collective-permute-start.18 = (bf16[128,1024]{1,0:T(8,128)(2,1)S(1)}, bf16[128,1024]{1,0:T(8,128)(2,1)S(1)}, u32[]{:S(2)}, u32[]{:S(2)}) collective-permute-start(bf16[128,1024]{1,0:T(8,128)(2,1)S(1)} %constant_dynamic-update-slice_fusion.refs_0_), channel_id=1, source_target_pairs={{0,1},{1,0},{2,3},{3,2},{4,5},{5,4},{6,7},{7,6},{8,9},{9,8},{10,11... | collective-permute-start | bytes 786440 | tf_op jit(solution)/shard_map/ppermute | solution.py:134
  72.0 10.9 %collective-permute-start.14 = (bf16[8,40,384]{2,1,0:T(8,128)(2,1)S(1)}, bf16[8,40,384]{2,1,0:T(8,128)(2,1)S(1)}, u32[]{:S(2)}, u32[]{:S(2)}) collective-permute-start(bf16[8,40,384]{2,1,0:T(8,128)(2,1)S(1)} %collective-permute-done.13.refs_11_), channel_id=1, source_target_pairs={{0,8},{1,9},{2,10},{3,11},{4,12},{5,13},{6,14},{7,15},{8,16},{9,17... | collective-permute-start | bytes 737288 | tf_op jit(solution)/shard_map/ppermute | solution.py:134
  72.0 10.9 %collective-permute-start.15 = (bf16[16,1024]{1,0:T(8,128)(2,1)S(1)}, bf16[16,1024]{1,0:T(8,128)(2,1)S(1)}, u32[]{:S(2)}, u32[]{:S(2)}) collective-permute-start(bf16[16,1024]{1,0:T(8,128)(2,1)S(1)} %select_select_fusion), channel_id=1, source_target_pairs={{0,8},{1,9},{2,10},{3,11},{4,12},{5,13},{6,14},{7,15},{8,16},{9,17... | collective-permute-start | bytes 98312 | tf_op jit(solution)/shard_map/ppermute | solution.py:134
  84.4 8.8 %collective-permute-start.19 = (bf16[128,1024]{1,0:T(8,128)(2,1)S(1)}, bf16[128,1024]{1,0:T(8,128)(2,1)S(1)}, u32[]{:S(2)}, u32[]{:S(2)}) collective-permute-start(bf16[128,1024]{1,0:T(8,128)(2,1)S(1)} %collective-permute-done.4.refs_2_.refs_6_), channel_id=1, source_target_pairs={{0,1},{1,0},{2,3},{3,2},{4,5},{5,4},{6,7},{7,6},{8,9},{9,8},{10,11... | collective-permute-start | bytes 786440 | tf_op jit(solution)/shard_map/ppermute | solution.py:134
  84.5 10.5 %collective-permute-start.20 = (bf16[128,1024]{1,0:T(8,128)(2,1)S(1)}, bf16[128,1024]{1,0:T(8,128)(2,1)S(1)}, u32[]{:S(2)}, u32[]{:S(2)}) collective-permute-start(bf16[128,1024]{1,0:T(8,128)(2,1)S(1)} %collective-permute-done.4.refs_2_.refs_6_), channel_id=1, source_target_pairs={{0,8},{1,9},{2,10},{3,11},{4,12},{5,13},{6,14},{7,15},{8,16},{9,17... | collective-permute-start | bytes 786440 | tf_op jit(solution)/shard_map/ppermute | solution.py:134
  84.6 12.2 %collective-permute-start.21 = (bf16[128,1024]{1,0:T(8,128)(2,1)}, bf16[128,1024]{1,0:T(8,128)(2,1)S(1)}, u32[]{:S(2)}, u32[]{:S(2)}) collective-permute-start(bf16[128,1024]{1,0:T(8,128)(2,1)} %broadcast_select_fusion.1), channel_id=1, source_target_pairs={{0,2},{1,5},{2,0},{3,7},{4,6},{5,1},{6,4},{7,3},{8,10},{9,13},{10,... | collective-permute-start | bytes 786440 | tf_op jit(solution)/shard_map/ppermute | solution.py:134
  85.7 11.1 %collective-permute-start.22 = (bf16[128,1024]{1,0:T(8,128)(2,1)S(1)}, bf16[128,1024]{1,0:T(8,128)(2,1)S(1)}, u32[]{:S(2)}, u32[]{:S(2)}) collective-permute-start(bf16[128,1024]{1,0:T(8,128)(2,1)S(1)} %collective-permute-done.16.refs_2_), channel_id=1, source_target_pairs={{0,1},{1,0},{2,3},{3,2},{4,5},{5,4},{6,7},{7,6},{8,9},{9,8},{10,11... | collective-permute-start | bytes 786440 | tf_op jit(solution)/shard_map/ppermute | solution.py:134
  85.8 11.0 %collective-permute-start.23 = (bf16[128,1024]{1,0:T(8,128)(2,1)S(1)}, bf16[128,1024]{1,0:T(8,128)(2,1)S(1)}, u32[]{:S(2)}, u32[]{:S(2)}) collective-permute-start(bf16[128,1024]{1,0:T(8,128)(2,1)S(1)} %collective-permute-done.17.refs_4_), channel_id=1, source_target_pairs={{0,1},{1,0},{2,3},{3,2},{4,5},{5,4},{6,7},{7,6},{8,9},{9,8},{10,11... | collective-permute-start | bytes 786440 | tf_op jit(solution)/shard_map/ppermute | solution.py:134
  96.8 11.6 %collective-permute-start.24 = (bf16[128,1024]{1,0:T(8,128)(2,1)S(1)}, bf16[128,1024]{1,0:T(8,128)(2,1)S(1)}, u32[]{:S(2)}, u32[]{:S(2)}) collective-permute-start(bf16[128,1024]{1,0:T(8,128)(2,1)S(1)} %collective-permute-done.20.refs_2_.refs_8_), channel_id=1, source_target_pairs={{0,1},{1,0},{2,3},{3,2},{4,5},{5,4},{6,7},{7,6},{8,9},{9,8},{10,11... | collective-permute-start | bytes 786440 | tf_op jit(solution)/shard_map/ppermute | solution.py:134
  96.9 11.5 %collective-permute-start.25 = (bf16[128,1024]{1,0:T(8,128)(2,1)S(1)}, bf16[128,1024]{1,0:T(8,128)(2,1)S(1)}, u32[]{:S(2)}, u32[]{:S(2)}) collective-permute-start(bf16[128,1024]{1,0:T(8,128)(2,1)S(1)} %collective-permute-done.20.refs_2_.refs_8_), channel_id=1, source_target_pairs={{0,8},{1,9},{2,10},{3,11},{4,12},{5,13},{6,14},{7,15},{8,16},{9,17... | collective-permute-start | bytes 786440 | tf_op jit(solution)/shard_map/ppermute | solution.py:134
  97.0 11.5 %collective-permute-start.26 = (bf16[128,1024]{1,0:T(8,128)(2,1)S(1)}, bf16[128,1024]{1,0:T(8,128)(2,1)S(1)}, u32[]{:S(2)}, u32[]{:S(2)}) collective-permute-start(bf16[128,1024]{1,0:T(8,128)(2,1)S(1)} %collective-permute-done.21.refs_6_), channel_id=1, source_target_pairs={{0,1},{1,0},{2,3},{3,2},{4,5},{5,4},{6,7},{7,6},{8,9},{9,8},{10,11... | collective-permute-start | bytes 786440 | tf_op jit(solution)/shard_map/ppermute | solution.py:134
  113.0 10.4 %collective-permute-start.29 = (bf16[128,1024]{1,0:T(8,128)(2,1)}, bf16[128,1024]{1,0:T(8,128)(2,1)S(1)}, u32[]{:S(2)}, u32[]{:S(2)}) collective-permute-start(bf16[128,1024]{1,0:T(8,128)(2,1)} %get-tuple-element.578.refs_0_), channel_id=1, source_target_pairs={{0,8},{1,9},{2,10},{3,11},{4,12},{5,13},{6,14},{7,15},{8,16},{9,17... | collective-permute-start | bytes 786440 | tf_op jit(solution)/shard_map/ppermute | solution.py:134
  123.5 10.5 %collective-permute-start.31 = (bf16[128,1024]{1,0:T(8,128)(2,1)S(1)}, bf16[128,1024]{1,0:T(8,128)(2,1)S(1)}, u32[]{:S(2)}, u32[]{:S(2)}) collective-permute-start(bf16[128,1024]{1,0:T(8,128)(2,1)S(1)} %collective-permute-done.29.refs_0_.refs_2_), channel_id=1, source_target_pairs={{0,8},{1,9},{2,10},{3,11},{4,12},{5,13},{6,14},{7,15},{8,16},{9,17... | collective-permute-start | bytes 786440 | tf_op jit(solution)/shard_map/ppermute | solution.py:134
  134.0 10.5 %collective-permute-start.33 = (bf16[128,1024]{1,0:T(8,128)(2,1)S(1)}, bf16[128,1024]{1,0:T(8,128)(2,1)S(1)}, u32[]{:S(2)}, u32[]{:S(2)}) collective-permute-start(bf16[128,1024]{1,0:T(8,128)(2,1)S(1)} %collective-permute-done.31.refs_0_.refs_4_), channel_id=1, source_target_pairs={{0,8},{1,9},{2,10},{3,11},{4,12},{5,13},{6,14},{7,15},{8,16},{9,17... | collective-permute-start | bytes 786440 | tf_op jit(solution)/shard_map/ppermute | solution.py:134
  151.0 10.5 %collective-permute-start.37 = (bf16[128,1024]{1,0:T(8,128)(2,1)S(1)}, bf16[128,1024]{1,0:T(8,128)(2,1)S(1)}, u32[]{:S(2)}, u32[]{:S(2)}) collective-permute-start(bf16[128,1024]{1,0:T(8,128)(2,1)S(1)} %add_convert_fusion.6), channel_id=1, source_target_pairs={{0,8},{1,9},{2,10},{3,11},{4,12},{5,13},{6,14},{7,15},{8,16},{9,17... | collective-permute-start | bytes 786440 | tf_op jit(solution)/shard_map/ppermute | solution.py:134
  161.6 10.5 %collective-permute-start.39 = (bf16[128,1024]{1,0:T(8,128)(2,1)S(1)}, bf16[128,1024]{1,0:T(8,128)(2,1)S(1)}, u32[]{:S(2)}, u32[]{:S(2)}) collective-permute-start(bf16[128,1024]{1,0:T(8,128)(2,1)S(1)} %add_convert_fusion.5), channel_id=1, source_target_pairs={{0,8},{1,9},{2,10},{3,11},{4,12},{5,13},{6,14},{7,15},{8,16},{9,17... | collective-permute-start | bytes 786440 | tf_op jit(solution)/shard_map/ppermute | solution.py:134
  172.3 7.3 %collective-permute-start.40 = (bf16[128,1024]{1,0:T(8,128)(2,1)}, bf16[128,1024]{1,0:T(8,128)(2,1)S(1)}, u32[]{:S(2)}, u32[]{:S(2)}) collective-permute-start(bf16[128,1024]{1,0:T(8,128)(2,1)} %get-tuple-element.576), channel_id=1, source_target_pairs={{0,1},{1,0},{2,3},{3,2},{4,5},{5,4},{6,7},{7,6},{8,9},{9,8},{10,11... | collective-permute-start | bytes 786440 | tf_op jit(solution)/shard_map/ppermute | solution.py:134
  172.3 10.5 %collective-permute-start.41 = (bf16[128,1024]{1,0:T(8,128)(2,1)S(1)}, bf16[128,1024]{1,0:T(8,128)(2,1)S(1)}, u32[]{:S(2)}, u32[]{:S(2)}) collective-permute-start(bf16[128,1024]{1,0:T(8,128)(2,1)S(1)} %add_convert_fusion.4), channel_id=1, source_target_pairs={{0,8},{1,9},{2,10},{3,11},{4,12},{5,13},{6,14},{7,15},{8,16},{9,17... | collective-permute-start | bytes 786440 | tf_op jit(solution)/shard_map/ppermute | solution.py:134
  172.6 10.2 %collective-permute-start.42 = (bf16[128,1024]{1,0:T(8,128)(2,1)S(1)}, bf16[128,1024]{1,0:T(8,128)(2,1)S(1)}, u32[]{:S(2)}, u32[]{:S(2)}) collective-permute-start(bf16[128,1024]{1,0:T(8,128)(2,1)S(1)} %copy-done.73), channel_id=1, source_target_pairs={{0,1},{1,0},{2,3},{3,2},{4,5},{5,4},{6,7},{7,6},{8,9},{9,8},{10,11... | collective-permute-start | bytes 786440 | tf_op jit(solution)/shard_map/ppermute | solution.py:134
  187.4 13.6 %collective-permute-start.43 = (bf16[128,1024]{1,0:T(8,128)(2,1)S(1)}, bf16[128,1024]{1,0:T(8,128)(2,1)S(1)}, u32[]{:S(2)}, u32[]{:S(2)}) collective-permute-start(bf16[128,1024]{1,0:T(8,128)(2,1)S(1)} %add_convert_fusion.3), channel_id=1, source_target_pairs={{0,8},{1,9},{2,10},{3,11},{4,12},{5,13},{6,14},{7,15},{8,16},{9,17... | collective-permute-start | bytes 786440 | tf_op jit(solution)/shard_map/ppermute | solution.py:134
  187.5 13.5 %collective-permute-start.44 = (bf16[128,1024]{1,0:T(8,128)(2,1)S(1)}, bf16[128,1024]{1,0:T(8,128)(2,1)S(1)}, u32[]{:S(2)}, u32[]{:S(2)}) collective-permute-start(bf16[128,1024]{1,0:T(8,128)(2,1)S(1)} %copy-done.68), channel_id=1, source_target_pairs={{0,1},{1,0},{2,3},{3,2},{4,5},{5,4},{6,7},{7,6},{8,9},{9,8},{10,11... | collective-permute-start | bytes 786440 | tf_op jit(solution)/shard_map/ppermute | solution.py:134
  187.5 13.4 %all-to-all-start.3 = ((bf16[8,128,128]{2,1,0:T(8,128)(2,1)}), bf16[8,128,128]{2,1,0:T(8,128)(2,1)S(1)}, u32[]{:S(2)}, u32[]{:S(2)}) async-start(bf16[8,128,128]{2,1,0:T(8,128)(2,1)} %get-tuple-element.626), calls=%async_computation.3 | async-start | bytes 524288 | tf_op jit(solution)/shard_map/all_to_all | solution.py:179
  191.0 87.5 %reduce-scatter.5.cloned.1.call-start = ((), (), s32[]{:S(2)}) async-start(), calls=%async_computation.10 | async-start | bytes 1474560 | tf_op jit(solution)/shard_map/reduce_scatter | solution.py:960
  204.9 6.9 %collective-permute-start.45 = (bf16[128,1024]{1,0:T(8,128)(2,1)S(1)}, bf16[128,1024]{1,0:T(8,128)(2,1)S(1)}, u32[]{:S(2)}, u32[]{:S(2)}) collective-permute-start(bf16[128,1024]{1,0:T(8,128)(2,1)S(1)} %copy-done.43), channel_id=1, source_target_pairs={{0,2},{1,3},{2,0},{3,1},{4,6},{5,7},{6,4},{7,5},{8,10},{9,11},{10,... | collective-permute-start | bytes 786440 | tf_op jit(solution)/shard_map/ppermute | solution.py:134
  211.8 9.7 %collective-permute-start.49 = (bf16[128,1024]{1,0:T(8,128)(2,1)S(1)}, bf16[128,1024]{1,0:T(8,128)(2,1)S(1)}, u32[]{:S(2)}, u32[]{:S(2)}) collective-permute-start(bf16[128,1024]{1,0:T(8,128)(2,1)S(1)} %add_convert_fusion.2), channel_id=1, source_target_pairs={{0,8},{1,9},{2,10},{3,11},{4,12},{5,13},{6,14},{7,15},{8,16},{9,17... | collective-permute-start | bytes 786440 | tf_op jit(solution)/shard_map/ppermute | solution.py:134
  211.9 9.6 %collective-permute-start.50 = (bf16[128,1024]{1,0:T(8,128)(2,1)S(1)}, bf16[128,1024]{1,0:T(8,128)(2,1)S(1)}, u32[]{:S(2)}, u32[]{:S(2)}) collective-permute-start(bf16[128,1024]{1,0:T(8,128)(2,1)S(1)} %copy-done.67), channel_id=1, source_target_pairs={{0,1},{1,0},{2,3},{3,2},{4,5},{5,4},{6,7},{7,6},{8,9},{9,8},{10,11... | collective-permute-start | bytes 786440 | tf_op jit(solution)/shard_map/ppermute | solution.py:134
  212.0 9.6 %collective-permute-start.51 = (bf16[128,1024]{1,0:T(8,128)(2,1)S(1)}, bf16[128,1024]{1,0:T(8,128)(2,1)S(1)}, u32[]{:S(2)}, u32[]{:S(2)}) collective-permute-start(bf16[128,1024]{1,0:T(8,128)(2,1)S(1)} %broadcast_select_fusion), channel_id=1, source_target_pairs={{0,2},{1,5},{2,0},{3,7},{4,6},{5,1},{6,4},{7,3},{8,10},{9,13},{10,... | collective-permute-start | bytes 786440 | tf_op jit(solution)/shard_map/ppermute | solution.py:134
  213.5 8.0 %collective-permute-start.52 = (bf16[128,1024]{1,0:T(8,128)(2,1)S(1)}, bf16[128,1024]{1,0:T(8,128)(2,1)S(1)}, u32[]{:S(2)}, u32[]{:S(2)}) collective-permute-start(bf16[128,1024]{1,0:T(8,128)(2,1)S(1)} %collective-permute-done.45.refs_3_), channel_id=1, source_target_pairs={{0,1},{1,0},{2,3},{3,2},{4,5},{5,4},{6,7},{7,6},{8,9},{9,8},{10,11... | collective-permute-start | bytes 786440 | tf_op jit(solution)/shard_map/ppermute | solution.py:134
  213.5 8.0 %collective-permute-start.53 = (bf16[128,1024]{1,0:T(8,128)(2,1)S(1)}, bf16[128,1024]{1,0:T(8,128)(2,1)S(1)}, u32[]{:S(2)}, u32[]{:S(2)}) collective-permute-start(bf16[128,1024]{1,0:T(8,128)(2,1)S(1)} %collective-permute-done.46.refs_5_), channel_id=1, source_target_pairs={{0,1},{1,0},{2,3},{3,2},{4,5},{5,4},{6,7},{7,6},{8,9},{9,8},{10,11... | collective-permute-start | bytes 786440 | tf_op jit(solution)/shard_map/ppermute | solution.py:134
  221.6 9.5 %collective-permute-start.56 = (bf16[512,1024]{1,0:T(8,128)(2,1)}, bf16[512,1024]{1,0:T(8,128)(2,1)S(1)}, u32[]{:S(2)}, u32[]{:S(2)}) collective-permute-start(bf16[512,1024]{1,0:T(8,128)(2,1)} %get-tuple-element.679), channel_id=1, source_target_pairs={{0,1},{1,0},{2,3},{3,2},{4,5},{5,4},{6,7},{7,6},{8,9},{9,8},{10,11... | collective-permute-start | bytes 3145736 | tf_op jit(solution)/shard_map/ppermute | solution.py:134
  221.7 9.4 %collective-permute-start.54 = (bf16[128,1024]{1,0:T(8,128)(2,1)S(1)}, bf16[128,1024]{1,0:T(8,128)(2,1)S(1)}, u32[]{:S(2)}, u32[]{:S(2)}) collective-permute-start(bf16[128,1024]{1,0:T(8,128)(2,1)S(1)} %collective-permute-done.51.refs_7_), channel_id=1, source_target_pairs={{0,1},{1,0},{2,3},{3,2},{4,5},{5,4},{6,7},{7,6},{8,9},{9,8},{10,11... | collective-permute-start | bytes 786440 | tf_op jit(solution)/shard_map/ppermute | solution.py:134
  222.2 8.9 %collective-permute-start.55 = (bf16[256,384]{1,0:T(8,128)(2,1)}, bf16[256,384]{1,0:T(8,128)(2,1)S(1)}, u32[]{:S(2)}, u32[]{:S(2)}) collective-permute-start(bf16[256,384]{1,0:T(8,128)(2,1)} %get-tuple-element.678), channel_id=1, source_target_pairs={{0,8},{1,9},{2,10},{3,11},{4,12},{5,13},{6,14},{7,15},{8,16},{9,17... | collective-permute-start | bytes 589832 | tf_op jit(solution)/shard_map/ppermute | solution.py:134
  231.1 7.9 %collective-permute-start.57 = (bf16[256,384]{1,0:T(8,128)(2,1)S(1)}, bf16[256,384]{1,0:T(8,128)(2,1)S(1)}, u32[]{:S(2)}, u32[]{:S(2)}) collective-permute-start(bf16[256,384]{1,0:T(8,128)(2,1)S(1)} %add_convert_fusion.9), channel_id=1, source_target_pairs={{0,8},{1,9},{2,10},{3,11},{4,12},{5,13},{6,14},{7,15},{8,16},{9,17... | collective-permute-start | bytes 589832 | tf_op jit(solution)/shard_map/ppermute | solution.py:134
  239.1 9.0 %collective-permute-start.59 = (bf16[128,1024]{1,0:T(8,128)(2,1)S(1)}, bf16[128,1024]{1,0:T(8,128)(2,1)S(1)}, u32[]{:S(2)}, u32[]{:S(2)}) collective-permute-start(bf16[128,1024]{1,0:T(8,128)(2,1)S(1)} %copy-done.77), channel_id=1, source_target_pairs={{0,2},{1,5},{2,0},{3,7},{4,6},{5,1},{6,4},{7,3},{8,10},{9,13},{10,... | collective-permute-start | bytes 786440 | tf_op jit(solution)/shard_map/ppermute | solution.py:134
  240.6 7.5 %collective-permute-start.58 = (bf16[256,384]{1,0:T(8,128)(2,1)S(1)}, bf16[256,384]{1,0:T(8,128)(2,1)S(1)}, u32[]{:S(2)}, u32[]{:S(2)}) collective-permute-start(bf16[256,384]{1,0:T(8,128)(2,1)S(1)} %add_convert_fusion.8), channel_id=1, source_target_pairs={{0,8},{1,9},{2,10},{3,11},{4,12},{5,13},{6,14},{7,15},{8,16},{9,17... | collective-permute-start | bytes 589832 | tf_op jit(solution)/shard_map/ppermute | solution.py:134
  251.7 11.6 %collective-permute-start.60 = (bf16[128,1024]{1,0:T(8,128)(2,1)S(1)}, bf16[128,1024]{1,0:T(8,128)(2,1)S(1)}, u32[]{:S(2)}, u32[]{:S(2)}) collective-permute-start(bf16[128,1024]{1,0:T(8,128)(2,1)S(1)} %add_convert_fusion.1), channel_id=1, source_target_pairs={{0,8},{1,9},{2,10},{3,11},{4,12},{5,13},{6,14},{7,15},{8,16},{9,17... | collective-permute-start | bytes 786440 | tf_op jit(solution)/shard_map/ppermute | solution.py:134
  251.7 11.6 %collective-permute-start.61 = (bf16[128,1024]{1,0:T(8,128)(2,1)}, bf16[128,1024]{1,0:T(8,128)(2,1)S(1)}, u32[]{:S(2)}, u32[]{:S(2)}) collective-permute-start(bf16[128,1024]{1,0:T(8,128)(2,1)} %get-tuple-element.723), channel_id=1, source_target_pairs={{0,1},{1,0},{2,3},{3,2},{4,5},{5,4},{6,7},{7,6},{8,9},{9,8},{10,11... | collective-permute-start | bytes 786440 | tf_op jit(solution)/shard_map/ppermute | solution.py:134
  251.7 11.7 %collective-permute-start.62 = (bf16[128,1024]{1,0:T(8,128)(2,1)}, bf16[128,1024]{1,0:T(8,128)(2,1)S(1)}, u32[]{:S(2)}, u32[]{:S(2)}) collective-permute-start(bf16[128,1024]{1,0:T(8,128)(2,1)} %get-tuple-element.724), channel_id=1, source_target_pairs={{0,2},{1,3},{2,0},{3,1},{4,6},{5,7},{6,4},{7,5},{8,10},{9,11},{10,... | collective-permute-start | bytes 786440 | tf_op jit(solution)/shard_map/ppermute | solution.py:134
  252.5 10.9 %collective-permute-start.63 = (bf16[128,1024]{1,0:T(8,128)(2,1)}, bf16[128,1024]{1,0:T(8,128)(2,1)S(1)}, u32[]{:S(2)}, u32[]{:S(2)}) collective-permute-start(bf16[128,1024]{1,0:T(8,128)(2,1)} %get-tuple-element.725), channel_id=1, source_target_pairs={{0,4},{1,5},{2,6},{3,7},{4,0},{5,1},{6,2},{7,3},{8,12},{9,13},{10,... | collective-permute-start | bytes 786440 | tf_op jit(solution)/shard_map/ppermute | solution.py:134
  253.6 9.7 %all-to-all-start.4 = ((bf16[8,32,384]{2,1,0:T(8,128)(2,1)}), bf16[8,32,384]{2,1,0:T(8,128)(2,1)S(1)}, u32[]{:S(2)}, u32[]{:S(2)}) async-start(bf16[8,32,384]{2,1,0:T(8,128)(2,1)} %bitcast.12), calls=%async_computation.4 | async-start | bytes 393216 | tf_op jit(solution)/shard_map/all_to_all | solution.py:179
  264.1 28.7 %all-to-all-start.5 = ((bf16[8,32,1152]{2,1,0:T(8,128)(2,1)}), bf16[8,32,1152]{2,1,0:T(8,128)(2,1)S(1)}, u32[]{:S(2)}, u32[]{:S(2)}) async-start(bf16[8,32,1152]{2,1,0:T(8,128)(2,1)} %bitcast.43), calls=%async_computation.6 | async-start | bytes 1179648 | tf_op jit(solution)/shard_map/all_to_all | solution.py:185
  272.6 13.8 %collective-permute-start.64 = (bf16[48,1024]{1,0:T(8,128)(2,1)}, bf16[48,1024]{1,0:T(8,128)(2,1)S(1)}, u32[]{:S(2)}, u32[]{:S(2)}) collective-permute-start(bf16[48,1024]{1,0:T(8,128)(2,1)} %get-tuple-element.732), channel_id=1, source_target_pairs={{0,8},{1,9},{2,10},{3,11},{4,12},{5,13},{6,14},{7,15},{8,16},{9,17... | collective-permute-start | bytes 294920 | tf_op jit(solution)/shard_map/ppermute | solution.py:134
  274.6 18.1 %collective-permute-start.65 = (bf16[48,1024]{1,0:T(8,128)(2,1)}, bf16[48,1024]{1,0:T(8,128)(2,1)S(1)}, u32[]{:S(2)}, u32[]{:S(2)}) collective-permute-start(bf16[48,1024]{1,0:T(8,128)(2,1)} %get-tuple-element.733), channel_id=1, source_target_pairs={{0,16},{1,17},{2,18},{3,19},{4,20},{5,21},{6,22},{7,23},{8,24},{9,... | collective-permute-start | bytes 294920 | tf_op jit(solution)/shard_map/ppermute | solution.py:134
  277.0 15.8 %collective-permute-start.66 = (bf16[48,1024]{1,0:T(8,128)(2,1)S(1)}, bf16[48,1024]{1,0:T(8,128)(2,1)S(1)}, u32[]{:S(2)}, u32[]{:S(2)}) collective-permute-start(bf16[48,1024]{1,0:T(8,128)(2,1)S(1)} %copy-done.78), channel_id=1, source_target_pairs={{0,24},{1,25},{2,26},{3,27},{4,28},{5,29},{6,30},{7,31},{8,0},{9,1... | collective-permute-start | bytes 294920 | tf_op jit(solution)/shard_map/ppermute | solution.py:134
  (91 other events, 1327.5 us)
Sparse Core Ops, SparseCore 0:
  9.8 30.8 all-gather.5
  59.3 41.0 all-gather.3
  183.0 38.7 reduce-scatter.2
  224.6 28.3 reduce-scatter.4
where the time goes:
time: 307 us; the launch traced here: 306 us
  waiting for transfers between devices  122 us (40%)
  Pallas kernels  78.2 us (25%)
  starting transfers between devices  56.8 us (19%)
  between operations  15.1 us (5%)
  local copies, waits for them, and re-layouts  12.2 us (4%)
  blocking collectives  11 us (4%)
  other arithmetic  10.3 us (3%)
    ppermute x67, waiting for transfers between devices, one_step(): got.append(lax.ppermute(values[at], 'dp', self.pairs(move[1])))  104 us
    pallas_call x19, Pallas kernels, call(): pl.pallas_call(kernel, out_shape=out_shape, scratch_shapes=list(scratch),...  78.2 us
    ppermute x67, starting transfers between devices, one_step(): got.append(lax.ppermute(values[at], 'dp', self.pairs(move[1])))  37.4 us
    all_to_all x3, waiting for transfers between devices, exchange(): lax.all_to_all(blocks, 'dp', 0, 0, axis_index_groups=groups, tiled=True)  15.8 us
    all_to_all x1, blocking collectives, exchange(): lax.all_to_all(blocks, 'dp', 0, 0, axis_index_groups=groups, tiled=True)  11 us
    all_to_all x3, starting transfers between devices, exchange(): lax.all_to_all(blocks, 'dp', 0, 0, axis_index_groups=groups, tiled=True)  10.5 us
    all_to_all x2, starting transfers between devices, line_exchange(): lax.all_to_all(blocks, 'dp', 0, 0, axis_index_groups=groups, tiled=True)  8.75 us
    unnamed x159, local copies, waits for them, and re-layouts  7.38 us
  transfers between devices with their start and end apart: 76, of which 26 were waited for; matrix products, arithmetic and copies ran while one was open for 4% of the time, Pallas kernels for 25%

commit v1 on v0

v1 whole, which is shorter than its diff:
```python
import jax
import jax.numpy as jnp
from jax import lax
from jax.experimental import pallas as pl
from jax.experimental.pallas import tpu as pltpu
from jax.sharding import PartitionSpec as P

epsilon = 1e-05
TEAM = 8
HALO = 16
WIDE = jnp.float32
NARROW = jnp.bfloat16


def dot(left, right, contract):
    return lax.dot_general(left, right, (contract, ((), ())), preferred_element_type=WIDE)


def fetch(pairs, sems):
    copies = [pltpu.make_async_copy(a, b, sems.at[i]) for i, (a, b) in enumerate(pairs)]
    for copy in copies:
        copy.start()
    return copies


def shape(kind, *sizes):
    return jax.ShapeDtypeStruct(sizes, kind)


def call(kernel, name, out_shape, operands, scratch=(), flops=0, in_place=False):
    places = {}
    if in_place:
        spec = pl.BlockSpec(memory_space=pl.ANY)
        places["in_specs"] = [spec] * len(operands) if in_place is True else in_place
    size = sum(x.size * x.dtype.itemsize for x in operands)
    return pl.pallas_call(
        kernel,
        out_shape=out_shape,
        scratch_shapes=list(scratch),
        compiler_params=pltpu.CompilerParams(vmem_limit_bytes=60 * 2**20),
        cost_estimate=pl.CostEstimate(flops=flops, bytes_accessed=size, transcendentals=0),
        name=name,
        **places,
    )(*operands)


class Job:
    def __init__(self, steps):
        self.steps = steps
        self.result = None
        self.open = True
        self.request = None
        self.held = False
        self.send(None)

    def send(self, value):
        try:
            self.request = self.steps.send(value)
        except StopIteration as stop:
            self.result, self.open, self.request = stop.value, False, None


class Net:
    def __init__(self):
        self.count = lax.axis_size("dp")
        self.teams = self.count // TEAM
        self.index = lax.axis_index("dp")
        self.place = self.index % TEAM
        self.team = self.index // TEAM
        self.core = self.index % 2
        self.peer = (self.index // 2) % 4
        self.jobs = []
        self.waiting = []
        self.gate = []
        self.extra = []

    def pairs(self, move):
        if move[0] == "swap":
            return [(i, i ^ move[1]) for i in range(self.count)]
        if move[0] == "ring":
            return [(i, (i + move[1] * TEAM) % self.count) for i in range(self.count)]
        if move[0] == "mixed":
            return [(i, i ^ (2 if i % 2 == 0 else 4)) for i in range(self.count)]
        return [(i, i - TEAM) for i in range(TEAM, self.count)]

    def do(self, call, *operands):
        def steps():
            (got,) = yield [(operands, ("call", call))]
            return got

        return self.spawn(steps())

    def spawn(self, steps):
        job = Job(steps)
        if job.open:
            self.jobs.append(job)
        return job

    def need(self, *values):
        self.extra.extend(values)

    def later(self, value):
        return lax.optimization_barrier((value, self.gate))[0]

    def step(self, times=1):
        for _ in range(times):
            self.one_step()

    def one_step(self):
        ready = [job for job in self.jobs if job.request is not None and not job.held]
        values = [move[0] for job in ready for move in job.request]
        self.raw = []
        if values or self.waiting:
            values, _ = lax.optimization_barrier((values, (self.gate, self.extra)))
            self.extra = []
            at = 0
            for job in ready:
                span = 1
                got = []
                moves = job.request
                for move in moves:
                    if len(move) > 2:
                        span = move[2]
                    if move[1][0] == "call":
                        got.append(move[1][1](*values[at]))
                    else:
                        got.append(lax.ppermute(values[at], "dp", self.pairs(move[1])))
                    at += 1
                job.request = None
                self.raw.extend(zip([move[1] for move in moves], got))
                self.waiting.append([span, job, got])
        for entry in self.waiting:
            entry[0] -= 1
        done = [entry for entry in self.waiting if entry[0] <= 0]
        self.waiting = [entry for entry in self.waiting if entry[0] > 0]
        results = lax.optimization_barrier([entry[2] for entry in done])
        self.gate = results
        for (_, job, _), got in zip(done, results):
            job.send(got)
        self.jobs = [job for job in self.jobs if job.open]

    def until(self, *jobs):
        while any(job.open for job in jobs):
            self.one_step()
        return [job.result for job in jobs] if len(jobs) > 1 else jobs[0].result


    def blocks(self, value):
        across, along, twin = yield [
            (value, ("swap", 2)),
            (value, ("swap", 4)),
            (value, ("swap", 1)),
        ]
        corner, across_twin, along_twin = yield [
            (jnp.where(self.core == 0, along, across), ("mixed",)),
            (across, ("swap", 1)),
            (along, ("swap", 1)),
        ]
        (corner_twin,) = yield [(corner, ("swap", 1))]
        return [value, twin, across, across_twin, along, along_twin, corner, corner_twin]

    def blocks_direct(self, value):
        found = yield [(value, ("swap", mask)) for mask in (2, 4, 6, 1)]
        twins = yield [(block, ("swap", 1)) for block in found[:3]]
        return [value, found[3], found[0], twins[0], found[1], twins[1], found[2], twins[2]]

    def team_sum(self, odd, fold, span=1):
        (arrived,) = yield [(odd, ("swap", 1))]
        call, operands = fold(arrived)
        (parts,) = yield [(operands, ("call", call))]
        moved = yield [(part, ("swap", mask), span) for part, mask in zip(parts[1:], (6, 2, 4))]
        return [parts[0]] + moved

    def exchange(self, blocks):
        groups = [[base + q for q in range(TEAM)] for base in range(0, self.count, TEAM)]
        return lax.all_to_all(blocks, "dp", 0, 0, axis_index_groups=groups, tiled=True)

    def line_both(self, value):
        teams = self.teams
        found, up, down = {0: value}, value, value
        for step in range(1, teams // 2 + 1):
            moves = [(up, ("ring", 1))]
            if step < teams - step:
                moves.append((down, ("ring", teams - 1)))
            got = yield moves
            found[step], up = got[0], got[0]
            if len(got) > 1:
                found[teams - step], down = got[1], got[1]
        return jnp.concatenate([found[k] for k in range(teams)], 0)

    def line_send(self, parts, span=1):
        return (yield [(part, ("ring", k + 1), span) for k, part in enumerate(parts)])

    def line_sum(self, shares):
        total = shares[-1].astype(NARROW)
        for share in reversed(shares[:-1]):
            (got,) = yield [(total, ("ring", 1))]
            total = share + got.astype(WIDE)
            total = total if share is shares[0] else total.astype(NARROW)
        return total


def scale_of(values):
    return lax.rsqrt(jnp.mean(values * values, axis=1, keepdims=True) + epsilon)


def norm_back(upstream, normed, scaler, gain):
    scaled = upstream * gain
    return scaler * (scaled - normed * jnp.mean(scaled * normed, axis=1, keepdims=True))


def where_am_i():
    index = lax.axis_index("dp")
    return index % TEAM, index // TEAM


def at(start, size, step=16):
    return pl.ds(pl.multiple_of(start, step), size)


def summed_parts(left, right, arrived, turned, name, relative=False):
    rows, width = arrived.shape[0] // 4, arrived.shape[1]
    deep = left.shape[1]
    contract = ((1,), (1,)) if turned else ((1,), (0,))

    def kernel(left_in, right_in, arrived_in, own, corner, across, along, left, right, arrived, sems):
        place, _ = where_am_i()
        copies = [(right_in, right), (arrived_in, arrived)]
        for k in range(4):
            source = left_in
            if relative:
                source = left_in.at[at((place ^ (2 * k)) * rows, rows), :]
            else:
                source = left_in.at[k * rows : (k + 1) * rows, :]
            copies.append((source, left.at[k * rows : (k + 1) * rows, :]))
        for copy in fetch(copies, sems):
            copy.wait()
        total = dot(left[...], right[...], contract) + arrived[...].astype(WIDE)
        for k, out in ((3, corner), (1, across), (2, along), (0, own)):
            out[...] = total[k * rows : (k + 1) * rows].astype(out.dtype)

    outs = (shape(WIDE, rows, width),) + (shape(NARROW, rows, width),) * 3
    return call(
        kernel,
        name,
        outs,
        (left, right, arrived),
        [
            pltpu.VMEM((4 * rows, deep), NARROW),
            pltpu.VMEM(right.shape, NARROW),
            pltpu.VMEM(arrived.shape, NARROW),
            pltpu.SemaphoreType.DMA((6,)),
        ],
        8 * rows * deep * width,
        in_place=True,
    )


def pieces(ffpart, even, own):
    runs = []
    for z in range(own // ffpart):
        for start, stop in ((0, even), (even, own)):
            low, high = max(z * ffpart, start), min((z + 1) * ffpart, stop)
            if low < high:
                at_gate = low if start == 0 else 2 * even + low - even
                at_up = even + low if start == 0 else own + low
                runs.append((z, low, high, at_gate, at_up))
    return runs


def in_prepare(weight, gains, marks, taps, teams):
    part, width = weight.shape
    features = width // 3
    channels = features // TEAM
    slots = max(128, TEAM * part) // part

    def kernel(weight, gain_one, gain_two, marks, taps, out, wide, small):
        index = lax.axis_index("dp")
        whole = weight[...].astype(WIDE)
        small[...] = jnp.zeros_like(small)
        for slot in range(slots):
            mine = lax.rem(index, slots) == slot
            for row, gain in enumerate((gain_one, gain_two)):
                value = gain[...].astype(WIDE)
                value = jnp.where(mine, value, jnp.zeros_like(value))
                small[row : row + 1, slot * part : (slot + 1) * part] = value
        small[0:1, 2 * channels :] = marks[...].astype(WIDE)
        for slot in range(teams):
            value = taps[...].astype(WIDE)
            value = jnp.where(index // TEAM == slot, value, jnp.zeros_like(value))
            for k in range(3):
                to = k * channels + slot * part
                small[2:3, to : to + part] = value[k : k + 1, :]
        for p in range(TEAM):
            for k in range(3):
                for z in range(teams):
                    source = k * features + (z * TEAM + p) * part
                    to = k * channels + z * part
                    wide[:, to : to + part] = whole[:, source : source + part]
            out[p, :part, :] = wide[...].astype(NARROW)
            out[p, part:, :] = small[...].astype(NARROW)

    return call(
        kernel,
        "in_prepare",
        shape(NARROW, TEAM, part + 8, 3 * channels),
        (weight, *gains, marks, taps),
        [pltpu.VMEM((part, 3 * channels), WIDE), pltpu.VMEM((8, 3 * channels), WIDE)],
    )


def in_finish(blocks, weight, gain, teams):
    part, width = weight.shape
    features = width // 3
    channels = features // TEAM

    def kernel(blocks, weight, gain, out, gain_grad):
        for p in range(TEAM):
            block = blocks[p].astype(WIDE)
            for k in range(3):
                for z in range(teams):
                    to = k * features + (z * TEAM + p) * part
                    source = k * channels + z * part
                    out[:, to : to + part] = block[:, source : source + part]
        product = jnp.sum(weight[...].astype(WIDE) * out[...], axis=1, keepdims=True)
        gain_grad[...] = product / gain[...].astype(WIDE)

    outs = (shape(WIDE, part, width), shape(WIDE, part, 1))
    return call(kernel, "in_finish", outs, (blocks, weight, gain))


def pair_prepare(gate, up, teams):
    part, inner = gate.shape
    own = inner // TEAM
    ffpart = own // teams
    even = own // 128 * 128
    runs = pieces(ffpart, even, own)

    def kernel(gate, up, out, wide):
        gates, ups = gate[...].astype(WIDE), up[...].astype(WIDE)
        for p in range(TEAM):
            for z, low, high, at_gate, at_up in runs:
                source = (z * TEAM + p) * ffpart + low - z * ffpart
                size = high - low
                wide[:, at_gate : at_gate + size] = gates[:, source : source + size]
                wide[:, at_up : at_up + size] = ups[:, source : source + size]
            out[p] = wide[...].astype(NARROW)

    out = shape(NARROW, TEAM, part, 2 * own)
    scratch = [pltpu.VMEM((part, 2 * own), WIDE)]
    return call(kernel, "pair_prepare", out, (gate, up), scratch)


def pair_finish(blocks, gate, up, gain, teams):
    part, inner = gate.shape
    own = inner // TEAM
    ffpart = own // teams
    even = own // 128 * 128
    runs = pieces(ffpart, even, own)

    def kernel(blocks, gate, up, gain, gate_grad, up_grad, gain_grad):
        for p in range(TEAM):
            block = blocks[p].astype(WIDE)
            for z, low, high, at_gate, at_up in runs:
                to = (z * TEAM + p) * ffpart + low - z * ffpart
                size = high - low
                gate_grad[:, to : to + size] = block[:, at_gate : at_gate + size]
                up_grad[:, to : to + size] = block[:, at_up : at_up + size]
        product = gate[...].astype(WIDE) * gate_grad[...] + up[...].astype(WIDE) * up_grad[...]
        gain_grad[...] = jnp.sum(product, axis=1, keepdims=True) / gain[...].astype(WIDE)

    outs = (shape(WIDE, part, inner), shape(WIDE, part, inner), shape(WIDE, part, 1))
    return call(kernel, "pair_finish", outs, (blocks, gate, up, gain))


def mixer_forward(blocks, before, weights):
    rows, features = blocks[0].shape
    tokens = TEAM * rows
    count, _, channels = weights.shape
    channels = channels // 3
    teams = count // TEAM
    share, part = features // teams, features // count

    def kernel(*refs):
        blocks, (before, weights), refs = refs[:TEAM], refs[TEAM : TEAM + 2], refs[TEAM + 2 :]
        normed, mixed, gated, conv, mixer_in, in_own, gain, gain_two, taps, keeps = refs[:10]
        hs, small, sems = refs[10:]
        place, team = where_am_i()
        copies = [(weights.at[:, part:, :], small)]
        for d in range(count):
            to = in_own.at[d * part : (d + 1) * part, :]
            copies.append((weights.at[d, :part, :], to))
        for m in range(TEAM):
            copies.append((blocks[m], hs.at[at(HALO + (place ^ m) * rows, rows), :]))
        copies.append((before, hs.at[:HALO, :]))
        for copy in fetch(copies, sems):
            copy.wait()
        first = hs[:HALO, :]
        hs[:HALO, :] = jnp.where(team > 0, first, jnp.zeros_like(first))
        total = jnp.zeros((1, 3 * channels), WIDE)
        gain[...] = jnp.zeros_like(gain)
        gain_two[...] = jnp.zeros_like(gain_two)
        span = max(share, 128)
        for z in range(teams):
            both = sum(small[z * TEAM + p].astype(WIDE) for p in range(TEAM))
            one, two = both[0:1], both[1:2]
            total = total + small[z * TEAM + place].astype(WIDE)[2:3]
            to = slice(z * share // span * span, z * share // span * span + span)
            gain[:, to] = gain[:, to] + one[:, :span]
            gain_two[:, to] = gain_two[:, to] + two[:, :span]
        taps[...] = jnp.zeros_like(taps)
        for k in range(3):
            taps[k : k + 1, :] = total[:, k * channels : (k + 1) * channels]
        marks = [
            1.0 - small[team * TEAM + p].astype(WIDE)[0:1, 2 * channels :] for p in range(TEAM)
        ]
        keep = jnp.concatenate([mark.reshape(rows, 1) for mark in marks], 0)
        keeps[8:, 0:1] = keep
        before_team = lax.rem(team + teams - 1, teams) * TEAM + TEAM - 1
        last = 1.0 - small[before_team].astype(WIDE)[0:1, 3 * channels - 1 :]
        keeps[7:8, 0:1] = last
        keeps[8:, 1:2] = keep * keeps[7 : 7 + tokens, 0:1]
        scale = gain[...]

        def norm(start, size):
            values = hs[at(start, size), :].astype(WIDE)
            values = values * scale_of(values) * scale
            normed[at(start, size), :] = values.astype(NARROW)

        norm(0, HALO)

        @pl.loop(0, TEAM)
        def _(step):
            norm(HALO + step * rows, rows)

        mixed[...] = dot(normed[...], in_own[...], ((1,), (0,)))
        gated[...] = (mixed[:, :channels] * mixed[:, 2 * channels :]).astype(NARROW).astype(WIDE)
        conv_out = (
            taps[2:3, :] * gated[HALO:, :]
            + taps[1:2, :] * (keeps[8:, 0:1] * gated[HALO - 1 : HALO - 1 + tokens, :])
            + taps[0:1, :] * (keeps[8:, 1:2] * gated[HALO - 2 : HALO - 2 + tokens, :])
        )
        conv[...] = conv_out
        mixer_in[...] = (mixed[HALO:, channels : 2 * channels] * conv_out).astype(NARROW)

    outs = (
        shape(NARROW, HALO + tokens, features),
        shape(WIDE, HALO + tokens, 3 * channels),
        shape(WIDE, HALO + tokens, channels),
        shape(WIDE, tokens, channels),
        shape(NARROW, tokens, channels),
        shape(NARROW, features, 3 * channels),
        shape(WIDE, 1, features),
        shape(WIDE, 1, features),
        shape(WIDE, 8, channels),
        shape(WIDE, 8 + tokens, 2),
    )
    return call(
        kernel,
        "mixer_forward",
        outs,
        (*blocks, before, weights),
        [
            pltpu.VMEM((HALO + tokens, features), NARROW),
            pltpu.VMEM((count, 8, 3 * channels), NARROW),
            pltpu.SemaphoreType.DMA((count + TEAM + 2,)),
        ],
        2 * tokens * features * 3 * channels,
        in_place=True,
    )


def out_rows(blocks, whole, teams):
    place, team = where_am_i()
    channels = blocks[0].shape[0]
    share = channels // teams
    copies = []
    for m, block in enumerate(blocks):
        for k in range(teams):
            to = (place ^ m) * channels + lax.rem(team - k + teams, teams) * share
            copies.append((block.at[k * share : (k + 1) * share, :], whole.at[at(to, share, 8), :]))
    return copies


def out_project(mixer_blocks, out_blocks, hidden_blocks, gain, teams):
    rows, features = hidden_blocks[0].shape
    tokens, channels = mixer_blocks[0].shape

    def kernel(*refs):
        mixer_in, out_in, hidden_in = [refs[k * TEAM : (k + 1) * TEAM] for k in range(3)]
        gain, resid, odd, even, mixer, turned, out, hidden, sems = refs[3 * TEAM :]
        place, _ = where_am_i()
        copies = out_rows(out_in, out, teams)
        for m in range(TEAM):
            to = mixer.at[:, at((place ^ m) * channels, channels, 128)]
            copies.append((mixer_in[m], to))
            copies.append((hidden_in[m], hidden.at[m]))
        for copy in fetch(copies, sems):
            copy.wait()
        for half, side in ((1, odd), (0, even)):
            for k in range(TEAM // 2):
                source = mixer[at((place ^ (2 * k + half)) * rows, rows), :]
                turned[k * rows : (k + 1) * rows, :] = source
            product = dot(turned[...], out[...], ((1,), (0,)))
            for k in range(TEAM // 2):
                span = slice(k * rows, (k + 1) * rows)
                total = hidden[2 * k + half].astype(WIDE) + product[span]
                side[span, :] = (total * scale_of(total) * gain[...]).astype(NARROW)
                if k + half == 0:
                    resid[...] = total

    outs = (shape(WIDE, rows, features),) + (shape(NARROW, tokens // 2, features),) * 2
    any_place, in_vmem = pl.BlockSpec(memory_space=pl.ANY), pl.BlockSpec(memory_space=pltpu.VMEM)
    return call(
        kernel,
        "out_project",
        outs,
        (*mixer_blocks, *out_blocks, *hidden_blocks, gain),
        [
            pltpu.VMEM((tokens, features), NARROW),
            pltpu.VMEM((tokens // 2, features), NARROW),
            pltpu.VMEM((features, features), NARROW),
            pltpu.VMEM((TEAM, rows, features), NARROW),
            pltpu.SemaphoreType.DMA((TEAM * teams + 2 * TEAM,)),
        ],
        2 * tokens * features * features,
        in_place=[any_place] * (3 * TEAM) + [in_vmem],
    )


def ffn_parts(gate, up, grad):
    sigmoid = 1.0 / (1.0 + jnp.exp(-gate))
    scaled = gate * sigmoid
    gate_grad = grad * up * sigmoid * (1.0 + gate * (1.0 - sigmoid))
    return scaled * up, gate_grad, grad * scaled


def ffn_block(inputs, upstream, pair, down, send):
    count = len(upstream)
    rows, features = upstream[0].shape
    own = down.shape[0]
    even = own // 128 * 128
    width = own - even
    total = count * rows

    def kernel(*refs):
        x_in, g_in, refs = refs[0], refs[1 : 1 + count], refs[1 + count :]
        pair_in, down_in, act, grads = refs[:4]
        xs, gs, pair, down, last, sems = refs[-6:]
        first = [(x_in, xs), (pair_in, pair)]
        second = [(g_in[k], gs.at[k * rows : (k + 1) * rows, :]) for k in range(count)]
        second.append((down_in, down))
        copies = fetch(first + second, sems)
        for copy in copies[:2]:
            copy.wait()
        x = xs[...]
        gate = dot(x, pair[:, :even], ((1,), (0,)))
        up = dot(x, pair[:, even : 2 * even], ((1,), (0,)))
        for copy in copies[2:]:
            copy.wait()
        g = gs[...]
        grad = dot(g, down[:even, :], ((1,), (1,)))
        value, gate_grad, up_grad = ffn_parts(gate, up, grad)
        act[:, :even] = value.astype(NARROW)
        grads[:, :even] = gate_grad.astype(NARROW)
        grads[:, even : 2 * even] = up_grad.astype(NARROW)
        last[:width, :] = down[even:, :]
        last[width:, :] = down[even:, :]
        both = dot(x, pair[:, 2 * even :], ((1,), (0,)))
        turned = pltpu.roll(both, width, 1)
        lower = lax.broadcasted_iota(jnp.int32, both.shape, 1) < width
        grad = dot(g, last[...], ((1,), (1,)))
        value, gate_grad, up_grad = ffn_parts(
            jnp.where(lower, both, turned), jnp.where(lower, turned, both), grad
        )
        act[:, even:] = value[:, :width].astype(NARROW)
        grads[:, 2 * even :] = jnp.where(lower, gate_grad, up_grad).astype(NARROW)
        if send:
            refs[4][...] = dot(grads[...], pair[...], ((1,), (1,))).astype(NARROW)

    outs = (shape(NARROW, total, own), shape(NARROW, total, 2 * own))
    if send:
        outs += (shape(NARROW, total, features),)
    return call(
        kernel,
        "ffn",
        outs,
        (inputs, *upstream, pair, down),
        [
            pltpu.VMEM((total, features), NARROW),
            pltpu.VMEM((total, features), NARROW),
            pltpu.VMEM((features, 2 * own), NARROW),
            pltpu.VMEM((own, features), NARROW),
            pltpu.VMEM((2 * width, features), NARROW),
            pltpu.SemaphoreType.DMA((count + 3,)),
        ],
        10 * total * features * own,
        in_place=True,
    )


def ffn_output(act, down):
    def kernel(act, down, out):
        out[...] = dot(act[...], down[...], ((1,), (0,))).astype(NARROW)

    rows, features = act.shape[0], down.shape[1]
    out = shape(NARROW, rows, features)
    return call(kernel, "ffn_output", out, (act, down), flops=2 * rows * features * down.shape[0])


def weight_grads(lefts, rights, name):
    deep, wide = lefts[0].shape[1], rights[0].shape[1]
    tokens = sum(left.shape[0] for left in lefts)

    def kernel(*refs):
        ins, (out, left, right, sems) = refs[: len(lefts) + len(rights)], refs[-4:]
        pairs = []
        for blocks, whole in ((ins[: len(lefts)], left), (ins[len(lefts) :], right)):
            row = 0
            for block in blocks:
                pairs.append((block, whole.at[row : row + block.shape[0], :]))
                row += block.shape[0]
        for copy in fetch(pairs, sems):
            copy.wait()
        for start in range(0, deep, 256):
            stop = min(start + 256, deep)
            total = dot(left[:, start:stop], right[...], ((0,), (0,)))
            out[start:stop, :] = total.astype(NARROW)

    return call(
        kernel,
        name,
        shape(NARROW, deep, wide),
        (*lefts, *rights),
        [
            pltpu.VMEM((tokens, deep), NARROW),
            pltpu.VMEM((tokens, wide), NARROW),
            pltpu.SemaphoreType.DMA((len(lefts) + len(rights),)),
        ],
        2 * tokens * deep * wide,
        in_place=True,
    )


def resid_back(parts, resid, gain, upstream, out_blocks, teams):
    rows, features = resid.shape
    channels = features // TEAM

    def kernel(own, corner, across, along, resid, gain, upstream, *refs):
        out_in, (resid_grad, rounded, mixer_grad, out, sems) = refs[:TEAM], refs[TEAM:]
        copies = fetch(out_rows(out_in, out, teams), sems)
        grad = own[...] + sum(part[...].astype(WIDE) for part in (corner, across, along))
        values = resid[...]
        scale = scale_of(values)
        grad = upstream[...].astype(WIDE) + norm_back(grad, values * scale, scale, gain[...])
        resid_grad[...] = grad
        rounded[...] = grad.astype(NARROW)
        for copy in copies:
            copy.wait()
        product = dot(rounded[...], out[...], ((1,), (1,))).astype(NARROW)
        for p in range(TEAM):
            mixer_grad[p] = product[:, p * channels : (p + 1) * channels]

    outs = (
        shape(WIDE, rows, features),
        shape(NARROW, rows, features),
        shape(NARROW, TEAM, rows, channels),
    )
    any_place, in_vmem = pl.BlockSpec(memory_space=pl.ANY), pl.BlockSpec(memory_space=pltpu.VMEM)
    return call(
        kernel,
        "resid_back",
        outs,
        (*parts, resid, gain, upstream, *out_blocks),
        [
            pltpu.VMEM((features, features), NARROW),
            pltpu.SemaphoreType.DMA((TEAM * teams,)),
        ],
        2 * rows * features * features,
        in_place=[in_vmem] * 7 + [any_place] * TEAM,
    )


def conv_back(mixer_grad, mixed, gated, conv, taps, keeps):
    tokens, channels = conv.shape

    def kernel(mixer_grad, mixed, gated, conv, taps, keeps, part, rim, taps_grad, ones, twos):
        grad = mixer_grad[...].astype(WIDE)
        conv_grad = grad * mixed[HALO:, channels : 2 * channels]
        one, two = keeps[8:, 0:1] * conv_grad, keeps[8:, 1:2] * conv_grad
        zeros = jnp.zeros((8, channels), WIDE)
        taps_grad[...] = zeros
        for k, (left, back) in enumerate(((two, 2), (one, 1), (conv_grad, 0))):
            product = left * gated[HALO - back : HALO - back + tokens, :]
            taps_grad[k : k + 1, :] = jnp.sum(product, axis=0, keepdims=True)
        ones[:tokens, :] = taps[1:2, :] * one
        twos[:tokens, :] = taps[0:1, :] * two
        ones[tokens:, :] = zeros
        twos[tokens:, :] = zeros
        rim[...] = zeros
        rim[6:7, :] = twos[0:1, :]
        rim[7:8, :] = twos[1:2, :] + ones[0:1, :]
        part[...] = taps[2:3, :] * conv_grad + ones[1 : tokens + 1, :] + twos[2 : tokens + 2, :]

    outs = (shape(WIDE, tokens, channels), shape(WIDE, 8, channels), shape(WIDE, 8, channels))
    scratch = [pltpu.VMEM((tokens + 8, channels), WIDE)] * 2
    return call(
        kernel, "conv_back", outs, (mixer_grad, mixed, gated, conv, taps, keeps), scratch
    )


def mixer_back(part, returned, mixer_grad, mixed, conv, normed, in_own, teams):
    tokens, channels = conv.shape
    features = in_own.shape[0]
    rows, share = tokens // TEAM, features // teams

    def kernel(*refs):
        part, returned, mixer_grad, mixed, conv, normed, in_own, grads, odd = refs[:9]
        shares, (side, whole, weight) = refs[9 : 9 + teams], refs[9 + teams :]
        place, team = where_am_i()
        whole[...] = part[...]
        whole[tokens - 8 :, :] = part[tokens - 8 :, :] + returned[...]
        gated_grad = whole[...]
        grads[:, :channels] = (gated_grad * mixed[HALO:, 2 * channels :]).astype(NARROW)
        grads[:, channels : 2 * channels] = (
            mixer_grad[...].astype(WIDE) * conv[...]
        ).astype(NARROW)
        grads[:, 2 * channels :] = (gated_grad * mixed[HALO:, :channels]).astype(NARROW)
        for chip in range(TEAM // 2):
            at_place = place ^ (2 * chip + 1)
            side[chip * rows : (chip + 1) * rows, :] = grads[at(at_place * rows, rows), :]
        step = features // 4
        for start in range(0, features, step):
            span = slice(start, start + step)
            weight[span, :] = dot(normed[HALO:, span], grads[...], ((0,), (0,)))
        for k in range(teams):
            owner = lax.rem(team + k, teams)
            shares[k][...] = weight[at(owner * share, share), :].astype(shares[k].dtype)
        odd[...] = dot(side[...], in_own[...], ((1,), (1,))).astype(NARROW)

    outs = (shape(NARROW, tokens, 3 * channels), shape(NARROW, tokens // 2, features))
    outs += tuple(
        shape(NARROW if k == teams - 1 else WIDE, share, 3 * channels) for k in range(teams)
    )
    grads, odd, *shares = call(
        kernel,
        "mixer_back",
        outs,
        (part, returned, mixer_grad, mixed, conv, normed, in_own),
        [
            pltpu.VMEM((tokens // 2, 3 * channels), NARROW),
            pltpu.VMEM((tokens, channels), WIDE),
            pltpu.VMEM((features, 3 * channels), WIDE),
        ],
        3 * tokens * features * 3 * channels,
    )
    return grads, odd, shares


def out_back(mixer_in, blocks, taps_grad, teams):
    rows, features = blocks[0].shape
    channels = mixer_in.shape[1]
    share = channels // teams
    low = (share + 15) // 16 * 16

    def kernel(*refs):
        mixer_in, blocks, taps_grad = refs[0], refs[1 : 1 + TEAM], refs[1 + TEAM]
        shares, (total,) = refs[2 + TEAM : 2 + TEAM + teams], refs[2 + TEAM + teams :]
        place, team = where_am_i()
        total[...] = sum(
            dot(mixer_in[at((place ^ m) * rows, rows), :], blocks[m][...], ((0,), (0,)))
            for m in range(TEAM)
        )
        for k in range(teams):
            owner = lax.rem(team + k, teams)
            kind = shares[k].dtype
            shares[k][...] = jnp.zeros_like(shares[k])
            shares[k][:share, :] = total[at(owner * share, share, 8), :].astype(kind)
            shares[k][low : low + 8, :channels] = taps_grad[...].astype(kind)

    outs = tuple(
        shape(NARROW if k == teams - 1 else WIDE, low + 16, features) for k in range(teams)
    )
    return call(
        kernel,
        "out_back",
        outs,
        (mixer_in, *blocks, taps_grad),
        [pltpu.VMEM((channels, features), WIDE)],
        2 * TEAM * rows * channels * features,
    ), low


def body(
    hidden_in,
    seq_start,
    mixer_gain,
    in_weight,
    conv_weight,
    out_weight,
    ffn_gain,
    gate_weight,
    up_weight,
    down_weight,
    cotangent,
):
    net = Net()
    teams = net.teams
    rows, features = hidden_in.shape
    inner = gate_weight.shape[2]
    part = features // net.count
    ffpart = inner // net.count
    channels = features // TEAM
    ffown = inner // TEAM
    line = [[p + TEAM * z for z in range(teams)] for p in range(TEAM)]


    def gather(value):
        return lax.all_gather(value, "dp", axis=0, tiled=True, axis_index_groups=line)

    def reduce(value):
        return lax.psum_scatter(
            value, "dp", scatter_dimension=0, tiled=True, axis_index_groups=line
        )

    down_own = gather(down_weight[0])
    hidden_job = net.spawn(net.blocks_direct(hidden_in))
    sent = in_prepare(
        in_weight[0],
        (mixer_gain, ffn_gain),
        seq_start.reshape(1, rows),
        conv_weight[0].T,
        teams,
    )
    net.need(sent)
    got_job = net.do(net.exchange, sent)
    pair_job = net.do(lambda *x: pair_prepare(*x, teams), gate_weight[0], up_weight[0])
    net.step()
    out_job = net.spawn(net.line_both(out_weight[0]))
    pair_job = net.do(net.exchange, pair_job.result)
    in_job = net.do(gather, got_job.result.reshape(TEAM * (part + 8), 3 * channels))
    net.until(pair_job, in_job, hidden_job)

    def last_rows():
        last = hidden_job.result[0][-HALO:]
        for m in range(1, TEAM):
            block = hidden_job.result[m][-HALO:]
            last = jnp.where(net.place == (TEAM - 1) ^ m, block, last)
        (before,) = yield [(last, ("ring", 1))]
        return before

    halo_job = net.spawn(last_rows())
    before, out_rows_here = net.until(halo_job, out_job)
    weights = in_job.result.reshape(net.count, part + 8, 3 * channels)
    pair_own = gather(net.later(pair_job.result.reshape(TEAM * part, 2 * ffown)))
    out_job = net.spawn(net.blocks(out_rows_here))

    mix_job = net.do(
        lambda *x: mixer_forward(x[:TEAM], x[TEAM], x[TEAM + 1]),
        *hidden_job.result, before, weights,
    )
    (normed, mixed, gated, conv, mixer_in, in_own, gain_one, gain_two, taps, keeps) = net.until(
        mix_job
    )
    mixer_job = net.spawn(net.blocks(mixer_in))
    net.step()
    upstream_job = net.spawn(net.blocks(cotangent))
    mixer_blocks, out_blocks = net.until(mixer_job, out_job)
    project_job = net.do(
        lambda *x: out_project(
            x[:TEAM], x[TEAM : 2 * TEAM], x[2 * TEAM : 3 * TEAM], x[3 * TEAM], teams
        ),
        *mixer_blocks, *out_blocks, *hidden_job.result, gain_two,
    )
    resid, in_odd, in_even = net.until(project_job)
    upstream = net.until(upstream_job)

    def ffn(inputs, which, send):
        operands = (inputs, *upstream[which::2], pair_own, down_own)
        return (lambda *x: ffn_block(x[0], x[1:5], x[5], x[6], send)), operands

    call, operands = ffn(in_odd, 1, True)
    act_odd, grads_odd, back_odd = net.until(net.do(call, *operands))
    call, operands = ffn(in_even, 0, False)
    even_job = net.do(call, *operands)
    ffn_job = net.spawn(
        net.team_sum(
            back_odd,
            lambda arrived: (
                lambda *x: summed_parts(*x, True, "ffn_back"),
                (even_job.result[1], pair_own, arrived),
            ),
        )
    )
    act_even, grads_even = net.until(even_job)
    net.step()
    pair_job = net.do(
        lambda *x: weight_grads(x[:2], x[2:], "pair_grads"),
        in_odd, in_even, grads_odd, grads_even,
    )
    odd_job = net.do(ffn_output, act_odd, down_own)
    ffn_grad = net.until(ffn_job)
    pair_sum = reduce(pair_job.result)

    back_job = net.do(
        lambda *x: resid_back(x[:4], *x[4:7], x[7:], teams),
        *ffn_grad, resid, gain_two, cotangent, *out_blocks,
    )
    resid_grad, rounded, mixer_grad = net.until(back_job)
    down_job = net.do(
        lambda *x: weight_grads(x[:2], x[2:], "down_grads"),
        act_odd, act_even, *upstream[1::2], *upstream[0::2],
    )
    rounded_job = net.spawn(net.blocks(rounded))
    mixer_grad = net.until(net.do(net.exchange, mixer_grad)).reshape(TEAM * rows, channels)
    rounded_job.held = True
    down_sum = reduce(down_job.result)
    output_job = net.spawn(
        net.team_sum(
            odd_job.result,
            lambda arrived: (
                lambda *x: summed_parts(*x, False, "ffn_output_sum"),
                (act_even, down_own, arrived),
            ),
            2,
        )
    )
    gated_part, rim, taps_grad = net.until(
        net.do(conv_back, mixer_grad, mixed, gated, conv, taps, keeps)
    )
    rounded_job.held = False

    def rim_steps():
        (returned,) = yield [(rim, ("back",))]
        return returned

    returned = net.until(net.spawn(rim_steps()))
    mixed_grad, normed_odd, shares = net.until(
        net.do(
            lambda *x: mixer_back(*x, teams),
            gated_part, returned, mixer_grad, mixed, conv, normed, in_own,
        )
    )
    in_job = net.spawn(net.line_sum(shares))
    normed_job = net.spawn(
        net.team_sum(
            normed_odd,
            lambda arrived: (
                lambda *x: summed_parts(*x, True, "mixer_back_sum", True),
                (mixed_grad, in_own, arrived),
            ),
            2,
        )
    )
    low = (part + 15) // 16 * 16
    out_job = net.do(
        lambda *x: out_back(x[0], x[1 : 1 + TEAM], x[1 + TEAM], teams)[0],
        mixer_in, *net.until(rounded_job), taps_grad,
    )
    net.until(out_job)
    out_job = net.spawn(net.line_sum(out_job.result))
    pair_job = net.do(net.exchange, pair_sum.reshape(TEAM, part, 2 * ffown))
    in_grad = net.until(in_job).astype(NARROW)
    in_job = net.do(net.exchange, in_grad.reshape(TEAM, part, 3 * channels))
    finish_job = net.do(
        lambda *x: pair_finish(*x, teams),
        net.until(pair_job), gate_weight[0], up_weight[0], ffn_gain.reshape(part, 1),
    )
    in_grad = net.until(in_job)
    grad_gate, grad_up, grad_ffn_gain = net.until(finish_job)
    normed_grad, ffn_out, out_pack = net.until(normed_job, output_job, out_job)
    in_grad, grad_mixer_gain = in_finish(
        in_grad, in_weight[0], mixer_gain.reshape(part, 1), teams
    )

    def total(parts):
        return sum([part.astype(WIDE) for part in parts[1:]], parts[0])

    own_hidden = hidden_in.astype(WIDE)
    scale_one = scale_of(own_hidden)
    grad_hidden = resid_grad + norm_back(
        total(normed_grad), own_hidden * scale_one, scale_one, gain_one
    )
    hidden_out = (resid + total(ffn_out)).astype(NARROW)
    grad_out = out_pack[:part]
    grad_conv = lax.dynamic_slice(out_pack, (low, net.team * part), (3, part)).T
    return (
        hidden_out,
        grad_hidden,
        grad_mixer_gain.reshape(1, part),
        in_grad[None],
        grad_conv[None],
        grad_out[None],
        grad_ffn_gain.reshape(1, part),
        grad_gate[None],
        grad_up[None],
        down_sum.astype(WIDE)[None],
    )


def solution(mesh):
    tokens, wide, deep = P("dp", None), P(None, "dp"), P(None, "dp", None)
    return jax.shard_map(
        body,
        mesh=mesh,
        in_specs=(tokens, P("dp"), wide, deep, deep, deep, wide, deep, deep, deep, tokens),
        out_specs=(tokens, tokens, wide, deep, deep, deep, wide, deep, deep, deep),
        check_vma=False,
    )
```

time: 307 us -> 274 us (0.89)
  waiting for transfers between devices: 122 us -> 69.6 us
  blocking collectives: 11 us -> 24.2 us
  starting transfers between devices: 56.8 us -> 64.7 us
  local copies, waits for them, and re-layouts: 12.2 us -> 8.11 us
  Pallas kernels: 78.2 us -> 81.4 us
    ppermute x67 -> x58, waiting for transfers between devices: 104 us -> 57.4 us  [one_step(): got.append(lax.ppermute(values[at], 'dp', self.pairs(move[1])))]
    all_gather x0 -> x1, blocking collectives: none -> 24.2 us  [gather(): lax.all_gather(value, 'dp', axis=0, tiled=True, axis_index_groups=line)]
    all_to_all x1 -> x0, blocking collectives: 11 us -> none  [exchange(): lax.all_to_all(blocks, 'dp', 0, 0, axis_index_groups=groups, tiled=True)]
    all_to_all x2 -> x0, starting transfers between devices: 8.75 us -> none  [line_exchange(): lax.all_to_all(blocks, 'dp', 0, 0, axis_index_groups=groups, tiled=True)]
    ppermute x67 -> x58, starting transfers between devices: 37.4 us -> 46 us  [one_step(): got.append(lax.ppermute(values[at], 'dp', self.pairs(move[1])))]
    all_to_all x3 -> x5, starting transfers between devices: 10.5 us -> 18.6 us  [exchange(): lax.all_to_all(blocks, 'dp', 0, 0, axis_index_groups=groups, tiled=True)]
    all_to_all x3 -> x5, waiting for transfers between devices: 15.8 us -> 11.2 us  [exchange(): lax.all_to_all(blocks, 'dp', 0, 0, axis_index_groups=groups, tiled=True)]
    pallas_call x19 -> x18, Pallas kernels: 78.2 us -> 81.4 us  [call(): pl.pallas_call(kernel, out_shape=out_shape, scratch_shapes=list(scratch),...]
  transfers between devices with their start and end apart: 76 -> 67, of which waited for: 26 -> 19; matrix products, arithmetic and copies ran while one was open for 4% -> 2% of each run, Pallas kernels for 25% -> 25%
where the time goes in v1:
time: 274 us; the launch traced here: 272 us
  Pallas kernels  81.4 us (30%)
  waiting for transfers between devices  69.6 us (25%)
  starting transfers between devices  64.7 us (24%)
  blocking collectives  24.2 us (9%)
  between operations  15 us (5%)
  other arithmetic  9.33 us (3%)
  local copies, waits for them, and re-layouts  8.11 us (3%)
    pallas_call x18, Pallas kernels, call(): pl.pallas_call(kernel, out_shape=out_shape, scratch_shapes=list(scratch),...  81.4 us
    ppermute x58, waiting for transfers between devices, one_step(): got.append(lax.ppermute(values[at], 'dp', self.pairs(move[1])))  57.4 us
    ppermute x58, starting transfers between devices, one_step(): got.append(lax.ppermute(values[at], 'dp', self.pairs(move[1])))  46 us
    all_gather x1, blocking collectives, gather(): lax.all_gather(value, 'dp', axis=0, tiled=True, axis_index_groups=line)  24.2 us
    all_to_all x5, starting transfers between devices, exchange(): lax.all_to_all(blocks, 'dp', 0, 0, axis_index_groups=groups, tiled=True)  18.6 us
    all_to_all x5, waiting for transfers between devices, exchange(): lax.all_to_all(blocks, 'dp', 0, 0, axis_index_groups=groups, tiled=True)  11.2 us
    unnamed x147, local copies, waits for them, and re-layouts  5.99 us
  transfers between devices with their start and end apart: 67, of which 19 were waited for; matrix products, arithmetic and copies ran while one was open for 2% of the time, Pallas kernels for 25%

profile of v1, /device:TPU:0, one launch (start us, length us, event | category | flops | bytes accessed | tf_op | source)
XLA Modules:
  0.0 272.3 jit_solution(12617038109177155538)
XLA Ops:
  7.9 2.0 in_prepare.1
  9.9 2.9 %collective-permute-start = (bf16[128,1024]{1,0:T(8,128)(2,1)}, bf16[128,1024]{1,0:T(8,128)(2,1)S(1)}, u32[]{:S(2)}, u32[]{:S(2)}) collective-permute-start(bf16[128,1024]{1,0:T(8,128)(2,1)} %refs_16_), channel_id=1, source_target_pairs={{0,2},{1,3},{2,0},{3,1},{4,6},{5,7},{6,4},{7,5},{8,10},{9,11},{10,... | collective-permute-start | bytes 786440 | tf_op jit(solution)/shard_map/ppermute | solution.py:127
  12.8 1.5 collective-permute-start.1
  14.4 4.3 %all-to-all-start = ((bf16[8,40,384]{2,1,0:T(8,128)(2,1)}), bf16[8,40,384]{2,1,0:T(8,128)(2,1)S(1)}, u32[]{:S(2)}, u32[]{:S(2)}) async-start(bf16[8,40,384]{2,1,0:T(8,128)(2,1)} %in_prepare.1), calls=%async_computation | async-start | bytes 491520 | tf_op jit(solution)/shard_map/all_to_all | solution.py:176
  18.7 2.3 pair_prepare.1
  21.0 8.1 %all-to-all-done = bf16[8,40,384]{2,1,0:T(8,128)(2,1)S(1)} async-done(((bf16[8,40,384]{2,1,0:T(8,128)(2,1)}), bf16[8,40,384]{2,1,0:T(8,128)(2,1)S(1)}, u32[]{:S(2)}, u32[]{:S(2)}) %all-to-all-start) | async-done | bytes 245792 | tf_op jit(solution)/shard_map/all_to_all | solution.py:176
  29.1 3.6 %all-to-all-start.1 = ((bf16[8,32,1152]{2,1,0:T(8,128)(2,1)}), bf16[8,32,1152]{2,1,0:T(8,128)(2,1)S(1)}, u32[]{:S(2)}, u32[]{:S(2)}) async-start(bf16[8,32,1152]{2,1,0:T(8,128)(2,1)} %pair_prepare.1), calls=%async_computation.1 | async-start | bytes 1179648 | tf_op jit(solution)/shard_map/all_to_all | solution.py:176
  33.6 1.6 collective-permute-start.7
  35.2 2.2 collective-permute-start.8
  37.4 24.2 %all_gather.9 = bf16[1280,384]{1,0:T(8,128)(2,1)} all-gather(bf16[320,384]{1,0:T(8,128)(2,1)S(1)} %bitcast.44), channel_id=1, replica_groups={{0,8,16,24},{1,9,17,25},{2,10,18,26},{3,11,19,27},{4,12,20,28},{5,13,21..., dimensions={0}, use_global_device_ids=true | all-gather | bytes 1228800 | tf_op jit(solution)/shard_map/all_gather | solution.py:819
  62.6 1.6 collective-permute-start.10
  64.1 4.8 %collective-permute-done.10.refs_8_ = bf16[16,1024]{1,0:T(8,128)(2,1)S(1)} collective-permute-done((bf16[16,1024]{1,0:T(8,128)(2,1)S(1)}, bf16[16,1024]{1,0:T(8,128)(2,1)S(1)}, u32[]{:S(2)}, u32[]{:S(2)}) %collective-permute-start.10) | collective-permute-done | bytes 32800 | tf_op jit(solution)/shard_map/ppermute | solution.py:127
  69.2 1.5 collective-permute-start.11
  70.7 1.5 collective-permute-start.12
  72.2 7.1 %mixer_forward.1 = (bf16[1040,1024]{1,0:T(8,128)(2,1)}, f32[1040,384]{1,0:T(8,128)}, f32[1040,128]{1,0:T(8,128)}, f32[1024,128]{1,0:T(8,128)}, bf16[1024,128]{1,...) custom-call(bf16[128,1024]{1,0:T(8,128)(2,1)} %refs_16_, ...), custom_call_target="tpu_custom_call" | custom-call | flops 805306368 | bytes 3112960 | tf_op jit(solution)/shard_map/mixer_forward/pallas_call | solution.py:36
  80.5 1.5 collective-permute-start.17
  82.6 5.6 %collective-permute-done.14.refs_14_.refs_6_ = bf16[128,1024]{1,0:T(8,128)(2,1)S(1)} collective-permute-done((bf16[128,1024]{1,0:T(8,128)(2,1)S(1)}, bf16[128,1024]{1,0:T(8,128)(2,1)S(1)}, u32[]{:S(2)}, u32[]{:S(2)}) %collective-permute-start.14) | collective-permute-done | bytes 262176 | tf_op jit(solution)/shard_map/ppermute | solution.py:127
  88.2 3.2 %collective-permute-done.17.refs_2_ = bf16[1024,128]{1,0:T(8,128)(2,1)S(1)} collective-permute-done((bf16[1024,128]{1,0:T(8,128)(2,1)}, bf16[1024,128]{1,0:T(8,128)(2,1)S(1)}, u32[]{:S(2)}, u32[]{:S(2)}) %collective-permute-start.17) | collective-permute-done | bytes 262176 | tf_op jit(solution)/shard_map/ppermute | solution.py:127
  92.7 1.5 collective-permute-start.24
  94.8 5.8 %collective-permute-done.21.refs_6_ = bf16[1024,128]{1,0:T(8,128)(2,1)S(1)} collective-permute-done((bf16[1024,128]{1,0:T(8,128)(2,1)S(1)}, bf16[1024,128]{1,0:T(8,128)(2,1)S(1)}, u32[]{:S(2)}, u32[]{:S(2)}) %collective-permute-start.21) | collective-permute-done | bytes 262176 | tf_op jit(solution)/shard_map/ppermute | solution.py:127
  100.6 3.0 %collective-permute-done.24.refs_2_.refs_7_ = bf16[128,1024]{1,0:T(8,128)(2,1)S(1)} collective-permute-done((bf16[128,1024]{1,0:T(8,128)(2,1)S(1)}, bf16[128,1024]{1,0:T(8,128)(2,1)S(1)}, u32[]{:S(2)}, u32[]{:S(2)}) %collective-permute-start.24) | collective-permute-done | bytes 262176 | tf_op jit(solution)/shard_map/ppermute | solution.py:127
  105.3 4.9 %collective-permute-done.28.refs_4_.refs_9_ = bf16[128,1024]{1,0:T(8,128)(2,1)S(1)} collective-permute-done((bf16[128,1024]{1,0:T(8,128)(2,1)S(1)}, bf16[128,1024]{1,0:T(8,128)(2,1)S(1)}, u32[]{:S(2)}, u32[]{:S(2)}) %collective-permute-start.28) | collective-permute-done | bytes 262176 | tf_op jit(solution)/shard_map/ppermute | solution.py:127
  110.5 7.8 %out_project.1 = (f32[128,1024]{1,0:T(8,128)}, bf16[512,1024]{1,0:T(8,128)(2,1)}, bf16[512,1024]{1,0:T(8,128)(2,1)}) custom-call(bf16[1024,128]{1,0:T(8,128)(2,1)} %get-tuple-element.626.refs_0_, bf16[1024,128]{1,0:T(8,128)(2,1)} %copy-done.68, bf16[1024,128]{1,0:T(8,128)(2,1)} %copy-done.55, bf16[1024,128]{1,0:T(8,128)(2,1)} %copy-done.70, ...), custom_call_target="tpu_custom_call" | custom-call | flops 2147483648 | bytes 6295552 | tf_op jit(solution)/shard_map/out_project/pallas_call | solution.py:36
  119.0 7.2 %ffn.2 = (bf16[512,576]{1,0:T(8,128)(2,1)}, bf16[512,1152]{1,0:T(8,128)(2,1)}, bf16[512,1024]{1,0:T(8,128)(2,1)}) custom-call(bf16[512,1024]{1,0:T(8,128)(2,1)} %get-tuple-element.519.refs_0_, bf16[128,1024]{1,0:T(8,128)(2,1)} %copy-done.42, bf16[128,1024]{1,0:T(8,128)(2,1)} %copy-done.44, bf16[128,1024]{1,0:T(8,128)(2,1)} %copy-done.45, ...), custom_call_target="tpu_custom_call" | custom-call | flops 3019898880 | bytes 5636096 | tf_op jit(solution)/shard_map/ffn/pallas_call | solution.py:36
  126.8 6.2 %ffn.3 = (bf16[512,576]{1,0:T(8,128)(2,1)}, bf16[512,1152]{1,0:T(8,128)(2,1)}) custom-call(bf16[512,1024]{1,0:T(8,128)(2,1)} %get-tuple-element.520.refs_0_.refs_1_, bf16[128,1024]{1,0:T(8,128)(2,1)} %refs_6_, bf16[128,1024]{1,0:T(8,128)(2,1)} %copy-done.11, bf16[128,1024]{1,0:T(8,128)(2,1)} %copy-done.12, bf16[128,1024]{1,0:T(8,128)(2,1)} %copy-done.43, ...), custom_call_target="tpu_custom_call" | custom-call | flops 3019898880 | bytes 5636096 | tf_op jit(solution)/shard_map/ffn/pallas_call | solution.py:36
  133.1 1.0 copy-done.17
  134.1 4.8 %ffn_back.1 = (f32[128,1024]{1,0:T(8,128)}, bf16[128,1024]{1,0:T(8,128)(2,1)}, bf16[128,1024]{1,0:T(8,128)(2,1)}, bf16[128,1024]{1,0:T(8,128)(2,1)}) custom-call(bf16[512,1152]{1,0:T(8,128)(2,1)} %get-tuple-element.522.left_in.refs_3_, bf16[1024,1152]{1,0:T(8,128)(2,1)} %all-gather.4.cloned.1.call-done.refs_5_.right_in, bf16[512,1024]{1,0:T(8,128)(2,1)} %copy-done.17), custom_call_target="tpu_custom_call" | custom-call | flops 1207959552 | bytes 4587520 | tf_op jit(solution)/shard_map/ffn_back/pallas_call | solution.py:36
  138.9 1.5 collective-permute-start.33
  141.0 1.5 collective-permute-start.35
  142.4 3.7 %ffn_output.1 = bf16[512,1024]{1,0:T(8,128)(2,1)} custom-call(bf16[512,576]{1,0:T(8,128)(2,1)} %get-tuple-element.548.act.refs_0_, bf16[576,1024]{1,0:T(8,128)(2,1)} %bitcast.34), custom_call_target="tpu_custom_call" | custom-call | flops 603979776 | bytes 1769472 | tf_op jit(solution)/shard_map/ffn_output/pallas_call | solution.py:36
  146.1 6.6 %pair_grads.1 = bf16[1024,1152]{1,0:T(8,128)(2,1)} custom-call(bf16[512,1024]{1,0:T(8,128)(2,1)} %get-tuple-element.519.refs_0_, bf16[512,1024]{1,0:T(8,128)(2,1)} %get-tuple-element.520.refs_0_.refs_1_, bf16[512,1152]{1,0:T(8,128)(2,1)} %get-tuple-element.521.refs_2_, bf16[512,1152]{1,0:T(8,128)(2,1)} %get-tuple-element.522.left_in.refs_3_), custom_call_target="tpu_custom_call" | custom-call | flops 2415919104 | bytes 4456448 | tf_op jit(solution)/shard_map/pair_grads/pallas_call | solution.py:36
  154.6 4.9 %resid_back.1 = (f32[128,1024]{1,0:T(8,128)}, bf16[128,1024]{1,0:T(8,128)(2,1)}, bf16[8,128,128]{2,1,0:T(8,128)(2,1)}) custom-call(f32[128,1024]{1,0:T(8,128)} %get-tuple-element.530.own, bf16[128,1024]{1,0:T(8,128)(2,1)} %copy-done.52, bf16[128,1024]{1,0:T(8,128)(2,1)} %copy-done.53, bf16[128,1024]{1,0:T(8,128)(2,1)} %copy-done.54, ...), custom_call_target="tpu_custom_call" | custom-call | flops 268435456 | bytes 4198400 | tf_op jit(solution)/shard_map/resid_back/pallas_call | solution.py:36
  159.5 1.2 collective-permute-start.36
  160.7 1.3 collective-permute-start.37
  162.0 3.4 %all-to-all-start.2 = ((bf16[8,128,128]{2,1,0:T(8,128)(2,1)}), bf16[8,128,128]{2,1,0:T(8,128)(2,1)S(1)}, u32[]{:S(2)}, u32[]{:S(2)}) async-start(bf16[8,128,128]{2,1,0:T(8,128)(2,1)} %get-tuple-element.561), calls=%async_computation.2 | async-start | bytes 524288 | tf_op jit(solution)/shard_map/all_to_all | solution.py:176
  165.5 4.7 %down_grads.1 = bf16[576,1024]{1,0:T(8,128)(2,1)} custom-call(bf16[512,576]{1,0:T(8,128)(2,1)} %get-tuple-element.548.act.refs_0_, bf16[512,576]{1,0:T(8,128)(2,1)} %get-tuple-element.584.refs_1_.left_in, bf16[128,1024]{1,0:T(8,128)(2,1)} %copy-done.42, bf16[128,1024]{1,0:T(8,128)(2,1)} %copy-done.44, bf16[128,1024]{1,0:T(8,128)(2,1)} %copy-done.45, ...), custom_call_target="tpu_custom_call" | custom-call | flops 1207959552 | bytes 3276800 | tf_op jit(solution)/shard_map/down_grads/pallas_call | solution.py:36
  170.2 2.1 all-to-all-done.2
  173.1 3.1 %conv_back.1 = (f32[1024,128]{1,0:T(8,128)}, f32[8,128]{1,0:T(8,128)}, f32[8,128]{1,0:T(8,128)}) custom-call(bf16[1024,128]{1,0:T(8,128)(2,1)} %bitcast.38, f32[1040,384]{1,0:T(8,128)} %get-tuple-element.607.mixed.refs_3_, f32[1040,128]{1,0:T(8,128)} %get-tuple-element.570.gated, f32[1024,128]{1,0:T(8,128)} %get-tuple-element.608.conv.refs_4_, ...), custom_call_target="tpu_custom_call" | custom-call | bytes 2928704 | tf_op jit(solution)/shard_map/conv_back/pallas_call | solution.py:36
  177.4 1.3 collective-permute-start.43
  178.7 3.8 %ffn_output_sum.1 = (f32[128,1024]{1,0:T(8,128)}, bf16[128,1024]{1,0:T(8,128)(2,1)}, bf16[128,1024]{1,0:T(8,128)(2,1)}, bf16[128,1024]{1,0:T(8,128)(2,1)}) custom-call(bf16[512,576]{1,0:T(8,128)(2,1)} %get-tuple-element.584.refs_1_.left_in, bf16[576,1024]{1,0:T(8,128)(2,1)} %bitcast.35, bf16[512,1024]{1,0:T(8,128)(2,1)} %copy-done.16), custom_call_target="tpu_custom_call" | custom-call | flops 603979776 | bytes 2818048 | tf_op jit(solution)/shard_map/ffn_output_sum/pallas_call | solution.py:36
  182.5 1.0 collective-permute-done.43.refs_1_
  184.1 5.9 %mixer_back.1 = (bf16[1024,384]{1,0:T(8,128)(2,1)}, bf16[512,1024]{1,0:T(8,128)(2,1)}, f32[256,384]{1,0:T(8,128)}, f32[256,384]{1,0:T(8,128)}, f32[256,384]{1,0:T(8,128)}, /*index=5*/bf16[256,384]{1,0:T(8,128)(2,1)}) custom-call(f32[1024,128]{1,0:T(8,128)} %get-tuple-element.604.refs_0_, f32[8,128]{1,0:T(8,128)} %copy-done.65, bf16[1024,128]{1,0:T(8,128)(2,1)} %bitcast.39, ...), custom_call_target="tpu_custom_call" | custom-call | flops 1207959552 | bytes 5828608 | tf_op jit(solution)/shard_map/mixer_back/pallas_call | solution.py:36
  190.4 2.1 collective-permute-start.44
  194.0 1.5 collective-permute-start.48
  195.5 3.2 %out_back.1 = (f32[48,1024]{1,0:T(8,128)}, f32[48,1024]{1,0:T(8,128)}, f32[48,1024]{1,0:T(8,128)}, bf16[48,1024]{1,0:T(8,128)(2,1)}) custom-call(bf16[1024,128]{1,0:T(8,128)(2,1)} %get-tuple-element.626.refs_0_, bf16[128,1024]{1,0:T(8,128)(2,1)} %get-tuple-element.627.refs_1_, bf16[128,1024]{1,0:T(8,128)(2,1)} %copy-done.46, bf16[128,1024]{1,0:T(8,128)(2,1)} %copy-done.13, ...), custom_call_target="tpu_custom_call" | custom-call | flops 268435456 | bytes 2363392 | tf_op jit(solution)/shard_map/out_back/pallas_call | solution.py:36
  198.7 2.1 collective-permute-done.44
  200.8 4.9 %collective-permute-done.45 = bf16[128,1024]{1,0:T(8,128)(2,1)S(1)} collective-permute-done((bf16[128,1024]{1,0:T(8,128)(2,1)}, bf16[128,1024]{1,0:T(8,128)(2,1)S(1)}, u32[]{:S(2)}, u32[]{:S(2)}) %collective-permute-start.45) | collective-permute-done | bytes 262176 | tf_op jit(solution)/shard_map/ppermute | solution.py:127
  206.4 3.5 %all-to-all-start.3 = ((bf16[8,32,1152]{2,1,0:T(8,128)(2,1)}), bf16[8,32,1152]{2,1,0:T(8,128)(2,1)S(1)}, u32[]{:S(2)}, u32[]{:S(2)}) async-start(bf16[8,32,1152]{2,1,0:T(8,128)(2,1)} %bitcast.47), calls=%async_computation.4 | async-start | bytes 1179648 | tf_op jit(solution)/shard_map/all_to_all | solution.py:176
  210.0 1.1 collective-permute-start.50
  211.4 3.3 %mixer_back_sum.1 = (f32[128,1024]{1,0:T(8,128)}, bf16[128,1024]{1,0:T(8,128)(2,1)}, bf16[128,1024]{1,0:T(8,128)(2,1)}, bf16[128,1024]{1,0:T(8,128)(2,1)}) custom-call(bf16[1024,384]{1,0:T(8,128)(2,1)} %get-tuple-element.650.left_in, bf16[1024,384]{1,0:T(8,128)(2,1)} %get-tuple-element.651.refs_6_.right_in, bf16[512,1024]{1,0:T(8,128)(2,1)} %copy-done.8), custom_call_target="tpu_custom_call" | custom-call | flops 402653184 | bytes 2621440 | tf_op jit(solution)/shard_map/mixer_back_sum/pallas_call | solution.py:36
  214.7 12.8 %collective-permute-done.51 = bf16[48,1024]{1,0:T(8,128)(2,1)S(1)} collective-permute-done((bf16[48,1024]{1,0:T(8,128)(2,1)}, bf16[48,1024]{1,0:T(8,128)(2,1)S(1)}, u32[]{:S(2)}, u32[]{:S(2)}) %collective-permute-start.51) | collective-permute-done | bytes 98336 | tf_op jit(solution)/shard_map/ppermute | solution.py:127
  228.2 1.0 add_convert_fusion.5
  229.3 2.4 collective-permute-start.55
  231.6 2.7 collective-permute-start.56
  235.0 2.7 %collective-permute-start.52 = (bf16[128,1024]{1,0:T(8,128)(2,1)}, bf16[128,1024]{1,0:T(8,128)(2,1)S(1)}, u32[]{:S(2)}, u32[]{:S(2)}) collective-permute-start(bf16[128,1024]{1,0:T(8,128)(2,1)} %get-tuple-element.666), channel_id=1, source_target_pairs={{0,6},{1,7},{2,4},{3,5},{4,2},{5,3},{6,0},{7,1},{8,14},{9,15},{10,... | collective-permute-start | bytes 786440 | tf_op jit(solution)/shard_map/ppermute | solution.py:127
  238.5 7.6 %collective-permute-done.56 = bf16[48,1024]{1,0:T(8,128)(2,1)S(1)} collective-permute-done((bf16[48,1024]{1,0:T(8,128)(2,1)S(1)}, bf16[48,1024]{1,0:T(8,128)(2,1)S(1)}, u32[]{:S(2)}, u32[]{:S(2)}) %collective-permute-start.56) | collective-permute-done | bytes 98336 | tf_op jit(solution)/shard_map/ppermute | solution.py:127
  247.0 3.8 %all-to-all-start.4 = ((bf16[8,32,384]{2,1,0:T(8,128)(2,1)}), bf16[8,32,384]{2,1,0:T(8,128)(2,1)S(1)}, u32[]{:S(2)}, u32[]{:S(2)}) async-start(bf16[8,32,384]{2,1,0:T(8,128)(2,1)} %bitcast.13), calls=%async_computation.5 | async-start | bytes 393216 | tf_op jit(solution)/shard_map/all_to_all | solution.py:176
  250.8 1.8 bitcast_convert_fusion
  253.3 2.7 pair_finish.1
  256.0 1.0 all-to-all-done.4.blocks
  258.2 1.4 fusion.5
  259.6 0.9 convert_add_fusion
  261.8 2.0 in_finish.1
  263.8 1.3 reduce
  (264 shorter events, 23.8 us)
Async XLA Ops:
  7.2 111.2 %all-gather.6.cloned.1.call-start = ((), (), s32[]{:S(2)}) async-start(), calls=%async_computation.10 | async-start | bytes 1474560 | tf_op jit(solution)/shard_map/all_gather | solution.py:819
  9.9 19.2 %collective-permute-start = (bf16[128,1024]{1,0:T(8,128)(2,1)}, bf16[128,1024]{1,0:T(8,128)(2,1)S(1)}, u32[]{:S(2)}, u32[]{:S(2)}) collective-permute-start(bf16[128,1024]{1,0:T(8,128)(2,1)} %refs_16_), channel_id=1, source_target_pairs={{0,2},{1,3},{2,0},{3,1},{4,6},{5,7},{6,4},{7,5},{8,10},{9,11},{10,... | collective-permute-start | bytes 786440 | tf_op jit(solution)/shard_map/ppermute | solution.py:127
  12.8 16.2 %collective-permute-start.1 = (bf16[128,1024]{1,0:T(8,128)(2,1)}, bf16[128,1024]{1,0:T(8,128)(2,1)S(1)}, u32[]{:S(2)}, u32[]{:S(2)}) collective-permute-start(bf16[128,1024]{1,0:T(8,128)(2,1)} %refs_16_), channel_id=1, source_target_pairs={{0,4},{1,5},{2,6},{3,7},{4,0},{5,1},{6,2},{7,3},{8,12},{9,13},{10,... | collective-permute-start | bytes 786440 | tf_op jit(solution)/shard_map/ppermute | solution.py:127
  14.4 14.7 %collective-permute-start.2 = (bf16[128,1024]{1,0:T(8,128)(2,1)}, bf16[128,1024]{1,0:T(8,128)(2,1)S(1)}, u32[]{:S(2)}, u32[]{:S(2)}) collective-permute-start(bf16[128,1024]{1,0:T(8,128)(2,1)} %refs_16_), channel_id=1, source_target_pairs={{0,6},{1,7},{2,4},{3,5},{4,2},{5,3},{6,0},{7,1},{8,14},{9,15},{10,... | collective-permute-start | bytes 786440 | tf_op jit(solution)/shard_map/ppermute | solution.py:127
  14.4 14.7 %collective-permute-start.3 = (bf16[128,1024]{1,0:T(8,128)(2,1)}, bf16[128,1024]{1,0:T(8,128)(2,1)S(1)}, u32[]{:S(2)}, u32[]{:S(2)}) collective-permute-start(bf16[128,1024]{1,0:T(8,128)(2,1)} %refs_16_), channel_id=1, source_target_pairs={{0,1},{1,0},{2,3},{3,2},{4,5},{5,4},{6,7},{7,6},{8,9},{9,8},{10,11... | collective-permute-start | bytes 786440 | tf_op jit(solution)/shard_map/ppermute | solution.py:127
  14.4 14.7 %all-to-all-start = ((bf16[8,40,384]{2,1,0:T(8,128)(2,1)}), bf16[8,40,384]{2,1,0:T(8,128)(2,1)S(1)}, u32[]{:S(2)}, u32[]{:S(2)}) async-start(bf16[8,40,384]{2,1,0:T(8,128)(2,1)} %in_prepare.1), calls=%async_computation | async-start | bytes 491520 | tf_op jit(solution)/shard_map/all_to_all | solution.py:176
  29.1 32.6 %all-to-all-start.1 = ((bf16[8,32,1152]{2,1,0:T(8,128)(2,1)}), bf16[8,32,1152]{2,1,0:T(8,128)(2,1)S(1)}, u32[]{:S(2)}, u32[]{:S(2)}) async-start(bf16[8,32,1152]{2,1,0:T(8,128)(2,1)} %pair_prepare.1), calls=%async_computation.1 | async-start | bytes 1179648 | tf_op jit(solution)/shard_map/all_to_all | solution.py:176
  32.7 85.9 %all-gather.4.cloned.1.call-start = ((), (), s32[]{:S(2)}) async-start(), calls=%async_computation.7 | async-start | bytes 2949120 | tf_op jit(solution)/shard_map/all_gather | solution.py:819
  32.8 28.9 %collective-permute-start.4 = (bf16[128,1024]{1,0:T(8,128)(2,1)S(1)}, bf16[128,1024]{1,0:T(8,128)(2,1)S(1)}, u32[]{:S(2)}, u32[]{:S(2)}) collective-permute-start(bf16[128,1024]{1,0:T(8,128)(2,1)S(1)} %collective-permute-done.refs_2_.refs_18_), channel_id=1, source_target_pairs={{0,1},{1,0},{2,3},{3,2},{4,5},{5,4},{6,7},{7,6},{8,9},{9,8},{10,11... | collective-permute-start | bytes 786440 | tf_op jit(solution)/shard_map/ppermute | solution.py:127
  33.1 28.5 %collective-permute-start.5 = (bf16[128,1024]{1,0:T(8,128)(2,1)S(1)}, bf16[128,1024]{1,0:T(8,128)(2,1)S(1)}, u32[]{:S(2)}, u32[]{:S(2)}) collective-permute-start(bf16[128,1024]{1,0:T(8,128)(2,1)S(1)} %collective-permute-done.1.refs_4_.refs_20_), channel_id=1, source_target_pairs={{0,1},{1,0},{2,3},{3,2},{4,5},{5,4},{6,7},{7,6},{8,9},{9,8},{10,11... | collective-permute-start | bytes 786440 | tf_op jit(solution)/shard_map/ppermute | solution.py:127
  33.3 28.3 %collective-permute-start.6 = (bf16[128,1024]{1,0:T(8,128)(2,1)S(1)}, bf16[128,1024]{1,0:T(8,128)(2,1)S(1)}, u32[]{:S(2)}, u32[]{:S(2)}) collective-permute-start(bf16[128,1024]{1,0:T(8,128)(2,1)S(1)} %collective-permute-done.2.refs_6_.refs_22_), channel_id=1, source_target_pairs={{0,1},{1,0},{2,3},{3,2},{4,5},{5,4},{6,7},{7,6},{8,9},{9,8},{10,11... | collective-permute-start | bytes 786440 | tf_op jit(solution)/shard_map/ppermute | solution.py:127
  33.6 28.0 %collective-permute-start.7 = (bf16[32,1024]{1,0:T(8,128)(2,1)S(1)}, bf16[32,1024]{1,0:T(8,128)(2,1)S(1)}, u32[]{:S(2)}, u32[]{:S(2)}) collective-permute-start(bf16[32,1024]{1,0:T(8,128)(2,1)S(1)} %bitcast.48), channel_id=1, source_target_pairs={{0,8},{1,9},{2,10},{3,11},{4,12},{5,13},{6,14},{7,15},{8,16},{9,17... | collective-permute-start | bytes 196616 | tf_op jit(solution)/shard_map/ppermute | solution.py:127
  35.2 26.4 %collective-permute-start.8 = (bf16[32,1024]{1,0:T(8,128)(2,1)S(1)}, bf16[32,1024]{1,0:T(8,128)(2,1)S(1)}, u32[]{:S(2)}, u32[]{:S(2)}) collective-permute-start(bf16[32,1024]{1,0:T(8,128)(2,1)S(1)} %bitcast.49), channel_id=1, source_target_pairs={{0,24},{1,25},{2,26},{3,27},{4,28},{5,29},{6,30},{7,31},{8,0},{9,1... | collective-permute-start | bytes 196616 | tf_op jit(solution)/shard_map/ppermute | solution.py:127
  62.5 6.5 %collective-permute-start.9 = (bf16[32,1024]{1,0:T(8,128)(2,1)S(1)}, bf16[32,1024]{1,0:T(8,128)(2,1)S(1)}, u32[]{:S(2)}, u32[]{:S(2)}) collective-permute-start(bf16[32,1024]{1,0:T(8,128)(2,1)S(1)} %collective-permute-done.7), channel_id=1, source_target_pairs={{0,8},{1,9},{2,10},{3,11},{4,12},{5,13},{6,14},{7,15},{8,16},{9,17... | collective-permute-start | bytes 196616 | tf_op jit(solution)/shard_map/ppermute | solution.py:127
  62.6 6.4 %collective-permute-start.10 = (bf16[16,1024]{1,0:T(8,128)(2,1)S(1)}, bf16[16,1024]{1,0:T(8,128)(2,1)S(1)}, u32[]{:S(2)}, u32[]{:S(2)}) collective-permute-start(bf16[16,1024]{1,0:T(8,128)(2,1)S(1)} %select_select_fusion), channel_id=1, source_target_pairs={{0,8},{1,9},{2,10},{3,11},{4,12},{5,13},{6,14},{7,15},{8,16},{9,17... | collective-permute-start | bytes 98312 | tf_op jit(solution)/shard_map/ppermute | solution.py:127
  69.1 137.3 %reduce-scatter.3.cloned.1.call-start = ((), (), s32[]{:S(2)}) async-start(), calls=%async_computation.8 | async-start | bytes 2949120 | tf_op jit(solution)/shard_map/reduce_scatter | solution.py:822
  69.2 10.1 %collective-permute-start.11 = (bf16[128,1024]{1,0:T(8,128)(2,1)S(1)}, bf16[128,1024]{1,0:T(8,128)(2,1)S(1)}, u32[]{:S(2)}, u32[]{:S(2)}) collective-permute-start(bf16[128,1024]{1,0:T(8,128)(2,1)S(1)} %pad_maximum_fusion.refs_8_.refs_0_), channel_id=1, source_target_pairs={{0,2},{1,3},{2,0},{3,1},{4,6},{5,7},{6,4},{7,5},{8,10},{9,11},{10,... | collective-permute-start | bytes 786440 | tf_op jit(solution)/shard_map/ppermute | solution.py:127
  70.7 8.7 %collective-permute-start.12 = (bf16[128,1024]{1,0:T(8,128)(2,1)S(1)}, bf16[128,1024]{1,0:T(8,128)(2,1)S(1)}, u32[]{:S(2)}, u32[]{:S(2)}) collective-permute-start(bf16[128,1024]{1,0:T(8,128)(2,1)S(1)} %pad_maximum_fusion.refs_8_.refs_0_), channel_id=1, source_target_pairs={{0,4},{1,5},{2,6},{3,7},{4,0},{5,1},{6,2},{7,3},{8,12},{9,13},{10,... | collective-permute-start | bytes 786440 | tf_op jit(solution)/shard_map/ppermute | solution.py:127
  72.1 7.2 %collective-permute-start.13 = (bf16[128,1024]{1,0:T(8,128)(2,1)S(1)}, bf16[128,1024]{1,0:T(8,128)(2,1)S(1)}, u32[]{:S(2)}, u32[]{:S(2)}) collective-permute-start(bf16[128,1024]{1,0:T(8,128)(2,1)S(1)} %pad_maximum_fusion.refs_8_.refs_0_), channel_id=1, source_target_pairs={{0,1},{1,0},{2,3},{3,2},{4,5},{5,4},{6,7},{7,6},{8,9},{9,8},{10,11... | collective-permute-start | bytes 786440 | tf_op jit(solution)/shard_map/ppermute | solution.py:127
  79.4 8.8 %collective-permute-start.14 = (bf16[128,1024]{1,0:T(8,128)(2,1)S(1)}, bf16[128,1024]{1,0:T(8,128)(2,1)S(1)}, u32[]{:S(2)}, u32[]{:S(2)}) collective-permute-start(bf16[128,1024]{1,0:T(8,128)(2,1)S(1)} %broadcast_select_fusion.3), channel_id=1, source_target_pairs={{0,2},{1,5},{2,0},{3,7},{4,6},{5,1},{6,4},{7,3},{8,10},{9,13},{10,... | collective-permute-start | bytes 786440 | tf_op jit(solution)/shard_map/ppermute | solution.py:127
  80.0 8.2 %collective-permute-start.15 = (bf16[128,1024]{1,0:T(8,128)(2,1)S(1)}, bf16[128,1024]{1,0:T(8,128)(2,1)S(1)}, u32[]{:S(2)}, u32[]{:S(2)}) collective-permute-start(bf16[128,1024]{1,0:T(8,128)(2,1)S(1)} %collective-permute-done.11.refs_10_.refs_2_), channel_id=1, source_target_pairs={{0,1},{1,0},{2,3},{3,2},{4,5},{5,4},{6,7},{7,6},{8,9},{9,8},{10,11... | collective-permute-start | bytes 786440 | tf_op jit(solution)/shard_map/ppermute | solution.py:127
  80.2 8.0 %collective-permute-start.16 = (bf16[128,1024]{1,0:T(8,128)(2,1)S(1)}, bf16[128,1024]{1,0:T(8,128)(2,1)S(1)}, u32[]{:S(2)}, u32[]{:S(2)}) collective-permute-start(bf16[128,1024]{1,0:T(8,128)(2,1)S(1)} %collective-permute-done.12.refs_12_.refs_4_), channel_id=1, source_target_pairs={{0,1},{1,0},{2,3},{3,2},{4,5},{5,4},{6,7},{7,6},{8,9},{9,8},{10,11... | collective-permute-start | bytes 786440 | tf_op jit(solution)/shard_map/ppermute | solution.py:127
  80.5 10.9 %collective-permute-start.17 = (bf16[1024,128]{1,0:T(8,128)(2,1)}, bf16[1024,128]{1,0:T(8,128)(2,1)S(1)}, u32[]{:S(2)}, u32[]{:S(2)}) collective-permute-start(bf16[1024,128]{1,0:T(8,128)(2,1)} %get-tuple-element.626.refs_0_), channel_id=1, source_target_pairs={{0,2},{1,3},{2,0},{3,1},{4,6},{5,7},{6,4},{7,5},{8,10},{9,11},{10,... | collective-permute-start | bytes 786440 | tf_op jit(solution)/shard_map/ppermute | solution.py:127
  82.0 9.5 %collective-permute-start.18 = (bf16[1024,128]{1,0:T(8,128)(2,1)}, bf16[1024,128]{1,0:T(8,128)(2,1)S(1)}, u32[]{:S(2)}, u32[]{:S(2)}) collective-permute-start(bf16[1024,128]{1,0:T(8,128)(2,1)} %get-tuple-element.626.refs_0_), channel_id=1, source_target_pairs={{0,4},{1,5},{2,6},{3,7},{4,0},{5,1},{6,2},{7,3},{8,12},{9,13},{10,... | collective-permute-start | bytes 786440 | tf_op jit(solution)/shard_map/ppermute | solution.py:127
  88.2 3.3 %collective-permute-start.19 = (bf16[1024,128]{1,0:T(8,128)(2,1)}, bf16[1024,128]{1,0:T(8,128)(2,1)S(1)}, u32[]{:S(2)}, u32[]{:S(2)}) collective-permute-start(bf16[1024,128]{1,0:T(8,128)(2,1)} %get-tuple-element.626.refs_0_), channel_id=1, source_target_pairs={{0,1},{1,0},{2,3},{3,2},{4,5},{5,4},{6,7},{7,6},{8,9},{9,8},{10,11... | collective-permute-start | bytes 786440 | tf_op jit(solution)/shard_map/ppermute | solution.py:127
  91.6 9.0 %collective-permute-start.21 = (bf16[1024,128]{1,0:T(8,128)(2,1)S(1)}, bf16[1024,128]{1,0:T(8,128)(2,1)S(1)}, u32[]{:S(2)}, u32[]{:S(2)}) collective-permute-start(bf16[1024,128]{1,0:T(8,128)(2,1)S(1)} %broadcast_select_fusion), channel_id=1, source_target_pairs={{0,2},{1,5},{2,0},{3,7},{4,6},{5,1},{6,4},{7,3},{8,10},{9,13},{10,... | collective-permute-start | bytes 786440 | tf_op jit(solution)/shard_map/ppermute | solution.py:127
  92.2 8.4 %collective-permute-start.22 = (bf16[1024,128]{1,0:T(8,128)(2,1)S(1)}, bf16[1024,128]{1,0:T(8,128)(2,1)S(1)}, u32[]{:S(2)}, u32[]{:S(2)}) collective-permute-start(bf16[1024,128]{1,0:T(8,128)(2,1)S(1)} %collective-permute-done.17.refs_2_), channel_id=1, source_target_pairs={{0,1},{1,0},{2,3},{3,2},{4,5},{5,4},{6,7},{7,6},{8,9},{9,8},{10,11... | collective-permute-start | bytes 786440 | tf_op jit(solution)/shard_map/ppermute | solution.py:127
  92.4 8.2 %collective-permute-start.23 = (bf16[1024,128]{1,0:T(8,128)(2,1)S(1)}, bf16[1024,128]{1,0:T(8,128)(2,1)S(1)}, u32[]{:S(2)}, u32[]{:S(2)}) collective-permute-start(bf16[1024,128]{1,0:T(8,128)(2,1)S(1)} %collective-permute-done.18.refs_4_), channel_id=1, source_target_pairs={{0,1},{1,0},{2,3},{3,2},{4,5},{5,4},{6,7},{7,6},{8,9},{9,8},{10,11... | collective-permute-start | bytes 786440 | tf_op jit(solution)/shard_map/ppermute | solution.py:127
  92.7 10.9 %collective-permute-start.24 = (bf16[128,1024]{1,0:T(8,128)(2,1)S(1)}, bf16[128,1024]{1,0:T(8,128)(2,1)S(1)}, u32[]{:S(2)}, u32[]{:S(2)}) collective-permute-start(bf16[128,1024]{1,0:T(8,128)(2,1)S(1)} %copy-done.6), channel_id=1, source_target_pairs={{0,2},{1,3},{2,0},{3,1},{4,6},{5,7},{6,4},{7,5},{8,10},{9,11},{10,... | collective-permute-start | bytes 786440 | tf_op jit(solution)/shard_map/ppermute | solution.py:127
  94.2 9.4 %collective-permute-start.25 = (bf16[128,1024]{1,0:T(8,128)(2,1)S(1)}, bf16[128,1024]{1,0:T(8,128)(2,1)S(1)}, u32[]{:S(2)}, u32[]{:S(2)}) collective-permute-start(bf16[128,1024]{1,0:T(8,128)(2,1)S(1)} %copy-done.6), channel_id=1, source_target_pairs={{0,4},{1,5},{2,6},{3,7},{4,0},{5,1},{6,2},{7,3},{8,12},{9,13},{10,... | collective-permute-start | bytes 786440 | tf_op jit(solution)/shard_map/ppermute | solution.py:127
  103.8 6.4 %collective-permute-start.28 = (bf16[128,1024]{1,0:T(8,128)(2,1)S(1)}, bf16[128,1024]{1,0:T(8,128)(2,1)S(1)}, u32[]{:S(2)}, u32[]{:S(2)}) collective-permute-start(bf16[128,1024]{1,0:T(8,128)(2,1)S(1)} %broadcast_select_fusion.2), channel_id=1, source_target_pairs={{0,2},{1,5},{2,0},{3,7},{4,6},{5,1},{6,4},{7,3},{8,10},{9,13},{10,... | collective-permute-start | bytes 786440 | tf_op jit(solution)/shard_map/ppermute | solution.py:127
  104.5 5.8 %collective-permute-start.29 = (bf16[128,1024]{1,0:T(8,128)(2,1)S(1)}, bf16[128,1024]{1,0:T(8,128)(2,1)S(1)}, u32[]{:S(2)}, u32[]{:S(2)}) collective-permute-start(bf16[128,1024]{1,0:T(8,128)(2,1)S(1)} %collective-permute-done.24.refs_2_.refs_7_), channel_id=1, source_target_pairs={{0,1},{1,0},{2,3},{3,2},{4,5},{5,4},{6,7},{7,6},{8,9},{9,8},{10,11... | collective-permute-start | bytes 786440 | tf_op jit(solution)/shard_map/ppermute | solution.py:127
  104.6 5.7 %collective-permute-start.30 = (bf16[128,1024]{1,0:T(8,128)(2,1)S(1)}, bf16[128,1024]{1,0:T(8,128)(2,1)S(1)}, u32[]{:S(2)}, u32[]{:S(2)}) collective-permute-start(bf16[128,1024]{1,0:T(8,128)(2,1)S(1)} %collective-permute-done.25.refs_3_.refs_8_), channel_id=1, source_target_pairs={{0,1},{1,0},{2,3},{3,2},{4,5},{5,4},{6,7},{7,6},{8,9},{9,8},{10,11... | collective-permute-start | bytes 786440 | tf_op jit(solution)/shard_map/ppermute | solution.py:127
  110.3 8.0 %collective-permute-start.31 = (bf16[128,1024]{1,0:T(8,128)(2,1)S(1)}, bf16[128,1024]{1,0:T(8,128)(2,1)S(1)}, u32[]{:S(2)}, u32[]{:S(2)}) collective-permute-start(bf16[128,1024]{1,0:T(8,128)(2,1)S(1)} %collective-permute-done.28.refs_4_.refs_9_), channel_id=1, source_target_pairs={{0,1},{1,0},{2,3},{3,2},{4,5},{5,4},{6,7},{7,6},{8,9},{9,8},{10,11... | collective-permute-start | bytes 786440 | tf_op jit(solution)/shard_map/ppermute | solution.py:127
  126.3 6.8 %collective-permute-start.32 = (bf16[512,1024]{1,0:T(8,128)(2,1)}, bf16[512,1024]{1,0:T(8,128)(2,1)S(1)}, u32[]{:S(2)}, u32[]{:S(2)}) collective-permute-start(bf16[512,1024]{1,0:T(8,128)(2,1)} %get-tuple-element.505), channel_id=1, source_target_pairs={{0,1},{1,0},{2,3},{3,2},{4,5},{5,4},{6,7},{7,6},{8,9},{9,8},{10,11... | collective-permute-start | bytes 3145736 | tf_op jit(solution)/shard_map/ppermute | solution.py:127
  138.9 13.9 %collective-permute-start.33 = (bf16[128,1024]{1,0:T(8,128)(2,1)}, bf16[128,1024]{1,0:T(8,128)(2,1)S(1)}, u32[]{:S(2)}, u32[]{:S(2)}) collective-permute-start(bf16[128,1024]{1,0:T(8,128)(2,1)} %get-tuple-element.516), channel_id=1, source_target_pairs={{0,6},{1,7},{2,4},{3,5},{4,2},{5,3},{6,0},{7,1},{8,14},{9,15},{10,... | collective-permute-start | bytes 786440 | tf_op jit(solution)/shard_map/ppermute | solution.py:127
  140.4 13.1 %collective-permute-start.34 = (bf16[128,1024]{1,0:T(8,128)(2,1)}, bf16[128,1024]{1,0:T(8,128)(2,1)S(1)}, u32[]{:S(2)}, u32[]{:S(2)}) collective-permute-start(bf16[128,1024]{1,0:T(8,128)(2,1)} %get-tuple-element.517), channel_id=1, source_target_pairs={{0,2},{1,3},{2,0},{3,1},{4,6},{5,7},{6,4},{7,5},{8,10},{9,11},{10,... | collective-permute-start | bytes 786440 | tf_op jit(solution)/shard_map/ppermute | solution.py:127
  141.0 13.0 %collective-permute-start.35 = (bf16[128,1024]{1,0:T(8,128)(2,1)}, bf16[128,1024]{1,0:T(8,128)(2,1)S(1)}, u32[]{:S(2)}, u32[]{:S(2)}) collective-permute-start(bf16[128,1024]{1,0:T(8,128)(2,1)} %get-tuple-element.518), channel_id=1, source_target_pairs={{0,4},{1,5},{2,6},{3,7},{4,0},{5,1},{6,2},{7,3},{8,12},{9,13},{10,... | collective-permute-start | bytes 786440 | tf_op jit(solution)/shard_map/ppermute | solution.py:127
  159.5 12.8 %collective-permute-start.36 = (bf16[128,1024]{1,0:T(8,128)(2,1)}, bf16[128,1024]{1,0:T(8,128)(2,1)S(1)}, u32[]{:S(2)}, u32[]{:S(2)}) collective-permute-start(bf16[128,1024]{1,0:T(8,128)(2,1)} %get-tuple-element.627.refs_1_), channel_id=1, source_target_pairs={{0,2},{1,3},{2,0},{3,1},{4,6},{5,7},{6,4},{7,5},{8,10},{9,11},{10,... | collective-permute-start | bytes 786440 | tf_op jit(solution)/shard_map/ppermute | solution.py:127
  160.7 11.6 %collective-permute-start.37 = (bf16[128,1024]{1,0:T(8,128)(2,1)}, bf16[128,1024]{1,0:T(8,128)(2,1)S(1)}, u32[]{:S(2)}, u32[]{:S(2)}) collective-permute-start(bf16[128,1024]{1,0:T(8,128)(2,1)} %get-tuple-element.627.refs_1_), channel_id=1, source_target_pairs={{0,4},{1,5},{2,6},{3,7},{4,0},{5,1},{6,2},{7,3},{8,12},{9,13},{10,... | collective-permute-start | bytes 786440 | tf_op jit(solution)/shard_map/ppermute | solution.py:127
  162.0 10.3 %collective-permute-start.38 = (bf16[128,1024]{1,0:T(8,128)(2,1)}, bf16[128,1024]{1,0:T(8,128)(2,1)S(1)}, u32[]{:S(2)}, u32[]{:S(2)}) collective-permute-start(bf16[128,1024]{1,0:T(8,128)(2,1)} %get-tuple-element.627.refs_1_), channel_id=1, source_target_pairs={{0,1},{1,0},{2,3},{3,2},{4,5},{5,4},{6,7},{7,6},{8,9},{9,8},{10,11... | collective-permute-start | bytes 786440 | tf_op jit(solution)/shard_map/ppermute | solution.py:127
  162.0 10.3 %all-to-all-start.2 = ((bf16[8,128,128]{2,1,0:T(8,128)(2,1)}), bf16[8,128,128]{2,1,0:T(8,128)(2,1)S(1)}, u32[]{:S(2)}, u32[]{:S(2)}) async-start(bf16[8,128,128]{2,1,0:T(8,128)(2,1)} %get-tuple-element.561), calls=%async_computation.2 | async-start | bytes 524288 | tf_op jit(solution)/shard_map/all_to_all | solution.py:176
  165.5 85.3 %reduce-scatter.5.cloned.1.call-start = ((), (), s32[]{:S(2)}) async-start(), calls=%async_computation.9 | async-start | bytes 1474560 | tf_op jit(solution)/shard_map/reduce_scatter | solution.py:822
  172.4 3.9 %collective-permute-start.39 = (bf16[512,1024]{1,0:T(8,128)(2,1)S(1)}, bf16[512,1024]{1,0:T(8,128)(2,1)S(1)}, u32[]{:S(2)}, u32[]{:S(2)}) collective-permute-start(bf16[512,1024]{1,0:T(8,128)(2,1)S(1)} %copy-done.15), channel_id=1, source_target_pairs={{0,1},{1,0},{2,3},{3,2},{4,5},{5,4},{6,7},{7,6},{8,9},{9,8},{10,11... | collective-permute-start | bytes 3145736 | tf_op jit(solution)/shard_map/ppermute | solution.py:127
  176.3 7.2 %collective-permute-start.40 = (bf16[128,1024]{1,0:T(8,128)(2,1)S(1)}, bf16[128,1024]{1,0:T(8,128)(2,1)S(1)}, u32[]{:S(2)}, u32[]{:S(2)}) collective-permute-start(bf16[128,1024]{1,0:T(8,128)(2,1)S(1)} %broadcast_select_fusion.1), channel_id=1, source_target_pairs={{0,2},{1,5},{2,0},{3,7},{4,6},{5,1},{6,4},{7,3},{8,10},{9,13},{10,... | collective-permute-start | bytes 786440 | tf_op jit(solution)/shard_map/ppermute | solution.py:127
  176.9 6.6 %collective-permute-start.41 = (bf16[128,1024]{1,0:T(8,128)(2,1)S(1)}, bf16[128,1024]{1,0:T(8,128)(2,1)S(1)}, u32[]{:S(2)}, u32[]{:S(2)}) collective-permute-start(bf16[128,1024]{1,0:T(8,128)(2,1)S(1)} %collective-permute-done.36.refs_3_), channel_id=1, source_target_pairs={{0,1},{1,0},{2,3},{3,2},{4,5},{5,4},{6,7},{7,6},{8,9},{9,8},{10,11... | collective-permute-start | bytes 786440 | tf_op jit(solution)/shard_map/ppermute | solution.py:127
  176.9 6.6 %collective-permute-start.42 = (bf16[128,1024]{1,0:T(8,128)(2,1)S(1)}, bf16[128,1024]{1,0:T(8,128)(2,1)S(1)}, u32[]{:S(2)}, u32[]{:S(2)}) collective-permute-start(bf16[128,1024]{1,0:T(8,128)(2,1)S(1)} %collective-permute-done.37.refs_5_), channel_id=1, source_target_pairs={{0,1},{1,0},{2,3},{3,2},{4,5},{5,4},{6,7},{7,6},{8,9},{9,8},{10,11... | collective-permute-start | bytes 786440 | tf_op jit(solution)/shard_map/ppermute | solution.py:127
  177.4 6.1 %collective-permute-start.43 = (f32[8,128]{1,0:T(8,128)}, f32[8,128]{1,0:T(8,128)S(1)}, u32[]{:S(2)}, u32[]{:S(2)}) collective-permute-start(f32[8,128]{1,0:T(8,128)} %get-tuple-element.591), channel_id=1, source_target_pairs={{8,0},{9,1},{10,2},{11,3},{12,4},{13,5},{14,6},{15,7},{16,8},{17,9... | collective-permute-start | bytes 12296 | tf_op jit(solution)/shard_map/ppermute | solution.py:127
  183.6 6.5 %collective-permute-start.47 = (bf16[128,1024]{1,0:T(8,128)(2,1)S(1)}, bf16[128,1024]{1,0:T(8,128)(2,1)S(1)}, u32[]{:S(2)}, u32[]{:S(2)}) collective-permute-start(bf16[128,1024]{1,0:T(8,128)(2,1)S(1)} %collective-permute-done.40.refs_7_), channel_id=1, source_target_pairs={{0,1},{1,0},{2,3},{3,2},{4,5},{5,4},{6,7},{7,6},{8,9},{9,8},{10,11... | collective-permute-start | bytes 786440 | tf_op jit(solution)/shard_map/ppermute | solution.py:127
  190.1 15.6 %collective-permute-start.49 = (bf16[512,1024]{1,0:T(8,128)(2,1)}, bf16[512,1024]{1,0:T(8,128)(2,1)S(1)}, u32[]{:S(2)}, u32[]{:S(2)}) collective-permute-start(bf16[512,1024]{1,0:T(8,128)(2,1)} %get-tuple-element.625), channel_id=1, source_target_pairs={{0,1},{1,0},{2,3},{3,2},{4,5},{5,4},{6,7},{7,6},{8,9},{9,8},{10,11... | collective-permute-start | bytes 3145736 | tf_op jit(solution)/shard_map/ppermute | solution.py:127
  190.4 10.3 %collective-permute-start.44 = (bf16[128,1024]{1,0:T(8,128)(2,1)}, bf16[128,1024]{1,0:T(8,128)(2,1)S(1)}, u32[]{:S(2)}, u32[]{:S(2)}) collective-permute-start(bf16[128,1024]{1,0:T(8,128)(2,1)} %get-tuple-element.600), channel_id=1, source_target_pairs={{0,6},{1,7},{2,4},{3,5},{4,2},{5,3},{6,0},{7,1},{8,14},{9,15},{10,... | collective-permute-start | bytes 786440 | tf_op jit(solution)/shard_map/ppermute | solution.py:127
  192.5 13.2 %collective-permute-start.45 = (bf16[128,1024]{1,0:T(8,128)(2,1)}, bf16[128,1024]{1,0:T(8,128)(2,1)S(1)}, u32[]{:S(2)}, u32[]{:S(2)}) collective-permute-start(bf16[128,1024]{1,0:T(8,128)(2,1)} %get-tuple-element.601), channel_id=1, source_target_pairs={{0,2},{1,3},{2,0},{3,1},{4,6},{5,7},{6,4},{7,5},{8,10},{9,11},{10,... | collective-permute-start | bytes 786440 | tf_op jit(solution)/shard_map/ppermute | solution.py:127
  193.3 12.4 %collective-permute-start.46 = (bf16[128,1024]{1,0:T(8,128)(2,1)}, bf16[128,1024]{1,0:T(8,128)(2,1)S(1)}, u32[]{:S(2)}, u32[]{:S(2)}) collective-permute-start(bf16[128,1024]{1,0:T(8,128)(2,1)} %get-tuple-element.602), channel_id=1, source_target_pairs={{0,4},{1,5},{2,6},{3,7},{4,0},{5,1},{6,2},{7,3},{8,12},{9,13},{10,... | collective-permute-start | bytes 786440 | tf_op jit(solution)/shard_map/ppermute | solution.py:127
  194.0 11.7 %collective-permute-start.48 = (bf16[256,384]{1,0:T(8,128)(2,1)}, bf16[256,384]{1,0:T(8,128)(2,1)S(1)}, u32[]{:S(2)}, u32[]{:S(2)}) collective-permute-start(bf16[256,384]{1,0:T(8,128)(2,1)} %get-tuple-element.624), channel_id=1, source_target_pairs={{0,8},{1,9},{2,10},{3,11},{4,12},{5,13},{6,14},{7,15},{8,16},{9,17... | collective-permute-start | bytes 589832 | tf_op jit(solution)/shard_map/ppermute | solution.py:127
  206.4 21.7 %all-to-all-start.3 = ((bf16[8,32,1152]{2,1,0:T(8,128)(2,1)}), bf16[8,32,1152]{2,1,0:T(8,128)(2,1)S(1)}, u32[]{:S(2)}, u32[]{:S(2)}) async-start(bf16[8,32,1152]{2,1,0:T(8,128)(2,1)} %bitcast.47), calls=%async_computation.4 | async-start | bytes 1179648 | tf_op jit(solution)/shard_map/all_to_all | solution.py:176
  210.0 18.1 %collective-permute-start.50 = (bf16[256,384]{1,0:T(8,128)(2,1)S(1)}, bf16[256,384]{1,0:T(8,128)(2,1)S(1)}, u32[]{:S(2)}, u32[]{:S(2)}) collective-permute-start(bf16[256,384]{1,0:T(8,128)(2,1)S(1)} %add_convert_fusion.3), channel_id=1, source_target_pairs={{0,8},{1,9},{2,10},{3,11},{4,12},{5,13},{6,14},{7,15},{8,16},{9,17... | collective-permute-start | bytes 589832 | tf_op jit(solution)/shard_map/ppermute | solution.py:127
  211.1 16.3 %collective-permute-start.51 = (bf16[48,1024]{1,0:T(8,128)(2,1)}, bf16[48,1024]{1,0:T(8,128)(2,1)S(1)}, u32[]{:S(2)}, u32[]{:S(2)}) collective-permute-start(bf16[48,1024]{1,0:T(8,128)(2,1)} %get-tuple-element.657), channel_id=1, source_target_pairs={{0,8},{1,9},{2,10},{3,11},{4,12},{5,13},{6,14},{7,15},{8,16},{9,17... | collective-permute-start | bytes 294920 | tf_op jit(solution)/shard_map/ppermute | solution.py:127
  229.3 16.9 %collective-permute-start.55 = (bf16[256,384]{1,0:T(8,128)(2,1)S(1)}, bf16[256,384]{1,0:T(8,128)(2,1)S(1)}, u32[]{:S(2)}, u32[]{:S(2)}) collective-permute-start(bf16[256,384]{1,0:T(8,128)(2,1)S(1)} %add_convert_fusion.2), channel_id=1, source_target_pairs={{0,8},{1,9},{2,10},{3,11},{4,12},{5,13},{6,14},{7,15},{8,16},{9,17... | collective-permute-start | bytes 589832 | tf_op jit(solution)/shard_map/ppermute | solution.py:127
  231.6 14.5 %collective-permute-start.56 = (bf16[48,1024]{1,0:T(8,128)(2,1)S(1)}, bf16[48,1024]{1,0:T(8,128)(2,1)S(1)}, u32[]{:S(2)}, u32[]{:S(2)}) collective-permute-start(bf16[48,1024]{1,0:T(8,128)(2,1)S(1)} %add_convert_fusion.5), channel_id=1, source_target_pairs={{0,8},{1,9},{2,10},{3,11},{4,12},{5,13},{6,14},{7,15},{8,16},{9,17... | collective-permute-start | bytes 294920 | tf_op jit(solution)/shard_map/ppermute | solution.py:127
  235.0 20.9 %collective-permute-start.52 = (bf16[128,1024]{1,0:T(8,128)(2,1)}, bf16[128,1024]{1,0:T(8,128)(2,1)S(1)}, u32[]{:S(2)}, u32[]{:S(2)}) collective-permute-start(bf16[128,1024]{1,0:T(8,128)(2,1)} %get-tuple-element.666), channel_id=1, source_target_pairs={{0,6},{1,7},{2,4},{3,5},{4,2},{5,3},{6,0},{7,1},{8,14},{9,15},{10,... | collective-permute-start | bytes 786440 | tf_op jit(solution)/shard_map/ppermute | solution.py:127
  237.8 18.2 %collective-permute-start.53 = (bf16[128,1024]{1,0:T(8,128)(2,1)}, bf16[128,1024]{1,0:T(8,128)(2,1)S(1)}, u32[]{:S(2)}, u32[]{:S(2)}) collective-permute-start(bf16[128,1024]{1,0:T(8,128)(2,1)} %get-tuple-element.667), channel_id=1, source_target_pairs={{0,2},{1,3},{2,0},{3,1},{4,6},{5,7},{6,4},{7,5},{8,10},{9,11},{10,... | collective-permute-start | bytes 786440 | tf_op jit(solution)/shard_map/ppermute | solution.py:127
  238.3 17.7 %collective-permute-start.54 = (bf16[128,1024]{1,0:T(8,128)(2,1)}, bf16[128,1024]{1,0:T(8,128)(2,1)S(1)}, u32[]{:S(2)}, u32[]{:S(2)}) collective-permute-start(bf16[128,1024]{1,0:T(8,128)(2,1)} %get-tuple-element.668), channel_id=1, source_target_pairs={{0,4},{1,5},{2,6},{3,7},{4,0},{5,1},{6,2},{7,3},{8,12},{9,13},{10,... | collective-permute-start | bytes 786440 | tf_op jit(solution)/shard_map/ppermute | solution.py:127
  246.9 9.1 %collective-permute-start.57 = (bf16[48,1024]{1,0:T(8,128)(2,1)S(1)}, bf16[48,1024]{1,0:T(8,128)(2,1)}, u32[]{:S(2)}, u32[]{:S(2)}) collective-permute-start(bf16[48,1024]{1,0:T(8,128)(2,1)S(1)} %add_convert_fusion.4), channel_id=1, source_target_pairs={{0,8},{1,9},{2,10},{3,11},{4,12},{5,13},{6,14},{7,15},{8,16},{9,17... | collective-permute-start | bytes 294920 | tf_op jit(solution)/shard_map/ppermute | solution.py:127
  247.0 10.0 %all-to-all-start.4 = ((bf16[8,32,384]{2,1,0:T(8,128)(2,1)}), bf16[8,32,384]{2,1,0:T(8,128)(2,1)S(1)}, u32[]{:S(2)}, u32[]{:S(2)}) async-start(bf16[8,32,384]{2,1,0:T(8,128)(2,1)} %bitcast.13), calls=%async_computation.5 | async-start | bytes 393216 | tf_op jit(solution)/shard_map/all_to_all | solution.py:176
  (76 other events, 901.6 us)
Sparse Core Ops, SparseCore 0:
  9.6 37.1 all-gather.5
  69.2 49.3 all-gather.3
  154.1 47.1 reduce-scatter.2
  203.4 40.8 reduce-scatter.4

commit v2 on v1

--- a/solution.py
+++ b/solution.py
@@ -164,11 +164,15 @@
         twins = yield [(block, ("swap", 1)) for block in found[:3]]
         return [value, found[3], found[0], twins[0], found[1], twins[1], found[2], twins[2]]
 
-    def team_sum(self, odd, fold, span=1):
+    def team_sum(self, odd, fold, split=False, span=1):
         (arrived,) = yield [(odd, ("swap", 1))]
         call, operands = fold(arrived)
         (parts,) = yield [(operands, ("call", call))]
-        moved = yield [(part, ("swap", mask), span) for part, mask in zip(parts[1:], (6, 2, 4))]
+        sends = [(part, ("swap", mask), span) for part, mask in zip(parts[1:], (6, 2, 4))]
+        if split:
+            sides = yield sends[1:]
+            return [parts[0]] + (yield sends[:1]) + sides
+        moved = yield sends
         return [parts[0]] + moved
 
     def exchange(self, blocks):
@@ -323,9 +327,9 @@
                     source = k * channels + z * part
                     out[:, to : to + part] = block[:, source : source + part]
         product = jnp.sum(weight[...].astype(WIDE) * out[...], axis=1, keepdims=True)
-        gain_grad[...] = product / gain[...].astype(WIDE)
-
-    outs = (shape(WIDE, part, width), shape(WIDE, part, 1))
+        gain_grad[...] = (product / gain[...].astype(WIDE)).reshape(1, part)
+
+    outs = (shape(WIDE, part, width), shape(WIDE, 1, part))
     return call(kernel, "in_finish", outs, (blocks, weight, gain))
 
 
@@ -367,9 +371,10 @@
                 gate_grad[:, to : to + size] = block[:, at_gate : at_gate + size]
                 up_grad[:, to : to + size] = block[:, at_up : at_up + size]
         product = gate[...].astype(WIDE) * gate_grad[...] + up[...].astype(WIDE) * up_grad[...]
-        gain_grad[...] = jnp.sum(product, axis=1, keepdims=True) / gain[...].astype(WIDE)
-
-    outs = (shape(WIDE, part, inner), shape(WIDE, part, inner), shape(WIDE, part, 1))
+        total = jnp.sum(product, axis=1, keepdims=True) / gain[...].astype(WIDE)
+        gain_grad[...] = total.reshape(1, part)
+
+    outs = (shape(WIDE, part, inner), shape(WIDE, part, inner), shape(WIDE, 1, part))
     return call(kernel, "pair_finish", outs, (blocks, gate, up, gain))
 
 
@@ -535,77 +540,83 @@
     return scaled * up, gate_grad, grad * scaled
 
 
-def ffn_block(inputs, upstream, pair, down, send):
+def ffn_block(odd, even, upstream, pair, down):
     count = len(upstream)
     rows, features = upstream[0].shape
     own = down.shape[0]
-    even = own // 128 * 128
-    width = own - even
-    total = count * rows
-
-    def kernel(*refs):
-        x_in, g_in, refs = refs[0], refs[1 : 1 + count], refs[1 + count :]
-        pair_in, down_in, act, grads = refs[:4]
-        xs, gs, pair, down, last, sems = refs[-6:]
-        first = [(x_in, xs), (pair_in, pair)]
+    units = own // 128 * 128
+    width = own - units
+    half = odd.shape[0]
+
+    def kernel(odd_in, even_in, *refs):
+        g_in, (pair_in, down_in), refs = refs[:count], refs[count : count + 2], refs[count + 2 :]
+        acts, grads, weight = refs[:2], refs[2:4], refs[4]
+        xs, gs, pair, down, last, all_grads, sems = refs[5:]
+        first = [(odd_in, xs.at[:half, :]), (pair_in, pair)]
         second = [(g_in[k], gs.at[k * rows : (k + 1) * rows, :]) for k in range(count)]
-        second.append((down_in, down))
+        second += [(down_in, down), (even_in, xs.at[half:, :])]
         copies = fetch(first + second, sems)
         for copy in copies[:2]:
             copy.wait()
-        x = xs[...]
-        gate = dot(x, pair[:, :even], ((1,), (0,)))
-        up = dot(x, pair[:, even : 2 * even], ((1,), (0,)))
-        for copy in copies[2:]:
-            copy.wait()
-        g = gs[...]
-        grad = dot(g, down[:even, :], ((1,), (1,)))
-        value, gate_grad, up_grad = ffn_parts(gate, up, grad)
-        act[:, :even] = value.astype(NARROW)
-        grads[:, :even] = gate_grad.astype(NARROW)
-        grads[:, even : 2 * even] = up_grad.astype(NARROW)
-        last[:width, :] = down[even:, :]
-        last[width:, :] = down[even:, :]
-        both = dot(x, pair[:, 2 * even :], ((1,), (0,)))
-        turned = pltpu.roll(both, width, 1)
-        lower = lax.broadcasted_iota(jnp.int32, both.shape, 1) < width
-        grad = dot(g, last[...], ((1,), (1,)))
-        value, gate_grad, up_grad = ffn_parts(
-            jnp.where(lower, both, turned), jnp.where(lower, turned, both), grad
-        )
-        act[:, even:] = value[:, :width].astype(NARROW)
-        grads[:, 2 * even :] = jnp.where(lower, gate_grad, up_grad).astype(NARROW)
-        if send:
-            refs[4][...] = dot(grads[...], pair[...], ((1,), (1,))).astype(NARROW)
-
-    outs = (shape(NARROW, total, own), shape(NARROW, total, 2 * own))
-    if send:
-        outs += (shape(NARROW, total, features),)
+        for side in range(2):
+            span = slice(side * half, (side + 1) * half)
+            act, grad_out = acts[side], grads[side]
+            x = xs[span, :]
+            gate = dot(x, pair[:, :units], ((1,), (0,)))
+            up = dot(x, pair[:, units : 2 * units], ((1,), (0,)))
+            if side == 0:
+                for copy in copies[2:]:
+                    copy.wait()
+                last[:width, :] = down[units:, :]
+                last[width:, :] = down[units:, :]
+            g = gs[span, :]
+            grad = dot(g, down[:units, :], ((1,), (1,)))
+            value, gate_grad, up_grad = ffn_parts(gate, up, grad)
+            act[:, :units] = value.astype(NARROW)
+            all_grads[span, :units] = gate_grad.astype(NARROW)
+            all_grads[span, units : 2 * units] = up_grad.astype(NARROW)
+            both = dot(x, pair[:, 2 * units :], ((1,), (0,)))
+            turned = pltpu.roll(both, width, 1)
+            lower = lax.broadcasted_iota(jnp.int32, both.shape, 1) < width
+            grad = dot(g, last[...], ((1,), (1,)))
+            value, gate_grad, up_grad = ffn_parts(
+                jnp.where(lower, both, turned), jnp.where(lower, turned, both), grad
+            )
+            act[:, units:] = value[:, :width].astype(NARROW)
+            all_grads[span, 2 * units :] = jnp.where(lower, gate_grad, up_grad).astype(NARROW)
+            grad_out[...] = all_grads[span, :]
+        for start in range(0, features, 256):
+            total = dot(xs[:, start : start + 256], all_grads[...], ((0,), (0,)))
+            weight[start : start + 256, :] = total.astype(NARROW)
+
+    outs = (shape(NARROW, half, own),) * 2 + (shape(NARROW, half, 2 * own),) * 2
     return call(
         kernel,
         "ffn",
-        outs,
-        (inputs, *upstream, pair, down),
+        outs + (shape(NARROW, features, 2 * own),),
+        (odd, even, *upstream, pair, down),
         [
-            pltpu.VMEM((total, features), NARROW),
-            pltpu.VMEM((total, features), NARROW),
+            pltpu.VMEM((2 * half, features), NARROW),
+            pltpu.VMEM((2 * half, features), NARROW),
             pltpu.VMEM((features, 2 * own), NARROW),
             pltpu.VMEM((own, features), NARROW),
             pltpu.VMEM((2 * width, features), NARROW),
-            pltpu.SemaphoreType.DMA((count + 3,)),
+            pltpu.VMEM((2 * half, 2 * own), NARROW),
+            pltpu.SemaphoreType.DMA((count + 4,)),
         ],
-        10 * total * features * own,
+        20 * half * features * own,
         in_place=True,
     )
 
 
-def ffn_output(act, down):
-    def kernel(act, down, out):
-        out[...] = dot(act[...], down[...], ((1,), (0,))).astype(NARROW)
-
-    rows, features = act.shape[0], down.shape[1]
-    out = shape(NARROW, rows, features)
-    return call(kernel, "ffn_output", out, (act, down), flops=2 * rows * features * down.shape[0])
+def product(left, right, turned, name):
+    contract = ((1,), (1,)) if turned else ((1,), (0,))
+
+    def kernel(left, right, out):
+        out[...] = dot(left[...], right[...], contract).astype(NARROW)
+
+    rows, wide = left.shape[0], right.shape[0 if turned else 1]
+    return call(kernel, name, shape(NARROW, rows, wide), (left, right), flops=2 * rows * right.size)
 
 
 def weight_grads(lefts, rights, name):
@@ -840,6 +851,8 @@
     pair_job = net.do(net.exchange, pair_job.result)
     in_job = net.do(gather, got_job.result.reshape(TEAM * (part + 8), 3 * channels))
     net.until(pair_job, in_job, hidden_job)
+    pair_own = gather(pair_job.result.reshape(TEAM * part, 2 * ffown))
+    upstream_job = net.spawn(net.blocks(cotangent))
 
     def last_rows():
         last = hidden_job.result[0][-HALO:]
@@ -851,8 +864,8 @@
 
     halo_job = net.spawn(last_rows())
     before, out_rows_here = net.until(halo_job, out_job)
+    upstream_job.held = True
     weights = in_job.result.reshape(net.count, part + 8, 3 * channels)
-    pair_own = gather(net.later(pair_job.result.reshape(TEAM * part, 2 * ffown)))
     out_job = net.spawn(net.blocks(out_rows_here))
 
     mix_job = net.do(
@@ -863,8 +876,8 @@
         mix_job
     )
     mixer_job = net.spawn(net.blocks(mixer_in))
-    net.step()
-    upstream_job = net.spawn(net.blocks(cotangent))
+    net.step(2)
+    upstream_job.held = False
     mixer_blocks, out_blocks = net.until(mixer_job, out_job)
     project_job = net.do(
         lambda *x: out_project(
@@ -875,46 +888,26 @@
     resid, in_odd, in_even = net.until(project_job)
     upstream = net.until(upstream_job)
 
-    def ffn(inputs, which, send):
-        operands = (inputs, *upstream[which::2], pair_own, down_own)
-        return (lambda *x: ffn_block(x[0], x[1:5], x[5], x[6], send)), operands
-
-    call, operands = ffn(in_odd, 1, True)
-    act_odd, grads_odd, back_odd = net.until(net.do(call, *operands))
-    call, operands = ffn(in_even, 0, False)
-    even_job = net.do(call, *operands)
+    ffn_job = net.do(
+        lambda *x: ffn_block(x[0], x[1], x[2 : 2 + TEAM], x[2 + TEAM], x[3 + TEAM]),
+        in_odd, in_even, *upstream[1::2], *upstream[0::2], pair_own, down_own,
+    )
+    act_odd, act_even, grads_odd, grads_even, pair_all = net.until(ffn_job)
+    pair_sum = reduce(pair_all)
+    back_odd = net.until(
+        net.do(lambda *x: product(*x, True, "ffn_back_odd"), grads_odd, pair_own)
+    )
     ffn_job = net.spawn(
         net.team_sum(
             back_odd,
             lambda arrived: (
                 lambda *x: summed_parts(*x, True, "ffn_back"),
-                (even_job.result[1], pair_own, arrived),
+                (grads_even, pair_own, arrived),
             ),
         )
     )
-    act_even, grads_even = net.until(even_job)
+    odd_job = net.do(lambda *x: product(*x, False, "ffn_output"), act_odd, down_own)
     net.step()
-    pair_job = net.do(
-        lambda *x: weight_grads(x[:2], x[2:], "pair_grads"),
-        in_odd, in_even, grads_odd, grads_even,
-    )
-    odd_job = net.do(ffn_output, act_odd, down_own)
-    ffn_grad = net.until(ffn_job)
-    pair_sum = reduce(pair_job.result)
-
-    back_job = net.do(
-        lambda *x: resid_back(x[:4], *x[4:7], x[7:], teams),
-        *ffn_grad, resid, gain_two, cotangent, *out_blocks,
-    )
-    resid_grad, rounded, mixer_grad = net.until(back_job)
-    down_job = net.do(
-        lambda *x: weight_grads(x[:2], x[2:], "down_grads"),
-        act_odd, act_even, *upstream[1::2], *upstream[0::2],
-    )
-    rounded_job = net.spawn(net.blocks(rounded))
-    mixer_grad = net.until(net.do(net.exchange, mixer_grad)).reshape(TEAM * rows, channels)
-    rounded_job.held = True
-    down_sum = reduce(down_job.result)
     output_job = net.spawn(
         net.team_sum(
             odd_job.result,
@@ -922,13 +915,31 @@
                 lambda *x: summed_parts(*x, False, "ffn_output_sum"),
                 (act_even, down_own, arrived),
             ),
-            2,
+            True,
         )
     )
+    net.step()
+    down_job = net.do(
+        lambda *x: weight_grads(x[:2], x[2:], "down_grads"),
+        act_odd, act_even, *upstream[1::2], *upstream[0::2],
+    )
+    ffn_grad = net.until(ffn_job)
+    down_sum = reduce(down_job.result)
+
+    back_job = net.do(
+        lambda *x: resid_back(x[:4], *x[4:7], x[7:], teams),
+        *ffn_grad, resid, gain_two, cotangent, *out_blocks,
+    )
+    resid_grad, rounded, mixer_grad = net.until(back_job)
+    output_job.held = True
+    rounded_job = net.spawn(net.blocks(rounded))
+    mixer_grad = net.until(net.do(net.exchange, mixer_grad)).reshape(TEAM * rows, channels)
+    rounded_job.held = True
     gated_part, rim, taps_grad = net.until(
         net.do(conv_back, mixer_grad, mixed, gated, conv, taps, keeps)
     )
     rounded_job.held = False
+    output_job.held = False
 
     def rim_steps():
         (returned,) = yield [(rim, ("back",))]
@@ -942,6 +953,7 @@
         )
     )
     in_job = net.spawn(net.line_sum(shares))
+    pair_job = net.do(net.exchange, pair_sum.reshape(TEAM, part, 2 * ffown))
     normed_job = net.spawn(
         net.team_sum(
             normed_odd,
@@ -949,7 +961,7 @@
                 lambda *x: summed_parts(*x, True, "mixer_back_sum", True),
                 (mixed_grad, in_own, arrived),
             ),
-            2,
+            span=2,
         )
     )
     low = (part + 15) // 16 * 16
@@ -958,8 +970,8 @@
         mixer_in, *net.until(rounded_job), taps_grad,
     )
     net.until(out_job)
+    net.need(down_sum)
     out_job = net.spawn(net.line_sum(out_job.result))
-    pair_job = net.do(net.exchange, pair_sum.reshape(TEAM, part, 2 * ffown))
     in_grad = net.until(in_job).astype(NARROW)
     in_job = net.do(net.exchange, in_grad.reshape(TEAM, part, 3 * channels))
     finish_job = net.do(
@@ -987,11 +999,11 @@
     return (
         hidden_out,
         grad_hidden,
-        grad_mixer_gain.reshape(1, part),
+        grad_mixer_gain,
         in_grad[None],
         grad_conv[None],
         grad_out[None],
-        grad_ffn_gain.reshape(1, part),
+        grad_ffn_gain,
         grad_gate[None],
         grad_up[None],
         down_sum.astype(WIDE)[None],

time: 274 us -> 262 us (0.956)
  blocking collectives: 24.2 us -> 35.3 us
  waiting for transfers between devices: 69.6 us -> 59.1 us
  starting transfers between devices: 64.7 us -> 59 us
  Pallas kernels: 81.4 us -> 77.7 us
    all_to_all x0 -> x1, blocking collectives: none -> 11 us  [exchange(): lax.all_to_all(blocks, 'dp', 0, 0, axis_index_groups=groups, tiled=True)]
    ppermute x58, waiting for transfers between devices: 57.4 us -> 49 us  [one_step(): got.append(lax.ppermute(values[at], 'dp', self.pairs(move[1])))]
    ppermute x58, starting transfers between devices: 46 us -> 42 us  [one_step(): got.append(lax.ppermute(values[at], 'dp', self.pairs(move[1])))]
    pallas_call x18 -> x17, Pallas kernels: 81.4 us -> 77.7 us  [call(): pl.pallas_call(kernel, out_shape=out_shape, scratch_shapes=list(scratch),...]
    all_to_all x5 -> x4, starting transfers between devices: 18.6 us -> 16.6 us  [exchange(): lax.all_to_all(blocks, 'dp', 0, 0, axis_index_groups=groups, tiled=True)]
    all_to_all x5 -> x4, waiting for transfers between devices: 11.2 us -> 9.25 us  [exchange(): lax.all_to_all(blocks, 'dp', 0, 0, axis_index_groups=groups, tiled=True)]
    unnamed x147 -> x143, local copies, waits for them, and re-layouts: 5.99 us -> 4.11 us
  transfers between devices with their start and end apart: 67 -> 66, of which waited for: 19 -> 18; matrix products, arithmetic and copies ran while one was open for 2% -> 3% of each run, Pallas kernels for 25% -> 25%
where the time goes in v2:
time: 262 us; the launch traced here: 261 us
  Pallas kernels  77.7 us (30%)
  waiting for transfers between devices  59.1 us (23%)
  starting transfers between devices  59 us (23%)
  blocking collectives  35.3 us (13%)
  between operations  14.9 us (6%)
  other arithmetic  8.5 us (3%)
  local copies, waits for them, and re-layouts  6.23 us (2%)
    pallas_call x17, Pallas kernels, call(): pl.pallas_call(kernel, out_shape=out_shape, scratch_shapes=list(scratch),...  77.7 us
    ppermute x58, waiting for transfers between devices, one_step(): got.append(lax.ppermute(values[at], 'dp', self.pairs(move[1])))  49 us
    ppermute x58, starting transfers between devices, one_step(): got.append(lax.ppermute(values[at], 'dp', self.pairs(move[1])))  42 us
    all_gather x1, blocking collectives, gather(): lax.all_gather(value, 'dp', axis=0, tiled=True, axis_index_groups=line)  24.3 us
    all_to_all x4, starting transfers between devices, exchange(): lax.all_to_all(blocks, 'dp', 0, 0, axis_index_groups=groups, tiled=True)  16.6 us
    all_to_all x1, blocking collectives, exchange(): lax.all_to_all(blocks, 'dp', 0, 0, axis_index_groups=groups, tiled=True)  11 us
    all_to_all x4, waiting for transfers between devices, exchange(): lax.all_to_all(blocks, 'dp', 0, 0, axis_index_groups=groups, tiled=True)  9.25 us
  transfers between devices with their start and end apart: 66, of which 18 were waited for; matrix products, arithmetic and copies ran while one was open for 3% of the time, Pallas kernels for 25%

profile of v2, /device:TPU:0, one launch (start us, length us, event | category | flops | bytes accessed | tf_op | source)
XLA Modules:
  0.0 260.7 jit_solution(6032467188091039135)
XLA Ops:
  7.9 2.0 in_prepare.1
  9.9 2.9 %collective-permute-start = (bf16[128,1024]{1,0:T(8,128)(2,1)}, bf16[128,1024]{1,0:T(8,128)(2,1)S(1)}, u32[]{:S(2)}, u32[]{:S(2)}) collective-permute-start(bf16[128,1024]{1,0:T(8,128)(2,1)} %refs_16_), channel_id=1, source_target_pairs={{0,2},{1,3},{2,0},{3,1},{4,6},{5,7},{6,4},{7,5},{8,10},{9,11},{10,... | collective-permute-start | bytes 786440 | tf_op jit(solution)/shard_map/ppermute | solution.py:127
  12.8 1.5 collective-permute-start.1
  14.4 4.3 %all-to-all-start = ((bf16[8,40,384]{2,1,0:T(8,128)(2,1)}), bf16[8,40,384]{2,1,0:T(8,128)(2,1)S(1)}, u32[]{:S(2)}, u32[]{:S(2)}) async-start(bf16[8,40,384]{2,1,0:T(8,128)(2,1)} %in_prepare.1), calls=%async_computation | async-start | bytes 491520 | tf_op jit(solution)/shard_map/all_to_all | solution.py:180
  18.7 2.3 pair_prepare.1
  21.0 8.1 %all-to-all-done = bf16[8,40,384]{2,1,0:T(8,128)(2,1)S(1)} async-done(((bf16[8,40,384]{2,1,0:T(8,128)(2,1)}), bf16[8,40,384]{2,1,0:T(8,128)(2,1)S(1)}, u32[]{:S(2)}, u32[]{:S(2)}) %all-to-all-start) | async-done | bytes 245792 | tf_op jit(solution)/shard_map/all_to_all | solution.py:180
  29.1 3.7 %all-to-all-start.1 = ((bf16[8,32,1152]{2,1,0:T(8,128)(2,1)}), bf16[8,32,1152]{2,1,0:T(8,128)(2,1)S(1)}, u32[]{:S(2)}, u32[]{:S(2)}) async-start(bf16[8,32,1152]{2,1,0:T(8,128)(2,1)} %pair_prepare.1), calls=%async_computation.1 | async-start | bytes 1179648 | tf_op jit(solution)/shard_map/all_to_all | solution.py:180
  32.9 1.6 collective-permute-start.7
  34.5 2.2 collective-permute-start.8
  37.3 24.3 %all_gather.9 = bf16[1280,384]{1,0:T(8,128)(2,1)} all-gather(bf16[320,384]{1,0:T(8,128)(2,1)S(1)} %bitcast.41), channel_id=1, replica_groups={{0,8,16,24},{1,9,17,25},{2,10,18,26},{3,11,19,27},{4,12,20,28},{5,13,21..., dimensions={0}, use_global_device_ids=true | all-gather | bytes 1228800 | tf_op jit(solution)/shard_map/all_gather | solution.py:830
  63.5 1.6 collective-permute-start.10
  65.1 1.5 collective-permute-start.11
  66.6 1.5 collective-permute-start.13
  68.1 5.6 %collective-permute-done.13.refs_8_ = bf16[16,1024]{1,0:T(8,128)(2,1)S(1)} collective-permute-done((bf16[16,1024]{1,0:T(8,128)(2,1)S(1)}, bf16[16,1024]{1,0:T(8,128)(2,1)S(1)}, u32[]{:S(2)}, u32[]{:S(2)}) %collective-permute-start.13) | collective-permute-done | bytes 32800 | tf_op jit(solution)/shard_map/ppermute | solution.py:127
  74.8 7.1 %mixer_forward.1 = (bf16[1040,1024]{1,0:T(8,128)(2,1)}, f32[1040,384]{1,0:T(8,128)}, f32[1040,128]{1,0:T(8,128)}, f32[1024,128]{1,0:T(8,128)}, bf16[1024,128]{1,...) custom-call(bf16[128,1024]{1,0:T(8,128)(2,1)} %refs_16_, ...), custom_call_target="tpu_custom_call" | custom-call | flops 805306368 | bytes 3112960 | tf_op jit(solution)/shard_map/mixer_forward/pallas_call | solution.py:36
  82.0 1.7 collective-permute-start.17
  84.3 1.2 collective-permute-start.20
  86.3 3.3 %collective-permute-done.17.refs_14_.refs_6_ = bf16[128,1024]{1,0:T(8,128)(2,1)S(1)} collective-permute-done((bf16[128,1024]{1,0:T(8,128)(2,1)S(1)}, bf16[128,1024]{1,0:T(8,128)(2,1)S(1)}, u32[]{:S(2)}, u32[]{:S(2)}) %collective-permute-start.17) | collective-permute-done | bytes 262176 | tf_op jit(solution)/shard_map/ppermute | solution.py:127
  89.7 4.4 %collective-permute-done.20.refs_2_ = bf16[1024,128]{1,0:T(8,128)(2,1)S(1)} collective-permute-done((bf16[1024,128]{1,0:T(8,128)(2,1)}, bf16[1024,128]{1,0:T(8,128)(2,1)S(1)}, u32[]{:S(2)}, u32[]{:S(2)}) %collective-permute-start.20) | collective-permute-done | bytes 262176 | tf_op jit(solution)/shard_map/ppermute | solution.py:127
  94.2 1.7 collective-permute-start.24
  96.5 4.2 %collective-permute-done.24.refs_6_ = bf16[1024,128]{1,0:T(8,128)(2,1)S(1)} collective-permute-done((bf16[1024,128]{1,0:T(8,128)(2,1)S(1)}, bf16[1024,128]{1,0:T(8,128)(2,1)S(1)}, u32[]{:S(2)}, u32[]{:S(2)}) %collective-permute-start.24) | collective-permute-done | bytes 262176 | tf_op jit(solution)/shard_map/ppermute | solution.py:127
  100.7 1.7 collective-permute-start.27
  103.0 4.2 %collective-permute-done.27.refs_7_.refs_9_ = bf16[128,1024]{1,0:T(8,128)(2,1)S(1)} collective-permute-done((bf16[128,1024]{1,0:T(8,128)(2,1)S(1)}, bf16[128,1024]{1,0:T(8,128)(2,1)S(1)}, u32[]{:S(2)}, u32[]{:S(2)}) %collective-permute-start.27) | collective-permute-done | bytes 262176 | tf_op jit(solution)/shard_map/ppermute | solution.py:127
  108.1 7.8 %out_project.1 = (f32[128,1024]{1,0:T(8,128)}, bf16[512,1024]{1,0:T(8,128)(2,1)}, bf16[512,1024]{1,0:T(8,128)(2,1)}) custom-call(bf16[1024,128]{1,0:T(8,128)(2,1)} %get-tuple-element.622.refs_0_, bf16[1024,128]{1,0:T(8,128)(2,1)} %collective-permute-done.22.refs_1_, bf16[1024,128]{1,0:T(8,128)(2,1)} %copy-done.48, bf16[1024,128]{1,0:T(8,128)(2,1)} %copy-done.66, ...), custom_call_target="tpu_custom_call" | custom-call | flops 2147483648 | bytes 6295552 | tf_op jit(solution)/shard_map/out_project/pallas_call | solution.py:36
  116.6 11.6 %ffn.1 = (bf16[512,576]{1,0:T(8,128)(2,1)}, bf16[512,576]{1,0:T(8,128)(2,1)}, bf16[512,1152]{1,0:T(8,128)(2,1)}, bf16[512,1152]{1,0:T(8,128)(2,1)}, bf16[1024,1152]{1,0:T(8,128)(2,1)}) custom-call(bf16[512,1024]{1,0:T(8,128)(2,1)} %get-tuple-element.481.odd_in, bf16[512,1024]{1,0:T(8,128)(2,1)} %get-tuple-element.482.even_in, bf16[128,1024]{1,0:T(8,128)(2,1)} %copy-done.31, ...), custom_call_target="tpu_custom_call" | custom-call | flops 6039797760 | bytes 7733248 | tf_op jit(solution)/shard_map/ffn/pallas_call | solution.py:36
  128.5 4.6 %ffn_back_odd.1 = bf16[512,1024]{1,0:T(8,128)(2,1)} custom-call(bf16[512,1152]{1,0:T(8,128)(2,1)} %get-tuple-element.498.left, bf16[1024,1152]{1,0:T(8,128)(2,1)} %all-gather.4.cloned.1.call-done.refs_8_.right.right_in), custom_call_target="tpu_custom_call" | custom-call | flops 1207959552 | bytes 3538944 | tf_op jit(solution)/shard_map/ffn_back_odd/pallas_call | solution.py:36
  133.6 3.4 %ffn_output.1 = bf16[512,1024]{1,0:T(8,128)(2,1)} custom-call(bf16[512,576]{1,0:T(8,128)(2,1)} %get-tuple-element.528.left.refs_0_, bf16[576,1024]{1,0:T(8,128)(2,1)} %bitcast.31), custom_call_target="tpu_custom_call" | custom-call | flops 603979776 | bytes 1769472 | tf_op jit(solution)/shard_map/ffn_output/pallas_call | solution.py:36
  137.0 1.0 copy-done.15
  138.0 4.8 %ffn_back.1 = (f32[128,1024]{1,0:T(8,128)}, bf16[128,1024]{1,0:T(8,128)(2,1)}, bf16[128,1024]{1,0:T(8,128)(2,1)}, bf16[128,1024]{1,0:T(8,128)(2,1)}) custom-call(bf16[512,1152]{1,0:T(8,128)(2,1)} %get-tuple-element.505.left_in, bf16[1024,1152]{1,0:T(8,128)(2,1)} %all-gather.4.cloned.1.call-done.refs_8_.right.right_in, bf16[512,1024]{1,0:T(8,128)(2,1)} %copy-done.15), custom_call_target="tpu_custom_call" | custom-call | flops 1207959552 | bytes 4587520 | tf_op jit(solution)/shard_map/ffn_back/pallas_call | solution.py:36
  142.9 2.7 %collective-permute-start.34 = (bf16[128,1024]{1,0:T(8,128)(2,1)}, bf16[128,1024]{1,0:T(8,128)(2,1)S(1)}, u32[]{:S(2)}, u32[]{:S(2)}) collective-permute-start(bf16[128,1024]{1,0:T(8,128)(2,1)} %get-tuple-element.518), channel_id=1, source_target_pairs={{0,6},{1,7},{2,4},{3,5},{4,2},{5,3},{6,0},{7,1},{8,14},{9,15},{10,... | collective-permute-start | bytes 786440 | tf_op jit(solution)/shard_map/ppermute | solution.py:127
  146.4 3.7 %ffn_output_sum.1 = (f32[128,1024]{1,0:T(8,128)}, bf16[128,1024]{1,0:T(8,128)(2,1)}, bf16[128,1024]{1,0:T(8,128)(2,1)}, bf16[128,1024]{1,0:T(8,128)(2,1)}) custom-call(bf16[512,576]{1,0:T(8,128)(2,1)} %get-tuple-element.529.left_in.refs_1_, bf16[576,1024]{1,0:T(8,128)(2,1)} %bitcast.32, bf16[512,1024]{1,0:T(8,128)(2,1)} %copy-done.14), custom_call_target="tpu_custom_call" | custom-call | flops 603979776 | bytes 2818048 | tf_op jit(solution)/shard_map/ffn_output_sum/pallas_call | solution.py:36
  150.2 4.7 %down_grads.1 = bf16[576,1024]{1,0:T(8,128)(2,1)} custom-call(bf16[512,576]{1,0:T(8,128)(2,1)} %get-tuple-element.528.left.refs_0_, bf16[512,576]{1,0:T(8,128)(2,1)} %get-tuple-element.529.left_in.refs_1_, bf16[128,1024]{1,0:T(8,128)(2,1)} %copy-done.31, bf16[128,1024]{1,0:T(8,128)(2,1)} %copy-done.37, bf16[128,1024]{1,0:T(8,128)(2,1)} %copy-done.38, ...), custom_call_target="tpu_custom_call" | custom-call | flops 1207959552 | bytes 3276800 | tf_op jit(solution)/shard_map/down_grads/pallas_call | solution.py:36
  154.9 3.2 %collective-permute-done.35.across = bf16[128,1024]{1,0:T(8,128)(2,1)S(1)} collective-permute-done((bf16[128,1024]{1,0:T(8,128)(2,1)}, bf16[128,1024]{1,0:T(8,128)(2,1)S(1)}, u32[]{:S(2)}, u32[]{:S(2)}) %collective-permute-start.35) | collective-permute-done | bytes 262176 | tf_op jit(solution)/shard_map/ppermute | solution.py:127
  158.2 1.6 collective-permute-start.37
  159.8 1.3 collective-permute-start.38
  161.2 4.9 %resid_back.1 = (f32[128,1024]{1,0:T(8,128)}, bf16[128,1024]{1,0:T(8,128)(2,1)}, bf16[8,128,128]{2,1,0:T(8,128)(2,1)}) custom-call(f32[128,1024]{1,0:T(8,128)} %get-tuple-element.548.own, bf16[128,1024]{1,0:T(8,128)(2,1)} %copy-done.44, bf16[128,1024]{1,0:T(8,128)(2,1)} %copy-done.45, bf16[128,1024]{1,0:T(8,128)(2,1)} %copy-done.46, ...), custom_call_target="tpu_custom_call" | custom-call | flops 268435456 | bytes 4198400 | tf_op jit(solution)/shard_map/resid_back/pallas_call | solution.py:36
  166.3 1.4 collective-permute-done.38
  168.0 1.6 collective-permute-start.40
  169.7 11.0 %all_to_all.25 = bf16[8,128,128]{2,1,0:T(8,128)(2,1)} all-to-all(bf16[8,128,128]{2,1,0:T(8,128)(2,1)} %get-tuple-element.574), channel_id=1, replica_groups={{0,1,2,3,4,5,6,7},{8,9,10,11,12,13,14,15},{16,17,18,19,20,21,22,23},{24..., dimensions={0} | all-to-all | bytes 524288 | tf_op jit(solution)/shard_map/all_to_all | solution.py:180
  180.7 3.6 %conv_back.1 = (f32[1024,128]{1,0:T(8,128)}, f32[8,128]{1,0:T(8,128)}, f32[8,128]{1,0:T(8,128)}) custom-call(bf16[1024,128]{1,0:T(8,128)(2,1)} %bitcast.35, f32[1040,384]{1,0:T(8,128)} %get-tuple-element.602.mixed.refs_3_, f32[1040,128]{1,0:T(8,128)} %get-tuple-element.581.gated, f32[1024,128]{1,0:T(8,128)} %get-tuple-element.603.conv.refs_4_, ...), custom_call_target="tpu_custom_call" | custom-call | bytes 2928704 | tf_op jit(solution)/shard_map/conv_back/pallas_call | solution.py:36
  184.8 1.5 collective-permute-start.43
  186.8 1.3 collective-permute-start.46
  188.1 4.7 %collective-permute-done.46.refs_1_ = f32[8,128]{1,0:T(8,128)S(1)} collective-permute-done((f32[8,128]{1,0:T(8,128)}, f32[8,128]{1,0:T(8,128)S(1)}, u32[]{:S(2)}, u32[]{:S(2)}) %collective-permute-start.46) | collective-permute-done | bytes 4128 | tf_op jit(solution)/shard_map/ppermute | solution.py:127
  192.8 1.7 collective-permute-done.43.refs_7_
  194.5 1.2 collective-permute-start.47
  195.7 5.9 %mixer_back.1 = (bf16[1024,384]{1,0:T(8,128)(2,1)}, bf16[512,1024]{1,0:T(8,128)(2,1)}, f32[256,384]{1,0:T(8,128)}, f32[256,384]{1,0:T(8,128)}, f32[256,384]{1,0:T(8,128)}, /*index=5*/bf16[256,384]{1,0:T(8,128)(2,1)}) custom-call(f32[1024,128]{1,0:T(8,128)} %get-tuple-element.599.refs_0_, f32[8,128]{1,0:T(8,128)} %copy-done.61, bf16[1024,128]{1,0:T(8,128)(2,1)} %bitcast.36, ...), custom_call_target="tpu_custom_call" | custom-call | flops 1207959552 | bytes 5828608 | tf_op jit(solution)/shard_map/mixer_back/pallas_call | solution.py:36
  201.9 3.5 %all-to-all-start.3 = ((bf16[8,32,1152]{2,1,0:T(8,128)(2,1)}), bf16[8,32,1152]{2,1,0:T(8,128)(2,1)S(1)}, u32[]{:S(2)}, u32[]{:S(2)}) async-start(bf16[8,32,1152]{2,1,0:T(8,128)(2,1)} %bitcast.44), calls=%async_computation.4 | async-start | bytes 1179648 | tf_op jit(solution)/shard_map/all_to_all | solution.py:180
  205.7 3.2 %out_back.1 = (f32[48,1024]{1,0:T(8,128)}, f32[48,1024]{1,0:T(8,128)}, f32[48,1024]{1,0:T(8,128)}, bf16[48,1024]{1,0:T(8,128)(2,1)}) custom-call(bf16[1024,128]{1,0:T(8,128)(2,1)} %get-tuple-element.622.refs_0_, bf16[128,1024]{1,0:T(8,128)(2,1)} %get-tuple-element.623.refs_1_, bf16[128,1024]{1,0:T(8,128)(2,1)} %copy-done.39, bf16[128,1024]{1,0:T(8,128)(2,1)} %copy-done.12, ...), custom_call_target="tpu_custom_call" | custom-call | flops 268435456 | bytes 2363392 | tf_op jit(solution)/shard_map/out_back/pallas_call | solution.py:36
  208.9 5.8 %collective-permute-done.48 = bf16[256,384]{1,0:T(8,128)(2,1)S(1)} collective-permute-done((bf16[256,384]{1,0:T(8,128)(2,1)}, bf16[256,384]{1,0:T(8,128)(2,1)S(1)}, u32[]{:S(2)}, u32[]{:S(2)}) %collective-permute-start.48) | collective-permute-done | bytes 196640 | tf_op jit(solution)/shard_map/ppermute | solution.py:127
  214.7 1.2 all-to-all-done.3.blocks
  218.1 3.4 %mixer_back_sum.1 = (f32[128,1024]{1,0:T(8,128)}, bf16[128,1024]{1,0:T(8,128)(2,1)}, bf16[128,1024]{1,0:T(8,128)(2,1)}, bf16[128,1024]{1,0:T(8,128)(2,1)}) custom-call(bf16[1024,384]{1,0:T(8,128)(2,1)} %get-tuple-element.644.left_in, bf16[1024,384]{1,0:T(8,128)(2,1)} %get-tuple-element.645.refs_6_.right_in, bf16[512,1024]{1,0:T(8,128)(2,1)} %copy-done.7), custom_call_target="tpu_custom_call" | custom-call | flops 402653184 | bytes 2621440 | tf_op jit(solution)/shard_map/mixer_back_sum/pallas_call | solution.py:36
  221.5 2.4 collective-permute-done.51
  223.9 2.1 collective-permute-done.50
  226.0 1.0 add_convert_fusion.5
  227.0 1.0 add_convert_fusion.2
  228.2 1.8 add_convert_fusion
  230.0 2.4 collective-permute-start.52
  234.5 2.1 collective-permute-done.55
  237.3 5.1 %all-to-all-start.4 = ((bf16[8,32,384]{2,1,0:T(8,128)(2,1)}), bf16[8,32,384]{2,1,0:T(8,128)(2,1)S(1)}, u32[]{:S(2)}, u32[]{:S(2)}) async-start(bf16[8,32,384]{2,1,0:T(8,128)(2,1)} %bitcast.13), calls=%async_computation.6 | async-start | bytes 393216 | tf_op jit(solution)/shard_map/all_to_all | solution.py:180
  242.4 0.9 bitcast_convert_fusion
  244.0 2.7 %pair_finish.1 = (f32[32,4608]{1,0:T(8,128)}, f32[32,4608]{1,0:T(8,128)}, f32[1,32]{1,0:T(1,128)}) custom-call(bf16[8,32,1152]{2,1,0:T(8,128)(2,1)} %copy-done.2, bf16[32,4608]{1,0:T(8,128)(2,1)} %bitcast.38, bf16[32,4608]{1,0:T(8,128)(2,1)} %bitcast.40, bf16[32,1]{1,0:T(8,128)(2,1)} %copy.21.gain), custom_call_target="tpu_custom_call" | custom-call | bytes 1179712 | tf_op jit(solution)/shard_map/pair_finish/pallas_call | solution.py:36
  246.7 2.7 %collective-permute-done.57 = bf16[48,1024]{1,0:T(8,128)(2,1)S(1)} collective-permute-done((bf16[48,1024]{1,0:T(8,128)(2,1)S(1)}, bf16[48,1024]{1,0:T(8,128)(2,1)S(1)}, u32[]{:S(2)}, u32[]{:S(2)}) %collective-permute-start.57) | collective-permute-done | bytes 98336 | tf_op jit(solution)/shard_map/ppermute | solution.py:127
  249.8 1.1 fusion.5
  252.1 2.0 in_finish.1
  (256 shorter events, 19.7 us)
Async XLA Ops:
  7.2 108.8 %all-gather.6.cloned.1.call-start = ((), (), s32[]{:S(2)}) async-start(), calls=%async_computation.10 | async-start | bytes 1474560 | tf_op jit(solution)/shard_map/all_gather | solution.py:830
  9.9 19.2 %collective-permute-start = (bf16[128,1024]{1,0:T(8,128)(2,1)}, bf16[128,1024]{1,0:T(8,128)(2,1)S(1)}, u32[]{:S(2)}, u32[]{:S(2)}) collective-permute-start(bf16[128,1024]{1,0:T(8,128)(2,1)} %refs_16_), channel_id=1, source_target_pairs={{0,2},{1,3},{2,0},{3,1},{4,6},{5,7},{6,4},{7,5},{8,10},{9,11},{10,... | collective-permute-start | bytes 786440 | tf_op jit(solution)/shard_map/ppermute | solution.py:127
  12.8 16.2 %collective-permute-start.1 = (bf16[128,1024]{1,0:T(8,128)(2,1)}, bf16[128,1024]{1,0:T(8,128)(2,1)S(1)}, u32[]{:S(2)}, u32[]{:S(2)}) collective-permute-start(bf16[128,1024]{1,0:T(8,128)(2,1)} %refs_16_), channel_id=1, source_target_pairs={{0,4},{1,5},{2,6},{3,7},{4,0},{5,1},{6,2},{7,3},{8,12},{9,13},{10,... | collective-permute-start | bytes 786440 | tf_op jit(solution)/shard_map/ppermute | solution.py:127
  14.4 14.7 %collective-permute-start.2 = (bf16[128,1024]{1,0:T(8,128)(2,1)}, bf16[128,1024]{1,0:T(8,128)(2,1)S(1)}, u32[]{:S(2)}, u32[]{:S(2)}) collective-permute-start(bf16[128,1024]{1,0:T(8,128)(2,1)} %refs_16_), channel_id=1, source_target_pairs={{0,6},{1,7},{2,4},{3,5},{4,2},{5,3},{6,0},{7,1},{8,14},{9,15},{10,... | collective-permute-start | bytes 786440 | tf_op jit(solution)/shard_map/ppermute | solution.py:127
  14.4 14.7 %collective-permute-start.3 = (bf16[128,1024]{1,0:T(8,128)(2,1)}, bf16[128,1024]{1,0:T(8,128)(2,1)S(1)}, u32[]{:S(2)}, u32[]{:S(2)}) collective-permute-start(bf16[128,1024]{1,0:T(8,128)(2,1)} %refs_16_), channel_id=1, source_target_pairs={{0,1},{1,0},{2,3},{3,2},{4,5},{5,4},{6,7},{7,6},{8,9},{9,8},{10,11... | collective-permute-start | bytes 786440 | tf_op jit(solution)/shard_map/ppermute | solution.py:127
  14.4 14.7 %all-to-all-start = ((bf16[8,40,384]{2,1,0:T(8,128)(2,1)}), bf16[8,40,384]{2,1,0:T(8,128)(2,1)S(1)}, u32[]{:S(2)}, u32[]{:S(2)}) async-start(bf16[8,40,384]{2,1,0:T(8,128)(2,1)} %in_prepare.1), calls=%async_computation | async-start | bytes 491520 | tf_op jit(solution)/shard_map/all_to_all | solution.py:180
  29.1 32.5 %all-to-all-start.1 = ((bf16[8,32,1152]{2,1,0:T(8,128)(2,1)}), bf16[8,32,1152]{2,1,0:T(8,128)(2,1)S(1)}, u32[]{:S(2)}, u32[]{:S(2)}) async-start(bf16[8,32,1152]{2,1,0:T(8,128)(2,1)} %pair_prepare.1), calls=%async_computation.1 | async-start | bytes 1179648 | tf_op jit(solution)/shard_map/all_to_all | solution.py:180
  32.8 83.2 %all-gather.4.cloned.1.call-start = ((), (), s32[]{:S(2)}) async-start(), calls=%async_computation.7 | async-start | bytes 2949120 | tf_op jit(solution)/shard_map/all_gather | solution.py:830
  32.9 28.7 %collective-permute-start.7 = (bf16[32,1024]{1,0:T(8,128)(2,1)S(1)}, bf16[32,1024]{1,0:T(8,128)(2,1)S(1)}, u32[]{:S(2)}, u32[]{:S(2)}) collective-permute-start(bf16[32,1024]{1,0:T(8,128)(2,1)S(1)} %bitcast.45), channel_id=1, source_target_pairs={{0,8},{1,9},{2,10},{3,11},{4,12},{5,13},{6,14},{7,15},{8,16},{9,17... | collective-permute-start | bytes 196616 | tf_op jit(solution)/shard_map/ppermute | solution.py:127
  34.5 27.1 %collective-permute-start.8 = (bf16[32,1024]{1,0:T(8,128)(2,1)S(1)}, bf16[32,1024]{1,0:T(8,128)(2,1)S(1)}, u32[]{:S(2)}, u32[]{:S(2)}) collective-permute-start(bf16[32,1024]{1,0:T(8,128)(2,1)S(1)} %bitcast.46), channel_id=1, source_target_pairs={{0,24},{1,25},{2,26},{3,27},{4,28},{5,29},{6,30},{7,31},{8,0},{9,1... | collective-permute-start | bytes 196616 | tf_op jit(solution)/shard_map/ppermute | solution.py:127
  36.8 24.8 %collective-permute-start.4 = (bf16[128,1024]{1,0:T(8,128)(2,1)S(1)}, bf16[128,1024]{1,0:T(8,128)(2,1)S(1)}, u32[]{:S(2)}, u32[]{:S(2)}) collective-permute-start(bf16[128,1024]{1,0:T(8,128)(2,1)S(1)} %collective-permute-done.refs_2_.refs_18_), channel_id=1, source_target_pairs={{0,1},{1,0},{2,3},{3,2},{4,5},{5,4},{6,7},{7,6},{8,9},{9,8},{10,11... | collective-permute-start | bytes 786440 | tf_op jit(solution)/shard_map/ppermute | solution.py:127
  36.8 24.8 %collective-permute-start.5 = (bf16[128,1024]{1,0:T(8,128)(2,1)S(1)}, bf16[128,1024]{1,0:T(8,128)(2,1)S(1)}, u32[]{:S(2)}, u32[]{:S(2)}) collective-permute-start(bf16[128,1024]{1,0:T(8,128)(2,1)S(1)} %collective-permute-done.1.refs_4_.refs_20_), channel_id=1, source_target_pairs={{0,1},{1,0},{2,3},{3,2},{4,5},{5,4},{6,7},{7,6},{8,9},{9,8},{10,11... | collective-permute-start | bytes 786440 | tf_op jit(solution)/shard_map/ppermute | solution.py:127
  37.3 24.4 %collective-permute-start.6 = (bf16[128,1024]{1,0:T(8,128)(2,1)S(1)}, bf16[128,1024]{1,0:T(8,128)(2,1)S(1)}, u32[]{:S(2)}, u32[]{:S(2)}) collective-permute-start(bf16[128,1024]{1,0:T(8,128)(2,1)S(1)} %collective-permute-done.2.refs_6_.refs_22_), channel_id=1, source_target_pairs={{0,1},{1,0},{2,3},{3,2},{4,5},{5,4},{6,7},{7,6},{8,9},{9,8},{10,11... | collective-permute-start | bytes 786440 | tf_op jit(solution)/shard_map/ppermute | solution.py:127
  62.6 139.1 %reduce-scatter.3.cloned.1.call-start = ((), (), s32[]{:S(2)}) async-start(), calls=%async_computation.8 | async-start | bytes 2949120 | tf_op jit(solution)/shard_map/reduce_scatter | solution.py:833
  63.5 10.2 %collective-permute-start.10 = (bf16[128,1024]{1,0:T(8,128)(2,1)S(1)}, bf16[128,1024]{1,0:T(8,128)(2,1)S(1)}, u32[]{:S(2)}, u32[]{:S(2)}) collective-permute-start(bf16[128,1024]{1,0:T(8,128)(2,1)S(1)} %copy-done.5), channel_id=1, source_target_pairs={{0,2},{1,3},{2,0},{3,1},{4,6},{5,7},{6,4},{7,5},{8,10},{9,11},{10,... | collective-permute-start | bytes 786440 | tf_op jit(solution)/shard_map/ppermute | solution.py:127
  65.1 8.6 %collective-permute-start.11 = (bf16[128,1024]{1,0:T(8,128)(2,1)S(1)}, bf16[128,1024]{1,0:T(8,128)(2,1)S(1)}, u32[]{:S(2)}, u32[]{:S(2)}) collective-permute-start(bf16[128,1024]{1,0:T(8,128)(2,1)S(1)} %copy-done.5), channel_id=1, source_target_pairs={{0,4},{1,5},{2,6},{3,7},{4,0},{5,1},{6,2},{7,3},{8,12},{9,13},{10,... | collective-permute-start | bytes 786440 | tf_op jit(solution)/shard_map/ppermute | solution.py:127
  66.6 7.2 %collective-permute-start.12 = (bf16[128,1024]{1,0:T(8,128)(2,1)S(1)}, bf16[128,1024]{1,0:T(8,128)(2,1)S(1)}, u32[]{:S(2)}, u32[]{:S(2)}) collective-permute-start(bf16[128,1024]{1,0:T(8,128)(2,1)S(1)} %copy-done.5), channel_id=1, source_target_pairs={{0,1},{1,0},{2,3},{3,2},{4,5},{5,4},{6,7},{7,6},{8,9},{9,8},{10,11... | collective-permute-start | bytes 786440 | tf_op jit(solution)/shard_map/ppermute | solution.py:127
  66.6 7.1 %collective-permute-start.9 = (bf16[32,1024]{1,0:T(8,128)(2,1)S(1)}, bf16[32,1024]{1,0:T(8,128)(2,1)S(1)}, u32[]{:S(2)}, u32[]{:S(2)}) collective-permute-start(bf16[32,1024]{1,0:T(8,128)(2,1)S(1)} %collective-permute-done.7), channel_id=1, source_target_pairs={{0,8},{1,9},{2,10},{3,11},{4,12},{5,13},{6,14},{7,15},{8,16},{9,17... | collective-permute-start | bytes 196616 | tf_op jit(solution)/shard_map/ppermute | solution.py:127
  66.6 7.1 %collective-permute-start.13 = (bf16[16,1024]{1,0:T(8,128)(2,1)S(1)}, bf16[16,1024]{1,0:T(8,128)(2,1)S(1)}, u32[]{:S(2)}, u32[]{:S(2)}) collective-permute-start(bf16[16,1024]{1,0:T(8,128)(2,1)S(1)} %select_select_fusion), channel_id=1, source_target_pairs={{0,8},{1,9},{2,10},{3,11},{4,12},{5,13},{6,14},{7,15},{8,16},{9,17... | collective-permute-start | bytes 98312 | tf_op jit(solution)/shard_map/ppermute | solution.py:127
  73.8 8.1 %collective-permute-start.14 = (bf16[128,1024]{1,0:T(8,128)(2,1)S(1)}, bf16[128,1024]{1,0:T(8,128)(2,1)S(1)}, u32[]{:S(2)}, u32[]{:S(2)}) collective-permute-start(bf16[128,1024]{1,0:T(8,128)(2,1)S(1)} %pad_maximum_fusion.refs_8_.refs_0_), channel_id=1, source_target_pairs={{0,2},{1,3},{2,0},{3,1},{4,6},{5,7},{6,4},{7,5},{8,10},{9,11},{10,... | collective-permute-start | bytes 786440 | tf_op jit(solution)/shard_map/ppermute | solution.py:127
  74.4 7.6 %collective-permute-start.15 = (bf16[128,1024]{1,0:T(8,128)(2,1)S(1)}, bf16[128,1024]{1,0:T(8,128)(2,1)S(1)}, u32[]{:S(2)}, u32[]{:S(2)}) collective-permute-start(bf16[128,1024]{1,0:T(8,128)(2,1)S(1)} %pad_maximum_fusion.refs_8_.refs_0_), channel_id=1, source_target_pairs={{0,4},{1,5},{2,6},{3,7},{4,0},{5,1},{6,2},{7,3},{8,12},{9,13},{10,... | collective-permute-start | bytes 786440 | tf_op jit(solution)/shard_map/ppermute | solution.py:127
  74.8 7.2 %collective-permute-start.16 = (bf16[128,1024]{1,0:T(8,128)(2,1)S(1)}, bf16[128,1024]{1,0:T(8,128)(2,1)S(1)}, u32[]{:S(2)}, u32[]{:S(2)}) collective-permute-start(bf16[128,1024]{1,0:T(8,128)(2,1)S(1)} %pad_maximum_fusion.refs_8_.refs_0_), channel_id=1, source_target_pairs={{0,1},{1,0},{2,3},{3,2},{4,5},{5,4},{6,7},{7,6},{8,9},{9,8},{10,11... | collective-permute-start | bytes 786440 | tf_op jit(solution)/shard_map/ppermute | solution.py:127
  82.0 7.6 %collective-permute-start.17 = (bf16[128,1024]{1,0:T(8,128)(2,1)S(1)}, bf16[128,1024]{1,0:T(8,128)(2,1)S(1)}, u32[]{:S(2)}, u32[]{:S(2)}) collective-permute-start(bf16[128,1024]{1,0:T(8,128)(2,1)S(1)} %get-tuple-element.420), channel_id=1, source_target_pairs={{0,2},{1,5},{2,0},{3,7},{4,6},{5,1},{6,4},{7,3},{8,10},{9,13},{10,... | collective-permute-start | bytes 786440 | tf_op jit(solution)/shard_map/ppermute | solution.py:127
  83.7 5.9 %collective-permute-start.18 = (bf16[128,1024]{1,0:T(8,128)(2,1)S(1)}, bf16[128,1024]{1,0:T(8,128)(2,1)S(1)}, u32[]{:S(2)}, u32[]{:S(2)}) collective-permute-start(bf16[128,1024]{1,0:T(8,128)(2,1)S(1)} %collective-permute-done.14.refs_10_.refs_2_), channel_id=1, source_target_pairs={{0,1},{1,0},{2,3},{3,2},{4,5},{5,4},{6,7},{7,6},{8,9},{9,8},{10,11... | collective-permute-start | bytes 786440 | tf_op jit(solution)/shard_map/ppermute | solution.py:127
  84.0 5.7 %collective-permute-start.19 = (bf16[128,1024]{1,0:T(8,128)(2,1)S(1)}, bf16[128,1024]{1,0:T(8,128)(2,1)S(1)}, u32[]{:S(2)}, u32[]{:S(2)}) collective-permute-start(bf16[128,1024]{1,0:T(8,128)(2,1)S(1)} %collective-permute-done.15.refs_12_.refs_4_), channel_id=1, source_target_pairs={{0,1},{1,0},{2,3},{3,2},{4,5},{5,4},{6,7},{7,6},{8,9},{9,8},{10,11... | collective-permute-start | bytes 786440 | tf_op jit(solution)/shard_map/ppermute | solution.py:127
  84.3 9.8 %collective-permute-start.20 = (bf16[1024,128]{1,0:T(8,128)(2,1)}, bf16[1024,128]{1,0:T(8,128)(2,1)S(1)}, u32[]{:S(2)}, u32[]{:S(2)}) collective-permute-start(bf16[1024,128]{1,0:T(8,128)(2,1)} %get-tuple-element.622.refs_0_), channel_id=1, source_target_pairs={{0,2},{1,3},{2,0},{3,1},{4,6},{5,7},{6,4},{7,5},{8,10},{9,11},{10,... | collective-permute-start | bytes 786440 | tf_op jit(solution)/shard_map/ppermute | solution.py:127
  85.5 8.6 %collective-permute-start.21 = (bf16[1024,128]{1,0:T(8,128)(2,1)}, bf16[1024,128]{1,0:T(8,128)(2,1)S(1)}, u32[]{:S(2)}, u32[]{:S(2)}) collective-permute-start(bf16[1024,128]{1,0:T(8,128)(2,1)} %get-tuple-element.622.refs_0_), channel_id=1, source_target_pairs={{0,4},{1,5},{2,6},{3,7},{4,0},{5,1},{6,2},{7,3},{8,12},{9,13},{10,... | collective-permute-start | bytes 786440 | tf_op jit(solution)/shard_map/ppermute | solution.py:127
  89.6 4.5 %collective-permute-start.22 = (bf16[1024,128]{1,0:T(8,128)(2,1)}, bf16[1024,128]{1,0:T(8,128)(2,1)}, u32[]{:S(2)}, u32[]{:S(2)}) collective-permute-start(bf16[1024,128]{1,0:T(8,128)(2,1)} %get-tuple-element.622.refs_0_), channel_id=1, source_target_pairs={{0,1},{1,0},{2,3},{3,2},{4,5},{5,4},{6,7},{7,6},{8,9},{9,8},{10,11... | collective-permute-start | bytes 786440 | tf_op jit(solution)/shard_map/ppermute | solution.py:127
  94.2 6.4 %collective-permute-start.24 = (bf16[1024,128]{1,0:T(8,128)(2,1)S(1)}, bf16[1024,128]{1,0:T(8,128)(2,1)S(1)}, u32[]{:S(2)}, u32[]{:S(2)}) collective-permute-start(bf16[1024,128]{1,0:T(8,128)(2,1)S(1)} %broadcast_select_fusion), channel_id=1, source_target_pairs={{0,2},{1,5},{2,0},{3,7},{4,6},{5,1},{6,4},{7,3},{8,10},{9,13},{10,... | collective-permute-start | bytes 786440 | tf_op jit(solution)/shard_map/ppermute | solution.py:127
  95.9 4.8 %collective-permute-start.25 = (bf16[1024,128]{1,0:T(8,128)(2,1)S(1)}, bf16[1024,128]{1,0:T(8,128)(2,1)S(1)}, u32[]{:S(2)}, u32[]{:S(2)}) collective-permute-start(bf16[1024,128]{1,0:T(8,128)(2,1)S(1)} %collective-permute-done.20.refs_2_), channel_id=1, source_target_pairs={{0,1},{1,0},{2,3},{3,2},{4,5},{5,4},{6,7},{7,6},{8,9},{9,8},{10,11... | collective-permute-start | bytes 786440 | tf_op jit(solution)/shard_map/ppermute | solution.py:127
  96.1 4.6 %collective-permute-start.26 = (bf16[1024,128]{1,0:T(8,128)(2,1)S(1)}, bf16[1024,128]{1,0:T(8,128)(2,1)S(1)}, u32[]{:S(2)}, u32[]{:S(2)}) collective-permute-start(bf16[1024,128]{1,0:T(8,128)(2,1)S(1)} %collective-permute-done.21.refs_4_), channel_id=1, source_target_pairs={{0,1},{1,0},{2,3},{3,2},{4,5},{5,4},{6,7},{7,6},{8,9},{9,8},{10,11... | collective-permute-start | bytes 786440 | tf_op jit(solution)/shard_map/ppermute | solution.py:127
  100.7 6.4 %collective-permute-start.27 = (bf16[128,1024]{1,0:T(8,128)(2,1)S(1)}, bf16[128,1024]{1,0:T(8,128)(2,1)S(1)}, u32[]{:S(2)}, u32[]{:S(2)}) collective-permute-start(bf16[128,1024]{1,0:T(8,128)(2,1)S(1)} %get-tuple-element.440), channel_id=1, source_target_pairs={{0,2},{1,5},{2,0},{3,7},{4,6},{5,1},{6,4},{7,3},{8,10},{9,13},{10,... | collective-permute-start | bytes 786440 | tf_op jit(solution)/shard_map/ppermute | solution.py:127
  102.4 4.8 %collective-permute-start.28 = (bf16[128,1024]{1,0:T(8,128)(2,1)S(1)}, bf16[128,1024]{1,0:T(8,128)(2,1)S(1)}, u32[]{:S(2)}, u32[]{:S(2)}) collective-permute-start(bf16[128,1024]{1,0:T(8,128)(2,1)S(1)} %collective-permute-done.10.refs_5_.refs_7_), channel_id=1, source_target_pairs={{0,1},{1,0},{2,3},{3,2},{4,5},{5,4},{6,7},{7,6},{8,9},{9,8},{10,11... | collective-permute-start | bytes 786440 | tf_op jit(solution)/shard_map/ppermute | solution.py:127
  102.4 4.7 %collective-permute-start.29 = (bf16[128,1024]{1,0:T(8,128)(2,1)S(1)}, bf16[128,1024]{1,0:T(8,128)(2,1)S(1)}, u32[]{:S(2)}, u32[]{:S(2)}) collective-permute-start(bf16[128,1024]{1,0:T(8,128)(2,1)S(1)} %collective-permute-done.11.refs_6_.refs_8_), channel_id=1, source_target_pairs={{0,1},{1,0},{2,3},{3,2},{4,5},{5,4},{6,7},{7,6},{8,9},{9,8},{10,11... | collective-permute-start | bytes 786440 | tf_op jit(solution)/shard_map/ppermute | solution.py:127
  102.9 4.3 %collective-permute-start.30 = (bf16[1024,128]{1,0:T(8,128)(2,1)S(1)}, bf16[1024,128]{1,0:T(8,128)(2,1)S(1)}, u32[]{:S(2)}, u32[]{:S(2)}) collective-permute-start(bf16[1024,128]{1,0:T(8,128)(2,1)S(1)} %collective-permute-done.24.refs_6_), channel_id=1, source_target_pairs={{0,1},{1,0},{2,3},{3,2},{4,5},{5,4},{6,7},{7,6},{8,9},{9,8},{10,11... | collective-permute-start | bytes 786440 | tf_op jit(solution)/shard_map/ppermute | solution.py:127
  108.0 7.9 %collective-permute-start.31 = (bf16[128,1024]{1,0:T(8,128)(2,1)S(1)}, bf16[128,1024]{1,0:T(8,128)(2,1)S(1)}, u32[]{:S(2)}, u32[]{:S(2)}) collective-permute-start(bf16[128,1024]{1,0:T(8,128)(2,1)S(1)} %collective-permute-done.27.refs_7_.refs_9_), channel_id=1, source_target_pairs={{0,1},{1,0},{2,3},{3,2},{4,5},{5,4},{6,7},{7,6},{8,9},{9,8},{10,11... | collective-permute-start | bytes 786440 | tf_op jit(solution)/shard_map/ppermute | solution.py:127
  128.2 88.4 %reduce-scatter.5.cloned.1.call-start = ((), (), s32[]{:S(2)}) async-start(), calls=%async_computation.9 | async-start | bytes 1474560 | tf_op jit(solution)/shard_map/reduce_scatter | solution.py:833
  137.0 5.8 %collective-permute-start.33 = (bf16[512,1024]{1,0:T(8,128)(2,1)}, bf16[512,1024]{1,0:T(8,128)(2,1)S(1)}, u32[]{:S(2)}, u32[]{:S(2)}) collective-permute-start(bf16[512,1024]{1,0:T(8,128)(2,1)} %ffn_output.1), channel_id=1, source_target_pairs={{0,1},{1,0},{2,3},{3,2},{4,5},{5,4},{6,7},{7,6},{8,9},{9,8},{10,11... | collective-permute-start | bytes 3145736 | tf_op jit(solution)/shard_map/ppermute | solution.py:127
  142.9 12.0 %collective-permute-start.34 = (bf16[128,1024]{1,0:T(8,128)(2,1)}, bf16[128,1024]{1,0:T(8,128)(2,1)S(1)}, u32[]{:S(2)}, u32[]{:S(2)}) collective-permute-start(bf16[128,1024]{1,0:T(8,128)(2,1)} %get-tuple-element.518), channel_id=1, source_target_pairs={{0,6},{1,7},{2,4},{3,5},{4,2},{5,3},{6,0},{7,1},{8,14},{9,15},{10,... | collective-permute-start | bytes 786440 | tf_op jit(solution)/shard_map/ppermute | solution.py:127
  145.5 12.6 %collective-permute-start.35 = (bf16[128,1024]{1,0:T(8,128)(2,1)}, bf16[128,1024]{1,0:T(8,128)(2,1)S(1)}, u32[]{:S(2)}, u32[]{:S(2)}) collective-permute-start(bf16[128,1024]{1,0:T(8,128)(2,1)} %get-tuple-element.519), channel_id=1, source_target_pairs={{0,2},{1,3},{2,0},{3,1},{4,6},{5,7},{6,4},{7,5},{8,10},{9,11},{10,... | collective-permute-start | bytes 786440 | tf_op jit(solution)/shard_map/ppermute | solution.py:127
  146.0 12.1 %collective-permute-start.36 = (bf16[128,1024]{1,0:T(8,128)(2,1)}, bf16[128,1024]{1,0:T(8,128)(2,1)S(1)}, u32[]{:S(2)}, u32[]{:S(2)}) collective-permute-start(bf16[128,1024]{1,0:T(8,128)(2,1)} %get-tuple-element.520), channel_id=1, source_target_pairs={{0,4},{1,5},{2,6},{3,7},{4,0},{5,1},{6,2},{7,3},{8,12},{9,13},{10,... | collective-permute-start | bytes 786440 | tf_op jit(solution)/shard_map/ppermute | solution.py:127
  158.2 8.1 %collective-permute-start.37 = (bf16[128,1024]{1,0:T(8,128)(2,1)S(1)}, bf16[128,1024]{1,0:T(8,128)(2,1)S(1)}, u32[]{:S(2)}, u32[]{:S(2)}) collective-permute-start(bf16[128,1024]{1,0:T(8,128)(2,1)S(1)} %copy-done.69), channel_id=1, source_target_pairs={{0,2},{1,3},{2,0},{3,1},{4,6},{5,7},{6,4},{7,5},{8,10},{9,11},{10,... | collective-permute-start | bytes 786440 | tf_op jit(solution)/shard_map/ppermute | solution.py:127
  159.8 7.9 %collective-permute-start.38 = (bf16[128,1024]{1,0:T(8,128)(2,1)S(1)}, bf16[128,1024]{1,0:T(8,128)(2,1)S(1)}, u32[]{:S(2)}, u32[]{:S(2)}) collective-permute-start(bf16[128,1024]{1,0:T(8,128)(2,1)S(1)} %copy-done.67), channel_id=1, source_target_pairs={{0,4},{1,5},{2,6},{3,7},{4,0},{5,1},{6,2},{7,3},{8,12},{9,13},{10,... | collective-permute-start | bytes 786440 | tf_op jit(solution)/shard_map/ppermute | solution.py:127
  167.6 13.0 %collective-permute-start.39 = (bf16[128,1024]{1,0:T(8,128)(2,1)}, bf16[128,1024]{1,0:T(8,128)(2,1)S(1)}, u32[]{:S(2)}, u32[]{:S(2)}) collective-permute-start(bf16[128,1024]{1,0:T(8,128)(2,1)} %get-tuple-element.623.refs_1_), channel_id=1, source_target_pairs={{0,2},{1,3},{2,0},{3,1},{4,6},{5,7},{6,4},{7,5},{8,10},{9,11},{10,... | collective-permute-start | bytes 786440 | tf_op jit(solution)/shard_map/ppermute | solution.py:127
  168.0 12.6 %collective-permute-start.40 = (bf16[128,1024]{1,0:T(8,128)(2,1)}, bf16[128,1024]{1,0:T(8,128)(2,1)S(1)}, u32[]{:S(2)}, u32[]{:S(2)}) collective-permute-start(bf16[128,1024]{1,0:T(8,128)(2,1)} %get-tuple-element.623.refs_1_), channel_id=1, source_target_pairs={{0,4},{1,5},{2,6},{3,7},{4,0},{5,1},{6,2},{7,3},{8,12},{9,13},{10,... | collective-permute-start | bytes 786440 | tf_op jit(solution)/shard_map/ppermute | solution.py:127
  169.7 11.0 %collective-permute-start.41 = (bf16[128,1024]{1,0:T(8,128)(2,1)}, bf16[128,1024]{1,0:T(8,128)(2,1)S(1)}, u32[]{:S(2)}, u32[]{:S(2)}) collective-permute-start(bf16[128,1024]{1,0:T(8,128)(2,1)} %get-tuple-element.623.refs_1_), channel_id=1, source_target_pairs={{0,1},{1,0},{2,3},{3,2},{4,5},{5,4},{6,7},{7,6},{8,9},{9,8},{10,11... | collective-permute-start | bytes 786440 | tf_op jit(solution)/shard_map/ppermute | solution.py:127
  184.4 8.4 %collective-permute-start.42 = (bf16[128,1024]{1,0:T(8,128)(2,1)S(1)}, bf16[128,1024]{1,0:T(8,128)(2,1)S(1)}, u32[]{:S(2)}, u32[]{:S(2)}) collective-permute-start(bf16[128,1024]{1,0:T(8,128)(2,1)S(1)} %copy-done.64), channel_id=1, source_target_pairs={{0,6},{1,7},{2,4},{3,5},{4,2},{5,3},{6,0},{7,1},{8,14},{9,15},{10,... | collective-permute-start | bytes 786440 | tf_op jit(solution)/shard_map/ppermute | solution.py:127
  184.8 9.7 %collective-permute-start.43 = (bf16[128,1024]{1,0:T(8,128)(2,1)S(1)}, bf16[128,1024]{1,0:T(8,128)(2,1)S(1)}, u32[]{:S(2)}, u32[]{:S(2)}) collective-permute-start(bf16[128,1024]{1,0:T(8,128)(2,1)S(1)} %broadcast_select_fusion.1), channel_id=1, source_target_pairs={{0,2},{1,5},{2,0},{3,7},{4,6},{5,1},{6,4},{7,3},{8,10},{9,13},{10,... | collective-permute-start | bytes 786440 | tf_op jit(solution)/shard_map/ppermute | solution.py:127
  186.3 8.2 %collective-permute-start.44 = (bf16[128,1024]{1,0:T(8,128)(2,1)S(1)}, bf16[128,1024]{1,0:T(8,128)(2,1)S(1)}, u32[]{:S(2)}, u32[]{:S(2)}) collective-permute-start(bf16[128,1024]{1,0:T(8,128)(2,1)S(1)} %collective-permute-done.39.refs_3_), channel_id=1, source_target_pairs={{0,1},{1,0},{2,3},{3,2},{4,5},{5,4},{6,7},{7,6},{8,9},{9,8},{10,11... | collective-permute-start | bytes 786440 | tf_op jit(solution)/shard_map/ppermute | solution.py:127
  186.3 8.2 %collective-permute-start.45 = (bf16[128,1024]{1,0:T(8,128)(2,1)S(1)}, bf16[128,1024]{1,0:T(8,128)(2,1)S(1)}, u32[]{:S(2)}, u32[]{:S(2)}) collective-permute-start(bf16[128,1024]{1,0:T(8,128)(2,1)S(1)} %collective-permute-done.40.refs_5_), channel_id=1, source_target_pairs={{0,1},{1,0},{2,3},{3,2},{4,5},{5,4},{6,7},{7,6},{8,9},{9,8},{10,11... | collective-permute-start | bytes 786440 | tf_op jit(solution)/shard_map/ppermute | solution.py:127
  186.8 6.0 %collective-permute-start.46 = (f32[8,128]{1,0:T(8,128)}, f32[8,128]{1,0:T(8,128)S(1)}, u32[]{:S(2)}, u32[]{:S(2)}) collective-permute-start(f32[8,128]{1,0:T(8,128)} %get-tuple-element.592), channel_id=1, source_target_pairs={{8,0},{9,1},{10,2},{11,3},{12,4},{13,5},{14,6},{15,7},{16,8},{17,9... | collective-permute-start | bytes 12296 | tf_op jit(solution)/shard_map/ppermute | solution.py:127
  194.5 7.1 %collective-permute-start.47 = (bf16[128,1024]{1,0:T(8,128)(2,1)S(1)}, bf16[128,1024]{1,0:T(8,128)(2,1)S(1)}, u32[]{:S(2)}, u32[]{:S(2)}) collective-permute-start(bf16[128,1024]{1,0:T(8,128)(2,1)S(1)} %collective-permute-done.43.refs_7_), channel_id=1, source_target_pairs={{0,1},{1,0},{2,3},{3,2},{4,5},{5,4},{6,7},{7,6},{8,9},{9,8},{10,11... | collective-permute-start | bytes 786440 | tf_op jit(solution)/shard_map/ppermute | solution.py:127
  201.7 14.2 %collective-permute-start.49 = (bf16[512,1024]{1,0:T(8,128)(2,1)}, bf16[512,1024]{1,0:T(8,128)(2,1)S(1)}, u32[]{:S(2)}, u32[]{:S(2)}) collective-permute-start(bf16[512,1024]{1,0:T(8,128)(2,1)} %get-tuple-element.621), channel_id=1, source_target_pairs={{0,1},{1,0},{2,3},{3,2},{4,5},{5,4},{6,7},{7,6},{8,9},{9,8},{10,11... | collective-permute-start | bytes 3145736 | tf_op jit(solution)/shard_map/ppermute | solution.py:127
  201.9 13.9 %all-to-all-start.3 = ((bf16[8,32,1152]{2,1,0:T(8,128)(2,1)}), bf16[8,32,1152]{2,1,0:T(8,128)(2,1)S(1)}, u32[]{:S(2)}, u32[]{:S(2)}) async-start(bf16[8,32,1152]{2,1,0:T(8,128)(2,1)} %bitcast.44), calls=%async_computation.4 | async-start | bytes 1179648 | tf_op jit(solution)/shard_map/all_to_all | solution.py:180
  205.5 9.2 %collective-permute-start.48 = (bf16[256,384]{1,0:T(8,128)(2,1)}, bf16[256,384]{1,0:T(8,128)(2,1)S(1)}, u32[]{:S(2)}, u32[]{:S(2)}) collective-permute-start(bf16[256,384]{1,0:T(8,128)(2,1)} %get-tuple-element.619), channel_id=1, source_target_pairs={{0,8},{1,9},{2,10},{3,11},{4,12},{5,13},{6,14},{7,15},{8,16},{9,17... | collective-permute-start | bytes 589832 | tf_op jit(solution)/shard_map/ppermute | solution.py:127
  216.6 7.3 %collective-permute-start.51 = (bf16[48,1024]{1,0:T(8,128)(2,1)}, bf16[48,1024]{1,0:T(8,128)(2,1)}, u32[]{:S(2)}, u32[]{:S(2)}) collective-permute-start(bf16[48,1024]{1,0:T(8,128)(2,1)} %get-tuple-element.651), channel_id=1, source_target_pairs={{0,8},{1,9},{2,10},{3,11},{4,12},{5,13},{6,14},{7,15},{8,16},{9,17... | collective-permute-start | bytes 294920 | tf_op jit(solution)/shard_map/ppermute | solution.py:127
  216.6 9.4 %collective-permute-start.50 = (bf16[256,384]{1,0:T(8,128)(2,1)}, bf16[256,384]{1,0:T(8,128)(2,1)}, u32[]{:S(2)}, u32[]{:S(2)}) collective-permute-start(bf16[256,384]{1,0:T(8,128)(2,1)} %add_convert_fusion.3), channel_id=1, source_target_pairs={{0,8},{1,9},{2,10},{3,11},{4,12},{5,13},{6,14},{7,15},{8,16},{9,17... | collective-permute-start | bytes 589832 | tf_op jit(solution)/shard_map/ppermute | solution.py:127
  228.0 6.5 %collective-permute-start.56 = (bf16[48,1024]{1,0:T(8,128)(2,1)S(1)}, bf16[48,1024]{1,0:T(8,128)(2,1)S(1)}, u32[]{:S(2)}, u32[]{:S(2)}) collective-permute-start(bf16[48,1024]{1,0:T(8,128)(2,1)S(1)} %add_convert_fusion.5), channel_id=1, source_target_pairs={{0,8},{1,9},{2,10},{3,11},{4,12},{5,13},{6,14},{7,15},{8,16},{9,17... | collective-permute-start | bytes 294920 | tf_op jit(solution)/shard_map/ppermute | solution.py:127
  228.1 8.5 %collective-permute-start.55 = (bf16[256,384]{1,0:T(8,128)(2,1)S(1)}, bf16[256,384]{1,0:T(8,128)(2,1)S(1)}, u32[]{:S(2)}, u32[]{:S(2)}) collective-permute-start(bf16[256,384]{1,0:T(8,128)(2,1)S(1)} %add_convert_fusion.2), channel_id=1, source_target_pairs={{0,8},{1,9},{2,10},{3,11},{4,12},{5,13},{6,14},{7,15},{8,16},{9,17... | collective-permute-start | bytes 589832 | tf_op jit(solution)/shard_map/ppermute | solution.py:127
  230.0 16.7 %collective-permute-start.52 = (bf16[128,1024]{1,0:T(8,128)(2,1)}, bf16[128,1024]{1,0:T(8,128)(2,1)S(1)}, u32[]{:S(2)}, u32[]{:S(2)}) collective-permute-start(bf16[128,1024]{1,0:T(8,128)(2,1)} %get-tuple-element.658), channel_id=1, source_target_pairs={{0,6},{1,7},{2,4},{3,5},{4,2},{5,3},{6,0},{7,1},{8,14},{9,15},{10,... | collective-permute-start | bytes 786440 | tf_op jit(solution)/shard_map/ppermute | solution.py:127
  232.4 14.3 %collective-permute-start.53 = (bf16[128,1024]{1,0:T(8,128)(2,1)}, bf16[128,1024]{1,0:T(8,128)(2,1)S(1)}, u32[]{:S(2)}, u32[]{:S(2)}) collective-permute-start(bf16[128,1024]{1,0:T(8,128)(2,1)} %get-tuple-element.659), channel_id=1, source_target_pairs={{0,2},{1,3},{2,0},{3,1},{4,6},{5,7},{6,4},{7,5},{8,10},{9,11},{10,... | collective-permute-start | bytes 786440 | tf_op jit(solution)/shard_map/ppermute | solution.py:127
  232.9 13.7 %collective-permute-start.54 = (bf16[128,1024]{1,0:T(8,128)(2,1)}, bf16[128,1024]{1,0:T(8,128)(2,1)S(1)}, u32[]{:S(2)}, u32[]{:S(2)}) collective-permute-start(bf16[128,1024]{1,0:T(8,128)(2,1)} %get-tuple-element.660), channel_id=1, source_target_pairs={{0,4},{1,5},{2,6},{3,7},{4,0},{5,1},{6,2},{7,3},{8,12},{9,13},{10,... | collective-permute-start | bytes 786440 | tf_op jit(solution)/shard_map/ppermute | solution.py:127
  237.3 12.1 %all-to-all-start.4 = ((bf16[8,32,384]{2,1,0:T(8,128)(2,1)}), bf16[8,32,384]{2,1,0:T(8,128)(2,1)S(1)}, u32[]{:S(2)}, u32[]{:S(2)}) async-start(bf16[8,32,384]{2,1,0:T(8,128)(2,1)} %bitcast.13), calls=%async_computation.6 | async-start | bytes 393216 | tf_op jit(solution)/shard_map/all_to_all | solution.py:180
  242.4 7.0 %collective-permute-start.57 = (bf16[48,1024]{1,0:T(8,128)(2,1)S(1)}, bf16[48,1024]{1,0:T(8,128)(2,1)S(1)}, u32[]{:S(2)}, u32[]{:S(2)}) collective-permute-start(bf16[48,1024]{1,0:T(8,128)(2,1)S(1)} %add_convert_fusion.4), channel_id=1, source_target_pairs={{0,8},{1,9},{2,10},{3,11},{4,12},{5,13},{6,14},{7,15},{8,16},{9,17... | collective-permute-start | bytes 294920 | tf_op jit(solution)/shard_map/ppermute | solution.py:127
  (73 other events, 866.0 us)
Sparse Core Ops, SparseCore 0:
  9.6 38.1 all-gather.5
  62.7 49.6 all-gather.3
  128.4 46.5 reduce-scatter.2
  177.1 28.7 reduce-scatter.4

commit v3 on v2

--- a/solution.py
+++ b/solution.py
@@ -170,8 +170,8 @@
         (parts,) = yield [(operands, ("call", call))]
         sends = [(part, ("swap", mask), span) for part, mask in zip(parts[1:], (6, 2, 4))]
         if split:
-            sides = yield sends[1:]
-            return [parts[0]] + (yield sends[:1]) + sides
+            corner = yield sends[:1]
+            return [parts[0]] + corner + (yield sends[1:])
         moved = yield sends
         return [parts[0]] + moved
 
@@ -499,14 +499,19 @@
         for m in range(TEAM):
             to = mixer.at[:, at((place ^ m) * channels, channels, 128)]
             copies.append((mixer_in[m], to))
-            copies.append((hidden_in[m], hidden.at[m]))
-        for copy in fetch(copies, sems):
+        first = len(copies)
+        copies += [(hidden_in[m], hidden.at[m]) for m in range(TEAM)]
+        copies = fetch(copies, sems)
+        for copy in copies[:first]:
             copy.wait()
         for half, side in ((1, odd), (0, even)):
             for k in range(TEAM // 2):
                 source = mixer[at((place ^ (2 * k + half)) * rows, rows), :]
                 turned[k * rows : (k + 1) * rows, :] = source
             product = dot(turned[...], out[...], ((1,), (0,)))
+            if half == 1:
+                for copy in copies[first:]:
+                    copy.wait()
             for k in range(TEAM // 2):
                 span = slice(k * rows, (k + 1) * rows)
                 total = hidden[2 * k + half].astype(WIDE) + product[span]
@@ -550,8 +555,8 @@
 
     def kernel(odd_in, even_in, *refs):
         g_in, (pair_in, down_in), refs = refs[:count], refs[count : count + 2], refs[count + 2 :]
-        acts, grads, weight = refs[:2], refs[2:4], refs[4]
-        xs, gs, pair, down, last, all_grads, sems = refs[5:]
+        acts, grads, weight, back = refs[:2], refs[2:4], refs[4], refs[5]
+        xs, gs, pair, down, last, all_grads, sems = refs[6:]
         first = [(odd_in, xs.at[:half, :]), (pair_in, pair)]
         second = [(g_in[k], gs.at[k * rows : (k + 1) * rows, :]) for k in range(count)]
         second += [(down_in, down), (even_in, xs.at[half:, :])]
@@ -585,6 +590,7 @@
             act[:, units:] = value[:, :width].astype(NARROW)
             all_grads[span, 2 * units :] = jnp.where(lower, gate_grad, up_grad).astype(NARROW)
             grad_out[...] = all_grads[span, :]
+        back[...] = dot(all_grads[:half, :], pair[...], ((1,), (1,))).astype(NARROW)
         for start in range(0, features, 256):
             total = dot(xs[:, start : start + 256], all_grads[...], ((0,), (0,)))
             weight[start : start + 256, :] = total.astype(NARROW)
@@ -593,7 +599,7 @@
     return call(
         kernel,
         "ffn",
-        outs + (shape(NARROW, features, 2 * own),),
+        outs + (shape(NARROW, features, 2 * own), shape(NARROW, half, features)),
         (odd, even, *upstream, pair, down),
         [
             pltpu.VMEM((2 * half, features), NARROW),
@@ -876,9 +882,8 @@
         mix_job
     )
     mixer_job = net.spawn(net.blocks(mixer_in))
-    net.step(2)
+    mixer_blocks, out_blocks = net.until(mixer_job, out_job)
     upstream_job.held = False
-    mixer_blocks, out_blocks = net.until(mixer_job, out_job)
     project_job = net.do(
         lambda *x: out_project(
             x[:TEAM], x[TEAM : 2 * TEAM], x[2 * TEAM : 3 * TEAM], x[3 * TEAM], teams
@@ -892,11 +897,8 @@
         lambda *x: ffn_block(x[0], x[1], x[2 : 2 + TEAM], x[2 + TEAM], x[3 + TEAM]),
         in_odd, in_even, *upstream[1::2], *upstream[0::2], pair_own, down_own,
     )
-    act_odd, act_even, grads_odd, grads_even, pair_all = net.until(ffn_job)
+    act_odd, act_even, _, grads_even, pair_all, back_odd = net.until(ffn_job)
     pair_sum = reduce(pair_all)
-    back_odd = net.until(
-        net.do(lambda *x: product(*x, True, "ffn_back_odd"), grads_odd, pair_own)
-    )
     ffn_job = net.spawn(
         net.team_sum(
             back_odd,
@@ -926,6 +928,7 @@
     ffn_grad = net.until(ffn_job)
     down_sum = reduce(down_job.result)
 
+    output_job.held = True
     back_job = net.do(
         lambda *x: resid_back(x[:4], *x[4:7], x[7:], teams),
         *ffn_grad, resid, gain_two, cotangent, *out_blocks,
@@ -946,6 +949,7 @@
         return returned
 
     returned = net.until(net.spawn(rim_steps()))
+    output_job.held = True
     mixed_grad, normed_odd, shares = net.until(
         net.do(
             lambda *x: mixer_back(*x, teams),
@@ -970,6 +974,7 @@
         mixer_in, *net.until(rounded_job), taps_grad,
     )
     net.until(out_job)
+    output_job.held = False
     net.need(down_sum)
     out_job = net.spawn(net.line_sum(out_job.result))
     in_grad = net.until(in_job).astype(NARROW)

time: 262 us -> 257 us (0.981)
  Pallas kernels: 77.7 us -> 74.1 us
  local copies, waits for them, and re-layouts: 6.23 us -> 9.16 us
    pallas_call x17 -> x16, Pallas kernels: 77.7 us -> 74.1 us  [call(): pl.pallas_call(kernel, out_shape=out_shape, scratch_shapes=list(scratch),...]
    unnamed x143 -> x139, local copies, waits for them, and re-layouts: 4.11 us -> 7.03 us
  transfers between devices with their start and end apart: 66 -> 66, of which waited for: 18 -> 15; matrix products, arithmetic and copies ran while one was open for 3% -> 3% of each run, Pallas kernels for 25% -> 23%
where the time goes in v3:
time: 257 us; the launch traced here: 256 us
  Pallas kernels  74.1 us (29%)
  waiting for transfers between devices  57.4 us (22%)
  starting transfers between devices  56.8 us (22%)
  blocking collectives  35 us (14%)
  between operations  14.9 us (6%)
  local copies, waits for them, and re-layouts  9.16 us (4%)
  other arithmetic  8.82 us (3%)
    pallas_call x16, Pallas kernels, call(): pl.pallas_call(kernel, out_shape=out_shape, scratch_shapes=list(scratch),...  74.1 us
    ppermute x58, waiting for transfers between devices, one_step(): got.append(lax.ppermute(values[at], 'dp', self.pairs(move[1])))  47.7 us
    ppermute x58, starting transfers between devices, one_step(): got.append(lax.ppermute(values[at], 'dp', self.pairs(move[1])))  41.7 us
    all_gather x1, blocking collectives, gather(): lax.all_gather(value, 'dp', axis=0, tiled=True, axis_index_groups=line)  24 us
    all_to_all x4, starting transfers between devices, exchange(): lax.all_to_all(blocks, 'dp', 0, 0, axis_index_groups=groups, tiled=True)  14.9 us
    all_to_all x1, blocking collectives, exchange(): lax.all_to_all(blocks, 'dp', 0, 0, axis_index_groups=groups, tiled=True)  11 us
    all_to_all x4, waiting for transfers between devices, exchange(): lax.all_to_all(blocks, 'dp', 0, 0, axis_index_groups=groups, tiled=True)  8.9 us
    unnamed x139, local copies, waits for them, and re-layouts  7.03 us
  transfers between devices with their start and end apart: 66, of which 15 were waited for; matrix products, arithmetic and copies ran while one was open for 3% of the time, Pallas kernels for 23%

profile of v3, /device:TPU:0, one launch (start us, length us, event | category | flops | bytes accessed | tf_op | source)
XLA Modules:
  0.0 256.2 jit_solution(11404750307084926588)
XLA Ops:
  7.9 2.0 in_prepare.1
  9.9 2.9 %collective-permute-start = (bf16[128,1024]{1,0:T(8,128)(2,1)}, bf16[128,1024]{1,0:T(8,128)(2,1)S(1)}, u32[]{:S(2)}, u32[]{:S(2)}) collective-permute-start(bf16[128,1024]{1,0:T(8,128)(2,1)} %refs_16_), channel_id=1, source_target_pairs={{0,2},{1,3},{2,0},{3,1},{4,6},{5,7},{6,4},{7,5},{8,10},{9,11},{10,... | collective-permute-start | bytes 786440 | tf_op jit(solution)/shard_map/ppermute | solution.py:127
  12.8 1.5 collective-permute-start.1
  14.4 4.3 %all-to-all-start = ((bf16[8,40,384]{2,1,0:T(8,128)(2,1)}), bf16[8,40,384]{2,1,0:T(8,128)(2,1)S(1)}, u32[]{:S(2)}, u32[]{:S(2)}) async-start(bf16[8,40,384]{2,1,0:T(8,128)(2,1)} %in_prepare.1), calls=%async_computation | async-start | bytes 491520 | tf_op jit(solution)/shard_map/all_to_all | solution.py:180
  18.7 2.3 pair_prepare.1
  21.0 8.1 %all-to-all-done = bf16[8,40,384]{2,1,0:T(8,128)(2,1)S(1)} async-done(((bf16[8,40,384]{2,1,0:T(8,128)(2,1)}), bf16[8,40,384]{2,1,0:T(8,128)(2,1)S(1)}, u32[]{:S(2)}, u32[]{:S(2)}) %all-to-all-start) | async-done | bytes 245792 | tf_op jit(solution)/shard_map/all_to_all | solution.py:180
  29.1 3.7 %all-to-all-start.1 = ((bf16[8,32,1152]{2,1,0:T(8,128)(2,1)}), bf16[8,32,1152]{2,1,0:T(8,128)(2,1)S(1)}, u32[]{:S(2)}, u32[]{:S(2)}) async-start(bf16[8,32,1152]{2,1,0:T(8,128)(2,1)} %pair_prepare.1), calls=%async_computation.1 | async-start | bytes 1179648 | tf_op jit(solution)/shard_map/all_to_all | solution.py:180
  33.8 1.6 collective-permute-start.7
  35.3 2.2 collective-permute-start.8
  37.6 24.0 %all_gather.9 = bf16[1280,384]{1,0:T(8,128)(2,1)} all-gather(bf16[320,384]{1,0:T(8,128)(2,1)S(1)} %bitcast.41), channel_id=1, replica_groups={{0,8,16,24},{1,9,17,25},{2,10,18,26},{3,11,19,27},{4,12,20,28},{5,13,21..., dimensions={0}, use_global_device_ids=true | all-gather | bytes 1228800 | tf_op jit(solution)/shard_map/all_gather | solution.py:836
  61.7 0.9 copy-done.1
  63.5 1.5 collective-permute-start.10
  65.0 1.5 collective-permute-start.11
  66.5 1.6 collective-permute-start.13
  68.1 5.5 %collective-permute-done.13.refs_8_ = bf16[16,1024]{1,0:T(8,128)(2,1)S(1)} collective-permute-done((bf16[16,1024]{1,0:T(8,128)(2,1)S(1)}, bf16[16,1024]{1,0:T(8,128)(2,1)S(1)}, u32[]{:S(2)}, u32[]{:S(2)}) %collective-permute-start.13) | collective-permute-done | bytes 32800 | tf_op jit(solution)/shard_map/ppermute | solution.py:127
  74.9 7.1 %mixer_forward.1 = (bf16[1040,1024]{1,0:T(8,128)(2,1)}, f32[1040,384]{1,0:T(8,128)}, f32[1040,128]{1,0:T(8,128)}, f32[1024,128]{1,0:T(8,128)}, bf16[1024,128]{1,...) custom-call(bf16[128,1024]{1,0:T(8,128)(2,1)} %refs_16_, ...), custom_call_target="tpu_custom_call" | custom-call | flops 805306368 | bytes 3112960 | tf_op jit(solution)/shard_map/mixer_forward/pallas_call | solution.py:36
  82.1 1.6 collective-permute-start.17
  84.1 1.2 collective-permute-start.20
  86.2 3.6 %collective-permute-done.17.refs_14_.refs_6_ = bf16[128,1024]{1,0:T(8,128)(2,1)S(1)} collective-permute-done((bf16[128,1024]{1,0:T(8,128)(2,1)S(1)}, bf16[128,1024]{1,0:T(8,128)(2,1)S(1)}, u32[]{:S(2)}, u32[]{:S(2)}) %collective-permute-start.17) | collective-permute-done | bytes 262176 | tf_op jit(solution)/shard_map/ppermute | solution.py:127
  89.8 4.3 %collective-permute-done.20.refs_2_ = bf16[1024,128]{1,0:T(8,128)(2,1)S(1)} collective-permute-done((bf16[1024,128]{1,0:T(8,128)(2,1)}, bf16[1024,128]{1,0:T(8,128)(2,1)S(1)}, u32[]{:S(2)}, u32[]{:S(2)}) %collective-permute-start.20) | collective-permute-done | bytes 262176 | tf_op jit(solution)/shard_map/ppermute | solution.py:127
  94.2 1.6 collective-permute-start.24
  96.3 4.3 %collective-permute-done.24.refs_6_ = bf16[1024,128]{1,0:T(8,128)(2,1)S(1)} collective-permute-done((bf16[1024,128]{1,0:T(8,128)(2,1)S(1)}, bf16[1024,128]{1,0:T(8,128)(2,1)S(1)}, u32[]{:S(2)}, u32[]{:S(2)}) %collective-permute-start.24) | collective-permute-done | bytes 262176 | tf_op jit(solution)/shard_map/ppermute | solution.py:127
  103.7 1.5 collective-permute-start.28
  105.7 7.5 %out_project.1 = (f32[128,1024]{1,0:T(8,128)}, bf16[512,1024]{1,0:T(8,128)(2,1)}, bf16[512,1024]{1,0:T(8,128)(2,1)}) custom-call(bf16[1024,128]{1,0:T(8,128)(2,1)} %get-tuple-element.619.refs_0_, bf16[1024,128]{1,0:T(8,128)(2,1)} %collective-permute-done.22.refs_1_, bf16[1024,128]{1,0:T(8,128)(2,1)} %copy-done.48, bf16[1024,128]{1,0:T(8,128)(2,1)} %copy-done.66, ...), custom_call_target="tpu_custom_call" | custom-call | flops 2147483648 | bytes 6295552 | tf_op jit(solution)/shard_map/out_project/pallas_call | solution.py:36
  113.5 1.4 collective-permute-done.31.refs_3_.refs_5_
  115.7 13.2 %ffn.1 = (bf16[512,576]{1,0:T(8,128)(2,1)}, bf16[512,576]{1,0:T(8,128)(2,1)}, bf16[512,1152]{1,0:T(8,128)(2,1)}, bf16[512,1152]{1,0:T(8,128)(2,1)}, bf16[1024,11...) custom-call(bf16[512,1024]{1,0:T(8,128)(2,1)} %get-tuple-element.482.odd_in, bf16[512,1024]{1,0:T(8,128)(2,1)} %get-tuple-element.483.even_in, ...), custom_call_target="tpu_custom_call" | custom-call | flops 6039797760 | bytes 7733248 | tf_op jit(solution)/shard_map/ffn/pallas_call | solution.py:36
  128.9 1.1 copy-done.63
  130.2 3.4 %ffn_output.1 = bf16[512,1024]{1,0:T(8,128)(2,1)} custom-call(bf16[512,576]{1,0:T(8,128)(2,1)} %get-tuple-element.532.left.refs_0_, bf16[576,1024]{1,0:T(8,128)(2,1)} %bitcast.31), custom_call_target="tpu_custom_call" | custom-call | flops 603979776 | bytes 1769472 | tf_op jit(solution)/shard_map/ffn_output/pallas_call | solution.py:36
  134.6 4.8 %ffn_back.1 = (f32[128,1024]{1,0:T(8,128)}, bf16[128,1024]{1,0:T(8,128)(2,1)}, bf16[128,1024]{1,0:T(8,128)(2,1)}, bf16[128,1024]{1,0:T(8,128)(2,1)}) custom-call(bf16[512,1152]{1,0:T(8,128)(2,1)} %get-tuple-element.509.left_in, bf16[1024,1152]{1,0:T(8,128)(2,1)} %all-gather.4.cloned.1.call-done.refs_8_.right_in, bf16[512,1024]{1,0:T(8,128)(2,1)} %copy-done.15), custom_call_target="tpu_custom_call" | custom-call | flops 1207959552 | bytes 4587520 | tf_op jit(solution)/shard_map/ffn_back/pallas_call | solution.py:36
  139.4 1.7 collective-permute-start.34
  141.1 1.3 collective-permute-start.35
  143.0 3.7 %ffn_output_sum.1 = (f32[128,1024]{1,0:T(8,128)}, bf16[128,1024]{1,0:T(8,128)(2,1)}, bf16[128,1024]{1,0:T(8,128)(2,1)}, bf16[128,1024]{1,0:T(8,128)(2,1)}) custom-call(bf16[512,576]{1,0:T(8,128)(2,1)} %get-tuple-element.533.left_in.refs_1_, bf16[576,1024]{1,0:T(8,128)(2,1)} %bitcast.32, bf16[512,1024]{1,0:T(8,128)(2,1)} %copy-done.14), custom_call_target="tpu_custom_call" | custom-call | flops 603979776 | bytes 2818048 | tf_op jit(solution)/shard_map/ffn_output_sum/pallas_call | solution.py:36
  146.7 4.6 %down_grads.1 = bf16[576,1024]{1,0:T(8,128)(2,1)} custom-call(bf16[512,576]{1,0:T(8,128)(2,1)} %get-tuple-element.532.left.refs_0_, bf16[512,576]{1,0:T(8,128)(2,1)} %get-tuple-element.533.left_in.refs_1_, bf16[128,1024]{1,0:T(8,128)(2,1)} %copy-done.30, bf16[128,1024]{1,0:T(8,128)(2,1)} %copy-done.37, bf16[128,1024]{1,0:T(8,128)(2,1)} %copy-done.38, ...), custom_call_target="tpu_custom_call" | custom-call | flops 1207959552 | bytes 3276800 | tf_op jit(solution)/shard_map/down_grads/pallas_call | solution.py:36
  151.4 3.5 %collective-permute-done.35.across = bf16[128,1024]{1,0:T(8,128)(2,1)S(1)} collective-permute-done((bf16[128,1024]{1,0:T(8,128)(2,1)}, bf16[128,1024]{1,0:T(8,128)(2,1)S(1)}, u32[]{:S(2)}, u32[]{:S(2)}) %collective-permute-start.35) | collective-permute-done | bytes 262176 | tf_op jit(solution)/shard_map/ppermute | solution.py:127
  155.7 4.9 %resid_back.1 = (f32[128,1024]{1,0:T(8,128)}, bf16[128,1024]{1,0:T(8,128)(2,1)}, bf16[8,128,128]{2,1,0:T(8,128)(2,1)}) custom-call(f32[128,1024]{1,0:T(8,128)} %get-tuple-element.550.own, bf16[128,1024]{1,0:T(8,128)(2,1)} %copy-done.44, bf16[128,1024]{1,0:T(8,128)(2,1)} %copy-done.45, bf16[128,1024]{1,0:T(8,128)(2,1)} %copy-done.46, ...), custom_call_target="tpu_custom_call" | custom-call | flops 268435456 | bytes 4198400 | tf_op jit(solution)/shard_map/resid_back/pallas_call | solution.py:36
  160.6 0.9 collective-permute-start.37
  161.5 1.2 collective-permute-start.38
  162.7 11.0 %all_to_all.25 = bf16[8,128,128]{2,1,0:T(8,128)(2,1)} all-to-all(bf16[8,128,128]{2,1,0:T(8,128)(2,1)} %get-tuple-element.571), channel_id=1, replica_groups={{0,1,2,3,4,5,6,7},{8,9,10,11,12,13,14,15},{16,17,18,19,20,21,22,23},{24..., dimensions={0} | all-to-all | bytes 524288 | tf_op jit(solution)/shard_map/all_to_all | solution.py:180
  173.7 3.4 %conv_back.1 = (f32[1024,128]{1,0:T(8,128)}, f32[8,128]{1,0:T(8,128)}, f32[8,128]{1,0:T(8,128)}) custom-call(bf16[1024,128]{1,0:T(8,128)(2,1)} %bitcast.35, f32[1040,384]{1,0:T(8,128)} %get-tuple-element.599.mixed.refs_3_, f32[1040,128]{1,0:T(8,128)} %get-tuple-element.578.gated, f32[1024,128]{1,0:T(8,128)} %get-tuple-element.600.conv.refs_4_, ...), custom_call_target="tpu_custom_call" | custom-call | bytes 2928704 | tf_op jit(solution)/shard_map/conv_back/pallas_call | solution.py:36
  177.2 1.0 collective-permute-start.40
  178.2 1.1 collective-permute-start.41
  179.8 1.3 collective-permute-start.44
  181.1 4.4 %collective-permute-done.44.refs_1_ = f32[8,128]{1,0:T(8,128)S(1)} collective-permute-done((f32[8,128]{1,0:T(8,128)}, f32[8,128]{1,0:T(8,128)S(1)}, u32[]{:S(2)}, u32[]{:S(2)}) %collective-permute-start.44) | collective-permute-done | bytes 4128 | tf_op jit(solution)/shard_map/ppermute | solution.py:127
  185.7 1.8 collective-permute-done.41.refs_7_
  187.5 1.2 collective-permute-start.45
  188.7 5.9 %mixer_back.1 = (bf16[1024,384]{1,0:T(8,128)(2,1)}, bf16[512,1024]{1,0:T(8,128)(2,1)}, f32[256,384]{1,0:T(8,128)}, f32[256,384]{1,0:T(8,128)}, f32[256,384]{1,0:T(8,128)}, /*index=5*/bf16[256,384]{1,0:T(8,128)(2,1)}) custom-call(f32[1024,128]{1,0:T(8,128)} %get-tuple-element.596.refs_0_, f32[8,128]{1,0:T(8,128)} %copy-done.60, bf16[1024,128]{1,0:T(8,128)(2,1)} %bitcast.36, ...), custom_call_target="tpu_custom_call" | custom-call | flops 1207959552 | bytes 5828608 | tf_op jit(solution)/shard_map/mixer_back/pallas_call | solution.py:36
  195.0 3.5 %all-to-all-start.3 = ((bf16[8,32,1152]{2,1,0:T(8,128)(2,1)}), bf16[8,32,1152]{2,1,0:T(8,128)(2,1)S(1)}, u32[]{:S(2)}, u32[]{:S(2)}) async-start(bf16[8,32,1152]{2,1,0:T(8,128)(2,1)} %bitcast.44), calls=%async_computation.4 | async-start | bytes 1179648 | tf_op jit(solution)/shard_map/all_to_all | solution.py:180
  198.8 3.2 %out_back.1 = (f32[48,1024]{1,0:T(8,128)}, f32[48,1024]{1,0:T(8,128)}, f32[48,1024]{1,0:T(8,128)}, bf16[48,1024]{1,0:T(8,128)(2,1)}) custom-call(bf16[1024,128]{1,0:T(8,128)(2,1)} %get-tuple-element.619.refs_0_, bf16[128,1024]{1,0:T(8,128)(2,1)} %get-tuple-element.620.refs_1_, bf16[128,1024]{1,0:T(8,128)(2,1)} %copy-done.39, bf16[128,1024]{1,0:T(8,128)(2,1)} %copy-done.12, ...), custom_call_target="tpu_custom_call" | custom-call | flops 268435456 | bytes 2363392 | tf_op jit(solution)/shard_map/out_back/pallas_call | solution.py:36
  202.0 7.2 %collective-permute-done.46 = bf16[256,384]{1,0:T(8,128)(2,1)S(1)} collective-permute-done((bf16[256,384]{1,0:T(8,128)(2,1)}, bf16[256,384]{1,0:T(8,128)(2,1)S(1)}, u32[]{:S(2)}, u32[]{:S(2)}) %collective-permute-start.46) | collective-permute-done | bytes 196640 | tf_op jit(solution)/shard_map/ppermute | solution.py:127
  209.3 1.5 collective-permute-start.48
  210.8 1.5 collective-permute-start.49
  213.2 3.3 %mixer_back_sum.1 = (f32[128,1024]{1,0:T(8,128)}, bf16[128,1024]{1,0:T(8,128)(2,1)}, bf16[128,1024]{1,0:T(8,128)(2,1)}, bf16[128,1024]{1,0:T(8,128)(2,1)}) custom-call(bf16[1024,384]{1,0:T(8,128)(2,1)} %get-tuple-element.643.left_in, bf16[1024,384]{1,0:T(8,128)(2,1)} %get-tuple-element.644.refs_6_.right_in, bf16[512,1024]{1,0:T(8,128)(2,1)} %copy-done.7), custom_call_target="tpu_custom_call" | custom-call | flops 402653184 | bytes 2621440 | tf_op jit(solution)/shard_map/mixer_back_sum/pallas_call | solution.py:36
  216.6 5.8 %collective-permute-done.51 = bf16[48,1024]{1,0:T(8,128)(2,1)S(1)} collective-permute-done((bf16[48,1024]{1,0:T(8,128)(2,1)}, bf16[48,1024]{1,0:T(8,128)(2,1)S(1)}, u32[]{:S(2)}, u32[]{:S(2)}) %collective-permute-start.51) | collective-permute-done | bytes 98336 | tf_op jit(solution)/shard_map/ppermute | solution.py:127
  223.2 1.1 add_convert_fusion.2
  224.4 0.9 bitcast_convert_fusion
  225.9 1.4 collective-permute-start.53
  227.3 1.5 collective-permute-start.54
  228.8 4.7 %collective-permute-done.56 = bf16[48,1024]{1,0:T(8,128)(2,1)S(1)} collective-permute-done((bf16[48,1024]{1,0:T(8,128)(2,1)S(1)}, bf16[48,1024]{1,0:T(8,128)(2,1)S(1)}, u32[]{:S(2)}, u32[]{:S(2)}) %collective-permute-start.56) | collective-permute-done | bytes 98336 | tf_op jit(solution)/shard_map/ppermute | solution.py:127
  234.3 3.4 %all-to-all-start.4 = ((bf16[8,32,384]{2,1,0:T(8,128)(2,1)}), bf16[8,32,384]{2,1,0:T(8,128)(2,1)S(1)}, u32[]{:S(2)}, u32[]{:S(2)}) async-start(bf16[8,32,384]{2,1,0:T(8,128)(2,1)} %bitcast.13), calls=%async_computation.6 | async-start | bytes 393216 | tf_op jit(solution)/shard_map/all_to_all | solution.py:180
  237.8 1.9 add_convert_fusion
  240.3 2.7 %pair_finish.1 = (f32[32,4608]{1,0:T(8,128)}, f32[32,4608]{1,0:T(8,128)}, f32[1,32]{1,0:T(1,128)}) custom-call(bf16[8,32,1152]{2,1,0:T(8,128)(2,1)} %copy-done.2, bf16[32,4608]{1,0:T(8,128)(2,1)} %bitcast.38, bf16[32,4608]{1,0:T(8,128)(2,1)} %bitcast.40, bf16[32,1]{1,0:T(8,128)(2,1)} %copy.21.gain), custom_call_target="tpu_custom_call" | custom-call | bytes 1179712 | tf_op jit(solution)/shard_map/pair_finish/pallas_call | solution.py:36
  243.9 1.1 convert_add_fusion
  246.6 1.1 fusion.5
  247.6 2.0 in_finish.1
  (252 shorter events, 20.2 us)
Async XLA Ops:
  7.2 107.8 %all-gather.6.cloned.1.call-start = ((), (), s32[]{:S(2)}) async-start(), calls=%async_computation.10 | async-start | bytes 1474560 | tf_op jit(solution)/shard_map/all_gather | solution.py:836
  9.9 19.2 %collective-permute-start = (bf16[128,1024]{1,0:T(8,128)(2,1)}, bf16[128,1024]{1,0:T(8,128)(2,1)S(1)}, u32[]{:S(2)}, u32[]{:S(2)}) collective-permute-start(bf16[128,1024]{1,0:T(8,128)(2,1)} %refs_16_), channel_id=1, source_target_pairs={{0,2},{1,3},{2,0},{3,1},{4,6},{5,7},{6,4},{7,5},{8,10},{9,11},{10,... | collective-permute-start | bytes 786440 | tf_op jit(solution)/shard_map/ppermute | solution.py:127
  12.8 16.2 %collective-permute-start.1 = (bf16[128,1024]{1,0:T(8,128)(2,1)}, bf16[128,1024]{1,0:T(8,128)(2,1)S(1)}, u32[]{:S(2)}, u32[]{:S(2)}) collective-permute-start(bf16[128,1024]{1,0:T(8,128)(2,1)} %refs_16_), channel_id=1, source_target_pairs={{0,4},{1,5},{2,6},{3,7},{4,0},{5,1},{6,2},{7,3},{8,12},{9,13},{10,... | collective-permute-start | bytes 786440 | tf_op jit(solution)/shard_map/ppermute | solution.py:127
  14.4 14.7 %collective-permute-start.2 = (bf16[128,1024]{1,0:T(8,128)(2,1)}, bf16[128,1024]{1,0:T(8,128)(2,1)S(1)}, u32[]{:S(2)}, u32[]{:S(2)}) collective-permute-start(bf16[128,1024]{1,0:T(8,128)(2,1)} %refs_16_), channel_id=1, source_target_pairs={{0,6},{1,7},{2,4},{3,5},{4,2},{5,3},{6,0},{7,1},{8,14},{9,15},{10,... | collective-permute-start | bytes 786440 | tf_op jit(solution)/shard_map/ppermute | solution.py:127
  14.4 14.7 %collective-permute-start.3 = (bf16[128,1024]{1,0:T(8,128)(2,1)}, bf16[128,1024]{1,0:T(8,128)(2,1)S(1)}, u32[]{:S(2)}, u32[]{:S(2)}) collective-permute-start(bf16[128,1024]{1,0:T(8,128)(2,1)} %refs_16_), channel_id=1, source_target_pairs={{0,1},{1,0},{2,3},{3,2},{4,5},{5,4},{6,7},{7,6},{8,9},{9,8},{10,11... | collective-permute-start | bytes 786440 | tf_op jit(solution)/shard_map/ppermute | solution.py:127
  14.4 14.7 %all-to-all-start = ((bf16[8,40,384]{2,1,0:T(8,128)(2,1)}), bf16[8,40,384]{2,1,0:T(8,128)(2,1)S(1)}, u32[]{:S(2)}, u32[]{:S(2)}) async-start(bf16[8,40,384]{2,1,0:T(8,128)(2,1)} %in_prepare.1), calls=%async_computation | async-start | bytes 491520 | tf_op jit(solution)/shard_map/all_to_all | solution.py:180
  29.1 32.6 %all-to-all-start.1 = ((bf16[8,32,1152]{2,1,0:T(8,128)(2,1)}), bf16[8,32,1152]{2,1,0:T(8,128)(2,1)S(1)}, u32[]{:S(2)}, u32[]{:S(2)}) async-start(bf16[8,32,1152]{2,1,0:T(8,128)(2,1)} %pair_prepare.1), calls=%async_computation.1 | async-start | bytes 1179648 | tf_op jit(solution)/shard_map/all_to_all | solution.py:180
  32.8 82.1 %all-gather.4.cloned.1.call-start = ((), (), s32[]{:S(2)}) async-start(), calls=%async_computation.7 | async-start | bytes 2949120 | tf_op jit(solution)/shard_map/all_gather | solution.py:836
  32.9 28.8 %collective-permute-start.4 = (bf16[128,1024]{1,0:T(8,128)(2,1)S(1)}, bf16[128,1024]{1,0:T(8,128)(2,1)S(1)}, u32[]{:S(2)}, u32[]{:S(2)}) collective-permute-start(bf16[128,1024]{1,0:T(8,128)(2,1)S(1)} %collective-permute-done.refs_2_.refs_18_), channel_id=1, source_target_pairs={{0,1},{1,0},{2,3},{3,2},{4,5},{5,4},{6,7},{7,6},{8,9},{9,8},{10,11... | collective-permute-start | bytes 786440 | tf_op jit(solution)/shard_map/ppermute | solution.py:127
  33.2 28.4 %collective-permute-start.5 = (bf16[128,1024]{1,0:T(8,128)(2,1)S(1)}, bf16[128,1024]{1,0:T(8,128)(2,1)S(1)}, u32[]{:S(2)}, u32[]{:S(2)}) collective-permute-start(bf16[128,1024]{1,0:T(8,128)(2,1)S(1)} %collective-permute-done.1.refs_4_.refs_20_), channel_id=1, source_target_pairs={{0,1},{1,0},{2,3},{3,2},{4,5},{5,4},{6,7},{7,6},{8,9},{9,8},{10,11... | collective-permute-start | bytes 786440 | tf_op jit(solution)/shard_map/ppermute | solution.py:127
  33.5 28.2 %collective-permute-start.6 = (bf16[128,1024]{1,0:T(8,128)(2,1)S(1)}, bf16[128,1024]{1,0:T(8,128)(2,1)S(1)}, u32[]{:S(2)}, u32[]{:S(2)}) collective-permute-start(bf16[128,1024]{1,0:T(8,128)(2,1)S(1)} %collective-permute-done.2.refs_6_.refs_22_), channel_id=1, source_target_pairs={{0,1},{1,0},{2,3},{3,2},{4,5},{5,4},{6,7},{7,6},{8,9},{9,8},{10,11... | collective-permute-start | bytes 786440 | tf_op jit(solution)/shard_map/ppermute | solution.py:127
  33.8 27.9 %collective-permute-start.7 = (bf16[32,1024]{1,0:T(8,128)(2,1)S(1)}, bf16[32,1024]{1,0:T(8,128)(2,1)S(1)}, u32[]{:S(2)}, u32[]{:S(2)}) collective-permute-start(bf16[32,1024]{1,0:T(8,128)(2,1)S(1)} %bitcast.45), channel_id=1, source_target_pairs={{0,8},{1,9},{2,10},{3,11},{4,12},{5,13},{6,14},{7,15},{8,16},{9,17... | collective-permute-start | bytes 196616 | tf_op jit(solution)/shard_map/ppermute | solution.py:127
  35.3 26.3 %collective-permute-start.8 = (bf16[32,1024]{1,0:T(8,128)(2,1)S(1)}, bf16[32,1024]{1,0:T(8,128)(2,1)S(1)}, u32[]{:S(2)}, u32[]{:S(2)}) collective-permute-start(bf16[32,1024]{1,0:T(8,128)(2,1)S(1)} %bitcast.46), channel_id=1, source_target_pairs={{0,24},{1,25},{2,26},{3,27},{4,28},{5,29},{6,30},{7,31},{8,0},{9,1... | collective-permute-start | bytes 196616 | tf_op jit(solution)/shard_map/ppermute | solution.py:127
  62.6 132.1 %reduce-scatter.3.cloned.1.call-start = ((), (), s32[]{:S(2)}) async-start(), calls=%async_computation.8 | async-start | bytes 2949120 | tf_op jit(solution)/shard_map/reduce_scatter | solution.py:839
  63.5 10.1 %collective-permute-start.10 = (bf16[128,1024]{1,0:T(8,128)(2,1)S(1)}, bf16[128,1024]{1,0:T(8,128)(2,1)S(1)}, u32[]{:S(2)}, u32[]{:S(2)}) collective-permute-start(bf16[128,1024]{1,0:T(8,128)(2,1)S(1)} %copy-done.5), channel_id=1, source_target_pairs={{0,2},{1,3},{2,0},{3,1},{4,6},{5,7},{6,4},{7,5},{8,10},{9,11},{10,... | collective-permute-start | bytes 786440 | tf_op jit(solution)/shard_map/ppermute | solution.py:127
  65.0 8.6 %collective-permute-start.11 = (bf16[128,1024]{1,0:T(8,128)(2,1)S(1)}, bf16[128,1024]{1,0:T(8,128)(2,1)S(1)}, u32[]{:S(2)}, u32[]{:S(2)}) collective-permute-start(bf16[128,1024]{1,0:T(8,128)(2,1)S(1)} %copy-done.5), channel_id=1, source_target_pairs={{0,4},{1,5},{2,6},{3,7},{4,0},{5,1},{6,2},{7,3},{8,12},{9,13},{10,... | collective-permute-start | bytes 786440 | tf_op jit(solution)/shard_map/ppermute | solution.py:127
  66.5 7.2 %collective-permute-start.12 = (bf16[128,1024]{1,0:T(8,128)(2,1)S(1)}, bf16[128,1024]{1,0:T(8,128)(2,1)S(1)}, u32[]{:S(2)}, u32[]{:S(2)}) collective-permute-start(bf16[128,1024]{1,0:T(8,128)(2,1)S(1)} %copy-done.5), channel_id=1, source_target_pairs={{0,1},{1,0},{2,3},{3,2},{4,5},{5,4},{6,7},{7,6},{8,9},{9,8},{10,11... | collective-permute-start | bytes 786440 | tf_op jit(solution)/shard_map/ppermute | solution.py:127
  66.5 7.1 %collective-permute-start.9 = (bf16[32,1024]{1,0:T(8,128)(2,1)S(1)}, bf16[32,1024]{1,0:T(8,128)(2,1)S(1)}, u32[]{:S(2)}, u32[]{:S(2)}) collective-permute-start(bf16[32,1024]{1,0:T(8,128)(2,1)S(1)} %collective-permute-done.7), channel_id=1, source_target_pairs={{0,8},{1,9},{2,10},{3,11},{4,12},{5,13},{6,14},{7,15},{8,16},{9,17... | collective-permute-start | bytes 196616 | tf_op jit(solution)/shard_map/ppermute | solution.py:127
  66.5 7.1 %collective-permute-start.13 = (bf16[16,1024]{1,0:T(8,128)(2,1)S(1)}, bf16[16,1024]{1,0:T(8,128)(2,1)S(1)}, u32[]{:S(2)}, u32[]{:S(2)}) collective-permute-start(bf16[16,1024]{1,0:T(8,128)(2,1)S(1)} %select_select_fusion), channel_id=1, source_target_pairs={{0,8},{1,9},{2,10},{3,11},{4,12},{5,13},{6,14},{7,15},{8,16},{9,17... | collective-permute-start | bytes 98312 | tf_op jit(solution)/shard_map/ppermute | solution.py:127
  73.7 8.2 %collective-permute-start.14 = (bf16[128,1024]{1,0:T(8,128)(2,1)S(1)}, bf16[128,1024]{1,0:T(8,128)(2,1)S(1)}, u32[]{:S(2)}, u32[]{:S(2)}) collective-permute-start(bf16[128,1024]{1,0:T(8,128)(2,1)S(1)} %pad_maximum_fusion.refs_8_.refs_0_), channel_id=1, source_target_pairs={{0,2},{1,3},{2,0},{3,1},{4,6},{5,7},{6,4},{7,5},{8,10},{9,11},{10,... | collective-permute-start | bytes 786440 | tf_op jit(solution)/shard_map/ppermute | solution.py:127
  74.3 7.7 %collective-permute-start.15 = (bf16[128,1024]{1,0:T(8,128)(2,1)S(1)}, bf16[128,1024]{1,0:T(8,128)(2,1)S(1)}, u32[]{:S(2)}, u32[]{:S(2)}) collective-permute-start(bf16[128,1024]{1,0:T(8,128)(2,1)S(1)} %pad_maximum_fusion.refs_8_.refs_0_), channel_id=1, source_target_pairs={{0,4},{1,5},{2,6},{3,7},{4,0},{5,1},{6,2},{7,3},{8,12},{9,13},{10,... | collective-permute-start | bytes 786440 | tf_op jit(solution)/shard_map/ppermute | solution.py:127
  74.8 7.2 %collective-permute-start.16 = (bf16[128,1024]{1,0:T(8,128)(2,1)S(1)}, bf16[128,1024]{1,0:T(8,128)(2,1)S(1)}, u32[]{:S(2)}, u32[]{:S(2)}) collective-permute-start(bf16[128,1024]{1,0:T(8,128)(2,1)S(1)} %pad_maximum_fusion.refs_8_.refs_0_), channel_id=1, source_target_pairs={{0,1},{1,0},{2,3},{3,2},{4,5},{5,4},{6,7},{7,6},{8,9},{9,8},{10,11... | collective-permute-start | bytes 786440 | tf_op jit(solution)/shard_map/ppermute | solution.py:127
  82.1 7.7 %collective-permute-start.17 = (bf16[128,1024]{1,0:T(8,128)(2,1)S(1)}, bf16[128,1024]{1,0:T(8,128)(2,1)S(1)}, u32[]{:S(2)}, u32[]{:S(2)}) collective-permute-start(bf16[128,1024]{1,0:T(8,128)(2,1)S(1)} %broadcast_select_fusion.2), channel_id=1, source_target_pairs={{0,2},{1,5},{2,0},{3,7},{4,6},{5,1},{6,4},{7,3},{8,10},{9,13},{10,... | collective-permute-start | bytes 786440 | tf_op jit(solution)/shard_map/ppermute | solution.py:127
  83.6 6.1 %collective-permute-start.18 = (bf16[128,1024]{1,0:T(8,128)(2,1)S(1)}, bf16[128,1024]{1,0:T(8,128)(2,1)S(1)}, u32[]{:S(2)}, u32[]{:S(2)}) collective-permute-start(bf16[128,1024]{1,0:T(8,128)(2,1)S(1)} %collective-permute-done.14.refs_10_.refs_2_), channel_id=1, source_target_pairs={{0,1},{1,0},{2,3},{3,2},{4,5},{5,4},{6,7},{7,6},{8,9},{9,8},{10,11... | collective-permute-start | bytes 786440 | tf_op jit(solution)/shard_map/ppermute | solution.py:127
  83.9 5.9 %collective-permute-start.19 = (bf16[128,1024]{1,0:T(8,128)(2,1)S(1)}, bf16[128,1024]{1,0:T(8,128)(2,1)S(1)}, u32[]{:S(2)}, u32[]{:S(2)}) collective-permute-start(bf16[128,1024]{1,0:T(8,128)(2,1)S(1)} %collective-permute-done.15.refs_12_.refs_4_), channel_id=1, source_target_pairs={{0,1},{1,0},{2,3},{3,2},{4,5},{5,4},{6,7},{7,6},{8,9},{9,8},{10,11... | collective-permute-start | bytes 786440 | tf_op jit(solution)/shard_map/ppermute | solution.py:127
  84.1 10.0 %collective-permute-start.20 = (bf16[1024,128]{1,0:T(8,128)(2,1)}, bf16[1024,128]{1,0:T(8,128)(2,1)S(1)}, u32[]{:S(2)}, u32[]{:S(2)}) collective-permute-start(bf16[1024,128]{1,0:T(8,128)(2,1)} %get-tuple-element.619.refs_0_), channel_id=1, source_target_pairs={{0,2},{1,3},{2,0},{3,1},{4,6},{5,7},{6,4},{7,5},{8,10},{9,11},{10,... | collective-permute-start | bytes 786440 | tf_op jit(solution)/shard_map/ppermute | solution.py:127
  85.4 8.8 %collective-permute-start.21 = (bf16[1024,128]{1,0:T(8,128)(2,1)}, bf16[1024,128]{1,0:T(8,128)(2,1)S(1)}, u32[]{:S(2)}, u32[]{:S(2)}) collective-permute-start(bf16[1024,128]{1,0:T(8,128)(2,1)} %get-tuple-element.619.refs_0_), channel_id=1, source_target_pairs={{0,4},{1,5},{2,6},{3,7},{4,0},{5,1},{6,2},{7,3},{8,12},{9,13},{10,... | collective-permute-start | bytes 786440 | tf_op jit(solution)/shard_map/ppermute | solution.py:127
  89.8 4.4 %collective-permute-start.22 = (bf16[1024,128]{1,0:T(8,128)(2,1)}, bf16[1024,128]{1,0:T(8,128)(2,1)}, u32[]{:S(2)}, u32[]{:S(2)}) collective-permute-start(bf16[1024,128]{1,0:T(8,128)(2,1)} %get-tuple-element.619.refs_0_), channel_id=1, source_target_pairs={{0,1},{1,0},{2,3},{3,2},{4,5},{5,4},{6,7},{7,6},{8,9},{9,8},{10,11... | collective-permute-start | bytes 786440 | tf_op jit(solution)/shard_map/ppermute | solution.py:127
  94.2 2.2 collective-permute-start.23
  94.2 6.4 %collective-permute-start.24 = (bf16[1024,128]{1,0:T(8,128)(2,1)S(1)}, bf16[1024,128]{1,0:T(8,128)(2,1)S(1)}, u32[]{:S(2)}, u32[]{:S(2)}) collective-permute-start(bf16[1024,128]{1,0:T(8,128)(2,1)S(1)} %broadcast_select_fusion), channel_id=1, source_target_pairs={{0,2},{1,5},{2,0},{3,7},{4,6},{5,1},{6,4},{7,3},{8,10},{9,13},{10,... | collective-permute-start | bytes 786440 | tf_op jit(solution)/shard_map/ppermute | solution.py:127
  95.8 4.9 %collective-permute-start.25 = (bf16[1024,128]{1,0:T(8,128)(2,1)S(1)}, bf16[1024,128]{1,0:T(8,128)(2,1)S(1)}, u32[]{:S(2)}, u32[]{:S(2)}) collective-permute-start(bf16[1024,128]{1,0:T(8,128)(2,1)S(1)} %collective-permute-done.20.refs_2_), channel_id=1, source_target_pairs={{0,1},{1,0},{2,3},{3,2},{4,5},{5,4},{6,7},{7,6},{8,9},{9,8},{10,11... | collective-permute-start | bytes 786440 | tf_op jit(solution)/shard_map/ppermute | solution.py:127
  96.0 4.7 %collective-permute-start.26 = (bf16[1024,128]{1,0:T(8,128)(2,1)S(1)}, bf16[1024,128]{1,0:T(8,128)(2,1)S(1)}, u32[]{:S(2)}, u32[]{:S(2)}) collective-permute-start(bf16[1024,128]{1,0:T(8,128)(2,1)S(1)} %collective-permute-done.21.refs_4_), channel_id=1, source_target_pairs={{0,1},{1,0},{2,3},{3,2},{4,5},{5,4},{6,7},{7,6},{8,9},{9,8},{10,11... | collective-permute-start | bytes 786440 | tf_op jit(solution)/shard_map/ppermute | solution.py:127
  103.7 9.6 %collective-permute-start.28 = (bf16[128,1024]{1,0:T(8,128)(2,1)}, bf16[128,1024]{1,0:T(8,128)(2,1)S(1)}, u32[]{:S(2)}, u32[]{:S(2)}) collective-permute-start(bf16[128,1024]{1,0:T(8,128)(2,1)} %broadcast_select_fusion.3), channel_id=1, source_target_pairs={{0,2},{1,5},{2,0},{3,7},{4,6},{5,1},{6,4},{7,3},{8,10},{9,13},{10,... | collective-permute-start | bytes 786440 | tf_op jit(solution)/shard_map/ppermute | solution.py:127
  105.2 8.1 %collective-permute-start.29 = (bf16[128,1024]{1,0:T(8,128)(2,1)S(1)}, bf16[128,1024]{1,0:T(8,128)(2,1)S(1)}, u32[]{:S(2)}, u32[]{:S(2)}) collective-permute-start(bf16[128,1024]{1,0:T(8,128)(2,1)S(1)} %collective-permute-done.10.refs_5_.refs_7_), channel_id=1, source_target_pairs={{0,1},{1,0},{2,3},{3,2},{4,5},{5,4},{6,7},{7,6},{8,9},{9,8},{10,11... | collective-permute-start | bytes 786440 | tf_op jit(solution)/shard_map/ppermute | solution.py:127
  105.2 8.1 %collective-permute-start.30 = (bf16[128,1024]{1,0:T(8,128)(2,1)S(1)}, bf16[128,1024]{1,0:T(8,128)(2,1)S(1)}, u32[]{:S(2)}, u32[]{:S(2)}) collective-permute-start(bf16[128,1024]{1,0:T(8,128)(2,1)S(1)} %collective-permute-done.11.refs_6_.refs_8_), channel_id=1, source_target_pairs={{0,1},{1,0},{2,3},{3,2},{4,5},{5,4},{6,7},{7,6},{8,9},{9,8},{10,11... | collective-permute-start | bytes 786440 | tf_op jit(solution)/shard_map/ppermute | solution.py:127
  128.9 80.4 %reduce-scatter.5.cloned.1.call-start = ((), (), s32[]{:S(2)}) async-start(), calls=%async_computation.9 | async-start | bytes 1474560 | tf_op jit(solution)/shard_map/reduce_scatter | solution.py:839
  130.1 3.6 %collective-permute-start.32 = (bf16[512,1024]{1,0:T(8,128)(2,1)S(1)}, bf16[512,1024]{1,0:T(8,128)(2,1)S(1)}, u32[]{:S(2)}, u32[]{:S(2)}) collective-permute-start(bf16[512,1024]{1,0:T(8,128)(2,1)S(1)} %copy-done.63), channel_id=1, source_target_pairs={{0,1},{1,0},{2,3},{3,2},{4,5},{5,4},{6,7},{7,6},{8,9},{9,8},{10,11... | collective-permute-start | bytes 3145736 | tf_op jit(solution)/shard_map/ppermute | solution.py:127
  133.6 5.8 %collective-permute-start.33 = (bf16[512,1024]{1,0:T(8,128)(2,1)}, bf16[512,1024]{1,0:T(8,128)(2,1)S(1)}, u32[]{:S(2)}, u32[]{:S(2)}) collective-permute-start(bf16[512,1024]{1,0:T(8,128)(2,1)} %ffn_output.1), channel_id=1, source_target_pairs={{0,1},{1,0},{2,3},{3,2},{4,5},{5,4},{6,7},{7,6},{8,9},{9,8},{10,11... | collective-permute-start | bytes 3145736 | tf_op jit(solution)/shard_map/ppermute | solution.py:127
  139.4 12.0 %collective-permute-start.34 = (bf16[128,1024]{1,0:T(8,128)(2,1)}, bf16[128,1024]{1,0:T(8,128)(2,1)S(1)}, u32[]{:S(2)}, u32[]{:S(2)}) collective-permute-start(bf16[128,1024]{1,0:T(8,128)(2,1)} %get-tuple-element.522), channel_id=1, source_target_pairs={{0,6},{1,7},{2,4},{3,5},{4,2},{5,3},{6,0},{7,1},{8,14},{9,15},{10,... | collective-permute-start | bytes 786440 | tf_op jit(solution)/shard_map/ppermute | solution.py:127
  141.1 13.8 %collective-permute-start.35 = (bf16[128,1024]{1,0:T(8,128)(2,1)}, bf16[128,1024]{1,0:T(8,128)(2,1)S(1)}, u32[]{:S(2)}, u32[]{:S(2)}) collective-permute-start(bf16[128,1024]{1,0:T(8,128)(2,1)} %get-tuple-element.523), channel_id=1, source_target_pairs={{0,2},{1,3},{2,0},{3,1},{4,6},{5,7},{6,4},{7,5},{8,10},{9,11},{10,... | collective-permute-start | bytes 786440 | tf_op jit(solution)/shard_map/ppermute | solution.py:127
  142.5 12.4 %collective-permute-start.36 = (bf16[128,1024]{1,0:T(8,128)(2,1)}, bf16[128,1024]{1,0:T(8,128)(2,1)S(1)}, u32[]{:S(2)}, u32[]{:S(2)}) collective-permute-start(bf16[128,1024]{1,0:T(8,128)(2,1)} %get-tuple-element.524), channel_id=1, source_target_pairs={{0,4},{1,5},{2,6},{3,7},{4,0},{5,1},{6,2},{7,3},{8,12},{9,13},{10,... | collective-permute-start | bytes 786440 | tf_op jit(solution)/shard_map/ppermute | solution.py:127
  160.6 13.1 %collective-permute-start.37 = (bf16[128,1024]{1,0:T(8,128)(2,1)}, bf16[128,1024]{1,0:T(8,128)(2,1)S(1)}, u32[]{:S(2)}, u32[]{:S(2)}) collective-permute-start(bf16[128,1024]{1,0:T(8,128)(2,1)} %get-tuple-element.620.refs_1_), channel_id=1, source_target_pairs={{0,2},{1,3},{2,0},{3,1},{4,6},{5,7},{6,4},{7,5},{8,10},{9,11},{10,... | collective-permute-start | bytes 786440 | tf_op jit(solution)/shard_map/ppermute | solution.py:127
  161.5 12.2 %collective-permute-start.38 = (bf16[128,1024]{1,0:T(8,128)(2,1)}, bf16[128,1024]{1,0:T(8,128)(2,1)S(1)}, u32[]{:S(2)}, u32[]{:S(2)}) collective-permute-start(bf16[128,1024]{1,0:T(8,128)(2,1)} %get-tuple-element.620.refs_1_), channel_id=1, source_target_pairs={{0,4},{1,5},{2,6},{3,7},{4,0},{5,1},{6,2},{7,3},{8,12},{9,13},{10,... | collective-permute-start | bytes 786440 | tf_op jit(solution)/shard_map/ppermute | solution.py:127
  162.7 11.0 %collective-permute-start.39 = (bf16[128,1024]{1,0:T(8,128)(2,1)}, bf16[128,1024]{1,0:T(8,128)(2,1)S(1)}, u32[]{:S(2)}, u32[]{:S(2)}) collective-permute-start(bf16[128,1024]{1,0:T(8,128)(2,1)} %get-tuple-element.620.refs_1_), channel_id=1, source_target_pairs={{0,1},{1,0},{2,3},{3,2},{4,5},{5,4},{6,7},{7,6},{8,9},{9,8},{10,11... | collective-permute-start | bytes 786440 | tf_op jit(solution)/shard_map/ppermute | solution.py:127
  177.2 8.5 %collective-permute-start.40 = (bf16[128,1024]{1,0:T(8,128)(2,1)S(1)}, bf16[128,1024]{1,0:T(8,128)(2,1)S(1)}, u32[]{:S(2)}, u32[]{:S(2)}) collective-permute-start(bf16[128,1024]{1,0:T(8,128)(2,1)S(1)} %copy-done.64), channel_id=1, source_target_pairs={{0,6},{1,7},{2,4},{3,5},{4,2},{5,3},{6,0},{7,1},{8,14},{9,15},{10,... | collective-permute-start | bytes 786440 | tf_op jit(solution)/shard_map/ppermute | solution.py:127
  178.2 9.3 %collective-permute-start.41 = (bf16[128,1024]{1,0:T(8,128)(2,1)S(1)}, bf16[128,1024]{1,0:T(8,128)(2,1)S(1)}, u32[]{:S(2)}, u32[]{:S(2)}) collective-permute-start(bf16[128,1024]{1,0:T(8,128)(2,1)S(1)} %broadcast_select_fusion.1), channel_id=1, source_target_pairs={{0,2},{1,5},{2,0},{3,7},{4,6},{5,1},{6,4},{7,3},{8,10},{9,13},{10,... | collective-permute-start | bytes 786440 | tf_op jit(solution)/shard_map/ppermute | solution.py:127
  179.3 8.2 %collective-permute-start.42 = (bf16[128,1024]{1,0:T(8,128)(2,1)S(1)}, bf16[128,1024]{1,0:T(8,128)(2,1)S(1)}, u32[]{:S(2)}, u32[]{:S(2)}) collective-permute-start(bf16[128,1024]{1,0:T(8,128)(2,1)S(1)} %collective-permute-done.37.refs_3_), channel_id=1, source_target_pairs={{0,1},{1,0},{2,3},{3,2},{4,5},{5,4},{6,7},{7,6},{8,9},{9,8},{10,11... | collective-permute-start | bytes 786440 | tf_op jit(solution)/shard_map/ppermute | solution.py:127
  179.3 8.2 %collective-permute-start.43 = (bf16[128,1024]{1,0:T(8,128)(2,1)S(1)}, bf16[128,1024]{1,0:T(8,128)(2,1)S(1)}, u32[]{:S(2)}, u32[]{:S(2)}) collective-permute-start(bf16[128,1024]{1,0:T(8,128)(2,1)S(1)} %collective-permute-done.38.refs_5_), channel_id=1, source_target_pairs={{0,1},{1,0},{2,3},{3,2},{4,5},{5,4},{6,7},{7,6},{8,9},{9,8},{10,11... | collective-permute-start | bytes 786440 | tf_op jit(solution)/shard_map/ppermute | solution.py:127
  179.8 5.7 %collective-permute-start.44 = (f32[8,128]{1,0:T(8,128)}, f32[8,128]{1,0:T(8,128)S(1)}, u32[]{:S(2)}, u32[]{:S(2)}) collective-permute-start(f32[8,128]{1,0:T(8,128)} %get-tuple-element.589), channel_id=1, source_target_pairs={{8,0},{9,1},{10,2},{11,3},{12,4},{13,5},{14,6},{15,7},{16,8},{17,9... | collective-permute-start | bytes 12296 | tf_op jit(solution)/shard_map/ppermute | solution.py:127
  187.5 7.2 %collective-permute-start.45 = (bf16[128,1024]{1,0:T(8,128)(2,1)S(1)}, bf16[128,1024]{1,0:T(8,128)(2,1)S(1)}, u32[]{:S(2)}, u32[]{:S(2)}) collective-permute-start(bf16[128,1024]{1,0:T(8,128)(2,1)S(1)} %collective-permute-done.41.refs_7_), channel_id=1, source_target_pairs={{0,1},{1,0},{2,3},{3,2},{4,5},{5,4},{6,7},{7,6},{8,9},{9,8},{10,11... | collective-permute-start | bytes 786440 | tf_op jit(solution)/shard_map/ppermute | solution.py:127
  194.7 14.5 %collective-permute-start.47 = (bf16[512,1024]{1,0:T(8,128)(2,1)}, bf16[512,1024]{1,0:T(8,128)(2,1)S(1)}, u32[]{:S(2)}, u32[]{:S(2)}) collective-permute-start(bf16[512,1024]{1,0:T(8,128)(2,1)} %get-tuple-element.618), channel_id=1, source_target_pairs={{0,1},{1,0},{2,3},{3,2},{4,5},{5,4},{6,7},{7,6},{8,9},{9,8},{10,11... | collective-permute-start | bytes 3145736 | tf_op jit(solution)/shard_map/ppermute | solution.py:127
  195.0 14.2 %all-to-all-start.3 = ((bf16[8,32,1152]{2,1,0:T(8,128)(2,1)}), bf16[8,32,1152]{2,1,0:T(8,128)(2,1)S(1)}, u32[]{:S(2)}, u32[]{:S(2)}) async-start(bf16[8,32,1152]{2,1,0:T(8,128)(2,1)} %bitcast.44), calls=%async_computation.4 | async-start | bytes 1179648 | tf_op jit(solution)/shard_map/all_to_all | solution.py:180
  198.6 10.6 %collective-permute-start.46 = (bf16[256,384]{1,0:T(8,128)(2,1)}, bf16[256,384]{1,0:T(8,128)(2,1)S(1)}, u32[]{:S(2)}, u32[]{:S(2)}) collective-permute-start(bf16[256,384]{1,0:T(8,128)(2,1)} %get-tuple-element.616), channel_id=1, source_target_pairs={{0,8},{1,9},{2,10},{3,11},{4,12},{5,13},{6,14},{7,15},{8,16},{9,17... | collective-permute-start | bytes 589832 | tf_op jit(solution)/shard_map/ppermute | solution.py:127
  209.3 13.1 %collective-permute-start.48 = (bf16[128,1024]{1,0:T(8,128)(2,1)}, bf16[128,1024]{1,0:T(8,128)(2,1)S(1)}, u32[]{:S(2)}, u32[]{:S(2)}) collective-permute-start(bf16[128,1024]{1,0:T(8,128)(2,1)} %get-tuple-element.640), channel_id=1, source_target_pairs={{0,2},{1,3},{2,0},{3,1},{4,6},{5,7},{6,4},{7,5},{8,10},{9,11},{10,... | collective-permute-start | bytes 786440 | tf_op jit(solution)/shard_map/ppermute | solution.py:127
  210.8 11.5 %collective-permute-start.49 = (bf16[128,1024]{1,0:T(8,128)(2,1)}, bf16[128,1024]{1,0:T(8,128)(2,1)}, u32[]{:S(2)}, u32[]{:S(2)}) collective-permute-start(bf16[128,1024]{1,0:T(8,128)(2,1)} %get-tuple-element.641), channel_id=1, source_target_pairs={{0,4},{1,5},{2,6},{3,7},{4,0},{5,1},{6,2},{7,3},{8,12},{9,13},{10,... | collective-permute-start | bytes 786440 | tf_op jit(solution)/shard_map/ppermute | solution.py:127
  212.3 10.1 %collective-permute-start.50 = (bf16[256,384]{1,0:T(8,128)(2,1)S(1)}, bf16[256,384]{1,0:T(8,128)(2,1)S(1)}, u32[]{:S(2)}, u32[]{:S(2)}) collective-permute-start(bf16[256,384]{1,0:T(8,128)(2,1)S(1)} %add_convert_fusion.3), channel_id=1, source_target_pairs={{0,8},{1,9},{2,10},{3,11},{4,12},{5,13},{6,14},{7,15},{8,16},{9,17... | collective-permute-start | bytes 589832 | tf_op jit(solution)/shard_map/ppermute | solution.py:127
  212.3 10.0 %collective-permute-start.51 = (bf16[48,1024]{1,0:T(8,128)(2,1)}, bf16[48,1024]{1,0:T(8,128)(2,1)S(1)}, u32[]{:S(2)}, u32[]{:S(2)}) collective-permute-start(bf16[48,1024]{1,0:T(8,128)(2,1)} %get-tuple-element.650), channel_id=1, source_target_pairs={{0,8},{1,9},{2,10},{3,11},{4,12},{5,13},{6,14},{7,15},{8,16},{9,17... | collective-permute-start | bytes 294920 | tf_op jit(solution)/shard_map/ppermute | solution.py:127
  224.3 9.2 %collective-permute-start.55 = (bf16[256,384]{1,0:T(8,128)(2,1)S(1)}, bf16[256,384]{1,0:T(8,128)(2,1)S(1)}, u32[]{:S(2)}, u32[]{:S(2)}) collective-permute-start(bf16[256,384]{1,0:T(8,128)(2,1)S(1)} %add_convert_fusion.2), channel_id=1, source_target_pairs={{0,8},{1,9},{2,10},{3,11},{4,12},{5,13},{6,14},{7,15},{8,16},{9,17... | collective-permute-start | bytes 589832 | tf_op jit(solution)/shard_map/ppermute | solution.py:127
  224.3 9.1 %collective-permute-start.56 = (bf16[48,1024]{1,0:T(8,128)(2,1)S(1)}, bf16[48,1024]{1,0:T(8,128)(2,1)S(1)}, u32[]{:S(2)}, u32[]{:S(2)}) collective-permute-start(bf16[48,1024]{1,0:T(8,128)(2,1)S(1)} %add_convert_fusion.5), channel_id=1, source_target_pairs={{0,8},{1,9},{2,10},{3,11},{4,12},{5,13},{6,14},{7,15},{8,16},{9,17... | collective-permute-start | bytes 294920 | tf_op jit(solution)/shard_map/ppermute | solution.py:127
  225.3 17.7 %collective-permute-start.52 = (bf16[128,1024]{1,0:T(8,128)(2,1)}, bf16[128,1024]{1,0:T(8,128)(2,1)S(1)}, u32[]{:S(2)}, u32[]{:S(2)}) collective-permute-start(bf16[128,1024]{1,0:T(8,128)(2,1)} %get-tuple-element.659), channel_id=1, source_target_pairs={{0,6},{1,7},{2,4},{3,5},{4,2},{5,3},{6,0},{7,1},{8,14},{9,15},{10,... | collective-permute-start | bytes 786440 | tf_op jit(solution)/shard_map/ppermute | solution.py:127
  225.9 17.1 %collective-permute-start.53 = (bf16[128,1024]{1,0:T(8,128)(2,1)}, bf16[128,1024]{1,0:T(8,128)(2,1)S(1)}, u32[]{:S(2)}, u32[]{:S(2)}) collective-permute-start(bf16[128,1024]{1,0:T(8,128)(2,1)} %get-tuple-element.660), channel_id=1, source_target_pairs={{0,2},{1,3},{2,0},{3,1},{4,6},{5,7},{6,4},{7,5},{8,10},{9,11},{10,... | collective-permute-start | bytes 786440 | tf_op jit(solution)/shard_map/ppermute | solution.py:127
  227.3 15.7 %collective-permute-start.54 = (bf16[128,1024]{1,0:T(8,128)(2,1)}, bf16[128,1024]{1,0:T(8,128)(2,1)S(1)}, u32[]{:S(2)}, u32[]{:S(2)}) collective-permute-start(bf16[128,1024]{1,0:T(8,128)(2,1)} %get-tuple-element.661), channel_id=1, source_target_pairs={{0,4},{1,5},{2,6},{3,7},{4,0},{5,1},{6,2},{7,3},{8,12},{9,13},{10,... | collective-permute-start | bytes 786440 | tf_op jit(solution)/shard_map/ppermute | solution.py:127
  234.2 8.8 %collective-permute-start.57 = (bf16[48,1024]{1,0:T(8,128)(2,1)S(1)}, bf16[48,1024]{1,0:T(8,128)(2,1)}, u32[]{:S(2)}, u32[]{:S(2)}) collective-permute-start(bf16[48,1024]{1,0:T(8,128)(2,1)S(1)} %add_convert_fusion.4), channel_id=1, source_target_pairs={{0,8},{1,9},{2,10},{3,11},{4,12},{5,13},{6,14},{7,15},{8,16},{9,17... | collective-permute-start | bytes 294920 | tf_op jit(solution)/shard_map/ppermute | solution.py:127
  234.3 9.6 %all-to-all-start.4 = ((bf16[8,32,384]{2,1,0:T(8,128)(2,1)}), bf16[8,32,384]{2,1,0:T(8,128)(2,1)S(1)}, u32[]{:S(2)}, u32[]{:S(2)}) async-start(bf16[8,32,384]{2,1,0:T(8,128)(2,1)} %bitcast.13), calls=%async_computation.6 | async-start | bytes 393216 | tf_op jit(solution)/shard_map/all_to_all | solution.py:180
  (71 other events, 775.3 us)
Sparse Core Ops, SparseCore 0:
  9.6 37.1 all-gather.5
  62.7 49.5 all-gather.3
  129.0 45.4 reduce-scatter.2
  176.6 29.1 reduce-scatter.4

commit v4 on v3

--- a/solution.py
+++ b/solution.py
@@ -37,7 +37,7 @@
         kernel,
         out_shape=out_shape,
         scratch_shapes=list(scratch),
-        compiler_params=pltpu.CompilerParams(vmem_limit_bytes=60 * 2**20),
+        compiler_params=pltpu.CompilerParams(vmem_limit_bytes=56 * 2**20),
         cost_estimate=pl.CostEstimate(flops=flops, bytes_accessed=size, transcendentals=0),
         name=name,
         **places,

time: 257 us -> 256 us (level)
    unnamed x139 -> x141, local copies, waits for them, and re-layouts: 7.03 us -> 5.65 us
  transfers between devices with their start and end apart: 66 -> 66, of which waited for: 15 -> 15; matrix products, arithmetic and copies ran while one was open for 3% -> 2% of each run, Pallas kernels for 23% -> 23%
where the time goes in v4:
time: 256 us; the launch traced here: 255 us
  Pallas kernels  74.2 us (29%)
  waiting for transfers between devices  58.1 us (23%)
  starting transfers between devices  56.7 us (22%)
  blocking collectives  35 us (14%)
  between operations  15 us (6%)
  other arithmetic  8.11 us (3%)
  local copies, waits for them, and re-layouts  7.75 us (3%)
    pallas_call x16, Pallas kernels, call(): pl.pallas_call(kernel, out_shape=out_shape, scratch_shapes=list(scratch),...  74.2 us
    ppermute x58, waiting for transfers between devices, one_step(): got.append(lax.ppermute(values[at], 'dp', self.pairs(move[1])))  48.4 us
    ppermute x58, starting transfers between devices, one_step(): got.append(lax.ppermute(values[at], 'dp', self.pairs(move[1])))  41.6 us
    all_gather x1, blocking collectives, gather(): lax.all_gather(value, 'dp', axis=0, tiled=True, axis_index_groups=line)  24 us
    all_to_all x4, starting transfers between devices, exchange(): lax.all_to_all(blocks, 'dp', 0, 0, axis_index_groups=groups, tiled=True)  14.9 us
    all_to_all x1, blocking collectives, exchange(): lax.all_to_all(blocks, 'dp', 0, 0, axis_index_groups=groups, tiled=True)  11 us
    all_to_all x4, waiting for transfers between devices, exchange(): lax.all_to_all(blocks, 'dp', 0, 0, axis_index_groups=groups, tiled=True)  8.9 us
    unnamed x141, local copies, waits for them, and re-layouts  5.65 us
  transfers between devices with their start and end apart: 66, of which 15 were waited for; matrix products, arithmetic and copies ran while one was open for 2% of the time, Pallas kernels for 23%

profile of v4, /device:TPU:0, one launch (start us, length us, event | category | flops | bytes accessed | tf_op | source)
XLA Modules:
  0.0 254.8 jit_solution(7071126398496899919)
XLA Ops:
  7.9 2.0 in_prepare.1
  9.9 2.9 %collective-permute-start = (bf16[128,1024]{1,0:T(8,128)(2,1)}, bf16[128,1024]{1,0:T(8,128)(2,1)S(1)}, u32[]{:S(2)}, u32[]{:S(2)}) collective-permute-start(bf16[128,1024]{1,0:T(8,128)(2,1)} %refs_16_), channel_id=1, source_target_pairs={{0,2},{1,3},{2,0},{3,1},{4,6},{5,7},{6,4},{7,5},{8,10},{9,11},{10,... | collective-permute-start | bytes 786440 | tf_op jit(solution)/shard_map/ppermute | solution.py:127
  12.8 1.5 collective-permute-start.1
  14.4 4.3 %all-to-all-start = ((bf16[8,40,384]{2,1,0:T(8,128)(2,1)}), bf16[8,40,384]{2,1,0:T(8,128)(2,1)S(1)}, u32[]{:S(2)}, u32[]{:S(2)}) async-start(bf16[8,40,384]{2,1,0:T(8,128)(2,1)} %in_prepare.1), calls=%async_computation | async-start | bytes 491520 | tf_op jit(solution)/shard_map/all_to_all | solution.py:180
  18.7 2.3 pair_prepare.1
  21.0 8.1 %all-to-all-done = bf16[8,40,384]{2,1,0:T(8,128)(2,1)S(1)} async-done(((bf16[8,40,384]{2,1,0:T(8,128)(2,1)}), bf16[8,40,384]{2,1,0:T(8,128)(2,1)S(1)}, u32[]{:S(2)}, u32[]{:S(2)}) %all-to-all-start) | async-done | bytes 245792 | tf_op jit(solution)/shard_map/all_to_all | solution.py:180
  29.1 3.7 %all-to-all-start.1 = ((bf16[8,32,1152]{2,1,0:T(8,128)(2,1)}), bf16[8,32,1152]{2,1,0:T(8,128)(2,1)S(1)}, u32[]{:S(2)}, u32[]{:S(2)}) async-start(bf16[8,32,1152]{2,1,0:T(8,128)(2,1)} %pair_prepare.1), calls=%async_computation.1 | async-start | bytes 1179648 | tf_op jit(solution)/shard_map/all_to_all | solution.py:180
  33.8 1.6 collective-permute-start.7
  35.3 2.2 collective-permute-start.8
  37.6 24.0 %all_gather.9 = bf16[1280,384]{1,0:T(8,128)(2,1)} all-gather(bf16[320,384]{1,0:T(8,128)(2,1)S(1)} %bitcast.41), channel_id=1, replica_groups={{0,8,16,24},{1,9,17,25},{2,10,18,26},{3,11,19,27},{4,12,20,28},{5,13,21..., dimensions={0}, use_global_device_ids=true | all-gather | bytes 1228800 | tf_op jit(solution)/shard_map/all_gather | solution.py:836
  63.5 1.5 collective-permute-start.10
  65.0 1.5 collective-permute-start.11
  66.5 1.6 collective-permute-start.13
  68.1 5.5 %collective-permute-done.13.refs_8_ = bf16[16,1024]{1,0:T(8,128)(2,1)S(1)} collective-permute-done((bf16[16,1024]{1,0:T(8,128)(2,1)S(1)}, bf16[16,1024]{1,0:T(8,128)(2,1)S(1)}, u32[]{:S(2)}, u32[]{:S(2)}) %collective-permute-start.13) | collective-permute-done | bytes 32800 | tf_op jit(solution)/shard_map/ppermute | solution.py:127
  74.9 7.1 %mixer_forward.1 = (bf16[1040,1024]{1,0:T(8,128)(2,1)}, f32[1040,384]{1,0:T(8,128)}, f32[1040,128]{1,0:T(8,128)}, f32[1024,128]{1,0:T(8,128)}, bf16[1024,128]{1,...) custom-call(bf16[128,1024]{1,0:T(8,128)(2,1)} %refs_16_, ...), custom_call_target="tpu_custom_call" | custom-call | flops 805306368 | bytes 3112960 | tf_op jit(solution)/shard_map/mixer_forward/pallas_call | solution.py:36
  82.1 1.6 collective-permute-start.17
  84.2 1.2 collective-permute-start.20
  86.2 3.6 %collective-permute-done.17.refs_14_.refs_6_ = bf16[128,1024]{1,0:T(8,128)(2,1)S(1)} collective-permute-done((bf16[128,1024]{1,0:T(8,128)(2,1)S(1)}, bf16[128,1024]{1,0:T(8,128)(2,1)S(1)}, u32[]{:S(2)}, u32[]{:S(2)}) %collective-permute-start.17) | collective-permute-done | bytes 262176 | tf_op jit(solution)/shard_map/ppermute | solution.py:127
  89.8 4.3 %collective-permute-done.20.refs_2_ = bf16[1024,128]{1,0:T(8,128)(2,1)S(1)} collective-permute-done((bf16[1024,128]{1,0:T(8,128)(2,1)}, bf16[1024,128]{1,0:T(8,128)(2,1)S(1)}, u32[]{:S(2)}, u32[]{:S(2)}) %collective-permute-start.20) | collective-permute-done | bytes 262176 | tf_op jit(solution)/shard_map/ppermute | solution.py:127
  94.3 1.6 collective-permute-start.24
  96.4 4.3 %collective-permute-done.24.refs_6_ = bf16[1024,128]{1,0:T(8,128)(2,1)S(1)} collective-permute-done((bf16[1024,128]{1,0:T(8,128)(2,1)S(1)}, bf16[1024,128]{1,0:T(8,128)(2,1)S(1)}, u32[]{:S(2)}, u32[]{:S(2)}) %collective-permute-start.24) | collective-permute-done | bytes 262176 | tf_op jit(solution)/shard_map/ppermute | solution.py:127
  100.8 1.5 collective-permute-done.27.refs_7_
  102.3 1.5 collective-permute-start.28
  104.5 7.5 %out_project.1 = (f32[128,1024]{1,0:T(8,128)}, bf16[512,1024]{1,0:T(8,128)(2,1)}, bf16[512,1024]{1,0:T(8,128)(2,1)}) custom-call(bf16[1024,128]{1,0:T(8,128)(2,1)} %get-tuple-element.619.refs_0_, bf16[1024,128]{1,0:T(8,128)(2,1)} %copy-done.65, bf16[1024,128]{1,0:T(8,128)(2,1)} %copy-done.48, bf16[1024,128]{1,0:T(8,128)(2,1)} %copy-done.67, ...), custom_call_target="tpu_custom_call" | custom-call | flops 2147483648 | bytes 6295552 | tf_op jit(solution)/shard_map/out_project/pallas_call | solution.py:36
  112.2 1.5 collective-permute-done.31.refs_3_.refs_5_
  114.4 13.2 %ffn.1 = (bf16[512,576]{1,0:T(8,128)(2,1)}, bf16[512,576]{1,0:T(8,128)(2,1)}, bf16[512,1152]{1,0:T(8,128)(2,1)}, bf16[512,1152]{1,0:T(8,128)(2,1)}, bf16[1024,11...) custom-call(bf16[512,1024]{1,0:T(8,128)(2,1)} %get-tuple-element.482.odd_in, bf16[512,1024]{1,0:T(8,128)(2,1)} %get-tuple-element.483.even_in, ...), custom_call_target="tpu_custom_call" | custom-call | flops 6039797760 | bytes 7733248 | tf_op jit(solution)/shard_map/ffn/pallas_call | solution.py:36
  127.6 1.1 copy-done.63
  128.9 3.4 %ffn_output.1 = bf16[512,1024]{1,0:T(8,128)(2,1)} custom-call(bf16[512,576]{1,0:T(8,128)(2,1)} %get-tuple-element.532.left.refs_0_, bf16[576,1024]{1,0:T(8,128)(2,1)} %bitcast.31), custom_call_target="tpu_custom_call" | custom-call | flops 603979776 | bytes 1769472 | tf_op jit(solution)/shard_map/ffn_output/pallas_call | solution.py:36
  133.3 4.8 %ffn_back.1 = (f32[128,1024]{1,0:T(8,128)}, bf16[128,1024]{1,0:T(8,128)(2,1)}, bf16[128,1024]{1,0:T(8,128)(2,1)}, bf16[128,1024]{1,0:T(8,128)(2,1)}) custom-call(bf16[512,1152]{1,0:T(8,128)(2,1)} %get-tuple-element.509.left_in, bf16[1024,1152]{1,0:T(8,128)(2,1)} %all-gather.4.cloned.1.call-done.refs_8_.right_in, bf16[512,1024]{1,0:T(8,128)(2,1)} %copy-done.15), custom_call_target="tpu_custom_call" | custom-call | flops 1207959552 | bytes 4587520 | tf_op jit(solution)/shard_map/ffn_back/pallas_call | solution.py:36
  138.2 1.5 collective-permute-start.34
  139.7 1.5 collective-permute-start.35
  141.7 3.7 %ffn_output_sum.1 = (f32[128,1024]{1,0:T(8,128)}, bf16[128,1024]{1,0:T(8,128)(2,1)}, bf16[128,1024]{1,0:T(8,128)(2,1)}, bf16[128,1024]{1,0:T(8,128)(2,1)}) custom-call(bf16[512,576]{1,0:T(8,128)(2,1)} %get-tuple-element.533.left_in.refs_1_, bf16[576,1024]{1,0:T(8,128)(2,1)} %bitcast.32, bf16[512,1024]{1,0:T(8,128)(2,1)} %copy-done.14), custom_call_target="tpu_custom_call" | custom-call | flops 603979776 | bytes 2818048 | tf_op jit(solution)/shard_map/ffn_output_sum/pallas_call | solution.py:36
  145.5 4.6 %down_grads.1 = bf16[576,1024]{1,0:T(8,128)(2,1)} custom-call(bf16[512,576]{1,0:T(8,128)(2,1)} %get-tuple-element.532.left.refs_0_, bf16[512,576]{1,0:T(8,128)(2,1)} %get-tuple-element.533.left_in.refs_1_, bf16[128,1024]{1,0:T(8,128)(2,1)} %copy-done.30, bf16[128,1024]{1,0:T(8,128)(2,1)} %copy-done.37, bf16[128,1024]{1,0:T(8,128)(2,1)} %copy-done.38, ...), custom_call_target="tpu_custom_call" | custom-call | flops 1207959552 | bytes 3276800 | tf_op jit(solution)/shard_map/down_grads/pallas_call | solution.py:36
  150.1 3.5 %collective-permute-done.35.across = bf16[128,1024]{1,0:T(8,128)(2,1)S(1)} collective-permute-done((bf16[128,1024]{1,0:T(8,128)(2,1)}, bf16[128,1024]{1,0:T(8,128)(2,1)S(1)}, u32[]{:S(2)}, u32[]{:S(2)}) %collective-permute-start.35) | collective-permute-done | bytes 262176 | tf_op jit(solution)/shard_map/ppermute | solution.py:127
  154.4 4.9 %resid_back.1 = (f32[128,1024]{1,0:T(8,128)}, bf16[128,1024]{1,0:T(8,128)(2,1)}, bf16[8,128,128]{2,1,0:T(8,128)(2,1)}) custom-call(f32[128,1024]{1,0:T(8,128)} %get-tuple-element.550.own, bf16[128,1024]{1,0:T(8,128)(2,1)} %copy-done.44, bf16[128,1024]{1,0:T(8,128)(2,1)} %copy-done.45, bf16[128,1024]{1,0:T(8,128)(2,1)} %copy-done.46, ...), custom_call_target="tpu_custom_call" | custom-call | flops 268435456 | bytes 4198400 | tf_op jit(solution)/shard_map/resid_back/pallas_call | solution.py:36
  159.3 0.9 collective-permute-start.37
  160.3 1.0 collective-permute-start.38
  161.2 11.0 %all_to_all.25 = bf16[8,128,128]{2,1,0:T(8,128)(2,1)} all-to-all(bf16[8,128,128]{2,1,0:T(8,128)(2,1)} %get-tuple-element.571), channel_id=1, replica_groups={{0,1,2,3,4,5,6,7},{8,9,10,11,12,13,14,15},{16,17,18,19,20,21,22,23},{24..., dimensions={0} | all-to-all | bytes 524288 | tf_op jit(solution)/shard_map/all_to_all | solution.py:180
  172.3 3.4 %conv_back.1 = (f32[1024,128]{1,0:T(8,128)}, f32[8,128]{1,0:T(8,128)}, f32[8,128]{1,0:T(8,128)}) custom-call(bf16[1024,128]{1,0:T(8,128)(2,1)} %bitcast.35, f32[1040,384]{1,0:T(8,128)} %get-tuple-element.599.mixed.refs_3_, f32[1040,128]{1,0:T(8,128)} %get-tuple-element.578.gated, f32[1024,128]{1,0:T(8,128)} %get-tuple-element.600.conv.refs_4_, ...), custom_call_target="tpu_custom_call" | custom-call | bytes 2928704 | tf_op jit(solution)/shard_map/conv_back/pallas_call | solution.py:36
  175.8 1.2 collective-permute-start.40
  177.0 0.9 collective-permute-start.41
  178.4 1.3 collective-permute-start.44
  179.7 4.4 %collective-permute-done.44.refs_1_ = f32[8,128]{1,0:T(8,128)S(1)} collective-permute-done((f32[8,128]{1,0:T(8,128)}, f32[8,128]{1,0:T(8,128)S(1)}, u32[]{:S(2)}, u32[]{:S(2)}) %collective-permute-start.44) | collective-permute-done | bytes 4128 | tf_op jit(solution)/shard_map/ppermute | solution.py:127
  184.3 1.8 collective-permute-done.41.refs_7_
  186.1 1.2 collective-permute-start.45
  187.3 5.9 %mixer_back.1 = (bf16[1024,384]{1,0:T(8,128)(2,1)}, bf16[512,1024]{1,0:T(8,128)(2,1)}, f32[256,384]{1,0:T(8,128)}, f32[256,384]{1,0:T(8,128)}, f32[256,384]{1,0:T(8,128)}, /*index=5*/bf16[256,384]{1,0:T(8,128)(2,1)}) custom-call(f32[1024,128]{1,0:T(8,128)} %get-tuple-element.596.refs_0_, f32[8,128]{1,0:T(8,128)} %copy-done.60, bf16[1024,128]{1,0:T(8,128)(2,1)} %bitcast.36, ...), custom_call_target="tpu_custom_call" | custom-call | flops 1207959552 | bytes 5828608 | tf_op jit(solution)/shard_map/mixer_back/pallas_call | solution.py:36
  193.6 3.5 %all-to-all-start.3 = ((bf16[8,32,1152]{2,1,0:T(8,128)(2,1)}), bf16[8,32,1152]{2,1,0:T(8,128)(2,1)S(1)}, u32[]{:S(2)}, u32[]{:S(2)}) async-start(bf16[8,32,1152]{2,1,0:T(8,128)(2,1)} %bitcast.44), calls=%async_computation.4 | async-start | bytes 1179648 | tf_op jit(solution)/shard_map/all_to_all | solution.py:180
  197.3 3.2 %out_back.1 = (f32[48,1024]{1,0:T(8,128)}, f32[48,1024]{1,0:T(8,128)}, f32[48,1024]{1,0:T(8,128)}, bf16[48,1024]{1,0:T(8,128)(2,1)}) custom-call(bf16[1024,128]{1,0:T(8,128)(2,1)} %get-tuple-element.619.refs_0_, bf16[128,1024]{1,0:T(8,128)(2,1)} %get-tuple-element.620.refs_1_, bf16[128,1024]{1,0:T(8,128)(2,1)} %copy-done.39, bf16[128,1024]{1,0:T(8,128)(2,1)} %copy-done.12, ...), custom_call_target="tpu_custom_call" | custom-call | flops 268435456 | bytes 2363392 | tf_op jit(solution)/shard_map/out_back/pallas_call | solution.py:36
  200.6 7.2 %collective-permute-done.46 = bf16[256,384]{1,0:T(8,128)(2,1)S(1)} collective-permute-done((bf16[256,384]{1,0:T(8,128)(2,1)}, bf16[256,384]{1,0:T(8,128)(2,1)S(1)}, u32[]{:S(2)}, u32[]{:S(2)}) %collective-permute-start.46) | collective-permute-done | bytes 196640 | tf_op jit(solution)/shard_map/ppermute | solution.py:127
  207.9 1.5 collective-permute-start.48
  209.5 1.5 collective-permute-start.49
  211.8 3.3 %mixer_back_sum.1 = (f32[128,1024]{1,0:T(8,128)}, bf16[128,1024]{1,0:T(8,128)(2,1)}, bf16[128,1024]{1,0:T(8,128)(2,1)}, bf16[128,1024]{1,0:T(8,128)(2,1)}) custom-call(bf16[1024,384]{1,0:T(8,128)(2,1)} %get-tuple-element.643.left_in, bf16[1024,384]{1,0:T(8,128)(2,1)} %get-tuple-element.644.refs_6_.right_in, bf16[512,1024]{1,0:T(8,128)(2,1)} %copy-done.7), custom_call_target="tpu_custom_call" | custom-call | flops 402653184 | bytes 2621440 | tf_op jit(solution)/shard_map/mixer_back_sum/pallas_call | solution.py:36
  215.2 5.8 %collective-permute-done.51 = bf16[48,1024]{1,0:T(8,128)(2,1)S(1)} collective-permute-done((bf16[48,1024]{1,0:T(8,128)(2,1)}, bf16[48,1024]{1,0:T(8,128)(2,1)S(1)}, u32[]{:S(2)}, u32[]{:S(2)}) %collective-permute-start.51) | collective-permute-done | bytes 98336 | tf_op jit(solution)/shard_map/ppermute | solution.py:127
  221.8 1.1 add_convert_fusion.2
  223.0 0.9 bitcast_convert_fusion
  224.5 1.4 collective-permute-start.53
  225.9 1.5 collective-permute-start.54
  227.4 4.7 %collective-permute-done.56 = bf16[48,1024]{1,0:T(8,128)(2,1)S(1)} collective-permute-done((bf16[48,1024]{1,0:T(8,128)(2,1)S(1)}, bf16[48,1024]{1,0:T(8,128)(2,1)S(1)}, u32[]{:S(2)}, u32[]{:S(2)}) %collective-permute-start.56) | collective-permute-done | bytes 98336 | tf_op jit(solution)/shard_map/ppermute | solution.py:127
  232.9 3.4 %all-to-all-start.4 = ((bf16[8,32,384]{2,1,0:T(8,128)(2,1)}), bf16[8,32,384]{2,1,0:T(8,128)(2,1)S(1)}, u32[]{:S(2)}, u32[]{:S(2)}) async-start(bf16[8,32,384]{2,1,0:T(8,128)(2,1)} %bitcast.13), calls=%async_computation.6 | async-start | bytes 393216 | tf_op jit(solution)/shard_map/all_to_all | solution.py:180
  236.4 1.9 add_convert_fusion
  239.0 2.7 %pair_finish.1 = (f32[32,4608]{1,0:T(8,128)}, f32[32,4608]{1,0:T(8,128)}, f32[1,32]{1,0:T(1,128)}) custom-call(bf16[8,32,1152]{2,1,0:T(8,128)(2,1)} %copy-done.2, bf16[32,4608]{1,0:T(8,128)(2,1)} %bitcast.38, bf16[32,4608]{1,0:T(8,128)(2,1)} %bitcast.40, bf16[32,1]{1,0:T(8,128)(2,1)} %copy.21.gain), custom_call_target="tpu_custom_call" | custom-call | bytes 1179712 | tf_op jit(solution)/shard_map/pair_finish/pallas_call | solution.py:36
  242.5 1.1 convert_add_fusion
  245.2 1.1 fusion.5
  246.2 2.0 in_finish.1
  (254 shorter events, 18.2 us)
Async XLA Ops:
  7.2 106.5 %all-gather.6.cloned.1.call-start = ((), (), s32[]{:S(2)}) async-start(), calls=%async_computation.10 | async-start | bytes 1474560 | tf_op jit(solution)/shard_map/all_gather | solution.py:836
  9.9 19.2 %collective-permute-start = (bf16[128,1024]{1,0:T(8,128)(2,1)}, bf16[128,1024]{1,0:T(8,128)(2,1)S(1)}, u32[]{:S(2)}, u32[]{:S(2)}) collective-permute-start(bf16[128,1024]{1,0:T(8,128)(2,1)} %refs_16_), channel_id=1, source_target_pairs={{0,2},{1,3},{2,0},{3,1},{4,6},{5,7},{6,4},{7,5},{8,10},{9,11},{10,... | collective-permute-start | bytes 786440 | tf_op jit(solution)/shard_map/ppermute | solution.py:127
  12.8 16.2 %collective-permute-start.1 = (bf16[128,1024]{1,0:T(8,128)(2,1)}, bf16[128,1024]{1,0:T(8,128)(2,1)S(1)}, u32[]{:S(2)}, u32[]{:S(2)}) collective-permute-start(bf16[128,1024]{1,0:T(8,128)(2,1)} %refs_16_), channel_id=1, source_target_pairs={{0,4},{1,5},{2,6},{3,7},{4,0},{5,1},{6,2},{7,3},{8,12},{9,13},{10,... | collective-permute-start | bytes 786440 | tf_op jit(solution)/shard_map/ppermute | solution.py:127
  14.4 14.7 %collective-permute-start.2 = (bf16[128,1024]{1,0:T(8,128)(2,1)}, bf16[128,1024]{1,0:T(8,128)(2,1)S(1)}, u32[]{:S(2)}, u32[]{:S(2)}) collective-permute-start(bf16[128,1024]{1,0:T(8,128)(2,1)} %refs_16_), channel_id=1, source_target_pairs={{0,6},{1,7},{2,4},{3,5},{4,2},{5,3},{6,0},{7,1},{8,14},{9,15},{10,... | collective-permute-start | bytes 786440 | tf_op jit(solution)/shard_map/ppermute | solution.py:127
  14.4 14.7 %collective-permute-start.3 = (bf16[128,1024]{1,0:T(8,128)(2,1)}, bf16[128,1024]{1,0:T(8,128)(2,1)S(1)}, u32[]{:S(2)}, u32[]{:S(2)}) collective-permute-start(bf16[128,1024]{1,0:T(8,128)(2,1)} %refs_16_), channel_id=1, source_target_pairs={{0,1},{1,0},{2,3},{3,2},{4,5},{5,4},{6,7},{7,6},{8,9},{9,8},{10,11... | collective-permute-start | bytes 786440 | tf_op jit(solution)/shard_map/ppermute | solution.py:127
  14.4 14.7 %all-to-all-start = ((bf16[8,40,384]{2,1,0:T(8,128)(2,1)}), bf16[8,40,384]{2,1,0:T(8,128)(2,1)S(1)}, u32[]{:S(2)}, u32[]{:S(2)}) async-start(bf16[8,40,384]{2,1,0:T(8,128)(2,1)} %in_prepare.1), calls=%async_computation | async-start | bytes 491520 | tf_op jit(solution)/shard_map/all_to_all | solution.py:180
  29.1 32.6 %all-to-all-start.1 = ((bf16[8,32,1152]{2,1,0:T(8,128)(2,1)}), bf16[8,32,1152]{2,1,0:T(8,128)(2,1)S(1)}, u32[]{:S(2)}, u32[]{:S(2)}) async-start(bf16[8,32,1152]{2,1,0:T(8,128)(2,1)} %pair_prepare.1), calls=%async_computation.1 | async-start | bytes 1179648 | tf_op jit(solution)/shard_map/all_to_all | solution.py:180
  32.8 80.8 %all-gather.4.cloned.1.call-start = ((), (), s32[]{:S(2)}) async-start(), calls=%async_computation.7 | async-start | bytes 2949120 | tf_op jit(solution)/shard_map/all_gather | solution.py:836
  32.9 28.8 %collective-permute-start.4 = (bf16[128,1024]{1,0:T(8,128)(2,1)S(1)}, bf16[128,1024]{1,0:T(8,128)(2,1)S(1)}, u32[]{:S(2)}, u32[]{:S(2)}) collective-permute-start(bf16[128,1024]{1,0:T(8,128)(2,1)S(1)} %collective-permute-done.refs_2_.refs_18_), channel_id=1, source_target_pairs={{0,1},{1,0},{2,3},{3,2},{4,5},{5,4},{6,7},{7,6},{8,9},{9,8},{10,11... | collective-permute-start | bytes 786440 | tf_op jit(solution)/shard_map/ppermute | solution.py:127
  33.2 28.4 %collective-permute-start.5 = (bf16[128,1024]{1,0:T(8,128)(2,1)S(1)}, bf16[128,1024]{1,0:T(8,128)(2,1)S(1)}, u32[]{:S(2)}, u32[]{:S(2)}) collective-permute-start(bf16[128,1024]{1,0:T(8,128)(2,1)S(1)} %collective-permute-done.1.refs_4_.refs_20_), channel_id=1, source_target_pairs={{0,1},{1,0},{2,3},{3,2},{4,5},{5,4},{6,7},{7,6},{8,9},{9,8},{10,11... | collective-permute-start | bytes 786440 | tf_op jit(solution)/shard_map/ppermute | solution.py:127
  33.5 28.2 %collective-permute-start.6 = (bf16[128,1024]{1,0:T(8,128)(2,1)S(1)}, bf16[128,1024]{1,0:T(8,128)(2,1)S(1)}, u32[]{:S(2)}, u32[]{:S(2)}) collective-permute-start(bf16[128,1024]{1,0:T(8,128)(2,1)S(1)} %collective-permute-done.2.refs_6_.refs_22_), channel_id=1, source_target_pairs={{0,1},{1,0},{2,3},{3,2},{4,5},{5,4},{6,7},{7,6},{8,9},{9,8},{10,11... | collective-permute-start | bytes 786440 | tf_op jit(solution)/shard_map/ppermute | solution.py:127
  33.8 27.9 %collective-permute-start.7 = (bf16[32,1024]{1,0:T(8,128)(2,1)S(1)}, bf16[32,1024]{1,0:T(8,128)(2,1)S(1)}, u32[]{:S(2)}, u32[]{:S(2)}) collective-permute-start(bf16[32,1024]{1,0:T(8,128)(2,1)S(1)} %bitcast.45), channel_id=1, source_target_pairs={{0,8},{1,9},{2,10},{3,11},{4,12},{5,13},{6,14},{7,15},{8,16},{9,17... | collective-permute-start | bytes 196616 | tf_op jit(solution)/shard_map/ppermute | solution.py:127
  35.3 26.3 %collective-permute-start.8 = (bf16[32,1024]{1,0:T(8,128)(2,1)S(1)}, bf16[32,1024]{1,0:T(8,128)(2,1)S(1)}, u32[]{:S(2)}, u32[]{:S(2)}) collective-permute-start(bf16[32,1024]{1,0:T(8,128)(2,1)S(1)} %bitcast.46), channel_id=1, source_target_pairs={{0,24},{1,25},{2,26},{3,27},{4,28},{5,29},{6,30},{7,31},{8,0},{9,1... | collective-permute-start | bytes 196616 | tf_op jit(solution)/shard_map/ppermute | solution.py:127
  62.6 130.7 %reduce-scatter.3.cloned.1.call-start = ((), (), s32[]{:S(2)}) async-start(), calls=%async_computation.8 | async-start | bytes 2949120 | tf_op jit(solution)/shard_map/reduce_scatter | solution.py:839
  63.5 10.1 %collective-permute-start.10 = (bf16[128,1024]{1,0:T(8,128)(2,1)S(1)}, bf16[128,1024]{1,0:T(8,128)(2,1)S(1)}, u32[]{:S(2)}, u32[]{:S(2)}) collective-permute-start(bf16[128,1024]{1,0:T(8,128)(2,1)S(1)} %copy-done.5), channel_id=1, source_target_pairs={{0,2},{1,3},{2,0},{3,1},{4,6},{5,7},{6,4},{7,5},{8,10},{9,11},{10,... | collective-permute-start | bytes 786440 | tf_op jit(solution)/shard_map/ppermute | solution.py:127
  65.0 8.6 %collective-permute-start.11 = (bf16[128,1024]{1,0:T(8,128)(2,1)S(1)}, bf16[128,1024]{1,0:T(8,128)(2,1)S(1)}, u32[]{:S(2)}, u32[]{:S(2)}) collective-permute-start(bf16[128,1024]{1,0:T(8,128)(2,1)S(1)} %copy-done.5), channel_id=1, source_target_pairs={{0,4},{1,5},{2,6},{3,7},{4,0},{5,1},{6,2},{7,3},{8,12},{9,13},{10,... | collective-permute-start | bytes 786440 | tf_op jit(solution)/shard_map/ppermute | solution.py:127
  66.5 7.2 %collective-permute-start.12 = (bf16[128,1024]{1,0:T(8,128)(2,1)S(1)}, bf16[128,1024]{1,0:T(8,128)(2,1)S(1)}, u32[]{:S(2)}, u32[]{:S(2)}) collective-permute-start(bf16[128,1024]{1,0:T(8,128)(2,1)S(1)} %copy-done.5), channel_id=1, source_target_pairs={{0,1},{1,0},{2,3},{3,2},{4,5},{5,4},{6,7},{7,6},{8,9},{9,8},{10,11... | collective-permute-start | bytes 786440 | tf_op jit(solution)/shard_map/ppermute | solution.py:127
  66.5 7.1 %collective-permute-start.9 = (bf16[32,1024]{1,0:T(8,128)(2,1)S(1)}, bf16[32,1024]{1,0:T(8,128)(2,1)S(1)}, u32[]{:S(2)}, u32[]{:S(2)}) collective-permute-start(bf16[32,1024]{1,0:T(8,128)(2,1)S(1)} %collective-permute-done.7), channel_id=1, source_target_pairs={{0,8},{1,9},{2,10},{3,11},{4,12},{5,13},{6,14},{7,15},{8,16},{9,17... | collective-permute-start | bytes 196616 | tf_op jit(solution)/shard_map/ppermute | solution.py:127
  66.5 7.1 %collective-permute-start.13 = (bf16[16,1024]{1,0:T(8,128)(2,1)S(1)}, bf16[16,1024]{1,0:T(8,128)(2,1)S(1)}, u32[]{:S(2)}, u32[]{:S(2)}) collective-permute-start(bf16[16,1024]{1,0:T(8,128)(2,1)S(1)} %select_select_fusion), channel_id=1, source_target_pairs={{0,8},{1,9},{2,10},{3,11},{4,12},{5,13},{6,14},{7,15},{8,16},{9,17... | collective-permute-start | bytes 98312 | tf_op jit(solution)/shard_map/ppermute | solution.py:127
  73.7 8.2 %collective-permute-start.14 = (bf16[128,1024]{1,0:T(8,128)(2,1)S(1)}, bf16[128,1024]{1,0:T(8,128)(2,1)S(1)}, u32[]{:S(2)}, u32[]{:S(2)}) collective-permute-start(bf16[128,1024]{1,0:T(8,128)(2,1)S(1)} %pad_maximum_fusion.refs_8_.refs_0_), channel_id=1, source_target_pairs={{0,2},{1,3},{2,0},{3,1},{4,6},{5,7},{6,4},{7,5},{8,10},{9,11},{10,... | collective-permute-start | bytes 786440 | tf_op jit(solution)/shard_map/ppermute | solution.py:127
  74.3 7.7 %collective-permute-start.15 = (bf16[128,1024]{1,0:T(8,128)(2,1)S(1)}, bf16[128,1024]{1,0:T(8,128)(2,1)S(1)}, u32[]{:S(2)}, u32[]{:S(2)}) collective-permute-start(bf16[128,1024]{1,0:T(8,128)(2,1)S(1)} %pad_maximum_fusion.refs_8_.refs_0_), channel_id=1, source_target_pairs={{0,4},{1,5},{2,6},{3,7},{4,0},{5,1},{6,2},{7,3},{8,12},{9,13},{10,... | collective-permute-start | bytes 786440 | tf_op jit(solution)/shard_map/ppermute | solution.py:127
  74.8 7.2 %collective-permute-start.16 = (bf16[128,1024]{1,0:T(8,128)(2,1)S(1)}, bf16[128,1024]{1,0:T(8,128)(2,1)S(1)}, u32[]{:S(2)}, u32[]{:S(2)}) collective-permute-start(bf16[128,1024]{1,0:T(8,128)(2,1)S(1)} %pad_maximum_fusion.refs_8_.refs_0_), channel_id=1, source_target_pairs={{0,1},{1,0},{2,3},{3,2},{4,5},{5,4},{6,7},{7,6},{8,9},{9,8},{10,11... | collective-permute-start | bytes 786440 | tf_op jit(solution)/shard_map/ppermute | solution.py:127
  82.1 7.7 %collective-permute-start.17 = (bf16[128,1024]{1,0:T(8,128)(2,1)S(1)}, bf16[128,1024]{1,0:T(8,128)(2,1)S(1)}, u32[]{:S(2)}, u32[]{:S(2)}) collective-permute-start(bf16[128,1024]{1,0:T(8,128)(2,1)S(1)} %broadcast_select_fusion.2), channel_id=1, source_target_pairs={{0,2},{1,5},{2,0},{3,7},{4,6},{5,1},{6,4},{7,3},{8,10},{9,13},{10,... | collective-permute-start | bytes 786440 | tf_op jit(solution)/shard_map/ppermute | solution.py:127
  83.6 6.1 %collective-permute-start.18 = (bf16[128,1024]{1,0:T(8,128)(2,1)S(1)}, bf16[128,1024]{1,0:T(8,128)(2,1)S(1)}, u32[]{:S(2)}, u32[]{:S(2)}) collective-permute-start(bf16[128,1024]{1,0:T(8,128)(2,1)S(1)} %collective-permute-done.14.refs_10_.refs_2_), channel_id=1, source_target_pairs={{0,1},{1,0},{2,3},{3,2},{4,5},{5,4},{6,7},{7,6},{8,9},{9,8},{10,11... | collective-permute-start | bytes 786440 | tf_op jit(solution)/shard_map/ppermute | solution.py:127
  83.9 5.9 %collective-permute-start.19 = (bf16[128,1024]{1,0:T(8,128)(2,1)S(1)}, bf16[128,1024]{1,0:T(8,128)(2,1)S(1)}, u32[]{:S(2)}, u32[]{:S(2)}) collective-permute-start(bf16[128,1024]{1,0:T(8,128)(2,1)S(1)} %collective-permute-done.15.refs_12_.refs_4_), channel_id=1, source_target_pairs={{0,1},{1,0},{2,3},{3,2},{4,5},{5,4},{6,7},{7,6},{8,9},{9,8},{10,11... | collective-permute-start | bytes 786440 | tf_op jit(solution)/shard_map/ppermute | solution.py:127
  84.2 10.0 %collective-permute-start.20 = (bf16[1024,128]{1,0:T(8,128)(2,1)}, bf16[1024,128]{1,0:T(8,128)(2,1)S(1)}, u32[]{:S(2)}, u32[]{:S(2)}) collective-permute-start(bf16[1024,128]{1,0:T(8,128)(2,1)} %get-tuple-element.619.refs_0_), channel_id=1, source_target_pairs={{0,2},{1,3},{2,0},{3,1},{4,6},{5,7},{6,4},{7,5},{8,10},{9,11},{10,... | collective-permute-start | bytes 786440 | tf_op jit(solution)/shard_map/ppermute | solution.py:127
  85.4 8.8 %collective-permute-start.21 = (bf16[1024,128]{1,0:T(8,128)(2,1)}, bf16[1024,128]{1,0:T(8,128)(2,1)S(1)}, u32[]{:S(2)}, u32[]{:S(2)}) collective-permute-start(bf16[1024,128]{1,0:T(8,128)(2,1)} %get-tuple-element.619.refs_0_), channel_id=1, source_target_pairs={{0,4},{1,5},{2,6},{3,7},{4,0},{5,1},{6,2},{7,3},{8,12},{9,13},{10,... | collective-permute-start | bytes 786440 | tf_op jit(solution)/shard_map/ppermute | solution.py:127
  89.8 4.4 %collective-permute-start.22 = (bf16[1024,128]{1,0:T(8,128)(2,1)}, bf16[1024,128]{1,0:T(8,128)(2,1)S(1)}, u32[]{:S(2)}, u32[]{:S(2)}) collective-permute-start(bf16[1024,128]{1,0:T(8,128)(2,1)} %get-tuple-element.619.refs_0_), channel_id=1, source_target_pairs={{0,1},{1,0},{2,3},{3,2},{4,5},{5,4},{6,7},{7,6},{8,9},{9,8},{10,11... | collective-permute-start | bytes 786440 | tf_op jit(solution)/shard_map/ppermute | solution.py:127
  94.2 2.2 collective-permute-start.23
  94.3 6.4 %collective-permute-start.24 = (bf16[1024,128]{1,0:T(8,128)(2,1)S(1)}, bf16[1024,128]{1,0:T(8,128)(2,1)S(1)}, u32[]{:S(2)}, u32[]{:S(2)}) collective-permute-start(bf16[1024,128]{1,0:T(8,128)(2,1)S(1)} %broadcast_select_fusion), channel_id=1, source_target_pairs={{0,2},{1,5},{2,0},{3,7},{4,6},{5,1},{6,4},{7,3},{8,10},{9,13},{10,... | collective-permute-start | bytes 786440 | tf_op jit(solution)/shard_map/ppermute | solution.py:127
  95.8 4.9 %collective-permute-start.25 = (bf16[1024,128]{1,0:T(8,128)(2,1)S(1)}, bf16[1024,128]{1,0:T(8,128)(2,1)S(1)}, u32[]{:S(2)}, u32[]{:S(2)}) collective-permute-start(bf16[1024,128]{1,0:T(8,128)(2,1)S(1)} %collective-permute-done.20.refs_2_), channel_id=1, source_target_pairs={{0,1},{1,0},{2,3},{3,2},{4,5},{5,4},{6,7},{7,6},{8,9},{9,8},{10,11... | collective-permute-start | bytes 786440 | tf_op jit(solution)/shard_map/ppermute | solution.py:127
  96.0 4.7 %collective-permute-start.26 = (bf16[1024,128]{1,0:T(8,128)(2,1)S(1)}, bf16[1024,128]{1,0:T(8,128)(2,1)S(1)}, u32[]{:S(2)}, u32[]{:S(2)}) collective-permute-start(bf16[1024,128]{1,0:T(8,128)(2,1)S(1)} %collective-permute-done.21.refs_4_), channel_id=1, source_target_pairs={{0,1},{1,0},{2,3},{3,2},{4,5},{5,4},{6,7},{7,6},{8,9},{9,8},{10,11... | collective-permute-start | bytes 786440 | tf_op jit(solution)/shard_map/ppermute | solution.py:127
  102.3 9.7 %collective-permute-start.28 = (bf16[128,1024]{1,0:T(8,128)(2,1)S(1)}, bf16[128,1024]{1,0:T(8,128)(2,1)S(1)}, u32[]{:S(2)}, u32[]{:S(2)}) collective-permute-start(bf16[128,1024]{1,0:T(8,128)(2,1)S(1)} %broadcast_select_fusion.3), channel_id=1, source_target_pairs={{0,2},{1,5},{2,0},{3,7},{4,6},{5,1},{6,4},{7,3},{8,10},{9,13},{10,... | collective-permute-start | bytes 786440 | tf_op jit(solution)/shard_map/ppermute | solution.py:127
  103.8 8.2 %collective-permute-start.29 = (bf16[128,1024]{1,0:T(8,128)(2,1)S(1)}, bf16[128,1024]{1,0:T(8,128)(2,1)S(1)}, u32[]{:S(2)}, u32[]{:S(2)}) collective-permute-start(bf16[128,1024]{1,0:T(8,128)(2,1)S(1)} %collective-permute-done.10.refs_5_.refs_7_), channel_id=1, source_target_pairs={{0,1},{1,0},{2,3},{3,2},{4,5},{5,4},{6,7},{7,6},{8,9},{9,8},{10,11... | collective-permute-start | bytes 786440 | tf_op jit(solution)/shard_map/ppermute | solution.py:127
  103.9 8.2 %collective-permute-start.30 = (bf16[128,1024]{1,0:T(8,128)(2,1)S(1)}, bf16[128,1024]{1,0:T(8,128)(2,1)S(1)}, u32[]{:S(2)}, u32[]{:S(2)}) collective-permute-start(bf16[128,1024]{1,0:T(8,128)(2,1)S(1)} %collective-permute-done.11.refs_6_.refs_8_), channel_id=1, source_target_pairs={{0,1},{1,0},{2,3},{3,2},{4,5},{5,4},{6,7},{7,6},{8,9},{9,8},{10,11... | collective-permute-start | bytes 786440 | tf_op jit(solution)/shard_map/ppermute | solution.py:127
  127.6 80.4 %reduce-scatter.5.cloned.1.call-start = ((), (), s32[]{:S(2)}) async-start(), calls=%async_computation.9 | async-start | bytes 1474560 | tf_op jit(solution)/shard_map/reduce_scatter | solution.py:839
  128.7 3.6 %collective-permute-start.32 = (bf16[512,1024]{1,0:T(8,128)(2,1)S(1)}, bf16[512,1024]{1,0:T(8,128)(2,1)S(1)}, u32[]{:S(2)}, u32[]{:S(2)}) collective-permute-start(bf16[512,1024]{1,0:T(8,128)(2,1)S(1)} %copy-done.63), channel_id=1, source_target_pairs={{0,1},{1,0},{2,3},{3,2},{4,5},{5,4},{6,7},{7,6},{8,9},{9,8},{10,11... | collective-permute-start | bytes 3145736 | tf_op jit(solution)/shard_map/ppermute | solution.py:127
  132.3 5.8 %collective-permute-start.33 = (bf16[512,1024]{1,0:T(8,128)(2,1)}, bf16[512,1024]{1,0:T(8,128)(2,1)S(1)}, u32[]{:S(2)}, u32[]{:S(2)}) collective-permute-start(bf16[512,1024]{1,0:T(8,128)(2,1)} %ffn_output.1), channel_id=1, source_target_pairs={{0,1},{1,0},{2,3},{3,2},{4,5},{5,4},{6,7},{7,6},{8,9},{9,8},{10,11... | collective-permute-start | bytes 3145736 | tf_op jit(solution)/shard_map/ppermute | solution.py:127
  138.2 12.0 %collective-permute-start.34 = (bf16[128,1024]{1,0:T(8,128)(2,1)}, bf16[128,1024]{1,0:T(8,128)(2,1)S(1)}, u32[]{:S(2)}, u32[]{:S(2)}) collective-permute-start(bf16[128,1024]{1,0:T(8,128)(2,1)} %get-tuple-element.522), channel_id=1, source_target_pairs={{0,6},{1,7},{2,4},{3,5},{4,2},{5,3},{6,0},{7,1},{8,14},{9,15},{10,... | collective-permute-start | bytes 786440 | tf_op jit(solution)/shard_map/ppermute | solution.py:127
  139.7 13.9 %collective-permute-start.35 = (bf16[128,1024]{1,0:T(8,128)(2,1)}, bf16[128,1024]{1,0:T(8,128)(2,1)S(1)}, u32[]{:S(2)}, u32[]{:S(2)}) collective-permute-start(bf16[128,1024]{1,0:T(8,128)(2,1)} %get-tuple-element.523), channel_id=1, source_target_pairs={{0,2},{1,3},{2,0},{3,1},{4,6},{5,7},{6,4},{7,5},{8,10},{9,11},{10,... | collective-permute-start | bytes 786440 | tf_op jit(solution)/shard_map/ppermute | solution.py:127
  141.2 12.4 %collective-permute-start.36 = (bf16[128,1024]{1,0:T(8,128)(2,1)}, bf16[128,1024]{1,0:T(8,128)(2,1)S(1)}, u32[]{:S(2)}, u32[]{:S(2)}) collective-permute-start(bf16[128,1024]{1,0:T(8,128)(2,1)} %get-tuple-element.524), channel_id=1, source_target_pairs={{0,4},{1,5},{2,6},{3,7},{4,0},{5,1},{6,2},{7,3},{8,12},{9,13},{10,... | collective-permute-start | bytes 786440 | tf_op jit(solution)/shard_map/ppermute | solution.py:127
  159.3 12.9 %collective-permute-start.37 = (bf16[128,1024]{1,0:T(8,128)(2,1)}, bf16[128,1024]{1,0:T(8,128)(2,1)S(1)}, u32[]{:S(2)}, u32[]{:S(2)}) collective-permute-start(bf16[128,1024]{1,0:T(8,128)(2,1)} %get-tuple-element.620.refs_1_), channel_id=1, source_target_pairs={{0,2},{1,3},{2,0},{3,1},{4,6},{5,7},{6,4},{7,5},{8,10},{9,11},{10,... | collective-permute-start | bytes 786440 | tf_op jit(solution)/shard_map/ppermute | solution.py:127
  160.3 12.0 %collective-permute-start.38 = (bf16[128,1024]{1,0:T(8,128)(2,1)}, bf16[128,1024]{1,0:T(8,128)(2,1)S(1)}, u32[]{:S(2)}, u32[]{:S(2)}) collective-permute-start(bf16[128,1024]{1,0:T(8,128)(2,1)} %get-tuple-element.620.refs_1_), channel_id=1, source_target_pairs={{0,4},{1,5},{2,6},{3,7},{4,0},{5,1},{6,2},{7,3},{8,12},{9,13},{10,... | collective-permute-start | bytes 786440 | tf_op jit(solution)/shard_map/ppermute | solution.py:127
  161.2 11.0 %collective-permute-start.39 = (bf16[128,1024]{1,0:T(8,128)(2,1)}, bf16[128,1024]{1,0:T(8,128)(2,1)S(1)}, u32[]{:S(2)}, u32[]{:S(2)}) collective-permute-start(bf16[128,1024]{1,0:T(8,128)(2,1)} %get-tuple-element.620.refs_1_), channel_id=1, source_target_pairs={{0,1},{1,0},{2,3},{3,2},{4,5},{5,4},{6,7},{7,6},{8,9},{9,8},{10,11... | collective-permute-start | bytes 786440 | tf_op jit(solution)/shard_map/ppermute | solution.py:127
  175.8 8.5 %collective-permute-start.40 = (bf16[128,1024]{1,0:T(8,128)(2,1)S(1)}, bf16[128,1024]{1,0:T(8,128)(2,1)S(1)}, u32[]{:S(2)}, u32[]{:S(2)}) collective-permute-start(bf16[128,1024]{1,0:T(8,128)(2,1)S(1)} %copy-done.64), channel_id=1, source_target_pairs={{0,6},{1,7},{2,4},{3,5},{4,2},{5,3},{6,0},{7,1},{8,14},{9,15},{10,... | collective-permute-start | bytes 786440 | tf_op jit(solution)/shard_map/ppermute | solution.py:127
  177.0 9.1 %collective-permute-start.41 = (bf16[128,1024]{1,0:T(8,128)(2,1)S(1)}, bf16[128,1024]{1,0:T(8,128)(2,1)S(1)}, u32[]{:S(2)}, u32[]{:S(2)}) collective-permute-start(bf16[128,1024]{1,0:T(8,128)(2,1)S(1)} %broadcast_select_fusion.1), channel_id=1, source_target_pairs={{0,2},{1,5},{2,0},{3,7},{4,6},{5,1},{6,4},{7,3},{8,10},{9,13},{10,... | collective-permute-start | bytes 786440 | tf_op jit(solution)/shard_map/ppermute | solution.py:127
  177.9 8.2 %collective-permute-start.42 = (bf16[128,1024]{1,0:T(8,128)(2,1)S(1)}, bf16[128,1024]{1,0:T(8,128)(2,1)S(1)}, u32[]{:S(2)}, u32[]{:S(2)}) collective-permute-start(bf16[128,1024]{1,0:T(8,128)(2,1)S(1)} %collective-permute-done.37.refs_3_), channel_id=1, source_target_pairs={{0,1},{1,0},{2,3},{3,2},{4,5},{5,4},{6,7},{7,6},{8,9},{9,8},{10,11... | collective-permute-start | bytes 786440 | tf_op jit(solution)/shard_map/ppermute | solution.py:127
  177.9 8.2 %collective-permute-start.43 = (bf16[128,1024]{1,0:T(8,128)(2,1)S(1)}, bf16[128,1024]{1,0:T(8,128)(2,1)S(1)}, u32[]{:S(2)}, u32[]{:S(2)}) collective-permute-start(bf16[128,1024]{1,0:T(8,128)(2,1)S(1)} %collective-permute-done.38.refs_5_), channel_id=1, source_target_pairs={{0,1},{1,0},{2,3},{3,2},{4,5},{5,4},{6,7},{7,6},{8,9},{9,8},{10,11... | collective-permute-start | bytes 786440 | tf_op jit(solution)/shard_map/ppermute | solution.py:127
  178.4 5.7 %collective-permute-start.44 = (f32[8,128]{1,0:T(8,128)}, f32[8,128]{1,0:T(8,128)S(1)}, u32[]{:S(2)}, u32[]{:S(2)}) collective-permute-start(f32[8,128]{1,0:T(8,128)} %get-tuple-element.589), channel_id=1, source_target_pairs={{8,0},{9,1},{10,2},{11,3},{12,4},{13,5},{14,6},{15,7},{16,8},{17,9... | collective-permute-start | bytes 12296 | tf_op jit(solution)/shard_map/ppermute | solution.py:127
  186.1 7.2 %collective-permute-start.45 = (bf16[128,1024]{1,0:T(8,128)(2,1)S(1)}, bf16[128,1024]{1,0:T(8,128)(2,1)S(1)}, u32[]{:S(2)}, u32[]{:S(2)}) collective-permute-start(bf16[128,1024]{1,0:T(8,128)(2,1)S(1)} %collective-permute-done.41.refs_7_), channel_id=1, source_target_pairs={{0,1},{1,0},{2,3},{3,2},{4,5},{5,4},{6,7},{7,6},{8,9},{9,8},{10,11... | collective-permute-start | bytes 786440 | tf_op jit(solution)/shard_map/ppermute | solution.py:127
  193.3 14.5 %collective-permute-start.47 = (bf16[512,1024]{1,0:T(8,128)(2,1)}, bf16[512,1024]{1,0:T(8,128)(2,1)S(1)}, u32[]{:S(2)}, u32[]{:S(2)}) collective-permute-start(bf16[512,1024]{1,0:T(8,128)(2,1)} %get-tuple-element.618), channel_id=1, source_target_pairs={{0,1},{1,0},{2,3},{3,2},{4,5},{5,4},{6,7},{7,6},{8,9},{9,8},{10,11... | collective-permute-start | bytes 3145736 | tf_op jit(solution)/shard_map/ppermute | solution.py:127
  193.6 14.2 %all-to-all-start.3 = ((bf16[8,32,1152]{2,1,0:T(8,128)(2,1)}), bf16[8,32,1152]{2,1,0:T(8,128)(2,1)S(1)}, u32[]{:S(2)}, u32[]{:S(2)}) async-start(bf16[8,32,1152]{2,1,0:T(8,128)(2,1)} %bitcast.44), calls=%async_computation.4 | async-start | bytes 1179648 | tf_op jit(solution)/shard_map/all_to_all | solution.py:180
  197.1 10.7 %collective-permute-start.46 = (bf16[256,384]{1,0:T(8,128)(2,1)}, bf16[256,384]{1,0:T(8,128)(2,1)S(1)}, u32[]{:S(2)}, u32[]{:S(2)}) collective-permute-start(bf16[256,384]{1,0:T(8,128)(2,1)} %get-tuple-element.616), channel_id=1, source_target_pairs={{0,8},{1,9},{2,10},{3,11},{4,12},{5,13},{6,14},{7,15},{8,16},{9,17... | collective-permute-start | bytes 589832 | tf_op jit(solution)/shard_map/ppermute | solution.py:127
  207.9 13.1 %collective-permute-start.48 = (bf16[128,1024]{1,0:T(8,128)(2,1)}, bf16[128,1024]{1,0:T(8,128)(2,1)S(1)}, u32[]{:S(2)}, u32[]{:S(2)}) collective-permute-start(bf16[128,1024]{1,0:T(8,128)(2,1)} %get-tuple-element.640), channel_id=1, source_target_pairs={{0,2},{1,3},{2,0},{3,1},{4,6},{5,7},{6,4},{7,5},{8,10},{9,11},{10,... | collective-permute-start | bytes 786440 | tf_op jit(solution)/shard_map/ppermute | solution.py:127
  209.5 11.5 %collective-permute-start.49 = (bf16[128,1024]{1,0:T(8,128)(2,1)}, bf16[128,1024]{1,0:T(8,128)(2,1)}, u32[]{:S(2)}, u32[]{:S(2)}) collective-permute-start(bf16[128,1024]{1,0:T(8,128)(2,1)} %get-tuple-element.641), channel_id=1, source_target_pairs={{0,4},{1,5},{2,6},{3,7},{4,0},{5,1},{6,2},{7,3},{8,12},{9,13},{10,... | collective-permute-start | bytes 786440 | tf_op jit(solution)/shard_map/ppermute | solution.py:127
  210.9 10.1 %collective-permute-start.50 = (bf16[256,384]{1,0:T(8,128)(2,1)S(1)}, bf16[256,384]{1,0:T(8,128)(2,1)S(1)}, u32[]{:S(2)}, u32[]{:S(2)}) collective-permute-start(bf16[256,384]{1,0:T(8,128)(2,1)S(1)} %add_convert_fusion.3), channel_id=1, source_target_pairs={{0,8},{1,9},{2,10},{3,11},{4,12},{5,13},{6,14},{7,15},{8,16},{9,17... | collective-permute-start | bytes 589832 | tf_op jit(solution)/shard_map/ppermute | solution.py:127
  210.9 10.0 %collective-permute-start.51 = (bf16[48,1024]{1,0:T(8,128)(2,1)}, bf16[48,1024]{1,0:T(8,128)(2,1)S(1)}, u32[]{:S(2)}, u32[]{:S(2)}) collective-permute-start(bf16[48,1024]{1,0:T(8,128)(2,1)} %get-tuple-element.650), channel_id=1, source_target_pairs={{0,8},{1,9},{2,10},{3,11},{4,12},{5,13},{6,14},{7,15},{8,16},{9,17... | collective-permute-start | bytes 294920 | tf_op jit(solution)/shard_map/ppermute | solution.py:127
  222.9 9.2 %collective-permute-start.55 = (bf16[256,384]{1,0:T(8,128)(2,1)S(1)}, bf16[256,384]{1,0:T(8,128)(2,1)S(1)}, u32[]{:S(2)}, u32[]{:S(2)}) collective-permute-start(bf16[256,384]{1,0:T(8,128)(2,1)S(1)} %add_convert_fusion.2), channel_id=1, source_target_pairs={{0,8},{1,9},{2,10},{3,11},{4,12},{5,13},{6,14},{7,15},{8,16},{9,17... | collective-permute-start | bytes 589832 | tf_op jit(solution)/shard_map/ppermute | solution.py:127
  223.0 9.1 %collective-permute-start.56 = (bf16[48,1024]{1,0:T(8,128)(2,1)S(1)}, bf16[48,1024]{1,0:T(8,128)(2,1)S(1)}, u32[]{:S(2)}, u32[]{:S(2)}) collective-permute-start(bf16[48,1024]{1,0:T(8,128)(2,1)S(1)} %add_convert_fusion.5), channel_id=1, source_target_pairs={{0,8},{1,9},{2,10},{3,11},{4,12},{5,13},{6,14},{7,15},{8,16},{9,17... | collective-permute-start | bytes 294920 | tf_op jit(solution)/shard_map/ppermute | solution.py:127
  223.9 17.7 %collective-permute-start.52 = (bf16[128,1024]{1,0:T(8,128)(2,1)}, bf16[128,1024]{1,0:T(8,128)(2,1)S(1)}, u32[]{:S(2)}, u32[]{:S(2)}) collective-permute-start(bf16[128,1024]{1,0:T(8,128)(2,1)} %get-tuple-element.659), channel_id=1, source_target_pairs={{0,6},{1,7},{2,4},{3,5},{4,2},{5,3},{6,0},{7,1},{8,14},{9,15},{10,... | collective-permute-start | bytes 786440 | tf_op jit(solution)/shard_map/ppermute | solution.py:127
  224.5 17.1 %collective-permute-start.53 = (bf16[128,1024]{1,0:T(8,128)(2,1)}, bf16[128,1024]{1,0:T(8,128)(2,1)S(1)}, u32[]{:S(2)}, u32[]{:S(2)}) collective-permute-start(bf16[128,1024]{1,0:T(8,128)(2,1)} %get-tuple-element.660), channel_id=1, source_target_pairs={{0,2},{1,3},{2,0},{3,1},{4,6},{5,7},{6,4},{7,5},{8,10},{9,11},{10,... | collective-permute-start | bytes 786440 | tf_op jit(solution)/shard_map/ppermute | solution.py:127
  225.9 15.7 %collective-permute-start.54 = (bf16[128,1024]{1,0:T(8,128)(2,1)}, bf16[128,1024]{1,0:T(8,128)(2,1)S(1)}, u32[]{:S(2)}, u32[]{:S(2)}) collective-permute-start(bf16[128,1024]{1,0:T(8,128)(2,1)} %get-tuple-element.661), channel_id=1, source_target_pairs={{0,4},{1,5},{2,6},{3,7},{4,0},{5,1},{6,2},{7,3},{8,12},{9,13},{10,... | collective-permute-start | bytes 786440 | tf_op jit(solution)/shard_map/ppermute | solution.py:127
  232.8 8.8 %collective-permute-start.57 = (bf16[48,1024]{1,0:T(8,128)(2,1)S(1)}, bf16[48,1024]{1,0:T(8,128)(2,1)}, u32[]{:S(2)}, u32[]{:S(2)}) collective-permute-start(bf16[48,1024]{1,0:T(8,128)(2,1)S(1)} %add_convert_fusion.4), channel_id=1, source_target_pairs={{0,8},{1,9},{2,10},{3,11},{4,12},{5,13},{6,14},{7,15},{8,16},{9,17... | collective-permute-start | bytes 294920 | tf_op jit(solution)/shard_map/ppermute | solution.py:127
  232.9 9.6 %all-to-all-start.4 = ((bf16[8,32,384]{2,1,0:T(8,128)(2,1)}), bf16[8,32,384]{2,1,0:T(8,128)(2,1)S(1)}, u32[]{:S(2)}, u32[]{:S(2)}) async-start(bf16[8,32,384]{2,1,0:T(8,128)(2,1)} %bitcast.13), calls=%async_computation.6 | async-start | bytes 393216 | tf_op jit(solution)/shard_map/all_to_all | solution.py:180
  (72 other events, 777.0 us)
Sparse Core Ops, SparseCore 0:
  9.6 37.1 all-gather.5
  62.7 49.5 all-gather.3
  127.7 45.3 reduce-scatter.2
  175.3 29.1 reduce-scatter.4

commit v5 on v4

--- a/solution.py
+++ b/solution.py
@@ -37,7 +37,7 @@
         kernel,
         out_shape=out_shape,
         scratch_shapes=list(scratch),
-        compiler_params=pltpu.CompilerParams(vmem_limit_bytes=56 * 2**20),
+        compiler_params=pltpu.CompilerParams(vmem_limit_bytes=52 * 2**20),
         cost_estimate=pl.CostEstimate(flops=flops, bytes_accessed=size, transcendentals=0),
         name=name,
         **places,
@@ -83,9 +83,9 @@
             return [(i, i ^ (2 if i % 2 == 0 else 4)) for i in range(self.count)]
         return [(i, i - TEAM) for i in range(TEAM, self.count)]
 
-    def do(self, call, *operands):
+    def do(self, call, *operands, span=1):
         def steps():
-            (got,) = yield [(operands, ("call", call))]
+            (got,) = yield [(operands, ("call", call), span)]
             return got
 
         return self.spawn(steps())
@@ -957,7 +957,7 @@
         )
     )
     in_job = net.spawn(net.line_sum(shares))
-    pair_job = net.do(net.exchange, pair_sum.reshape(TEAM, part, 2 * ffown))
+    pair_job = net.do(net.exchange, pair_sum.reshape(TEAM, part, 2 * ffown), span=2)
     normed_job = net.spawn(
         net.team_sum(
             normed_odd,

time: 256 us -> 256 us (level)
  Pallas kernels: 74.2 us -> 62.2 us
  local copies, waits for them, and re-layouts: 7.75 us -> 17.9 us
  other arithmetic: 8.11 us -> 12.3 us
  blocking collectives: 35 us -> 31.1 us
    pallas_call x16, Pallas kernels: 74.2 us -> 62.2 us  [call(): pl.pallas_call(kernel, out_shape=out_shape, scratch_shapes=list(scratch),...]
    unnamed x141 -> x125, local copies, waits for them, and re-layouts: 5.65 us -> 17 us
    reduce_scatter x2, waiting for transfers between devices: 0.04 us -> 2.85 us  [reduce(): lax.psum_scatter(value, 'dp', scatter_dimension=0, tiled=True, axis_index...]
    ppermute x58, waiting for transfers between devices: 48.4 us -> 45.8 us  [one_step(): got.append(lax.ppermute(values[at], 'dp', self.pairs(move[1])))]
    all_gather x1, blocking collectives: 24 us -> 21.5 us  [gather(): lax.all_gather(value, 'dp', axis=0, tiled=True, axis_index_groups=line)]
  transfers between devices with their start and end apart: 66 -> 66, of which waited for: 15 -> 18; matrix products, arithmetic and copies ran while one was open for 2% -> 3% of each run, Pallas kernels for 23% -> 19%
where the time goes in v5:
time: 256 us; the launch traced here: 254 us
  Pallas kernels  62.2 us (24%)
  waiting for transfers between devices  59 us (23%)
  starting transfers between devices  57 us (22%)
  blocking collectives  31.1 us (12%)
  local copies, waits for them, and re-layouts  17.9 us (7%)
  between operations  14.6 us (6%)
  other arithmetic  12.3 us (5%)
    pallas_call x16, Pallas kernels, call(): pl.pallas_call(kernel, out_shape=out_shape, scratch_shapes=list(scratch),...  62.2 us
    ppermute x58, waiting for transfers between devices, one_step(): got.append(lax.ppermute(values[at], 'dp', self.pairs(move[1])))  45.8 us
    ppermute x58, starting transfers between devices, one_step(): got.append(lax.ppermute(values[at], 'dp', self.pairs(move[1])))  41.8 us
    all_gather x1, blocking collectives, gather(): lax.all_gather(value, 'dp', axis=0, tiled=True, axis_index_groups=line)  21.5 us
    unnamed x125, local copies, waits for them, and re-layouts  17 us
    all_to_all x4, starting transfers between devices, exchange(): lax.all_to_all(blocks, 'dp', 0, 0, axis_index_groups=groups, tiled=True)  15.1 us
    all_to_all x1, blocking collectives, exchange(): lax.all_to_all(blocks, 'dp', 0, 0, axis_index_groups=groups, tiled=True)  9.67 us
    all_to_all x4, waiting for transfers between devices, exchange(): lax.all_to_all(blocks, 'dp', 0, 0, axis_index_groups=groups, tiled=True)  9.63 us
  transfers between devices with their start and end apart: 66, of which 18 were waited for; matrix products, arithmetic and copies ran while one was open for 3% of the time, Pallas kernels for 19%

profile of v5, /device:TPU:0, one launch (start us, length us, event | category | flops | bytes accessed | tf_op | source)
XLA Modules:
  0.0 254.2 jit_solution(2575178084518760545)
XLA Ops:
  11.5 1.0 in_prepare.1
  12.5 2.9 %collective-permute-start = (bf16[128,1024]{1,0:T(8,128)(2,1)}, bf16[128,1024]{1,0:T(8,128)(2,1)S(1)}, u32[]{:S(2)}, u32[]{:S(2)}) collective-permute-start(bf16[128,1024]{1,0:T(8,128)(2,1)} %refs_16_), channel_id=1, source_target_pairs={{0,2},{1,3},{2,0},{3,1},{4,6},{5,7},{6,4},{7,5},{8,10},{9,11},{10,... | collective-permute-start | bytes 786440 | tf_op jit(solution)/shard_map/ppermute | solution.py:127
  15.4 1.5 collective-permute-start.1
  16.9 4.3 %all-to-all-start = ((bf16[8,40,384]{2,1,0:T(8,128)(2,1)}), bf16[8,40,384]{2,1,0:T(8,128)(2,1)S(1)}, u32[]{:S(2)}, u32[]{:S(2)}) async-start(bf16[8,40,384]{2,1,0:T(8,128)(2,1)} %in_prepare.1), calls=%async_computation | async-start | bytes 491520 | tf_op jit(solution)/shard_map/all_to_all | solution.py:180
  23.2 1.2 pair_prepare.1
  24.4 7.2 %all-to-all-done = bf16[8,40,384]{2,1,0:T(8,128)(2,1)S(1)} async-done(((bf16[8,40,384]{2,1,0:T(8,128)(2,1)}), bf16[8,40,384]{2,1,0:T(8,128)(2,1)S(1)}, u32[]{:S(2)}, u32[]{:S(2)}) %all-to-all-start) | async-done | bytes 245792 | tf_op jit(solution)/shard_map/all_to_all | solution.py:180
  31.7 3.7 %all-to-all-start.1 = ((bf16[8,32,1152]{2,1,0:T(8,128)(2,1)}), bf16[8,32,1152]{2,1,0:T(8,128)(2,1)S(1)}, u32[]{:S(2)}, u32[]{:S(2)}) async-start(bf16[8,32,1152]{2,1,0:T(8,128)(2,1)} %pair_prepare.1), calls=%async_computation.1 | async-start | bytes 1179648 | tf_op jit(solution)/shard_map/all_to_all | solution.py:180
  36.3 1.6 collective-permute-start.7
  37.9 2.2 collective-permute-start.8
  40.2 21.5 %all_gather.9 = bf16[1280,384]{1,0:T(8,128)(2,1)} all-gather(bf16[320,384]{1,0:T(8,128)(2,1)S(1)} %bitcast.49), channel_id=1, replica_groups={{0,8,16,24},{1,9,17,25},{2,10,18,26},{3,11,19,27},{4,12,20,28},{5,13,21..., dimensions={0}, use_global_device_ids=true | all-gather | bytes 1228800 | tf_op jit(solution)/shard_map/all_gather | solution.py:836
  62.8 1.6 collective-permute-start.10
  64.4 1.5 collective-permute-start.11
  65.9 1.5 collective-permute-start.13
  67.4 5.6 %collective-permute-done.13.refs_8_ = bf16[16,1024]{1,0:T(8,128)(2,1)S(1)} collective-permute-done((bf16[16,1024]{1,0:T(8,128)(2,1)S(1)}, bf16[16,1024]{1,0:T(8,128)(2,1)S(1)}, u32[]{:S(2)}, u32[]{:S(2)}) %collective-permute-start.13) | collective-permute-done | bytes 32800 | tf_op jit(solution)/shard_map/ppermute | solution.py:127
  74.9 6.6 %mixer_forward.1 = (bf16[1040,1024]{1,0:T(8,128)(2,1)}, f32[1040,384]{1,0:T(8,128)}, f32[1040,128]{1,0:T(8,128)}, f32[1024,128]{1,0:T(8,128)}, bf16[1024,128]{1,...) custom-call(bf16[128,1024]{1,0:T(8,128)(2,1)S(1)} %copy-done, ...), custom_call_target="tpu_custom_call" | custom-call | flops 805306368 | bytes 3112960 | tf_op jit(solution)/shard_map/mixer_forward/pallas_call | solution.py:36
  82.1 1.0 broadcast_select_fusion.2
  83.1 1.5 collective-permute-start.17
  85.7 1.1 collective-permute-start.21
  86.8 4.5 %collective-permute-done.17.refs_14_.refs_6_ = bf16[128,1024]{1,0:T(8,128)(2,1)S(1)} collective-permute-done((bf16[128,1024]{1,0:T(8,128)(2,1)S(1)}, bf16[128,1024]{1,0:T(8,128)(2,1)S(1)}, u32[]{:S(2)}, u32[]{:S(2)}) %collective-permute-start.17) | collective-permute-done | bytes 262176 | tf_op jit(solution)/shard_map/ppermute | solution.py:127
  91.4 3.8 %collective-permute-done.20.refs_2_ = bf16[1024,128]{1,0:T(8,128)(2,1)S(1)} collective-permute-done((bf16[1024,128]{1,0:T(8,128)(2,1)S(1)}, bf16[1024,128]{1,0:T(8,128)(2,1)S(1)}, u32[]{:S(2)}, u32[]{:S(2)}) %collective-permute-start.20) | collective-permute-done | bytes 262176 | tf_op jit(solution)/shard_map/ppermute | solution.py:127
  95.3 1.5 collective-permute-start.24
  97.4 4.4 %collective-permute-done.24.refs_6_ = bf16[1024,128]{1,0:T(8,128)(2,1)S(1)} collective-permute-done((bf16[1024,128]{1,0:T(8,128)(2,1)S(1)}, bf16[1024,128]{1,0:T(8,128)(2,1)S(1)}, u32[]{:S(2)}, u32[]{:S(2)}) %collective-permute-start.24) | collective-permute-done | bytes 262176 | tf_op jit(solution)/shard_map/ppermute | solution.py:127
  101.8 1.5 collective-permute-done.27.refs_7_
  103.3 1.5 collective-permute-start.28
  105.3 6.5 %out_project.1 = (f32[128,1024]{1,0:T(8,128)}, bf16[512,1024]{1,0:T(8,128)(2,1)}, bf16[512,1024]{1,0:T(8,128)(2,1)}) custom-call(bf16[1024,128]{1,0:T(8,128)(2,1)S(1)} %get-tuple-element.619.refs_0_, bf16[1024,128]{1,0:T(8,128)(2,1)S(1)} %collective-permute-done.22.refs_1_, bf16[1024,128]{1,0:T(8,128)(2,1)S(1)} %collective-permute-done.20.refs_2_, ...), custom_call_target="tpu_custom_call" | custom-call | flops 2147483648 | bytes 6295552 | tf_op jit(solution)/shard_map/out_project/pallas_call | solution.py:36
  112.5 1.5 collective-permute-done.31.refs_3_.refs_5_
  114.1 12.9 %ffn.1 = (bf16[512,576]{1,0:T(8,128)(2,1)}, bf16[512,576]{1,0:T(8,128)(2,1)}, bf16[512,1152]{1,0:T(8,128)(2,1)}, bf16[512,1152]{1,0:T(8,128)(2,1)}, bf16[1024,11...) custom-call(bf16[512,1024]{1,0:T(8,128)(2,1)} %get-tuple-element.482.odd_in, bf16[512,1024]{1,0:T(8,128)(2,1)} %get-tuple-element.483.even_in, ...), custom_call_target="tpu_custom_call" | custom-call | flops 6039797760 | bytes 7733248 | tf_op jit(solution)/shard_map/ffn/pallas_call | solution.py:36
  128.8 2.3 ffn_output.1
  132.1 4.7 %ffn_back.1 = (f32[128,1024]{1,0:T(8,128)S(1)}, bf16[128,1024]{1,0:T(8,128)(2,1)}, bf16[128,1024]{1,0:T(8,128)(2,1)}, bf16[128,1024]{1,0:T(8,128)(2,1)}) custom-call(bf16[512,1152]{1,0:T(8,128)(2,1)} %get-tuple-element.509.left_in, bf16[1024,1152]{1,0:T(8,128)(2,1)} %all-gather.4.cloned.1.call-done.refs_8_.right_in, bf16[512,1024]{1,0:T(8,128)(2,1)} %copy-done.45), custom_call_target="tpu_custom_call" | custom-call | flops 1207959552 | bytes 4587520 | tf_op jit(solution)/shard_map/ffn_back/pallas_call | solution.py:36
  137.6 1.3 collective-permute-start.34
  138.9 1.3 collective-permute-start.35
  141.1 2.6 %ffn_output_sum.1 = (f32[128,1024]{1,0:T(8,128)S(1)}, bf16[128,1024]{1,0:T(8,128)(2,1)S(1)}, bf16[128,1024]{1,0:T(8,128)(2,1)S(1)}, bf16[128,1024]{1,0:T(8,128)(2,1)S(1)}) custom-call(bf16[512,576]{1,0:T(8,128)(2,1)S(1)} %copy-done.3, bf16[576,1024]{1,0:T(8,128)(2,1)} %bitcast.46, bf16[512,1024]{1,0:T(8,128)(2,1)} %copy-done.44), custom_call_target="tpu_custom_call" | custom-call | flops 603979776 | bytes 2818048 | tf_op jit(solution)/shard_map/ffn_output_sum/pallas_call | solution.py:36
  145.1 4.2 %down_grads.1 = bf16[576,1024]{1,0:T(8,128)(2,1)} custom-call(bf16[512,576]{1,0:T(8,128)(2,1)} %get-tuple-element.532.left.refs_0_, bf16[512,576]{1,0:T(8,128)(2,1)} %get-tuple-element.533.left_in.refs_1_, bf16[128,1024]{1,0:T(8,128)(2,1)S(1)} %collective-permute-done.12.refs_0_.refs_2_, bf16[128,1024]{1,0:T(8,128)(2,1)S(1)} %collective-permute-done.29.refs_1_.refs_3_, ...), custom_call_target="tpu_custom_call" | custom-call | flops 1207959552 | bytes 3276800 | tf_op jit(solution)/shard_map/down_grads/pallas_call | solution.py:36
  149.3 3.2 %collective-permute-done.35.across = bf16[128,1024]{1,0:T(8,128)(2,1)} collective-permute-done((bf16[128,1024]{1,0:T(8,128)(2,1)}, bf16[128,1024]{1,0:T(8,128)(2,1)}, u32[]{:S(2)}, u32[]{:S(2)}) %collective-permute-start.35) | collective-permute-done | bytes 262176 | tf_op jit(solution)/shard_map/ppermute | solution.py:127
  152.8 4.6 %resid_back.1 = (f32[128,1024]{1,0:T(8,128)}, bf16[128,1024]{1,0:T(8,128)(2,1)S(1)}, bf16[8,128,128]{2,1,0:T(8,128)(2,1)S(1)}) custom-call(f32[128,1024]{1,0:T(8,128)} %copy-done.15, bf16[128,1024]{1,0:T(8,128)(2,1)} %collective-permute-done.34.corner, bf16[128,1024]{1,0:T(8,128)(2,1)} %collective-permute-done.35.across, ...), custom_call_target="tpu_custom_call" | custom-call | flops 268435456 | bytes 4198400 | tf_op jit(solution)/shard_map/resid_back/pallas_call | solution.py:36
  158.4 1.1 collective-permute-start.38
  159.5 9.7 %all_to_all.25 = bf16[8,128,128]{2,1,0:T(8,128)(2,1)S(1)} all-to-all(bf16[8,128,128]{2,1,0:T(8,128)(2,1)S(1)} %get-tuple-element.571), channel_id=1, replica_groups={{0,1,2,3,4,5,6,7},{8,9,10,11,12,13,14,15},{16,17,18,19,20,21,22,23},{24..., dimensions={0} | all-to-all | bytes 524288 | tf_op jit(solution)/shard_map/all_to_all | solution.py:180
  169.2 2.1 conv_back.1
  171.4 1.8 collective-permute-start.40
  174.6 1.3 collective-permute-start.44
  175.9 4.2 %collective-permute-done.44.refs_1_ = f32[8,128]{1,0:T(8,128)S(1)} collective-permute-done((f32[8,128]{1,0:T(8,128)S(1)}, f32[8,128]{1,0:T(8,128)S(1)}, u32[]{:S(2)}, u32[]{:S(2)}) %collective-permute-start.44) | collective-permute-done | bytes 4128 | tf_op jit(solution)/shard_map/ppermute | solution.py:127
  180.1 2.3 collective-permute-done.41.refs_7_
  183.3 5.8 %mixer_back.1 = (bf16[1024,384]{1,0:T(8,128)(2,1)}, bf16[512,1024]{1,0:T(8,128)(2,1)}, f32[256,384]{1,0:T(8,128)S(1)}, f32[256,384]{1,0:T(8,128)S(1)}, f32[256,384]{1,0:T(8,128)S(1)}, /*index=5*/bf16[256,384]{1,0:T(8,128)(2,1)}) custom-call(f32[1024,128]{1,0:T(8,128)} %copy-done.16, f32[8,128]{1,0:T(8,128)S(1)} %collective-permute-done.44.refs_1_, ...), custom_call_target="tpu_custom_call" | custom-call | flops 1207959552 | bytes 5828608 | tf_op jit(solution)/shard_map/mixer_back/pallas_call | solution.py:36
  189.8 3.5 %all-to-all-start.3 = ((bf16[8,32,1152]{2,1,0:T(8,128)(2,1)}), bf16[8,32,1152]{2,1,0:T(8,128)(2,1)S(1)}, u32[]{:S(2)}, u32[]{:S(2)}) async-start(bf16[8,32,1152]{2,1,0:T(8,128)(2,1)} %bitcast.51), calls=%async_computation.4 | async-start | bytes 1179648 | tf_op jit(solution)/shard_map/all_to_all | solution.py:180
  195.3 2.0 out_back.1
  199.3 4.2 %collective-permute-done.46 = bf16[256,384]{1,0:T(8,128)(2,1)} collective-permute-done((bf16[256,384]{1,0:T(8,128)(2,1)}, bf16[256,384]{1,0:T(8,128)(2,1)}, u32[]{:S(2)}, u32[]{:S(2)}) %collective-permute-start.46) | collective-permute-done | bytes 196640 | tf_op jit(solution)/shard_map/ppermute | solution.py:127
  203.5 1.7 add_convert_fusion.3
  205.2 2.8 %reduce-scatter.5.cloned.1.call-done = bf16[144,1024]{1,0:T(8,128)(2,1)} async-done(((bf16[576,1024]{1,0:T(8,128)(2,1)}), bf16[144,1024]{1,0:T(8,128)(2,1)}) %reduce-scatter.5.cloned.1.call-update) | async-done | bytes 294928 | tf_op jit(solution)/shard_map/reduce_scatter | solution.py:839
  208.0 1.5 collective-permute-start.48
  209.5 1.5 collective-permute-start.49
  211.0 1.7 collective-permute-start.51
  212.8 3.2 %mixer_back_sum.1 = (f32[128,1024]{1,0:T(8,128)S(1)}, bf16[128,1024]{1,0:T(8,128)(2,1)}, bf16[128,1024]{1,0:T(8,128)(2,1)}, bf16[128,1024]{1,0:T(8,128)(2,1)}) custom-call(bf16[1024,384]{1,0:T(8,128)(2,1)} %get-tuple-element.642.left_in, bf16[1024,384]{1,0:T(8,128)(2,1)} %get-tuple-element.643.refs_6_.right_in, ...), custom_call_target="tpu_custom_call" | custom-call | flops 402653184 | bytes 2621440 | tf_op jit(solution)/shard_map/mixer_back_sum/pallas_call | solution.py:36
  216.0 5.0 %collective-permute-done.51 = bf16[48,1024]{1,0:T(8,128)(2,1)S(1)} collective-permute-done((bf16[48,1024]{1,0:T(8,128)(2,1)}, bf16[48,1024]{1,0:T(8,128)(2,1)S(1)}, u32[]{:S(2)}, u32[]{:S(2)}) %collective-permute-start.51) | collective-permute-done | bytes 98336 | tf_op jit(solution)/shard_map/ppermute | solution.py:127
  221.1 1.0 add_convert_fusion.2
  223.6 1.5 collective-permute-start.53
  225.1 1.5 collective-permute-start.54
  226.6 4.5 %collective-permute-done.56 = bf16[48,1024]{1,0:T(8,128)(2,1)S(1)} collective-permute-done((bf16[48,1024]{1,0:T(8,128)(2,1)S(1)}, bf16[48,1024]{1,0:T(8,128)(2,1)S(1)}, u32[]{:S(2)}, u32[]{:S(2)}) %collective-permute-start.56) | collective-permute-done | bytes 98336 | tf_op jit(solution)/shard_map/ppermute | solution.py:127
  231.9 3.5 %all-to-all-start.4 = ((bf16[8,32,384]{2,1,0:T(8,128)(2,1)}), bf16[8,32,384]{2,1,0:T(8,128)(2,1)S(1)}, u32[]{:S(2)}, u32[]{:S(2)}) async-start(bf16[8,32,384]{2,1,0:T(8,128)(2,1)} %bitcast.50), calls=%async_computation.6 | async-start | bytes 393216 | tf_op jit(solution)/shard_map/all_to_all | solution.py:180
  235.5 2.2 add_convert_fusion
  237.8 1.4 pair_finish.1
  239.3 2.4 all-to-all-done.4.blocks
  243.0 1.4 fusion.2
  244.4 2.3 fusion.5
  246.6 1.0 in_finish.1
  (238 shorter events, 31.5 us)
Async XLA Ops:
  7.2 106.9 %all-gather.6.cloned.1.call-start = ((), (), s32[]{:S(2)}) async-start(), calls=%async_computation.10 | async-start | bytes 1474560 | tf_op jit(solution)/shard_map/all_gather | solution.py:836
  12.5 19.2 %collective-permute-start = (bf16[128,1024]{1,0:T(8,128)(2,1)}, bf16[128,1024]{1,0:T(8,128)(2,1)S(1)}, u32[]{:S(2)}, u32[]{:S(2)}) collective-permute-start(bf16[128,1024]{1,0:T(8,128)(2,1)} %refs_16_), channel_id=1, source_target_pairs={{0,2},{1,3},{2,0},{3,1},{4,6},{5,7},{6,4},{7,5},{8,10},{9,11},{10,... | collective-permute-start | bytes 786440 | tf_op jit(solution)/shard_map/ppermute | solution.py:127
  15.4 16.2 %collective-permute-start.1 = (bf16[128,1024]{1,0:T(8,128)(2,1)}, bf16[128,1024]{1,0:T(8,128)(2,1)S(1)}, u32[]{:S(2)}, u32[]{:S(2)}) collective-permute-start(bf16[128,1024]{1,0:T(8,128)(2,1)} %refs_16_), channel_id=1, source_target_pairs={{0,4},{1,5},{2,6},{3,7},{4,0},{5,1},{6,2},{7,3},{8,12},{9,13},{10,... | collective-permute-start | bytes 786440 | tf_op jit(solution)/shard_map/ppermute | solution.py:127
  16.9 14.7 %collective-permute-start.2 = (bf16[128,1024]{1,0:T(8,128)(2,1)}, bf16[128,1024]{1,0:T(8,128)(2,1)S(1)}, u32[]{:S(2)}, u32[]{:S(2)}) collective-permute-start(bf16[128,1024]{1,0:T(8,128)(2,1)} %refs_16_), channel_id=1, source_target_pairs={{0,6},{1,7},{2,4},{3,5},{4,2},{5,3},{6,0},{7,1},{8,14},{9,15},{10,... | collective-permute-start | bytes 786440 | tf_op jit(solution)/shard_map/ppermute | solution.py:127
  16.9 14.8 %collective-permute-start.3 = (bf16[128,1024]{1,0:T(8,128)(2,1)}, bf16[128,1024]{1,0:T(8,128)(2,1)S(1)}, u32[]{:S(2)}, u32[]{:S(2)}) collective-permute-start(bf16[128,1024]{1,0:T(8,128)(2,1)} %refs_16_), channel_id=1, source_target_pairs={{0,1},{1,0},{2,3},{3,2},{4,5},{5,4},{6,7},{7,6},{8,9},{9,8},{10,11... | collective-permute-start | bytes 786440 | tf_op jit(solution)/shard_map/ppermute | solution.py:127
  16.9 14.7 %all-to-all-start = ((bf16[8,40,384]{2,1,0:T(8,128)(2,1)}), bf16[8,40,384]{2,1,0:T(8,128)(2,1)S(1)}, u32[]{:S(2)}, u32[]{:S(2)}) async-start(bf16[8,40,384]{2,1,0:T(8,128)(2,1)} %in_prepare.1), calls=%async_computation | async-start | bytes 491520 | tf_op jit(solution)/shard_map/all_to_all | solution.py:180
  31.7 30.0 %all-to-all-start.1 = ((bf16[8,32,1152]{2,1,0:T(8,128)(2,1)}), bf16[8,32,1152]{2,1,0:T(8,128)(2,1)S(1)}, u32[]{:S(2)}, u32[]{:S(2)}) async-start(bf16[8,32,1152]{2,1,0:T(8,128)(2,1)} %pair_prepare.1), calls=%async_computation.1 | async-start | bytes 1179648 | tf_op jit(solution)/shard_map/all_to_all | solution.py:180
  35.4 78.6 %all-gather.4.cloned.1.call-start = ((), (), s32[]{:S(2)}) async-start(), calls=%async_computation.7 | async-start | bytes 2949120 | tf_op jit(solution)/shard_map/all_gather | solution.py:836
  35.5 26.2 %collective-permute-start.4 = (bf16[128,1024]{1,0:T(8,128)(2,1)S(1)}, bf16[128,1024]{1,0:T(8,128)(2,1)S(1)}, u32[]{:S(2)}, u32[]{:S(2)}) collective-permute-start(bf16[128,1024]{1,0:T(8,128)(2,1)S(1)} %collective-permute-done.refs_2_.refs_18_), channel_id=1, source_target_pairs={{0,1},{1,0},{2,3},{3,2},{4,5},{5,4},{6,7},{7,6},{8,9},{9,8},{10,11... | collective-permute-start | bytes 786440 | tf_op jit(solution)/shard_map/ppermute | solution.py:127
  35.8 25.9 %collective-permute-start.5 = (bf16[128,1024]{1,0:T(8,128)(2,1)S(1)}, bf16[128,1024]{1,0:T(8,128)(2,1)S(1)}, u32[]{:S(2)}, u32[]{:S(2)}) collective-permute-start(bf16[128,1024]{1,0:T(8,128)(2,1)S(1)} %collective-permute-done.1.refs_4_.refs_20_), channel_id=1, source_target_pairs={{0,1},{1,0},{2,3},{3,2},{4,5},{5,4},{6,7},{7,6},{8,9},{9,8},{10,11... | collective-permute-start | bytes 786440 | tf_op jit(solution)/shard_map/ppermute | solution.py:127
  36.0 25.7 %collective-permute-start.6 = (bf16[128,1024]{1,0:T(8,128)(2,1)S(1)}, bf16[128,1024]{1,0:T(8,128)(2,1)S(1)}, u32[]{:S(2)}, u32[]{:S(2)}) collective-permute-start(bf16[128,1024]{1,0:T(8,128)(2,1)S(1)} %collective-permute-done.2.refs_6_.refs_22_), channel_id=1, source_target_pairs={{0,1},{1,0},{2,3},{3,2},{4,5},{5,4},{6,7},{7,6},{8,9},{9,8},{10,11... | collective-permute-start | bytes 786440 | tf_op jit(solution)/shard_map/ppermute | solution.py:127
  36.3 25.3 %collective-permute-start.7 = (bf16[32,1024]{1,0:T(8,128)(2,1)S(1)}, bf16[32,1024]{1,0:T(8,128)(2,1)S(1)}, u32[]{:S(2)}, u32[]{:S(2)}) collective-permute-start(bf16[32,1024]{1,0:T(8,128)(2,1)S(1)} %bitcast.52), channel_id=1, source_target_pairs={{0,8},{1,9},{2,10},{3,11},{4,12},{5,13},{6,14},{7,15},{8,16},{9,17... | collective-permute-start | bytes 196616 | tf_op jit(solution)/shard_map/ppermute | solution.py:127
  37.9 23.7 %collective-permute-start.8 = (bf16[32,1024]{1,0:T(8,128)(2,1)S(1)}, bf16[32,1024]{1,0:T(8,128)(2,1)S(1)}, u32[]{:S(2)}, u32[]{:S(2)}) collective-permute-start(bf16[32,1024]{1,0:T(8,128)(2,1)S(1)} %bitcast.53), channel_id=1, source_target_pairs={{0,24},{1,25},{2,26},{3,27},{4,28},{5,29},{6,30},{7,31},{8,0},{9,1... | collective-permute-start | bytes 196616 | tf_op jit(solution)/shard_map/ppermute | solution.py:127
  62.6 126.5 %reduce-scatter.3.cloned.1.call-start = ((), (), s32[]{:S(2)}) async-start(), calls=%async_computation.8 | async-start | bytes 2949120 | tf_op jit(solution)/shard_map/reduce_scatter | solution.py:839
  62.8 10.2 %collective-permute-start.10 = (bf16[128,1024]{1,0:T(8,128)(2,1)S(1)}, bf16[128,1024]{1,0:T(8,128)(2,1)S(1)}, u32[]{:S(2)}, u32[]{:S(2)}) collective-permute-start(bf16[128,1024]{1,0:T(8,128)(2,1)S(1)} %copy-done.9), channel_id=1, source_target_pairs={{0,2},{1,3},{2,0},{3,1},{4,6},{5,7},{6,4},{7,5},{8,10},{9,11},{10,... | collective-permute-start | bytes 786440 | tf_op jit(solution)/shard_map/ppermute | solution.py:127
  64.4 8.6 %collective-permute-start.11 = (bf16[128,1024]{1,0:T(8,128)(2,1)S(1)}, bf16[128,1024]{1,0:T(8,128)(2,1)S(1)}, u32[]{:S(2)}, u32[]{:S(2)}) collective-permute-start(bf16[128,1024]{1,0:T(8,128)(2,1)S(1)} %copy-done.9), channel_id=1, source_target_pairs={{0,4},{1,5},{2,6},{3,7},{4,0},{5,1},{6,2},{7,3},{8,12},{9,13},{10,... | collective-permute-start | bytes 786440 | tf_op jit(solution)/shard_map/ppermute | solution.py:127
  65.9 7.1 %collective-permute-start.12 = (bf16[128,1024]{1,0:T(8,128)(2,1)S(1)}, bf16[128,1024]{1,0:T(8,128)(2,1)S(1)}, u32[]{:S(2)}, u32[]{:S(2)}) collective-permute-start(bf16[128,1024]{1,0:T(8,128)(2,1)S(1)} %copy-done.9), channel_id=1, source_target_pairs={{0,1},{1,0},{2,3},{3,2},{4,5},{5,4},{6,7},{7,6},{8,9},{9,8},{10,11... | collective-permute-start | bytes 786440 | tf_op jit(solution)/shard_map/ppermute | solution.py:127
  65.9 7.1 %collective-permute-start.9 = (bf16[32,1024]{1,0:T(8,128)(2,1)S(1)}, bf16[32,1024]{1,0:T(8,128)(2,1)S(1)}, u32[]{:S(2)}, u32[]{:S(2)}) collective-permute-start(bf16[32,1024]{1,0:T(8,128)(2,1)S(1)} %collective-permute-done.7), channel_id=1, source_target_pairs={{0,8},{1,9},{2,10},{3,11},{4,12},{5,13},{6,14},{7,15},{8,16},{9,17... | collective-permute-start | bytes 196616 | tf_op jit(solution)/shard_map/ppermute | solution.py:127
  65.9 7.1 %collective-permute-start.13 = (bf16[16,1024]{1,0:T(8,128)(2,1)S(1)}, bf16[16,1024]{1,0:T(8,128)(2,1)S(1)}, u32[]{:S(2)}, u32[]{:S(2)}) collective-permute-start(bf16[16,1024]{1,0:T(8,128)(2,1)S(1)} %select_select_fusion), channel_id=1, source_target_pairs={{0,8},{1,9},{2,10},{3,11},{4,12},{5,13},{6,14},{7,15},{8,16},{9,17... | collective-permute-start | bytes 98312 | tf_op jit(solution)/shard_map/ppermute | solution.py:127
  73.8 7.9 %collective-permute-start.14 = (bf16[128,1024]{1,0:T(8,128)(2,1)S(1)}, bf16[128,1024]{1,0:T(8,128)(2,1)S(1)}, u32[]{:S(2)}, u32[]{:S(2)}) collective-permute-start(bf16[128,1024]{1,0:T(8,128)(2,1)S(1)} %pad_maximum_fusion.refs_8_.refs_0_), channel_id=1, source_target_pairs={{0,2},{1,3},{2,0},{3,1},{4,6},{5,7},{6,4},{7,5},{8,10},{9,11},{10,... | collective-permute-start | bytes 786440 | tf_op jit(solution)/shard_map/ppermute | solution.py:127
  74.4 7.8 %collective-permute-start.15 = (bf16[128,1024]{1,0:T(8,128)(2,1)S(1)}, bf16[128,1024]{1,0:T(8,128)(2,1)}, u32[]{:S(2)}, u32[]{:S(2)}) collective-permute-start(bf16[128,1024]{1,0:T(8,128)(2,1)S(1)} %pad_maximum_fusion.refs_8_.refs_0_), channel_id=1, source_target_pairs={{0,4},{1,5},{2,6},{3,7},{4,0},{5,1},{6,2},{7,3},{8,12},{9,13},{10,... | collective-permute-start | bytes 786440 | tf_op jit(solution)/shard_map/ppermute | solution.py:127
  74.9 7.3 %collective-permute-start.16 = (bf16[128,1024]{1,0:T(8,128)(2,1)S(1)}, bf16[128,1024]{1,0:T(8,128)(2,1)}, u32[]{:S(2)}, u32[]{:S(2)}) collective-permute-start(bf16[128,1024]{1,0:T(8,128)(2,1)S(1)} %pad_maximum_fusion.refs_8_.refs_0_), channel_id=1, source_target_pairs={{0,1},{1,0},{2,3},{3,2},{4,5},{5,4},{6,7},{7,6},{8,9},{9,8},{10,11... | collective-permute-start | bytes 786440 | tf_op jit(solution)/shard_map/ppermute | solution.py:127
  83.1 8.2 %collective-permute-start.17 = (bf16[128,1024]{1,0:T(8,128)(2,1)S(1)}, bf16[128,1024]{1,0:T(8,128)(2,1)S(1)}, u32[]{:S(2)}, u32[]{:S(2)}) collective-permute-start(bf16[128,1024]{1,0:T(8,128)(2,1)S(1)} %broadcast_select_fusion.2), channel_id=1, source_target_pairs={{0,2},{1,5},{2,0},{3,7},{4,6},{5,1},{6,4},{7,3},{8,10},{9,13},{10,... | collective-permute-start | bytes 786440 | tf_op jit(solution)/shard_map/ppermute | solution.py:127
  84.7 6.7 %collective-permute-start.18 = (bf16[128,1024]{1,0:T(8,128)(2,1)S(1)}, bf16[128,1024]{1,0:T(8,128)(2,1)S(1)}, u32[]{:S(2)}, u32[]{:S(2)}) collective-permute-start(bf16[128,1024]{1,0:T(8,128)(2,1)S(1)} %collective-permute-done.14.refs_10_.refs_2_), channel_id=1, source_target_pairs={{0,1},{1,0},{2,3},{3,2},{4,5},{5,4},{6,7},{7,6},{8,9},{9,8},{10,11... | collective-permute-start | bytes 786440 | tf_op jit(solution)/shard_map/ppermute | solution.py:127
  84.7 6.7 %collective-permute-start.19 = (bf16[128,1024]{1,0:T(8,128)(2,1)}, bf16[128,1024]{1,0:T(8,128)(2,1)S(1)}, u32[]{:S(2)}, u32[]{:S(2)}) collective-permute-start(bf16[128,1024]{1,0:T(8,128)(2,1)} %collective-permute-done.15.refs_12_.refs_4_), channel_id=1, source_target_pairs={{0,1},{1,0},{2,3},{3,2},{4,5},{5,4},{6,7},{7,6},{8,9},{9,8},{10,11... | collective-permute-start | bytes 786440 | tf_op jit(solution)/shard_map/ppermute | solution.py:127
  85.2 10.0 %collective-permute-start.20 = (bf16[1024,128]{1,0:T(8,128)(2,1)S(1)}, bf16[1024,128]{1,0:T(8,128)(2,1)S(1)}, u32[]{:S(2)}, u32[]{:S(2)}) collective-permute-start(bf16[1024,128]{1,0:T(8,128)(2,1)S(1)} %get-tuple-element.619.refs_0_), channel_id=1, source_target_pairs={{0,2},{1,3},{2,0},{3,1},{4,6},{5,7},{6,4},{7,5},{8,10},{9,11},{10,... | collective-permute-start | bytes 786440 | tf_op jit(solution)/shard_map/ppermute | solution.py:127
  85.7 9.5 %collective-permute-start.21 = (bf16[1024,128]{1,0:T(8,128)(2,1)S(1)}, bf16[1024,128]{1,0:T(8,128)(2,1)S(1)}, u32[]{:S(2)}, u32[]{:S(2)}) collective-permute-start(bf16[1024,128]{1,0:T(8,128)(2,1)S(1)} %get-tuple-element.619.refs_0_), channel_id=1, source_target_pairs={{0,4},{1,5},{2,6},{3,7},{4,0},{5,1},{6,2},{7,3},{8,12},{9,13},{10,... | collective-permute-start | bytes 786440 | tf_op jit(solution)/shard_map/ppermute | solution.py:127
  91.4 3.8 %collective-permute-start.22 = (bf16[1024,128]{1,0:T(8,128)(2,1)S(1)}, bf16[1024,128]{1,0:T(8,128)(2,1)S(1)}, u32[]{:S(2)}, u32[]{:S(2)}) collective-permute-start(bf16[1024,128]{1,0:T(8,128)(2,1)S(1)} %get-tuple-element.619.refs_0_), channel_id=1, source_target_pairs={{0,1},{1,0},{2,3},{3,2},{4,5},{5,4},{6,7},{7,6},{8,9},{9,8},{10,11... | collective-permute-start | bytes 786440 | tf_op jit(solution)/shard_map/ppermute | solution.py:127
  95.2 2.1 collective-permute-start.23
  95.3 6.4 %collective-permute-start.24 = (bf16[1024,128]{1,0:T(8,128)(2,1)S(1)}, bf16[1024,128]{1,0:T(8,128)(2,1)S(1)}, u32[]{:S(2)}, u32[]{:S(2)}) collective-permute-start(bf16[1024,128]{1,0:T(8,128)(2,1)S(1)} %broadcast_select_fusion), channel_id=1, source_target_pairs={{0,2},{1,5},{2,0},{3,7},{4,6},{5,1},{6,4},{7,3},{8,10},{9,13},{10,... | collective-permute-start | bytes 786440 | tf_op jit(solution)/shard_map/ppermute | solution.py:127
  96.9 4.9 %collective-permute-start.25 = (bf16[1024,128]{1,0:T(8,128)(2,1)S(1)}, bf16[1024,128]{1,0:T(8,128)(2,1)S(1)}, u32[]{:S(2)}, u32[]{:S(2)}) collective-permute-start(bf16[1024,128]{1,0:T(8,128)(2,1)S(1)} %collective-permute-done.20.refs_2_), channel_id=1, source_target_pairs={{0,1},{1,0},{2,3},{3,2},{4,5},{5,4},{6,7},{7,6},{8,9},{9,8},{10,11... | collective-permute-start | bytes 786440 | tf_op jit(solution)/shard_map/ppermute | solution.py:127
  96.9 4.9 %collective-permute-start.26 = (bf16[1024,128]{1,0:T(8,128)(2,1)S(1)}, bf16[1024,128]{1,0:T(8,128)(2,1)S(1)}, u32[]{:S(2)}, u32[]{:S(2)}) collective-permute-start(bf16[1024,128]{1,0:T(8,128)(2,1)S(1)} %collective-permute-done.21.refs_4_), channel_id=1, source_target_pairs={{0,1},{1,0},{2,3},{3,2},{4,5},{5,4},{6,7},{7,6},{8,9},{9,8},{10,11... | collective-permute-start | bytes 786440 | tf_op jit(solution)/shard_map/ppermute | solution.py:127
  103.3 8.5 %collective-permute-start.28 = (bf16[128,1024]{1,0:T(8,128)(2,1)S(1)}, bf16[128,1024]{1,0:T(8,128)(2,1)S(1)}, u32[]{:S(2)}, u32[]{:S(2)}) collective-permute-start(bf16[128,1024]{1,0:T(8,128)(2,1)S(1)} %broadcast_select_fusion.3), channel_id=1, source_target_pairs={{0,2},{1,5},{2,0},{3,7},{4,6},{5,1},{6,4},{7,3},{8,10},{9,13},{10,... | collective-permute-start | bytes 786440 | tf_op jit(solution)/shard_map/ppermute | solution.py:127
  104.8 7.1 %collective-permute-start.29 = (bf16[128,1024]{1,0:T(8,128)(2,1)S(1)}, bf16[128,1024]{1,0:T(8,128)(2,1)S(1)}, u32[]{:S(2)}, u32[]{:S(2)}) collective-permute-start(bf16[128,1024]{1,0:T(8,128)(2,1)S(1)} %collective-permute-done.10.refs_5_.refs_7_), channel_id=1, source_target_pairs={{0,1},{1,0},{2,3},{3,2},{4,5},{5,4},{6,7},{7,6},{8,9},{9,8},{10,11... | collective-permute-start | bytes 786440 | tf_op jit(solution)/shard_map/ppermute | solution.py:127
  104.8 7.1 %collective-permute-start.30 = (bf16[128,1024]{1,0:T(8,128)(2,1)S(1)}, bf16[128,1024]{1,0:T(8,128)(2,1)S(1)}, u32[]{:S(2)}, u32[]{:S(2)}) collective-permute-start(bf16[128,1024]{1,0:T(8,128)(2,1)S(1)} %collective-permute-done.11.refs_6_.refs_8_), channel_id=1, source_target_pairs={{0,1},{1,0},{2,3},{3,2},{4,5},{5,4},{6,7},{7,6},{8,9},{9,8},{10,11... | collective-permute-start | bytes 786440 | tf_op jit(solution)/shard_map/ppermute | solution.py:127
  127.7 80.3 %reduce-scatter.5.cloned.1.call-start = ((), (), s32[]{:S(2)}) async-start(), calls=%async_computation.9 | async-start | bytes 1474560 | tf_op jit(solution)/shard_map/reduce_scatter | solution.py:839
  127.8 3.3 %collective-permute-start.32 = (bf16[512,1024]{1,0:T(8,128)(2,1)}, bf16[512,1024]{1,0:T(8,128)(2,1)S(1)}, u32[]{:S(2)}, u32[]{:S(2)}) collective-permute-start(bf16[512,1024]{1,0:T(8,128)(2,1)} %get-tuple-element.504), channel_id=1, source_target_pairs={{0,1},{1,0},{2,3},{3,2},{4,5},{5,4},{6,7},{7,6},{8,9},{9,8},{10,11... | collective-permute-start | bytes 3145736 | tf_op jit(solution)/shard_map/ppermute | solution.py:127
  131.1 6.5 %collective-permute-start.33 = (bf16[512,1024]{1,0:T(8,128)(2,1)S(1)}, bf16[512,1024]{1,0:T(8,128)(2,1)S(1)}, u32[]{:S(2)}, u32[]{:S(2)}) collective-permute-start(bf16[512,1024]{1,0:T(8,128)(2,1)S(1)} %ffn_output.1), channel_id=1, source_target_pairs={{0,1},{1,0},{2,3},{3,2},{4,5},{5,4},{6,7},{7,6},{8,9},{9,8},{10,11... | collective-permute-start | bytes 3145736 | tf_op jit(solution)/shard_map/ppermute | solution.py:127
  137.6 11.7 %collective-permute-start.34 = (bf16[128,1024]{1,0:T(8,128)(2,1)}, bf16[128,1024]{1,0:T(8,128)(2,1)}, u32[]{:S(2)}, u32[]{:S(2)}) collective-permute-start(bf16[128,1024]{1,0:T(8,128)(2,1)} %get-tuple-element.522), channel_id=1, source_target_pairs={{0,6},{1,7},{2,4},{3,5},{4,2},{5,3},{6,0},{7,1},{8,14},{9,15},{10,... | collective-permute-start | bytes 786440 | tf_op jit(solution)/shard_map/ppermute | solution.py:127
  138.9 13.6 %collective-permute-start.35 = (bf16[128,1024]{1,0:T(8,128)(2,1)}, bf16[128,1024]{1,0:T(8,128)(2,1)}, u32[]{:S(2)}, u32[]{:S(2)}) collective-permute-start(bf16[128,1024]{1,0:T(8,128)(2,1)} %get-tuple-element.523), channel_id=1, source_target_pairs={{0,2},{1,3},{2,0},{3,1},{4,6},{5,7},{6,4},{7,5},{8,10},{9,11},{10,... | collective-permute-start | bytes 786440 | tf_op jit(solution)/shard_map/ppermute | solution.py:127
  140.2 12.6 %collective-permute-start.36 = (bf16[128,1024]{1,0:T(8,128)(2,1)}, bf16[128,1024]{1,0:T(8,128)(2,1)}, u32[]{:S(2)}, u32[]{:S(2)}) collective-permute-start(bf16[128,1024]{1,0:T(8,128)(2,1)} %get-tuple-element.524), channel_id=1, source_target_pairs={{0,4},{1,5},{2,6},{3,7},{4,0},{5,1},{6,2},{7,3},{8,12},{9,13},{10,... | collective-permute-start | bytes 786440 | tf_op jit(solution)/shard_map/ppermute | solution.py:127
  157.5 11.7 %collective-permute-start.37 = (bf16[128,1024]{1,0:T(8,128)(2,1)S(1)}, bf16[128,1024]{1,0:T(8,128)(2,1)S(1)}, u32[]{:S(2)}, u32[]{:S(2)}) collective-permute-start(bf16[128,1024]{1,0:T(8,128)(2,1)S(1)} %get-tuple-element.620.refs_1_), channel_id=1, source_target_pairs={{0,2},{1,3},{2,0},{3,1},{4,6},{5,7},{6,4},{7,5},{8,10},{9,11},{10,... | collective-permute-start | bytes 786440 | tf_op jit(solution)/shard_map/ppermute | solution.py:127
  158.4 10.8 %collective-permute-start.38 = (bf16[128,1024]{1,0:T(8,128)(2,1)S(1)}, bf16[128,1024]{1,0:T(8,128)(2,1)S(1)}, u32[]{:S(2)}, u32[]{:S(2)}) collective-permute-start(bf16[128,1024]{1,0:T(8,128)(2,1)S(1)} %get-tuple-element.620.refs_1_), channel_id=1, source_target_pairs={{0,4},{1,5},{2,6},{3,7},{4,0},{5,1},{6,2},{7,3},{8,12},{9,13},{10,... | collective-permute-start | bytes 786440 | tf_op jit(solution)/shard_map/ppermute | solution.py:127
  159.5 9.7 %collective-permute-start.39 = (bf16[128,1024]{1,0:T(8,128)(2,1)S(1)}, bf16[128,1024]{1,0:T(8,128)(2,1)S(1)}, u32[]{:S(2)}, u32[]{:S(2)}) collective-permute-start(bf16[128,1024]{1,0:T(8,128)(2,1)S(1)} %get-tuple-element.620.refs_1_), channel_id=1, source_target_pairs={{0,1},{1,0},{2,3},{3,2},{4,5},{5,4},{6,7},{7,6},{8,9},{9,8},{10,11... | collective-permute-start | bytes 786440 | tf_op jit(solution)/shard_map/ppermute | solution.py:127
  171.4 8.6 %collective-permute-start.40 = (bf16[128,1024]{1,0:T(8,128)(2,1)S(1)}, bf16[128,1024]{1,0:T(8,128)(2,1)S(1)}, u32[]{:S(2)}, u32[]{:S(2)}) collective-permute-start(bf16[128,1024]{1,0:T(8,128)(2,1)S(1)} %get-tuple-element.585), channel_id=1, source_target_pairs={{0,6},{1,7},{2,4},{3,5},{4,2},{5,3},{6,0},{7,1},{8,14},{9,15},{10,... | collective-permute-start | bytes 786440 | tf_op jit(solution)/shard_map/ppermute | solution.py:127
  173.3 9.1 %collective-permute-start.41 = (bf16[128,1024]{1,0:T(8,128)(2,1)S(1)}, bf16[128,1024]{1,0:T(8,128)(2,1)S(1)}, u32[]{:S(2)}, u32[]{:S(2)}) collective-permute-start(bf16[128,1024]{1,0:T(8,128)(2,1)S(1)} %broadcast_select_fusion.1), channel_id=1, source_target_pairs={{0,2},{1,5},{2,0},{3,7},{4,6},{5,1},{6,4},{7,3},{8,10},{9,13},{10,... | collective-permute-start | bytes 786440 | tf_op jit(solution)/shard_map/ppermute | solution.py:127
  174.1 8.3 %collective-permute-start.42 = (bf16[128,1024]{1,0:T(8,128)(2,1)S(1)}, bf16[128,1024]{1,0:T(8,128)(2,1)S(1)}, u32[]{:S(2)}, u32[]{:S(2)}) collective-permute-start(bf16[128,1024]{1,0:T(8,128)(2,1)S(1)} %collective-permute-done.37.refs_3_), channel_id=1, source_target_pairs={{0,1},{1,0},{2,3},{3,2},{4,5},{5,4},{6,7},{7,6},{8,9},{9,8},{10,11... | collective-permute-start | bytes 786440 | tf_op jit(solution)/shard_map/ppermute | solution.py:127
  174.1 9.1 %collective-permute-start.43 = (bf16[128,1024]{1,0:T(8,128)(2,1)S(1)}, bf16[128,1024]{1,0:T(8,128)(2,1)S(1)}, u32[]{:S(2)}, u32[]{:S(2)}) collective-permute-start(bf16[128,1024]{1,0:T(8,128)(2,1)S(1)} %collective-permute-done.38.refs_5_), channel_id=1, source_target_pairs={{0,1},{1,0},{2,3},{3,2},{4,5},{5,4},{6,7},{7,6},{8,9},{9,8},{10,11... | collective-permute-start | bytes 786440 | tf_op jit(solution)/shard_map/ppermute | solution.py:127
  174.6 5.5 %collective-permute-start.44 = (f32[8,128]{1,0:T(8,128)S(1)}, f32[8,128]{1,0:T(8,128)S(1)}, u32[]{:S(2)}, u32[]{:S(2)}) collective-permute-start(f32[8,128]{1,0:T(8,128)S(1)} %get-tuple-element.589), channel_id=1, source_target_pairs={{8,0},{9,1},{10,2},{11,3},{12,4},{13,5},{14,6},{15,7},{16,8},{17,9... | collective-permute-start | bytes 12296 | tf_op jit(solution)/shard_map/ppermute | solution.py:127
  183.1 6.0 %collective-permute-start.45 = (bf16[128,1024]{1,0:T(8,128)(2,1)S(1)}, bf16[128,1024]{1,0:T(8,128)(2,1)S(1)}, u32[]{:S(2)}, u32[]{:S(2)}) collective-permute-start(bf16[128,1024]{1,0:T(8,128)(2,1)S(1)} %collective-permute-done.41.refs_7_), channel_id=1, source_target_pairs={{0,1},{1,0},{2,3},{3,2},{4,5},{5,4},{6,7},{7,6},{8,9},{9,8},{10,11... | collective-permute-start | bytes 786440 | tf_op jit(solution)/shard_map/ppermute | solution.py:127
  189.1 14.4 %collective-permute-start.47 = (bf16[512,1024]{1,0:T(8,128)(2,1)}, bf16[512,1024]{1,0:T(8,128)(2,1)}, u32[]{:S(2)}, u32[]{:S(2)}) collective-permute-start(bf16[512,1024]{1,0:T(8,128)(2,1)} %get-tuple-element.618), channel_id=1, source_target_pairs={{0,1},{1,0},{2,3},{3,2},{4,5},{5,4},{6,7},{7,6},{8,9},{9,8},{10,11... | collective-permute-start | bytes 3145736 | tf_op jit(solution)/shard_map/ppermute | solution.py:127
  189.6 13.9 %collective-permute-start.46 = (bf16[256,384]{1,0:T(8,128)(2,1)}, bf16[256,384]{1,0:T(8,128)(2,1)}, u32[]{:S(2)}, u32[]{:S(2)}) collective-permute-start(bf16[256,384]{1,0:T(8,128)(2,1)} %get-tuple-element.617), channel_id=1, source_target_pairs={{0,8},{1,9},{2,10},{3,11},{4,12},{5,13},{6,14},{7,15},{8,16},{9,17... | collective-permute-start | bytes 589832 | tf_op jit(solution)/shard_map/ppermute | solution.py:127
  189.8 26.1 %all-to-all-start.3 = ((bf16[8,32,1152]{2,1,0:T(8,128)(2,1)}), bf16[8,32,1152]{2,1,0:T(8,128)(2,1)S(1)}, u32[]{:S(2)}, u32[]{:S(2)}) async-start(bf16[8,32,1152]{2,1,0:T(8,128)(2,1)} %bitcast.51), calls=%async_computation.4 | async-start | bytes 1179648 | tf_op jit(solution)/shard_map/all_to_all | solution.py:180
  208.0 13.0 %collective-permute-start.48 = (bf16[128,1024]{1,0:T(8,128)(2,1)}, bf16[128,1024]{1,0:T(8,128)(2,1)}, u32[]{:S(2)}, u32[]{:S(2)}) collective-permute-start(bf16[128,1024]{1,0:T(8,128)(2,1)} %copy-done.39), channel_id=1, source_target_pairs={{0,2},{1,3},{2,0},{3,1},{4,6},{5,7},{6,4},{7,5},{8,10},{9,11},{10,... | collective-permute-start | bytes 786440 | tf_op jit(solution)/shard_map/ppermute | solution.py:127
  209.5 11.5 %collective-permute-start.49 = (bf16[128,1024]{1,0:T(8,128)(2,1)}, bf16[128,1024]{1,0:T(8,128)(2,1)}, u32[]{:S(2)}, u32[]{:S(2)}) collective-permute-start(bf16[128,1024]{1,0:T(8,128)(2,1)} %copy-done.38), channel_id=1, source_target_pairs={{0,4},{1,5},{2,6},{3,7},{4,0},{5,1},{6,2},{7,3},{8,12},{9,13},{10,... | collective-permute-start | bytes 786440 | tf_op jit(solution)/shard_map/ppermute | solution.py:127
  211.0 10.0 %collective-permute-start.50 = (bf16[256,384]{1,0:T(8,128)(2,1)}, bf16[256,384]{1,0:T(8,128)(2,1)}, u32[]{:S(2)}, u32[]{:S(2)}) collective-permute-start(bf16[256,384]{1,0:T(8,128)(2,1)} %add_convert_fusion.3), channel_id=1, source_target_pairs={{0,8},{1,9},{2,10},{3,11},{4,12},{5,13},{6,14},{7,15},{8,16},{9,17... | collective-permute-start | bytes 589832 | tf_op jit(solution)/shard_map/ppermute | solution.py:127
  211.0 10.0 %collective-permute-start.51 = (bf16[48,1024]{1,0:T(8,128)(2,1)}, bf16[48,1024]{1,0:T(8,128)(2,1)S(1)}, u32[]{:S(2)}, u32[]{:S(2)}) collective-permute-start(bf16[48,1024]{1,0:T(8,128)(2,1)} %copy-done.40), channel_id=1, source_target_pairs={{0,8},{1,9},{2,10},{3,11},{4,12},{5,13},{6,14},{7,15},{8,16},{9,17... | collective-permute-start | bytes 294920 | tf_op jit(solution)/shard_map/ppermute | solution.py:127
  222.1 9.1 %collective-permute-start.55 = (bf16[256,384]{1,0:T(8,128)(2,1)S(1)}, bf16[256,384]{1,0:T(8,128)(2,1)S(1)}, u32[]{:S(2)}, u32[]{:S(2)}) collective-permute-start(bf16[256,384]{1,0:T(8,128)(2,1)S(1)} %add_convert_fusion.2), channel_id=1, source_target_pairs={{0,8},{1,9},{2,10},{3,11},{4,12},{5,13},{6,14},{7,15},{8,16},{9,17... | collective-permute-start | bytes 589832 | tf_op jit(solution)/shard_map/ppermute | solution.py:127
  222.1 9.0 %collective-permute-start.56 = (bf16[48,1024]{1,0:T(8,128)(2,1)S(1)}, bf16[48,1024]{1,0:T(8,128)(2,1)S(1)}, u32[]{:S(2)}, u32[]{:S(2)}) collective-permute-start(bf16[48,1024]{1,0:T(8,128)(2,1)S(1)} %add_convert_fusion.5), channel_id=1, source_target_pairs={{0,8},{1,9},{2,10},{3,11},{4,12},{5,13},{6,14},{7,15},{8,16},{9,17... | collective-permute-start | bytes 294920 | tf_op jit(solution)/shard_map/ppermute | solution.py:127
  223.1 16.1 %collective-permute-start.52 = (bf16[128,1024]{1,0:T(8,128)(2,1)}, bf16[128,1024]{1,0:T(8,128)(2,1)}, u32[]{:S(2)}, u32[]{:S(2)}) collective-permute-start(bf16[128,1024]{1,0:T(8,128)(2,1)} %get-tuple-element.659), channel_id=1, source_target_pairs={{0,6},{1,7},{2,4},{3,5},{4,2},{5,3},{6,0},{7,1},{8,14},{9,15},{10,... | collective-permute-start | bytes 786440 | tf_op jit(solution)/shard_map/ppermute | solution.py:127
  223.6 15.6 %collective-permute-start.53 = (bf16[128,1024]{1,0:T(8,128)(2,1)}, bf16[128,1024]{1,0:T(8,128)(2,1)}, u32[]{:S(2)}, u32[]{:S(2)}) collective-permute-start(bf16[128,1024]{1,0:T(8,128)(2,1)} %get-tuple-element.660), channel_id=1, source_target_pairs={{0,2},{1,3},{2,0},{3,1},{4,6},{5,7},{6,4},{7,5},{8,10},{9,11},{10,... | collective-permute-start | bytes 786440 | tf_op jit(solution)/shard_map/ppermute | solution.py:127
  225.1 14.1 %collective-permute-start.54 = (bf16[128,1024]{1,0:T(8,128)(2,1)}, bf16[128,1024]{1,0:T(8,128)(2,1)}, u32[]{:S(2)}, u32[]{:S(2)}) collective-permute-start(bf16[128,1024]{1,0:T(8,128)(2,1)} %get-tuple-element.661), channel_id=1, source_target_pairs={{0,4},{1,5},{2,6},{3,7},{4,0},{5,1},{6,2},{7,3},{8,12},{9,13},{10,... | collective-permute-start | bytes 786440 | tf_op jit(solution)/shard_map/ppermute | solution.py:127
  231.9 7.4 %collective-permute-start.57 = (bf16[48,1024]{1,0:T(8,128)(2,1)S(1)}, bf16[48,1024]{1,0:T(8,128)(2,1)S(1)}, u32[]{:S(2)}, u32[]{:S(2)}) collective-permute-start(bf16[48,1024]{1,0:T(8,128)(2,1)S(1)} %add_convert_fusion.4), channel_id=1, source_target_pairs={{0,8},{1,9},{2,10},{3,11},{4,12},{5,13},{6,14},{7,15},{8,16},{9,17... | collective-permute-start | bytes 294920 | tf_op jit(solution)/shard_map/ppermute | solution.py:127
  231.9 9.7 %all-to-all-start.4 = ((bf16[8,32,384]{2,1,0:T(8,128)(2,1)}), bf16[8,32,384]{2,1,0:T(8,128)(2,1)S(1)}, u32[]{:S(2)}, u32[]{:S(2)}) async-start(bf16[8,32,384]{2,1,0:T(8,128)(2,1)} %bitcast.50), calls=%async_computation.6 | async-start | bytes 393216 | tf_op jit(solution)/shard_map/all_to_all | solution.py:180
  (64 other events, 601.9 us)
Sparse Core Ops, SparseCore 0:
  9.6 35.3 all-gather.5
  62.8 49.3 all-gather.3
  127.8 45.0 reduce-scatter.2
  175.1 32.8 reduce-scatter.4
